TPU v7x, 32 devices: a whole 2x2x4 slice. The times are simulated.
32 devices in a mesh: seq: 8 (over z, x), fsdp: 4 (over y, core).
Axes of the slice: x: 2, y: 2, z: 4, core: 2. Of those that a mesh axis runs over, the one named last changes fastest.
Arguments:
- tokens: bfloat16 [4096, 1024], P(('seq', 'fsdp')), may hold values from -6 to 6
- cotangent: bfloat16 [4096, 1024], P(('seq', 'fsdp')), may hold values from -6 to 6
- seq_lengths: int32 [4], replicated, may hold values from 1 to 2048, 4096 in all
- w_qkv: bfloat16 [1024, 3072], P(('seq', 'fsdp')), may hold values from -0.1875 to 0.1875
- w_attn_out: bfloat16 [1024, 1024], P(('seq', 'fsdp')), may hold values from -0.75 to 0.75
- w_in: bfloat16 [1024, 5248], P(('seq', 'fsdp')), may hold values from -0.1875 to 0.1875
- w_mlp_out: bfloat16 [1024, 2624], P(('seq', 'fsdp')), may hold values from -0.125 to 0.125
- gain_attn: bfloat16 [1024], P(('seq', 'fsdp')), may hold values from 0.5 to 1.5
- gain_mlp: bfloat16 [1024], P(('seq', 'fsdp')), may hold values from 0.5 to 1.5
Outputs:
- output: bfloat16 [4096, 1024], P(('seq', 'fsdp'))
- input_grad: float32 [4096, 1024], P(('seq', 'fsdp'))
- grad_w_qkv: float32 [1024, 3072], P(('seq', 'fsdp'))
- grad_w_attn_out: float32 [1024, 1024], P(('seq', 'fsdp'))
- grad_w_in: float32 [1024, 5248], P(('seq', 'fsdp'))
- grad_w_mlp_out: float32 [1024, 2624], P(('seq', 'fsdp'))
- grad_gain_attn: float32 [1024], P(('seq', 'fsdp'))
- grad_gain_mlp: float32 [1024], P(('seq', 'fsdp'))
Inputs may be any that keep to these rules, and one draw needn't show every extreme that they name: `seq_lengths`: 4 lengths that add up to 4096; the longest is exactly 2048.
All inputs are finite; a program needn't handle non-finite values.
Results may differ from a plain program's by a relative error of at most 0.015.
Values may be sent and summed in bfloat16 or wider, within the bound.
No kernel may reach another device: no remote copies, remote signals or barrier semaphores. Data moves between devices by JAX's collectives and lax.ppermute only.
A program may use at most 256 MiB of HBM per device.

v0:
```python
import jax
import jax.numpy as jnp
from jax import lax
from jax.sharding import PartitionSpec as P

D = 1024
HEADS = 16
HDIM = 64
FF = 2624
HALF = 64


epsilon = 1e-05
masked_score = -1e30


def extended_2(cells, sides, width):
    for axis, dim in sides:
        count = lax.axis_size(axis)
        ends = count - 1
        head = lax.slice_in_dim(cells, 0, width, axis=dim)
        tail = lax.slice_in_dim(cells, cells.shape[dim] - width, cells.shape[dim], axis=dim)
        cells = jnp.concatenate(
            [
                lax.ppermute(tail, axis, [(i, (i + 1) % count) for i in range(ends)]),
                cells,
                lax.ppermute(head, axis, [((i + 1) % count, i) for i in range(ends)]),
            ],
            axis=dim,
        )
    return cells


def normalize(values):
    average = jnp.mean(values, axis=-1, keepdims=True)
    centered = values - average
    variance = jnp.mean(centered * centered, axis=-1, keepdims=True)
    inverse = lax.rsqrt(variance + epsilon)
    return (centered * inverse, inverse)


def norm_back(grad_out, normed, inverse, gain):
    grad_hat = grad_out * gain
    inner = (
        grad_hat
        - jnp.mean(grad_hat, axis=-1, keepdims=True)
        - normed * jnp.mean(grad_hat * normed, axis=-1, keepdims=True)
    )
    return (inverse * inner, jnp.sum(grad_out * normed, axis=0))


def rotate(flat, cosine, sine):
    split = flat.reshape(flat.shape[0], HEADS, HDIM)
    half_dim = HDIM // 2
    turned = jnp.concatenate([-split[..., half_dim:], split[..., :half_dim]], axis=-1)
    return (split * cosine[:, None, :] + turned * sine[:, None, :]).reshape(
        flat.shape[0], HEADS * HDIM
    )


def angles(position):
    freqs = 10000.0 ** (-(jnp.arange(HDIM // 2, dtype=jnp.float32) * 2.0) / HDIM)
    freqs = jnp.concatenate([freqs, freqs])
    turns = position.astype(jnp.float32)[:, None] * freqs[None, :]
    return (jnp.cos(turns), jnp.sin(turns))


def place(index, seq_lengths):
    seg_ends = jnp.cumsum(seq_lengths)
    seg_starts = seg_ends - seq_lengths
    segment = jnp.sum((index[:, None] >= seg_ends[None, :]).astype(jnp.int32), axis=1)
    seg_ids = jnp.arange(seq_lengths.shape[0], dtype=jnp.int32)
    begins = jnp.sum(
        jnp.where(segment[:, None] == seg_ids[None, :], seg_starts[None, :], 0), axis=1
    )
    return (segment, index - begins)


def geglu(gate_in, up_in):
    return jax.nn.gelu(gate_in, approximate=False) * up_in


def over_rows(left, right):
    return lax.dot_general(
        left, right, (((0,), (0,)), ((), ())), preferred_element_type=jnp.float32
    )


def over_cols(left, right):
    return lax.dot_general(
        left, right, (((1,), (1,)), ((), ())), preferred_element_type=jnp.float32
    )


def on_device(
    tokens, cotangent, seq_lengths, w_qkv, w_attn_out, w_in, w_mlp_out, gain_attn, gain_mlp
):
    row_count = tokens.shape[0]
    total = row_count * lax.axis_size(("seq", "fsdp"))
    first_row = lax.axis_index(("seq", "fsdp")) * row_count
    whole = (
        lax.all_gather(w_qkv, ("seq", "fsdp"), axis=0, tiled=True),
        lax.all_gather(w_attn_out, ("seq", "fsdp"), axis=0, tiled=True),
        lax.all_gather(w_in, ("seq", "fsdp"), axis=0, tiled=True),
        lax.all_gather(w_mlp_out, ("seq", "fsdp"), axis=0, tiled=True),
        lax.all_gather(gain_attn, ("seq", "fsdp"), axis=0, tiled=True),
        lax.all_gather(gain_mlp, ("seq", "fsdp"), axis=0, tiled=True),
    )
    qkv_full, attn_full, in_full, mlp_full, gain_one, gain_two = whole
    index = first_row + jnp.arange(row_count, dtype=jnp.int32)
    token_seg, position = place(index, seq_lengths)
    key_index = first_row - HALF + jnp.arange(row_count + 2 * HALF, dtype=jnp.int32)
    key_seg, unused = place(jnp.clip(key_index, 0, total - 1), seq_lengths)
    offset = index[:, None] - key_index[None, :]
    key_valid = (key_index >= 0) & (key_index < total)
    allowed = (
        (token_seg[:, None] == key_seg[None, :]) & (jnp.abs(offset) <= HALF) & key_valid[None, :]
    )
    cosine, sine = angles(position)
    scale = HDIM ** (-0.5)
    source = tokens.astype(jnp.float32)
    normed, inverse = normalize(source)
    attn_gain = gain_one.astype(jnp.float32)
    hidden = (normed * attn_gain).astype(jnp.bfloat16)
    packed = jnp.dot(hidden, qkv_full, preferred_element_type=jnp.float32)
    query = rotate(packed[:, :D], cosine, sine).astype(jnp.bfloat16)
    key_value = jnp.concatenate(
        [rotate(packed[:, D : 2 * D], cosine, sine), packed[:, 2 * D :]], axis=1
    ).astype(jnp.bfloat16)
    extended = extended_2(key_value, ((("seq", "fsdp"), 0),), HALF)
    query_heads = query.reshape(row_count, HEADS, HDIM)
    key_heads = extended[:, :D].reshape(-1, HEADS, HDIM)
    value_heads = extended[:, D:].reshape(-1, HEADS, HDIM)

    def scores_of():
        raw = (
            jnp.einsum("thd,shd->hts", query_heads, key_heads, preferred_element_type=jnp.float32)
            * scale
        )
        return jnp.where(allowed[None], raw, masked_score)

    scores = scores_of()
    peak_score = jnp.max(scores, axis=-1, keepdims=True)
    exponent = jnp.exp(scores - peak_score)
    partition = jnp.sum(exponent, axis=-1, keepdims=True)
    probability = exponent / partition
    log_total = peak_score + jnp.log(partition)
    attended = (
        jnp.einsum(
            "hts,shd->thd",
            probability.astype(jnp.bfloat16),
            value_heads,
            preferred_element_type=jnp.float32,
        )
        .reshape(row_count, D)
        .astype(jnp.bfloat16)
    )
    middle = source + jnp.dot(attended, attn_full, preferred_element_type=jnp.float32)
    normed_mid, inverse_mid = normalize(middle)
    mlp_gain = gain_two.astype(jnp.float32)
    lifted = (normed_mid * mlp_gain).astype(jnp.bfloat16)
    both = jnp.dot(lifted, in_full, preferred_element_type=jnp.float32)
    gate_part = both[:, :FF]
    up_part = both[:, FF:]
    mixed = geglu(gate_part, up_part).astype(jnp.bfloat16)
    output = (middle + over_cols(mixed, mlp_full)).astype(jnp.bfloat16)
    again = (
        lax.all_gather(w_qkv, ("seq", "fsdp"), axis=0, tiled=True),
        lax.all_gather(w_attn_out, ("seq", "fsdp"), axis=0, tiled=True),
        lax.all_gather(w_in, ("seq", "fsdp"), axis=0, tiled=True),
        lax.all_gather(w_mlp_out, ("seq", "fsdp"), axis=0, tiled=True),
    )
    qkv_back, attn_back, in_back, mlp_back = (again[0], again[1], again[2], again[3])
    grad_mlp_w = over_rows(cotangent, mixed)
    grad_mixed = jnp.dot(cotangent, mlp_back, preferred_element_type=jnp.float32)
    unused_value, gelu_back = jax.vjp(geglu, gate_part, up_part)
    grad_gate, grad_up = gelu_back(grad_mixed)
    grad_both = jnp.concatenate([grad_gate, grad_up], axis=1).astype(jnp.bfloat16)
    grad_in_w = over_rows(lifted, grad_both)
    grad_lifted = over_cols(grad_both, in_back)
    back_mid, grad_mlp_gain = norm_back(grad_lifted, normed_mid, inverse_mid, mlp_gain)
    grad_middle = cotangent.astype(jnp.float32) + back_mid
    grad_attn = grad_middle.astype(jnp.bfloat16)
    grad_attn_w = over_rows(attended, grad_attn)
    grad_attended = (
        over_cols(grad_attn, attn_back).astype(jnp.bfloat16).reshape(row_count, HEADS, HDIM)
    )
    prob_again = jnp.exp(scores_of() - log_total)
    grad_prob = jnp.einsum(
        "thd,shd->hts", grad_attended, value_heads, preferred_element_type=jnp.float32
    )
    grad_value = jnp.einsum(
        "hts,thd->shd",
        prob_again.astype(jnp.bfloat16),
        grad_attended,
        preferred_element_type=jnp.float32,
    )
    grad_scores = (
        prob_again * (grad_prob - jnp.sum(grad_prob * prob_again, axis=-1, keepdims=True))
    ).astype(jnp.bfloat16)
    grad_query = (
        jnp.einsum("hts,shd->thd", grad_scores, key_heads, preferred_element_type=jnp.float32)
        * scale
    )
    grad_key = (
        jnp.einsum("hts,thd->shd", grad_scores, query_heads, preferred_element_type=jnp.float32)
        * scale
    )
    grad_extended = jnp.concatenate([grad_key.reshape(-1, D), grad_value.reshape(-1, D)], axis=1)
    widened = extended_2(grad_extended.astype(jnp.bfloat16), ((("seq", "fsdp"), 0),), HALF).astype(
        grad_extended.dtype
    )
    grad_kv = widened[2 * HALF : 2 * HALF + row_count]
    grad_kv = grad_kv + jnp.pad(widened[:HALF], ((0, row_count - HALF), (0, 0)))
    grad_kv = grad_kv + jnp.pad(widened[row_count + 3 * HALF :], ((row_count - HALF, 0), (0, 0)))
    unused_turn, turn_back = jax.vjp(
        lambda query_in, key_in: (rotate(query_in, cosine, sine), rotate(key_in, cosine, sine)),
        packed[:, :D],
        packed[:, D : 2 * D],
    )
    grad_q_in, grad_k_in = turn_back((grad_query.reshape(row_count, D), grad_kv[:, :D]))
    grad_packed = jnp.concatenate([grad_q_in, grad_k_in, grad_kv[:, D:]], axis=1).astype(
        jnp.bfloat16
    )
    grad_qkv_w = over_rows(hidden, grad_packed)
    grad_hidden = over_cols(grad_packed, qkv_back)
    back_in, grad_attn_gain = norm_back(grad_hidden, normed, inverse, attn_gain)
    input_grad = grad_middle + back_in
    summed = (
        lax.psum_scatter(grad_qkv_w, ("seq", "fsdp"), scatter_dimension=0, tiled=True),
        lax.psum_scatter(grad_attn_w, ("seq", "fsdp"), scatter_dimension=0, tiled=True),
        lax.psum_scatter(grad_in_w, ("seq", "fsdp"), scatter_dimension=0, tiled=True),
        lax.psum_scatter(grad_mlp_w, ("seq", "fsdp"), scatter_dimension=0, tiled=True),
        lax.psum_scatter(grad_attn_gain, ("seq", "fsdp"), scatter_dimension=0, tiled=True),
        lax.psum_scatter(grad_mlp_gain, ("seq", "fsdp"), scatter_dimension=0, tiled=True),
    )
    return (output, input_grad, summed[0], summed[1], summed[2], summed[3], summed[4], summed[5])


def solution(mesh):
    in_specs = (
        P(("seq", "fsdp"), None),
        P(("seq", "fsdp"), None),
        P(),
        P(("seq", "fsdp"), None),
        P(("seq", "fsdp"), None),
        P(("seq", "fsdp"), None),
        P(("seq", "fsdp"), None),
        P(("seq", "fsdp")),
        P(("seq", "fsdp")),
    )
    out_specs = (
        P(("seq", "fsdp"), None),
        P(("seq", "fsdp"), None),
        P(("seq", "fsdp"), None),
        P(("seq", "fsdp"), None),
        P(("seq", "fsdp"), None),
        P(("seq", "fsdp"), None),
        P(("seq", "fsdp")),
        P(("seq", "fsdp")),
    )
    return jax.shard_map(
        on_device, mesh=mesh, in_specs=in_specs, out_specs=out_specs, check_vma=False
    )
```

profile of v0, /device:TPU:0, one launch (start us, length us, event | category | flops | bytes accessed | tf_op | source)
XLA Modules:
  0.0 1003.6 jit_solution(8506481332830666182)
XLA Ops:
  10.0 0.8 dynamic-update-slice
  10.9 0.8 dynamic-update-slice.1
  11.7 42.5 %all-reduce.10 = (bf16[1024]{0:T(1024)(128)(2,1)S(1)}, bf16[1024]{0:T(1024)(128)(2,1)S(1)}) all-reduce(bf16[1024]{0:T(1024)(128)(2,1)S(1)} %dynamic-update-slice, bf16[1024]{0:T(1024)(128)(2,1)S(1)} %dynamic-update-slice.1), channel_id=1, replica_groups=mesh['seq'=8,'fsdp'=4] {'seq','fsdp'}, use_global_device_ids=true, to_apply=%add.5 | all-reduce | flops 2048 | bytes 8192
  57.6 25.8 %all-gather.5.cloned.1.call-done = bf16[1024,3072]{1,0:T(8,128)(2,1)} async-done(((bf16[32,3072]{1,0:T(8,128)(2,1)}), bf16[1024,3072]{1,0:T(8,128)(2,1)}) %all-gather.5.cloned.1.call-update) | async-done | bytes 6291472 | tf_op jit(solution)/shard_map/all_gather | solution.py:102
  83.3 3.8 fusion.45
  87.2 1.0 fusion.49
  88.3 1.2 copy.63
  89.5 2.0 copy.59
  91.6 1.1 slice_negate_fusion.2
  92.7 1.1 maximum_multiply_fusion.1
  93.8 1.2 copy.64
  95.0 2.0 copy.60
  97.0 2.0 add_convert_fusion.3
  99.1 2.2 collective-permute-start
  101.3 1.5 collective-permute-start.1
  102.9 1.1 copy.65
  104.1 1.4 collective-permute-done.1
  105.9 1.0 copy.61
  108.6 1.0 convolution_convert_fusion.2
  109.7 31.5 %all-gather.7.cloned.1.call-done = bf16[1024,1024]{1,0:T(8,128)(2,1)} async-done(((bf16[32,1024]{1,0:T(8,128)(2,1)}), bf16[1024,1024]{1,0:T(8,128)(2,1)}) %all-gather.7.cloned.1.call-update) | async-done | bytes 2097168 | tf_op jit(solution)/shard_map/all_gather | solution.py:103
  141.2 2.1 fusion.54
  143.6 87.1 %all-gather.9.cloned.1.call-done = bf16[1024,5248]{1,0:T(8,128)(2,1)} async-done(((bf16[32,5248]{1,0:T(8,128)(2,1)}), bf16[1024,5248]{1,0:T(8,128)(2,1)}) %all-gather.9.cloned.1.call-update) | async-done | bytes 10747920 | tf_op jit(solution)/shard_map/all_gather | solution.py:104
  230.7 7.3 fusion.47
  238.0 60.2 %all-gather.11.cloned.1.call-done = bf16[1024,2624]{1,0:T(8,128)(2,1)} async-done(((bf16[32,2624]{1,0:T(8,128)(2,1)}), bf16[1024,2624]{1,0:T(8,128)(2,1)}) %all-gather.11.cloned.1.call-update) | async-done | bytes 5373968 | tf_op jit(solution)/shard_map/all_gather | solution.py:105
  298.1 8.4 add_convert_fusion
  306.6 1.4 multiply_convert_fusion.1
  308.0 5.7 multiply_reduce_fusion.1
  314.6 2.7 fusion.34
  317.4 6.8 convolution_bitcast_fusion
  324.2 11.9 %copy.72 = f32[1024,2624]{1,0:T(8,128)} copy(f32[1024,2624]{0,1:T(8,128)} %convolution_bitcast_fusion) | data formatting | bytes 21495808
  336.4 3.1 convolution_convert_fusion.1
  339.5 1.8 copy.69
  341.3 2.0 multiply_reduce_fusion
  346.1 2.2 collective-permute-start.2
  348.3 1.3 collective-permute-start.3
  350.3 2.7 collective-permute-done.3
  355.6 6.4 fusion.31
  362.2 1.0 copy-done.7
  363.2 10.0 fusion.15
  373.2 1.1 copy-done.3
  374.3 5.2 fusion.10
  379.6 5.1 fusion.28
  384.7 54.9 %all-reduce.9 = (f32[1024]{0:T(1024)S(1)}, f32[1024]{0:T(1024)S(1)}) all-reduce(f32[1024]{0:T(1024)S(1)} %get-tuple-element.42, f32[1024]{0:T(1024)S(1)} %copy-done.29), channel_id=6, replica_groups=mesh['seq'=8,'fsdp'=4] {'seq','fsdp'}, use_global_device_ids=true, to_apply=%region_20.21.clone | all-reduce | flops 2048 | bytes 16384
  440.8 1.0 fusion.27
  441.8 15.9 %reduce-scatter.9.cloned.1.call-done = f32[32,1024]{1,0:T(8,128)} async-done(((f32[1024,1024]{1,0:T(8,128)}), f32[32,1024]{1,0:T(8,128)}) %reduce-scatter.9.cloned.1.call-update) | async-done | bytes 131088 | tf_op jit(solution)/shard_map/reduce_scatter | solution.py:231
  457.7 145.8 %reduce-scatter.13.cloned.1.call-done = f32[32,2624]{1,0:T(8,128)} async-done(((f32[1024,2624]{1,0:T(8,128)}), f32[32,2624]{1,0:T(8,128)}) %reduce-scatter.13.cloned.1.call-update) | async-done | bytes 335888
  603.5 161.0 %reduce-scatter.7.cloned.1.call-done = f32[32,3072]{1,0:T(8,128)} async-done(((f32[1024,3072]{1,0:T(8,128)}), f32[32,3072]{1,0:T(8,128)}) %reduce-scatter.7.cloned.1.call-update) | async-done | bytes 393232 | tf_op jit(solution)/shard_map/reduce_scatter | solution.py:230
  764.5 232.2 %reduce-scatter.11.cloned.1.call-done = f32[32,5248]{1,0:T(8,128)} async-done(((f32[1024,5248]{1,0:T(8,128)}), f32[32,5248]{1,0:T(8,128)}) %reduce-scatter.11.cloned.1.call-update) | async-done | bytes 671760 | tf_op jit(solution)/shard_map/reduce_scatter | solution.py:232
  (142 shorter events, 16.9 us)
Async XLA Ops:
  7.2 50.0 %copy-start.1 = (bf16[128,1024]{1,0:T(8,128)(2,1)S(1)}, bf16[128,1024]{1,0:T(8,128)(2,1)}, u32[]{:S(2)}) copy-start(bf16[128,1024]{1,0:T(8,128)(2,1)} %param.9) | copy-start | bytes 786436
  7.2 76.1 %all-gather.5.cloned.1.call-start = ((), (), s32[]{:S(2)}) async-start(), calls=%async_computation.4 | async-start | bytes 6488064 | tf_op jit(solution)/shard_map/all_gather | solution.py:102
  7.9 133.3 %all-gather.7.cloned.1.call-start = ((), (), s32[]{:S(2)}) async-start(), calls=%async_computation.5 | async-start | bytes 2162688 | tf_op jit(solution)/shard_map/all_gather | solution.py:103
  8.7 222.0 %all-gather.9.cloned.1.call-start = ((), (), s32[]{:S(2)}) async-start(), calls=%async_computation.6 | async-start | bytes 11083776 | tf_op jit(solution)/shard_map/all_gather | solution.py:104
  9.4 288.7 %all-gather.11.cloned.1.call-start = ((), (), s32[]{:S(2)}) async-start(), calls=%async_computation.7 | async-start | bytes 5677056 | tf_op jit(solution)/shard_map/all_gather | solution.py:105
  10.0 447.7 %reduce-scatter.9.cloned.1.call-start = ((), (), s32[]{:S(2)}) async-start(), calls=%async_computation.9 | async-start | bytes 4325376 | tf_op jit(solution)/shard_map/reduce_scatter | solution.py:231
  55.1 0.9 copy-start.31
  55.3 0.8 copy-start.33
  57.3 29.9 %copy-start.23 = (f32[128]{0:T(128)}, f32[128]{0:T(128)S(1)}, u32[]{:S(2)}) copy-start(f32[128]{0:T(128)S(1)} %broadcast_multiply_fusion.9) | copy-start | bytes 1540
  57.6 29.6 %copy-start.27 = (f32[128]{0:T(128)}, f32[128]{0:T(128)S(1)}, u32[]{:S(2)}) copy-start(f32[128]{0:T(128)S(1)} %add_rsqrt_fusion.1) | copy-start | bytes 1540
  97.0 5.7 copy-start.32
  97.0 5.7 copy-start.34
  99.1 5.0 collective-permute-start
  101.3 4.2 collective-permute-start.1
  104.0 2.9 copy-start.8
  105.9 1.6 copy-start.4
  107.5 1.0 copy-start.11
  109.6 33.7 %copy-start.18 = (bf16[16,64,128]{2,1,0:T(8,128)(2,1)}, bf16[16,64,128]{2,1,0:T(8,128)(2,1)S(1)}, u32[]{:S(2)}) copy-start(bf16[16,64,128]{2,1,0:T(8,128)(2,1)S(1)} %convolution_convert_fusion.2) | copy-start | bytes 786436
  143.3 170.3 %copy-start.21 = (f32[128]{0:T(128)}, f32[128]{0:T(128)S(1)}, u32[]{:S(2)}) copy-start(f32[128]{0:T(128)S(1)} %broadcast_multiply_fusion.8) | copy-start | bytes 1540
  143.6 170.1 %copy-start.25 = (f32[128]{0:T(128)}, f32[128]{0:T(128)S(1)}, u32[]{:S(2)}) copy-start(f32[128]{0:T(128)S(1)} %add_rsqrt_fusion) | copy-start | bytes 1540
  143.6 154.6 %copy-start.12 = (bf16[128,1024]{1,0:T(8,128)(2,1)S(1)}, bf16[128,1024]{1,0:T(8,128)(2,1)}, u32[]{:S(2)}) copy-start(bf16[128,1024]{1,0:T(8,128)(2,1)} %param.10) | copy-start | bytes 786436
  298.1 8.4 copy-start.2
  298.1 9.8 copy-start
  308.0 5.7 copy-start.6
  308.0 5.7 copy-start.13
  313.7 1.0 copy-start.19
  317.3 286.2 %reduce-scatter.13.cloned.1.call-start = ((), (), s32[]{:S(2)}) async-start(), calls=%async_computation.11 | async-start | bytes 11354112
  336.1 428.4 %reduce-scatter.7.cloned.1.call-start = ((), (), s32[]{:S(2)}) async-start(), calls=%async_computation.8 | async-start | bytes 12976128 | tf_op jit(solution)/shard_map/reduce_scatter | solution.py:230
  343.3 1.0 copy-start.9
  344.3 0.9 copy-start.10
  345.8 3.8 copy-start.5
  345.8 3.8 copy-start.20
  346.1 4.2 collective-permute-start.2
  348.3 4.6 collective-permute-start.3
  350.3 4.8 copy-start.16
  353.8 0.7 copy-start.30
  354.9 0.7 copy-start.14
  355.0 0.7 copy-start.24
  355.0 0.7 copy-start.28
  362.1 1.1 copy-start.7
  362.1 1.1 copy-start.22
  362.1 1.1 copy-start.26
  362.1 634.6 %reduce-scatter.11.cloned.1.call-start = ((), (), s32[]{:S(2)}) async-start(), calls=%async_computation.10 | async-start | bytes 22167552 | tf_op jit(solution)/shard_map/reduce_scatter | solution.py:232
  373.2 1.1 copy-start.3
  374.3 5.3 copy-start.15
  374.3 5.3 copy-start.17
  379.6 5.1 copy-start.29
Sparse Core Ops, SparseCore 0:
  10.9 72.3 all-gather.4
  86.2 54.9 all-gather.6
  144.0 86.5 all-gather.8
  233.4 64.6 all-gather.10
  317.4 140.2 reduce-scatter.8
  464.1 139.3 reduce-scatter.12
  610.1 154.3 reduce-scatter.6
  767.5 229.1 reduce-scatter.10
where the time goes:
time: 1010 us; the launch traced here: 1000 us
  waiting for transfers between devices  766 us (76%)
  blocking collectives  97.4 us (10%)
  matrix products  71.9 us (7%)
  local copies, waits for them, and re-layouts  32.2 us (3%)
  between operations  14.7 us (1%)
  other arithmetic  13.5 us (1%)
    reduce_scatter x1, waiting for transfers between devices, on_device(): lax.psum_scatter(grad_in_w, ('seq', 'fsdp'), scatter_dimension=0, tiled=T...  232 us
    reduce_scatter x1, waiting for transfers between devices, on_device(): lax.psum_scatter(grad_qkv_w, ('seq', 'fsdp'), scatter_dimension=0, tiled=...  161 us
    unnamed x9, waiting for transfers between devices  148 us
    unnamed x2, blocking collectives  97.4 us
    all_gather x1, waiting for transfers between devices, on_device(): lax.all_gather(w_in, ('seq', 'fsdp'), axis=0, tiled=True)  87.1 us
    all_gather x1, waiting for transfers between devices, on_device(): lax.all_gather(w_mlp_out, ('seq', 'fsdp'), axis=0, tiled=True)  60.2 us
    all_gather x1, waiting for transfers between devices, on_device(): lax.all_gather(w_attn_out, ('seq', 'fsdp'), axis=0, tiled=True)  31.5 us
    dot_general x4, matrix products, over_rows(): lax.dot_general(left, right, (((0,), (0,)), ((), ())), preferred_element_...  26 us
  transfers between devices with their start and end apart: 12, of which 10 were waited for; matrix products, arithmetic and copies ran while one was open for 9% of the time, Pallas kernels for 0%

commit v1 on v0

v1 whole, which is shorter than its diff:
```python
import jax
import jax.numpy as jnp
from jax import lax
from jax.experimental import pallas as pl
from jax.experimental.pallas import tpu as pltpu
from jax.sharding import Mesh, PartitionSpec as P

D = 1024
HEADS = 16
HDIM = 64
FF = 2624
HALF = 64
OWN_HEADS = HEADS // 2
OWN = OWN_HEADS * HDIM
OWN_FF = FF // 2

EPSILON = 1e-05
MASKED = -1e30
ALL = ("seq", "fy", "core")
CHIPS = ("seq", "fy")
BF16 = jnp.bfloat16
F32 = jnp.float32


def my_bit(step):
    axis, bit = step
    return (lax.axis_index(axis) >> bit) & 1


def dim_of(step):
    axis, bit = step
    seq_bits = lax.axis_size("seq").bit_length() - 1
    return seq_bits if axis == "fy" else seq_bits - 1 - bit


def relayed(step):
    return step == ("seq", 2) and lax.axis_size("seq") == 8


def swap(cells, step):
    axis, bit = step
    count = lax.axis_size(axis)
    return lax.ppermute(cells, axis, [(i, i ^ (1 << bit)) for i in range(count)])


MIDDLE = [(2, 4), (3, 5), (4, 2), (5, 3)]
OUTWARD = [(2, 0), (3, 1), (4, 6), (5, 7)]
INWARD = [(0, 2), (1, 3), (6, 4), (7, 5)]


def gather_step(cells, step):
    if relayed(step):
        crossed = lax.ppermute(cells, "seq", MIDDLE)
        handed = lax.ppermute(crossed, "seq", OUTWARD)
        inner = my_bit(("seq", 1)) != my_bit(("seq", 2))
        got = jnp.where(inner, crossed, handed)
    else:
        got = swap(cells, step)
    high = my_bit(step) == 1
    return jnp.concatenate(
        [jnp.where(high, got, cells), jnp.where(high, cells, got)], axis=dim_of(step)
    )


def gather_chips(shard, steps):
    dims = lax.axis_size("seq").bit_length()
    cells = shard.reshape((1,) * dims + shard.shape)
    for step in steps:
        cells = gather_step(cells, step)
    return cells.reshape((-1,) + shard.shape)


def scatter_chips(cells, steps):
    dims = lax.axis_size("seq").bit_length()
    cells = cells.reshape((2,) * dims + cells.shape[1:])
    for i, step in enumerate(steps):
        bit, dim = my_bit(step), dim_of(step)
        kept = lax.dynamic_slice_in_dim(cells, bit, 1, axis=dim).astype(F32)
        sent = lax.dynamic_slice_in_dim(cells, 1 - bit, 1, axis=dim)
        if relayed(step):
            sent = (sent.astype(F32) + lax.ppermute(sent, "seq", INWARD).astype(F32)).astype(BF16)
            got = lax.ppermute(sent, "seq", MIDDLE)
        else:
            got = swap(sent, step)
        cells = kept + got.astype(F32)
        if i < len(steps) - 1:
            cells = cells.astype(BF16)
    return cells.reshape(cells.shape[dims:])


def pair(cells, core, dim):
    other = lax.ppermute(cells, "core", [(0, 1), (1, 0)])
    first = core == 0
    return jnp.concatenate(
        [jnp.where(first, cells, other), jnp.where(first, other, cells)], axis=dim
    )


def core_swap(cells):
    return lax.ppermute(cells, "core", [(0, 1), (1, 0)])


def step_orders():
    bits = lax.axis_size("seq").bit_length() - 1
    z = [("seq", b) for b in range(1, bits)]
    x, y = [("seq", 0)], [("fy", 0)]
    return z + x + y, z + y + x


def gather_split(mine, theirs, core):
    one, two = step_orders()
    a, b = gather_chips(mine, one), gather_chips(theirs, two)
    first = core == 0
    both = jnp.stack([jnp.where(first, a, b), jnp.where(first, b, a)], axis=1)
    return both.reshape(-1, mine.shape[-1])


def scatter_split(grad, rows, core):
    one, two = step_orders()
    chips = grad.shape[0] // (2 * rows)
    cells = grad.reshape(chips, 2, rows, grad.shape[-1])
    mine = lax.dynamic_index_in_dim(cells, core, 1, keepdims=False)
    theirs = lax.dynamic_index_in_dim(cells, 1 - core, 1, keepdims=False)
    mine = scatter_chips(mine, one[::-1])
    theirs = scatter_chips(theirs, two[::-1])
    other = core_swap(theirs)
    return jnp.where(core == 0, mine, other), jnp.where(core == 0, other, mine)


def place(index, seq_lengths):
    count = seq_lengths.shape[0]
    ids = jnp.arange(count, dtype=jnp.int32)
    ends = jnp.sum(jnp.where(ids[None, :] <= ids[:, None], seq_lengths[None, :], 0), axis=1)
    starts = ends - seq_lengths
    segment = jnp.sum((index[:, None] >= ends[None, :]).astype(jnp.int32), axis=1)
    begins = jnp.sum(jnp.where(segment[:, None] == ids[None, :], starts[None, :], 0), axis=1)
    return segment, index - begins


def angles(position):
    freqs = 10000.0 ** (-(jnp.arange(HDIM // 2, dtype=F32) * 2.0) / HDIM)
    freqs = jnp.concatenate([freqs] * 4)
    turns = position.astype(F32)[:, None] * freqs[None, :]
    sign = jnp.where(jnp.arange(128) % HDIM < HDIM // 2, -1.0, 1.0)
    return jnp.cos(turns), jnp.sin(turns) * sign[None, :]


def normalize(values):
    average = jnp.mean(values, axis=-1, keepdims=True)
    centered = values - average
    variance = jnp.mean(centered * centered, axis=-1, keepdims=True)
    inverse = lax.rsqrt(variance + EPSILON)
    return centered * inverse, inverse


def norm_back(grad_hat, normed, inverse):
    return inverse * (
        grad_hat
        - jnp.mean(grad_hat, axis=-1, keepdims=True)
        - normed * jnp.mean(grad_hat * normed, axis=-1, keepdims=True)
    )


def geglu(gate_in, up_in):
    return jax.nn.gelu(gate_in, approximate=False) * up_in


def contract(left, right, dims, out=F32):
    return lax.dot_general(left, right, ((dims[0], dims[1]), ((), ())), preferred_element_type=out)


def rows_dot(left, right):
    return contract(left, right, ((0,), (0,)))


def cols_dot(left, right):
    return contract(left, right, ((1,), (1,)))


def half_swap(values):
    lane = lax.broadcasted_iota(jnp.int32, values.shape, 1)
    left = pltpu.roll(values, 128 - HDIM // 2, 1)
    right = pltpu.roll(values, HDIM // 2, 1)
    return jnp.where(lane % HDIM < HDIM // 2, left, right)


def bias_of(q_seg, k_seg, block):
    row = lax.broadcasted_iota(jnp.int32, (128, 256), 0)
    col = lax.broadcasted_iota(jnp.int32, (128, 256), 1)
    near = jnp.abs(row + HALF - col) <= HALF
    same = q_seg[pl.ds(block * 128, 128), :] == k_seg[:, pl.ds(block * 128, 256)]
    return jnp.where(near & same, 0.0, MASKED)


def softmax_of(scores):
    exponent = jnp.exp(scores - jnp.max(scores, axis=-1, keepdims=True))
    return exponent * (1.0 / jnp.sum(exponent, axis=-1, keepdims=True))


def attend_kernel(packed, cosine, sine, q_seg, k_seg, query, keys, values, attended, bias):
    rows = query.shape[0]
    blocks = rows // 128
    for b in range(blocks):
        bias[b] = bias_of(q_seg, k_seg, b)
    first = lax.broadcasted_iota(jnp.int32, (1, 128), 1) < HDIM
    for p in range(OWN_HEADS // 2):
        at = slice(p * 128, (p + 1) * 128)
        u = packed[HALF : HALF + rows, at]
        q_cos, q_sin = cosine[HALF : HALF + rows, :], sine[HALF : HALF + rows, :]
        query[:, at] = (u * q_cos + half_swap(u) * q_sin).astype(BF16)
        u = packed[:, OWN + p * 128 : OWN + (p + 1) * 128]
        keys[:, at] = (u * cosine[...] + half_swap(u) * sine[...]).astype(BF16)
        values[:, at] = packed[:, 2 * OWN + p * 128 : 2 * OWN + (p + 1) * 128].astype(BF16)
        for b in range(blocks):
            q = query[b * 128 : (b + 1) * 128, at]
            k = keys[b * 128 : b * 128 + 256, at]
            v = values[b * 128 : b * 128 + 256, at]
            outs = []
            for side in (first, ~first):
                q_one = jnp.where(side, q, jnp.zeros_like(q))
                scores = contract(q_one, k, ((1,), (1,))) * (HDIM**-0.5) + bias[b]
                prob = softmax_of(scores).astype(BF16)
                outs.append(contract(prob, v, ((1,), (0,))))
            attended[b * 128 : (b + 1) * 128, at] = jnp.where(first, outs[0], outs[1]).astype(BF16)


def attend_back_kernel(
    query, keys, values, grad, cosine, sine, q_seg, k_seg, grad_q, grad_k, grad_v, bias
):
    rows = query.shape[0]
    blocks = rows // 128
    scale = HDIM**-0.5
    for b in range(blocks):
        bias[b] = bias_of(q_seg, k_seg, b)
    first = lax.broadcasted_iota(jnp.int32, (1, 128), 1) < HDIM
    grad_k[...] = jnp.zeros_like(grad_k)
    grad_v[...] = jnp.zeros_like(grad_v)
    for p in range(OWN_HEADS // 2):
        at = slice(p * 128, (p + 1) * 128)
        for b in range(blocks):
            here, span = slice(b * 128, (b + 1) * 128), slice(b * 128, b * 128 + 256)
            q, go = query[here, at], grad[here, at]
            k, v = keys[span, at], values[span, at]
            d_q = jnp.zeros((128, 128), F32)
            d_k = jnp.zeros((256, 128), F32)
            d_v = jnp.zeros((256, 128), F32)
            for side in (first, ~first):
                q_one = jnp.where(side, q, jnp.zeros_like(q))
                k_one = jnp.where(side, k, jnp.zeros_like(k))
                go_one = jnp.where(side, go, jnp.zeros_like(go))
                scores = contract(q_one, k, ((1,), (1,))) * scale + bias[b]
                prob = softmax_of(scores)
                grad_prob = contract(go_one, v, ((1,), (1,)))
                inner = jnp.sum(grad_prob * prob, axis=-1, keepdims=True)
                grad_scores = (prob * (grad_prob - inner)).astype(BF16)
                d_q = d_q + contract(grad_scores, k_one, ((1,), (0,)))
                d_k = d_k + contract(grad_scores, q_one, ((0,), (0,)))
                d_v = d_v + contract(prob.astype(BF16), go_one, ((0,), (0,)))
            d_q = d_q * scale
            at_q = slice(HALF + b * 128, HALF + (b + 1) * 128)
            turned = d_q * cosine[at_q, :] - half_swap(d_q) * sine[at_q, :]
            grad_q[here, at] = turned.astype(BF16)
            grad_k[span, at] += d_k * scale
            grad_v[span, at] += d_v
        d_k = grad_k[:, at]
        grad_k[:, at] = d_k * cosine[...] - half_swap(d_k) * sine[...]


VMEM_LIMIT = 48 * 1024 * 1024


def call_kernel(kernel, outs, blocks, flops, args):
    moved = sum(a.size * a.dtype.itemsize for a in args) + sum(
        o.size * o.dtype.itemsize for o in outs
    )
    return pl.pallas_call(
        kernel,
        out_shape=outs,
        in_specs=[pl.BlockSpec(memory_space=pltpu.VMEM)] * len(args),
        out_specs=[pl.BlockSpec(memory_space=pltpu.VMEM)] * len(outs),
        scratch_shapes=[pltpu.VMEM((blocks, 128, 256), F32)],
        compiler_params=pltpu.CompilerParams(vmem_limit_bytes=VMEM_LIMIT),
        cost_estimate=pl.CostEstimate(flops=flops, bytes_accessed=moved, transcendentals=0),
    )(*args)


def like(shape, dtype):
    return jax.ShapeDtypeStruct(shape, dtype)


def on_device(
    tokens, cotangent, seq_lengths, w_qkv, w_attn_out, w_in, w_mlp_out, gain_attn, gain_mlp
):
    share = tokens.shape[0]
    rows = 2 * share
    core = lax.axis_index("core")
    chip = lax.axis_index(CHIPS)
    chips = lax.axis_size(CHIPS)
    total = chips * rows
    shard = w_qkv.shape[0]
    first = core == 0

    gain_a = gain_attn.astype(F32)[:, None]
    gain_m = gain_mlp.astype(F32)[:, None]
    qkv_cells = (w_qkv.astype(F32) * gain_a).astype(BF16).reshape(shard, 3, 2, OWN)
    in_cells = (w_in.astype(F32) * gain_m).astype(BF16).reshape(shard, 2, 2, OWN_FF)
    mlp_cells = w_mlp_out.reshape(shard, 1, 2, OWN_FF)

    def full(cells):
        one = cells[:, :, 0].reshape(shard, -1)
        two = cells[:, :, 1].reshape(shard, -1)
        mine, sent = jnp.where(first, one, two), jnp.where(first, two, one)
        return gather_split(mine, core_swap(sent), core)

    qkv_full = full(qkv_cells)
    one, two = step_orders()
    half = D // 2
    left = gather_chips(w_attn_out[:, :half], one)
    right = gather_chips(w_attn_out[:, half:], two)
    attn_cells = jnp.concatenate([left, right], axis=-1)
    here = lax.dynamic_slice_in_dim(attn_cells, core * (chips // 2), chips // 2, 0)
    there = lax.dynamic_slice_in_dim(attn_cells, (1 - core) * (chips // 2), chips // 2, 0)
    back = core_swap(there)
    attn_full = jnp.stack(
        [jnp.where(first, here, back), jnp.where(first, back, here)], axis=1
    ).reshape(OWN, D)
    mlp_full = full(mlp_cells)
    in_full = full(in_cells)

    ours = pair(tokens, core, 0)
    cot = pair(cotangent, core, 0)
    ahead = [(i, i + 1) for i in range(chips - 1)]
    behind = [(i + 1, i) for i in range(chips - 1)]
    before = lax.ppermute(ours[rows - HALF :], CHIPS, ahead)
    after = lax.ppermute(ours[:HALF], CHIPS, behind)
    wide = jnp.concatenate([before, ours, after], axis=0)
    index = chip * rows - HALF + jnp.arange(rows + 2 * HALF, dtype=jnp.int32)
    segment, position = place(jnp.clip(index, 0, total - 1), seq_lengths)
    segment = jnp.where((index >= 0) & (index < total), segment, -1)
    q_seg = segment[HALF : HALF + rows][:, None]
    k_seg = segment[None, :]
    cosine, sine = angles(position)

    wide_normed, wide_inverse = normalize(wide.astype(F32))
    hidden = wide_normed.astype(BF16)
    packed = jnp.dot(hidden, qkv_full, preferred_element_type=F32)
    blocks = rows // 128
    flops = blocks * OWN_HEADS * 128 * 256 * 128 * 4
    query, keys, values, attended = call_kernel(
        attend_kernel,
        [
            like((rows, OWN), BF16),
            like((rows + 2 * HALF, OWN), BF16),
            like((rows + 2 * HALF, OWN), BF16),
            like((rows, OWN), BF16),
        ],
        blocks,
        flops,
        (packed, cosine, sine, q_seg, k_seg),
    )
    part = jnp.dot(attended, attn_full, preferred_element_type=F32)
    middle = ours.astype(F32) + (part + core_swap(part))
    normed_mid, inverse_mid = normalize(middle)
    lifted = normed_mid.astype(BF16)
    both = jnp.dot(lifted, in_full, preferred_element_type=F32)
    gate, up = both[:, :OWN_FF], both[:, OWN_FF:]
    mixed = geglu(gate, up).astype(BF16)

    grad_mixed = jnp.dot(cot, mlp_full, preferred_element_type=F32)
    unused, gelu_back = jax.vjp(geglu, gate, up)
    grad_gate, grad_up = gelu_back(grad_mixed)
    grad_both = jnp.concatenate([grad_gate, grad_up], axis=1).astype(BF16)
    grad_mlp_w = rows_dot(cot, mixed).astype(BF16)
    grad_in_w = rows_dot(lifted, grad_both).astype(BF16)
    mlp_low, mlp_high = scatter_split(grad_mlp_w, shard, core)
    in_low, in_high = scatter_split(grad_in_w, shard, core)

    part_lifted = cols_dot(grad_both, in_full)
    grad_hat = part_lifted + core_swap(part_lifted)
    grad_middle = cot.astype(F32) + norm_back(grad_hat, normed_mid, inverse_mid)
    grad_attn = grad_middle.astype(BF16)
    grad_attended = cols_dot(grad_attn, attn_full).astype(BF16)

    grad_q, grad_k, grad_v = call_kernel(
        attend_back_kernel,
        [
            like((rows, OWN), BF16),
            like((rows + 2 * HALF, OWN), F32),
            like((rows + 2 * HALF, OWN), F32),
        ],
        blocks,
        flops * 3,
        (query, keys, values, grad_attended, cosine, sine, q_seg, k_seg),
    )
    grad_kv = jnp.concatenate([grad_k, grad_v], axis=1)
    low_edge = lax.ppermute(grad_kv[:HALF].astype(BF16), CHIPS, behind)
    high_edge = lax.ppermute(grad_kv[HALF + rows :].astype(BF16), CHIPS, ahead)
    middle_kv = grad_kv[HALF : HALF + rows]
    gap = jnp.zeros((rows - 2 * HALF, 2 * OWN), F32)
    edges = jnp.concatenate([high_edge.astype(F32), gap, low_edge.astype(F32)], axis=0)
    grad_packed = jnp.concatenate([grad_q, (middle_kv + edges).astype(BF16)], axis=1)

    grad_attn_w = rows_dot(attended, grad_attn).astype(BF16)
    grad_attn_w = grad_attn_w.reshape(chips // 2, 2, shard, D)
    kept = lax.dynamic_index_in_dim(grad_attn_w, core, 1, keepdims=False)
    given = core_swap(lax.dynamic_index_in_dim(grad_attn_w, 1 - core, 1, keepdims=False))
    attn_rows = jnp.concatenate(
        [jnp.where(first, kept, given), jnp.where(first, given, kept)], axis=0
    )
    grad_attn_out = jnp.concatenate(
        [
            scatter_chips(attn_rows[..., :half], one[::-1]),
            scatter_chips(attn_rows[..., half:], two[::-1]),
        ],
        axis=-1,
    )

    own_hidden = hidden[HALF : HALF + rows]
    grad_qkv_w = rows_dot(own_hidden, grad_packed).astype(BF16)
    qkv_low, qkv_high = scatter_split(grad_qkv_w, shard, core)

    def own_rows(values):
        return lax.dynamic_slice_in_dim(values, core * share, share, 0)

    def other_rows(values):
        return lax.dynamic_slice_in_dim(values, (1 - core) * share, share, 0)

    part_hidden = cols_dot(grad_packed, qkv_full)
    grad_hidden = own_rows(part_hidden) + core_swap(other_rows(part_hidden))
    own_normed = own_rows(wide_normed[HALF : HALF + rows])
    own_inverse = own_rows(wide_inverse[HALF : HALF + rows])
    input_grad = own_rows(grad_middle) + norm_back(grad_hidden, own_normed, own_inverse)

    part_out = cols_dot(mixed, mlp_full)
    output = own_rows(middle) + (own_rows(part_out) + core_swap(other_rows(part_out)))

    def joined(low, high, parts):
        size = low.shape[1] // parts
        cuts = [slice(i * size, (i + 1) * size) for i in range(parts)]
        return jnp.concatenate([half_of[:, c] for c in cuts for half_of in (low, high)], axis=1)

    raw_qkv = joined(qkv_low, qkv_high, 3)
    raw_in = joined(in_low, in_high, 2)
    grad_gain_attn = jnp.sum(raw_qkv * w_qkv.astype(F32), axis=1)
    grad_gain_mlp = jnp.sum(raw_in * w_in.astype(F32), axis=1)
    return (
        output.astype(BF16),
        input_grad,
        raw_qkv * gain_a,
        grad_attn_out,
        raw_in * gain_m,
        joined(mlp_low, mlp_high, 1),
        grad_gain_attn,
        grad_gain_mlp,
    )


def solution(mesh):
    split = Mesh(mesh.devices.reshape(mesh.shape["seq"], -1, 2), ALL)
    two, one = P(ALL, None), P(ALL)
    return jax.shard_map(
        on_device,
        mesh=split,
        in_specs=(two, two, P(), two, two, two, two, one, one),
        out_specs=(two, two, two, two, two, two, one, one),
        check_vma=False,
    )
```

time: 1010 us -> 447 us (0.44)
  waiting for transfers between devices: 766 us -> 201 us
  starting transfers between devices: 7.69 us -> 135 us
  blocking collectives: 97.4 us -> 0 us
  matrix products: 71.9 us -> 21.8 us
  other arithmetic: 13.5 us -> 36.3 us
  between operations: 14.7 us -> 3.36 us
    reduce_scatter x3 -> x0, waiting for transfers between devices: 409 us -> none  [the longest x1 232 us: on_device(): lax.psum_scatter(grad_in_w, ('seq', 'fsdp'), scatter_dimension=0, tiled=T...]
    all_gather x4 -> x0, waiting for transfers between devices: 205 us -> none  [the longest x1 87.1 us: on_device(): lax.all_gather(w_in, ('seq', 'fsdp'), axis=0, tiled=True)]
    ppermute x4 -> x98, waiting for transfers between devices: 4.12 us -> 201 us  [the longest x48 170 us: swap(): return lax.ppermute(cells, axis, [(i, i ^ 1 << bit) for i in range(count)])]
    unnamed x9 -> x0, waiting for transfers between devices: 148 us -> none
    ppermute x4 -> x98, starting transfers between devices: 7.16 us -> 135 us  [the longest x48 78.8 us: swap(): return lax.ppermute(cells, axis, [(i, i ^ 1 << bit) for i in range(count)])]
    unnamed x2 -> x0, blocking collectives: 97.4 us -> none
    dot_general x18 -> x12, matrix products: 71.9 us -> 21.8 us  [the longest x8 13.4 us: contract(): lax.dot_general(left, right, ((dims[0], dims[1]), ((), ())), preferred_el...]
    unnamed x77 -> x57, local copies, waits for them, and re-layouts: 19.7 us -> 1.88 us
  transfers between devices with their start and end apart: 12 -> 98, of which waited for: 10 -> 35; matrix products, arithmetic and copies ran while one was open for 9% -> 15% of each run, Pallas kernels for 0% -> 2%
where the time goes in v1:
time: 447 us; the launch traced here: 438 us
  waiting for transfers between devices  201 us (45%)
  starting transfers between devices  135 us (30%)
  other arithmetic  36.3 us (8%)
  local copies, waits for them, and re-layouts  32.4 us (7%)
  matrix products  21.8 us (5%)
  Pallas kernels  8.45 us (2%)
    ppermute x48, waiting for transfers between devices, swap(): return lax.ppermute(cells, axis, [(i, i ^ 1 << bit) for i in range(count)])  170 us
    ppermute x48, starting transfers between devices, swap(): return lax.ppermute(cells, axis, [(i, i ^ 1 << bit) for i in range(count)])  78.8 us
    ppermute x8, starting transfers between devices, scatter_chips(): lax.ppermute(sent, 'seq', INWARD).astype(F32)  24.8 us
    ppermute x8, waiting for transfers between devices, gather_step(): handed = lax.ppermute(crossed, 'seq', OUTWARD)  20.1 us
    dot_general x8, matrix products, contract(): lax.dot_general(left, right, ((dims[0], dims[1]), ((), ())), preferred_el...  13.4 us
    ppermute x8, starting transfers between devices, gather_step(): handed = lax.ppermute(crossed, 'seq', OUTWARD)  10.8 us
  transfers between devices with their start and end apart: 98, of which 35 were waited for; matrix products, arithmetic and copies ran while one was open for 15% of the time, Pallas kernels for 2%

profile of v1, /device:TPU:0, one launch (start us, length us, event | category | flops | bytes accessed | tf_op | source)
XLA Modules:
  0.0 438.5 jit_solution(10856677444727079151)
XLA Ops:
  1.5 3.0 collective-permute-start.19
  19.9 9.2 %collective-permute-done.16 = bf16[1,2,1,1,32,512]{5,4,3,2,1,0:T(8,128)(2,1)S(1)} collective-permute-done((bf16[1,2,1,1,32,512]{5,4,3,2,1,0:T(8,128)(2,1)S(1)}, bf16[1,2,1,1,32,512]{5,4,3,2,1,0:T(8,128)(2,1)S(1)}, u32[]{:S(2)}, u32[]{:S(2)}) %collective-permute-start.16) | collective-permute-done | bytes 65568 | tf_op jit(solution)/shard_map/ppermute | solution.py:54
  30.5 5.3 %collective-permute-done.26 = bf16[1,1,1,1,32,2624]{5,4,3,2,1,0:T(8,128)(2,1)S(1)} collective-permute-done((bf16[1,1,1,1,32,2624]{5,4,3,2,1,0:T(8,128)(2,1)S(1)}, bf16[1,1,1,1,32,2624]{5,4,3,2,1,0:T(8,128)(2,1)S(1)}, u32[]{:S(2)}, u32[]{:S(2)}) %collective-permute-start.26) | collective-permute-done | bytes 167968 | tf_op jit(solution)/shard_map/ppermute | solution.py:43
  36.9 3.8 collective-permute-done.43
  40.7 4.6 %collective-permute-done.9 = bf16[1,1,1,1,32,1536]{5,4,3,2,1,0:T(8,128)(2,1)S(1)} collective-permute-done((bf16[1,1,1,1,32,1536]{5,4,3,2,1,0:T(8,128)(2,1)S(1)}, bf16[1,1,1,1,32,1536]{5,4,3,2,1,0:T(8,128)(2,1)S(1)}, u32[]{:S(2)}, u32[]{:S(2)}) %collective-permute-start.9) | collective-permute-done | bytes 98336 | tf_op jit(solution)/shard_map/ppermute | solution.py:43
  51.1 3.5 collective-permute-start.32
  56.0 2.1 collective-permute-done.32
  58.1 2.5 collective-permute-start.1
  66.9 2.3 collective-permute-start.18
  69.3 4.8 %collective-permute-done.39 = bf16[1,2,1,1,32,1312]{5,4,3,2,1,0:T(8,128)(2,1)S(1)} collective-permute-done((bf16[1,2,1,1,32,1312]{5,4,3,2,1,0:T(8,128)(2,1)S(1)}, bf16[1,2,1,1,32,1312]{5,4,3,2,1,0:T(8,128)(2,1)S(1)}, u32[]{:S(2)}, u32[]{:S(2)}) %collective-permute-start.39) | collective-permute-done | bytes 167968 | tf_op jit(solution)/shard_map/ppermute | solution.py:54
  74.0 2.2 collective-permute-start.23
  81.0 2.7 collective-permute-start.40
  84.0 3.0 collective-permute-done.5
  90.6 2.3 collective-permute-start.6
  96.5 6.2 %collective-permute-done.6 = bf16[2,2,1,1,32,1536]{5,4,3,2,1,0:T(8,128)(2,1)S(1)} collective-permute-done((bf16[2,2,1,1,32,1536]{5,4,3,2,1,0:T(8,128)(2,1)S(1)}, bf16[2,2,1,1,32,1536]{5,4,3,2,1,0:T(8,128)(2,1)S(1)}, u32[]{:S(2)}, u32[]{:S(2)}) %collective-permute-start.6) | collective-permute-done | bytes 393248 | tf_op jit(solution)/shard_map/ppermute | solution.py:43
  110.6 11.0 %collective-permute-done.41 = bf16[2,2,2,1,32,1312]{5,4,3,2,1,0:T(8,128)(2,1)S(1)} collective-permute-done((bf16[2,2,2,1,32,1312]{5,4,3,2,1,0:T(8,128)(2,1)S(1)}, bf16[2,2,2,1,32,1312]{5,4,3,2,1,0:T(8,128)(2,1)S(1)}, u32[]{:S(2)}, u32[]{:S(2)}) %collective-permute-start.41) | collective-permute-done | bytes 671776 | tf_op jit(solution)/shard_map/ppermute | solution.py:43
  125.8 27.5 %collective-permute-done.29 = bf16[2,2,1,1,32,2624]{5,4,3,2,1,0:T(8,128)(2,1)S(1)} collective-permute-done((bf16[2,2,1,1,32,2624]{5,4,3,2,1,0:T(8,128)(2,1)S(1)}, bf16[2,2,1,1,32,2624]{5,4,3,2,1,0:T(8,128)(2,1)S(1)}, u32[]{:S(2)}, u32[]{:S(2)}) %collective-permute-start.29) | collective-permute-done | bytes 671776 | tf_op jit(solution)/shard_map/ppermute | solution.py:43
  158.0 3.6 shard_map.152
  165.7 20.0 %collective-permute-done.30 = bf16[2,2,2,1,32,2624]{5,4,3,2,1,0:T(8,128)(2,1)} collective-permute-done((bf16[2,2,2,1,32,2624]{5,4,3,2,1,0:T(8,128)(2,1)}, bf16[2,2,2,1,32,2624]{5,4,3,2,1,0:T(8,128)(2,1)}, u32[]{:S(2)}, u32[]{:S(2)}) %collective-permute-start.30) | collective-permute-done | bytes 1343520 | tf_op jit(solution)/shard_map/ppermute | solution.py:43
  187.4 8.9 %collective-permute-done.36 = bf16[2,2,1,2,32,2624]{5,4,3,2,1,0:T(8,128)(2,1)S(1)} collective-permute-done((bf16[2,2,1,2,32,2624]{5,4,3,2,1,0:T(8,128)(2,1)S(1)}, bf16[2,2,1,2,32,2624]{5,4,3,2,1,0:T(8,128)(2,1)S(1)}, u32[]{:S(2)}, u32[]{:S(2)}) %collective-permute-start.36) | collective-permute-done | bytes 1343520 | tf_op jit(solution)/shard_map/ppermute | solution.py:43
  198.1 2.4 fusion.39
  200.6 4.1 add_convert_fusion.8
  206.2 2.4 convolution_convert_fusion.1
  208.6 2.7 fusion.11
  211.3 4.3 convolution_convert_fusion
  217.0 4.5 %copy.84 = bf16[1024,1312]{1,0:T(8,128)(2,1)} copy(bf16[1024,1312]{0,1:T(8,128)(2,1)} %convolution_convert_fusion.1) | data formatting | bytes 5373952 | tf_op jit(solution)/shard_map/convert_element_type | solution.py:373
  227.8 7.9 %copy.83 = bf16[1024,2624]{1,0:T(8,128)(2,1)} copy(bf16[1024,2624]{0,1:T(8,128)(2,1)} %convolution_convert_fusion) | data formatting | bytes 10747904 | tf_op jit(solution)/shard_map/convert_element_type | solution.py:374
  235.7 3.0 constant_dynamic-slice_fusion.18
  250.1 31.8 %collective-permute-done.88 = bf16[2,2,1,1,32,1312]{5,4,3,2,1,0:T(8,128)(2,1)S(1)} collective-permute-done((bf16[2,2,1,1,32,1312]{5,4,3,2,1,0:T(8,128)(2,1)S(1)}, bf16[2,2,1,1,32,1312]{5,4,3,2,1,0:T(8,128)(2,1)S(1)}, u32[]{:S(2)}, u32[]{:S(2)}) %collective-permute-start.88) | collective-permute-done | bytes 335904 | tf_op jit(solution)/shard_map/ppermute | solution.py:43
  282.0 4.1 collective-permute-start.89
  291.8 4.8 %shard_map.153 = (bf16[256,512]{1,0:T(8,128)(2,1)S(1)}, f32[384,512]{1,0:T(8,128)S(1)}, f32[384,512]{1,0:T(8,128)S(1)}) custom-call(bf16[256,512]{1,0:T(8,128)(2,1)S(1)} %get-tuple-element.16.query, bf16[384,512]{1,0:T(8,128)(2,1)S(1)} %get-tuple-element.17.keys, bf16[384,512]{1,0:T(8,128)(2,1)S(1)} %get-tuple-element.18.values, ...), custom_call_target="tpu_custom_call" | custom-call | flops 805306368 | bytes 3541504 | tf_op jit(solution)/shard_map/pallas_call | solution.py:276
  296.9 2.6 collective-permute-start.51
  302.7 3.7 collective-permute-done.52
  310.3 2.7 collective-permute-start.54
  315.7 3.9 collective-permute-start.96
  328.2 2.1 collective-permute-start.82
  332.4 19.1 %collective-permute-done.66 = bf16[2,2,2,1,32,512]{5,4,3,2,1,0:T(8,128)(2,1)S(1)} collective-permute-done((bf16[2,2,2,1,32,512]{5,4,3,2,1,0:T(8,128)(2,1)S(1)}, bf16[2,2,2,1,32,512]{5,4,3,2,1,0:T(8,128)(2,1)S(1)}, u32[]{:S(2)}, u32[]{:S(2)}) %collective-permute-start.66) | collective-permute-done | bytes 262176 | tf_op jit(solution)/shard_map/ppermute | solution.py:43
  352.7 6.4 %collective-permute-done.71 = bf16[2,2,1,2,32,512]{5,4,3,2,1,0:T(8,128)(2,1)S(1)} collective-permute-done((bf16[2,2,1,2,32,512]{5,4,3,2,1,0:T(8,128)(2,1)S(1)}, bf16[2,2,1,2,32,512]{5,4,3,2,1,0:T(8,128)(2,1)S(1)}, u32[]{:S(2)}, u32[]{:S(2)}) %collective-permute-start.71) | collective-permute-done | bytes 262176 | tf_op jit(solution)/shard_map/ppermute | solution.py:43
  360.6 3.4 collective-permute-done.67
  365.6 3.4 collective-permute-done.72
  369.0 5.6 %collective-permute-start.68 = (bf16[1,2,1,1,32,512]{5,4,3,2,1,0:T(8,128)(2,1)S(1)}, bf16[1,2,1,1,32,512]{5,4,3,2,1,0:T(8,128)(2,1)S(1)}, u32[]{:S(2)}, u32[]{:S(2)}) collective-permute-start(bf16[1,2,1,1,32,512]{5,4,3,2,1,0:T(8,128)(2,1)S(1)} %constant_dynamic-slice_fusion.24), channel_id=1, source_target_pairs={{0,8},{4,12},{24,16},{28,20},{1,9},{5,13},{25,17},{29,21},{2,10},{... | collective-permute-start | bytes 196616 | tf_op jit(solution)/shard_map/ppermute | solution.py:81
  382.9 10.4 %collective-permute-start.70 = (bf16[1,1,1,1,32,512]{5,4,3,2,1,0:T(8,128)(2,1)S(1)}, bf16[1,1,1,1,32,512]{5,4,3,2,1,0:T(8,128)(2,1)S(1)}, u32[]{:S(2)}, u32[]{:S(2)}) collective-permute-start(bf16[1,1,1,1,32,512]{5,4,3,2,1,0:T(8,128)(2,1)S(1)} %constant_dynamic-slice_fusion.23), channel_id=1, source_target_pairs={{0,8},{4,12},{8,0},{12,4},{16,24},{20,28},{24,16},{28,20},{1,9},{5... | collective-permute-start | bytes 98312 | tf_op jit(solution)/shard_map/ppermute | solution.py:43
  401.5 8.4 %collective-permute-start.56 = (bf16[1,2,1,1,32,1536]{5,4,3,2,1,0:T(8,128)(2,1)S(1)}, bf16[1,2,1,1,32,1536]{5,4,3,2,1,0:T(8,128)(2,1)S(1)}, u32[]{:S(2)}, u32[]{:S(2)}) collective-permute-start(bf16[1,2,1,1,32,1536]{5,4,3,2,1,0:T(8,128)(2,1)S(1)} %constant_dynamic-slice_fusion.33), channel_id=1, source_target_pairs={{0,8},{4,12},{24,16},{28,20},{1,9},{5,13},{25,17},{29,21},{2,10},{... | collective-permute-start | bytes 589832 | tf_op jit(solution)/shard_map/ppermute | solution.py:81
  411.4 3.1 collective-permute-done.56
  415.3 3.5 collective-permute-done.61
  419.6 3.8 collective-permute-start.80
  423.7 5.3 %collective-permute-start.63 = (bf16[1,1,1,1,32,1536]{5,4,3,2,1,0:T(8,128)(2,1)S(1)}, bf16[1,1,1,1,32,1536]{5,4,3,2,1,0:T(8,128)(2,1)S(1)}, u32[]{:S(2)}, u32[]{:S(2)}) collective-permute-start(bf16[1,1,1,1,32,1536]{5,4,3,2,1,0:T(8,128)(2,1)S(1)} %constant_dynamic-slice_fusion.27), channel_id=1, source_target_pairs={{0,8},{4,12},{8,0},{12,4},{16,24},{20,28},{24,16},{28,20},{1,9},{5... | collective-permute-start | bytes 294920 | tf_op jit(solution)/shard_map/ppermute | solution.py:43
  429.2 2.4 collective-permute-done.63
  (433 shorter events, 144.6 us)
Async XLA Ops:
  8.2 22.2 %collective-permute-start.42 = (bf16[32,1312]{1,0:T(8,128)(2,1)S(1)}, bf16[32,1312]{1,0:T(8,128)(2,1)S(1)}, u32[]{:S(2)}, u32[]{:S(2)}) collective-permute-start(bf16[32,1312]{1,0:T(8,128)(2,1)S(1)} %bitcast.162), channel_id=1, source_target_pairs={{0,1},{1,0},{2,3},{3,2},{4,5},{5,4},{6,7},{7,6},{8,9},{9,8},{10,11... | collective-permute-start | bytes 251912 | tf_op jit(solution)/shard_map/ppermute | solution.py:100
  9.0 27.2 %collective-permute-start.8 = (bf16[32,1536]{1,0:T(8,128)(2,1)S(1)}, bf16[32,1536]{1,0:T(8,128)(2,1)S(1)}, u32[]{:S(2)}, u32[]{:S(2)}) collective-permute-start(bf16[32,1536]{1,0:T(8,128)(2,1)S(1)} %bitcast.160), channel_id=1, source_target_pairs={{0,1},{1,0},{2,3},{3,2},{4,5},{5,4},{6,7},{7,6},{8,9},{9,8},{10,11... | collective-permute-start | bytes 294920 | tf_op jit(solution)/shard_map/ppermute | solution.py:100
  15.3 30.7 %collective-permute-start = (bf16[128,1024]{1,0:T(8,128)(2,1)S(1)}, bf16[128,1024]{1,0:T(8,128)(2,1)S(1)}, u32[]{:S(2)}, u32[]{:S(2)}) collective-permute-start(bf16[128,1024]{1,0:T(8,128)(2,1)S(1)} %copy-done.19), channel_id=1, source_target_pairs={{0,1},{1,0},{2,3},{3,2},{4,5},{5,4},{6,7},{7,6},{8,9},{9,8},{10,11... | collective-permute-start | bytes 786440 | tf_op jit(solution)/shard_map/ppermute | solution.py:92
  15.4 13.6 %collective-permute-start.16 = (bf16[1,2,1,1,32,512]{5,4,3,2,1,0:T(8,128)(2,1)S(1)}, bf16[1,2,1,1,32,512]{5,4,3,2,1,0:T(8,128)(2,1)S(1)}, u32[]{:S(2)}, u32[]{:S(2)}) collective-permute-start(bf16[1,2,1,1,32,512]{5,4,3,2,1,0:T(8,128)(2,1)S(1)} %collective-permute-done.15), channel_id=1, source_target_pairs={{8,0},{12,4},{16,24},{20,28},{9,1},{13,5},{17,25},{21,29},{10,2},{... | collective-permute-start | bytes 196616 | tf_op jit(solution)/shard_map/ppermute | solution.py:54
  29.0 18.6 %collective-permute-start.49 = (bf16[128,1024]{1,0:T(8,128)(2,1)S(1)}, bf16[128,1024]{1,0:T(8,128)(2,1)S(1)}, u32[]{:S(2)}, u32[]{:S(2)}) collective-permute-start(bf16[128,1024]{1,0:T(8,128)(2,1)S(1)} %copy-done.20), channel_id=1, source_target_pairs={{0,1},{1,0},{2,3},{3,2},{4,5},{5,4},{6,7},{7,6},{8,9},{9,8},{10,11... | collective-permute-start | bytes 786440 | tf_op jit(solution)/shard_map/ppermute | solution.py:92
  30.4 18.9 %collective-permute-start.31 = (bf16[32,2624]{1,0:T(8,128)(2,1)}, bf16[32,2624]{1,0:T(8,128)(2,1)S(1)}, u32[]{:S(2)}, u32[]{:S(2)}) collective-permute-start(bf16[32,2624]{1,0:T(8,128)(2,1)} %select_n.881), channel_id=1, source_target_pairs={{0,1},{1,0},{2,3},{3,2},{4,5},{5,4},{6,7},{7,6},{8,9},{9,8},{10,11... | collective-permute-start | bytes 503816 | tf_op jit(solution)/shard_map/ppermute | solution.py:100
  36.2 24.5 %collective-permute-start.38 = (bf16[1,2,1,1,32,1312]{5,4,3,2,1,0:T(8,128)(2,1)S(1)}, bf16[1,2,1,1,32,1312]{5,4,3,2,1,0:T(8,128)(2,1)S(1)}, u32[]{:S(2)}, u32[]{:S(2)}) collective-permute-start(bf16[1,2,1,1,32,1312]{5,4,3,2,1,0:T(8,128)(2,1)S(1)} %pad_maximum_fusion.40), channel_id=1, source_target_pairs={{8,16},{12,20},{16,8},{20,12},{9,17},{13,21},{17,9},{21,13},{10,18... | collective-permute-start | bytes 503816 | tf_op jit(solution)/shard_map/ppermute | solution.py:53
  45.3 21.6 %collective-permute-start.4 = (bf16[1,2,1,1,32,1536]{5,4,3,2,1,0:T(8,128)(2,1)S(1)}, bf16[1,2,1,1,32,1536]{5,4,3,2,1,0:T(8,128)(2,1)S(1)}, u32[]{:S(2)}, u32[]{:S(2)}) collective-permute-start(bf16[1,2,1,1,32,1536]{5,4,3,2,1,0:T(8,128)(2,1)S(1)} %pad_maximum_fusion.38), channel_id=1, source_target_pairs={{8,16},{12,20},{16,8},{20,12},{9,17},{13,21},{17,9},{21,13},{10,18... | collective-permute-start | bytes 589832 | tf_op jit(solution)/shard_map/ppermute | solution.py:53
  60.7 27.9 %collective-permute-start.27 = (bf16[1,2,1,1,32,2624]{5,4,3,2,1,0:T(8,128)(2,1)S(1)}, bf16[1,2,1,1,32,2624]{5,4,3,2,1,0:T(8,128)(2,1)S(1)}, u32[]{:S(2)}, u32[]{:S(2)}) collective-permute-start(bf16[1,2,1,1,32,2624]{5,4,3,2,1,0:T(8,128)(2,1)S(1)} %pad_maximum_fusion.33), channel_id=1, source_target_pairs={{8,16},{12,20},{16,8},{20,12},{9,17},{13,21},{17,9},{21,13},{10,18... | collective-permute-start | bytes 1007624 | tf_op jit(solution)/shard_map/ppermute | solution.py:53
  61.4 17.6 %collective-permute-start.10 = (bf16[1,2,1,1,32,1536]{5,4,3,2,1,0:T(8,128)(2,1)S(1)}, bf16[1,2,1,1,32,1536]{5,4,3,2,1,0:T(8,128)(2,1)S(1)}, u32[]{:S(2)}, u32[]{:S(2)}) collective-permute-start(bf16[1,2,1,1,32,1536]{5,4,3,2,1,0:T(8,128)(2,1)S(1)} %pad_maximum_fusion.39), channel_id=1, source_target_pairs={{8,16},{12,20},{16,8},{20,12},{9,17},{13,21},{17,9},{21,13},{10,18... | collective-permute-start | bytes 589832 | tf_op jit(solution)/shard_map/ppermute | solution.py:53
  63.4 14.0 %collective-permute-start.45 = (bf16[1,2,1,1,32,1312]{5,4,3,2,1,0:T(8,128)(2,1)S(1)}, bf16[1,2,1,1,32,1312]{5,4,3,2,1,0:T(8,128)(2,1)S(1)}, u32[]{:S(2)}, u32[]{:S(2)}) collective-permute-start(bf16[1,2,1,1,32,1312]{5,4,3,2,1,0:T(8,128)(2,1)S(1)} %collective-permute-done.44), channel_id=1, source_target_pairs={{8,0},{12,4},{16,24},{20,28},{9,1},{13,5},{17,25},{21,29},{10,2},{... | collective-permute-start | bytes 503816 | tf_op jit(solution)/shard_map/ppermute | solution.py:54
  79.0 14.0 %collective-permute-start.33 = (bf16[1,2,1,1,32,2624]{5,4,3,2,1,0:T(8,128)(2,1)S(1)}, bf16[1,2,1,1,32,2624]{5,4,3,2,1,0:T(8,128)(2,1)S(1)}, u32[]{:S(2)}, u32[]{:S(2)}) collective-permute-start(bf16[1,2,1,1,32,2624]{5,4,3,2,1,0:T(8,128)(2,1)S(1)} %pad_maximum_fusion.34), channel_id=1, source_target_pairs={{8,16},{12,20},{16,8},{20,12},{9,17},{13,21},{17,9},{21,13},{10,18... | collective-permute-start | bytes 1007624 | tf_op jit(solution)/shard_map/ppermute | solution.py:53
  88.5 17.2 %collective-permute-start.28 = (bf16[1,2,1,1,32,2624]{5,4,3,2,1,0:T(8,128)(2,1)S(1)}, bf16[1,2,1,1,32,2624]{5,4,3,2,1,0:T(8,128)(2,1)S(1)}, u32[]{:S(2)}, u32[]{:S(2)}) collective-permute-start(bf16[1,2,1,1,32,2624]{5,4,3,2,1,0:T(8,128)(2,1)S(1)} %collective-permute-done.27), channel_id=1, source_target_pairs={{8,0},{12,4},{16,24},{20,28},{9,1},{13,5},{17,25},{21,29},{10,2},{... | collective-permute-start | bytes 1007624 | tf_op jit(solution)/shard_map/ppermute | solution.py:54
  90.4 18.1 %collective-permute-start.24 = (bf16[8,32,1024]{2,1,0:T(8,128)(2,1)S(1)}, bf16[8,32,1024]{2,1,0:T(8,128)(2,1)S(1)}, u32[]{:S(2)}, u32[]{:S(2)}) collective-permute-start(bf16[8,32,1024]{2,1,0:T(8,128)(2,1)S(1)} %fusion.16), channel_id=1, source_target_pairs={{0,1},{1,0},{2,3},{3,2},{4,5},{5,4},{6,7},{7,6},{8,9},{9,8},{10,11... | collective-permute-start | bytes 1572872 | tf_op jit(solution)/shard_map/ppermute | solution.py:100
  102.6 19.0 %collective-permute-start.41 = (bf16[2,2,2,1,32,1312]{5,4,3,2,1,0:T(8,128)(2,1)S(1)}, bf16[2,2,2,1,32,1312]{5,4,3,2,1,0:T(8,128)(2,1)S(1)}, u32[]{:S(2)}, u32[]{:S(2)}) collective-permute-start(bf16[2,2,2,1,32,1312]{5,4,3,2,1,0:T(8,128)(2,1)S(1)} %pad_maximum_fusion.19), channel_id=1, source_target_pairs={{0,2},{2,0},{1,3},{3,1},{4,6},{6,4},{5,7},{7,5},{8,10},{10,8},{9,1... | collective-permute-start | bytes 2015240 | tf_op jit(solution)/shard_map/ppermute | solution.py:43
  104.3 19.1 %collective-permute-start.47 = (bf16[2,2,1,2,32,1312]{5,4,3,2,1,0:T(8,128)(2,1)S(1)}, bf16[2,2,1,2,32,1312]{5,4,3,2,1,0:T(8,128)(2,1)S(1)}, u32[]{:S(2)}, u32[]{:S(2)}) collective-permute-start(bf16[2,2,1,2,32,1312]{5,4,3,2,1,0:T(8,128)(2,1)S(1)} %pad_maximum_fusion.20), channel_id=1, source_target_pairs={{0,4},{4,0},{8,12},{12,8},{16,20},{20,16},{24,28},{28,24},{1,5},{5... | collective-permute-start | bytes 2015240 | tf_op jit(solution)/shard_map/ppermute | solution.py:43
  105.8 49.7 %collective-permute-start.7 = (bf16[2,2,2,1,32,1536]{5,4,3,2,1,0:T(8,128)(2,1)S(1)}, bf16[2,2,2,1,32,1536]{5,4,3,2,1,0:T(8,128)(2,1)S(1)}, u32[]{:S(2)}, u32[]{:S(2)}) collective-permute-start(bf16[2,2,2,1,32,1536]{5,4,3,2,1,0:T(8,128)(2,1)S(1)} %pad_maximum_fusion.16), channel_id=1, source_target_pairs={{0,2},{2,0},{1,3},{3,1},{4,6},{6,4},{5,7},{7,5},{8,10},{10,8},{9,1... | collective-permute-start | bytes 2359304 | tf_op jit(solution)/shard_map/ppermute | solution.py:43
  106.9 48.7 %collective-permute-start.13 = (bf16[2,2,1,2,32,1536]{5,4,3,2,1,0:T(8,128)(2,1)S(1)}, bf16[2,2,1,2,32,1536]{5,4,3,2,1,0:T(8,128)(2,1)S(1)}, u32[]{:S(2)}, u32[]{:S(2)}) collective-permute-start(bf16[2,2,1,2,32,1536]{5,4,3,2,1,0:T(8,128)(2,1)S(1)} %pad_maximum_fusion.17), channel_id=1, source_target_pairs={{0,4},{4,0},{8,12},{12,8},{16,20},{20,16},{24,28},{28,24},{1,5},{5... | collective-permute-start | bytes 2359304 | tf_op jit(solution)/shard_map/ppermute | solution.py:43
  108.5 44.8 %collective-permute-start.29 = (bf16[2,2,1,1,32,2624]{5,4,3,2,1,0:T(8,128)(2,1)S(1)}, bf16[2,2,1,1,32,2624]{5,4,3,2,1,0:T(8,128)(2,1)S(1)}, u32[]{:S(2)}, u32[]{:S(2)}) collective-permute-start(bf16[2,2,1,1,32,2624]{5,4,3,2,1,0:T(8,128)(2,1)S(1)} %pad_maximum_fusion.21), channel_id=1, source_target_pairs={{0,4},{4,0},{8,12},{12,8},{16,20},{20,16},{24,28},{28,24},{1,5},{5... | collective-permute-start | bytes 2015240 | tf_op jit(solution)/shard_map/ppermute | solution.py:43
  121.6 40.6 %collective-permute-start.35 = (bf16[2,2,1,1,32,2624]{5,4,3,2,1,0:T(8,128)(2,1)}, bf16[2,2,1,1,32,2624]{5,4,3,2,1,0:T(8,128)(2,1)}, u32[]{:S(2)}, u32[]{:S(2)}) collective-permute-start(bf16[2,2,1,1,32,2624]{5,4,3,2,1,0:T(8,128)(2,1)} %pad_maximum_fusion.22), channel_id=1, source_target_pairs={{0,2},{2,0},{1,3},{3,1},{4,6},{6,4},{5,7},{7,5},{8,10},{10,8},{9,1... | collective-permute-start | bytes 2015240 | tf_op jit(solution)/shard_map/ppermute | solution.py:43
  154.7 31.0 %collective-permute-start.30 = (bf16[2,2,2,1,32,2624]{5,4,3,2,1,0:T(8,128)(2,1)}, bf16[2,2,2,1,32,2624]{5,4,3,2,1,0:T(8,128)(2,1)}, u32[]{:S(2)}, u32[]{:S(2)}) collective-permute-start(bf16[2,2,2,1,32,2624]{5,4,3,2,1,0:T(8,128)(2,1)} %pad_maximum_fusion.9), channel_id=1, source_target_pairs={{0,2},{2,0},{1,3},{3,1},{4,6},{6,4},{5,7},{7,5},{8,10},{10,8},{9,1... | collective-permute-start | bytes 4030472 | tf_op jit(solution)/shard_map/ppermute | solution.py:43
  163.6 32.6 %collective-permute-start.36 = (bf16[2,2,1,2,32,2624]{5,4,3,2,1,0:T(8,128)(2,1)S(1)}, bf16[2,2,1,2,32,2624]{5,4,3,2,1,0:T(8,128)(2,1)S(1)}, u32[]{:S(2)}, u32[]{:S(2)}) collective-permute-start(bf16[2,2,1,2,32,2624]{5,4,3,2,1,0:T(8,128)(2,1)S(1)} %pad_maximum_fusion.10), channel_id=1, source_target_pairs={{0,4},{4,0},{8,12},{12,8},{16,20},{20,16},{24,28},{28,24},{1,5},{5... | collective-permute-start | bytes 4030472 | tf_op jit(solution)/shard_map/ppermute | solution.py:43
  216.5 26.0 %collective-permute-start.48 = (f32[128,1024]{1,0:T(8,128)}, f32[128,1024]{1,0:T(8,128)}, u32[]{:S(2)}, u32[]{:S(2)}) collective-permute-start(f32[128,1024]{1,0:T(8,128)} %constant_dynamic-slice_fusion.38), channel_id=1, source_target_pairs={{0,1},{1,0},{2,3},{3,2},{4,5},{5,4},{6,7},{7,6},{8,9},{9,8},{10,11... | collective-permute-start | bytes 1572872 | tf_op jit(solution)/shard_map/ppermute | solution.py:100
  216.5 71.1 %collective-permute-start.50 = (f32[256,1024]{1,0:T(8,128)}, f32[256,1024]{1,0:T(8,128)}, u32[]{:S(2)}, u32[]{:S(2)}) collective-permute-start(f32[256,1024]{1,0:T(8,128)} %fusion.11), channel_id=1, source_target_pairs={{0,1},{1,0},{2,3},{3,2},{4,5},{5,4},{6,7},{7,6},{8,9},{9,8},{10,11... | collective-permute-start | bytes 3145736 | tf_op jit(solution)/shard_map/ppermute | solution.py:100
  224.6 20.3 %collective-permute-start.87 = (bf16[2,2,2,1,32,1312]{5,4,3,2,1,0:T(8,128)(2,1)}, bf16[2,2,2,1,32,1312]{5,4,3,2,1,0:T(8,128)(2,1)}, u32[]{:S(2)}, u32[]{:S(2)}) collective-permute-start(bf16[2,2,2,1,32,1312]{5,4,3,2,1,0:T(8,128)(2,1)} %constant_dynamic-slice_fusion.7), channel_id=1, source_target_pairs={{0,2},{2,0},{1,3},{3,1},{4,6},{6,4},{5,7},{7,5},{8,10},{10,8},{9,1... | collective-permute-start | bytes 2015240 | tf_op jit(solution)/shard_map/ppermute | solution.py:43
  226.7 21.2 %collective-permute-start.92 = (bf16[2,2,1,2,32,1312]{5,4,3,2,1,0:T(8,128)(2,1)}, bf16[2,2,1,2,32,1312]{5,4,3,2,1,0:T(8,128)(2,1)}, u32[]{:S(2)}, u32[]{:S(2)}) collective-permute-start(bf16[2,2,1,2,32,1312]{5,4,3,2,1,0:T(8,128)(2,1)} %constant_dynamic-slice_fusion.2), channel_id=1, source_target_pairs={{0,4},{4,0},{8,12},{12,8},{16,20},{20,16},{24,28},{28,24},{1,5},{5... | collective-permute-start | bytes 2015240 | tf_op jit(solution)/shard_map/ppermute | solution.py:43
  240.0 73.1 %collective-permute-start.76 = (bf16[2,2,2,1,32,2624]{5,4,3,2,1,0:T(8,128)(2,1)}, bf16[2,2,2,1,32,2624]{5,4,3,2,1,0:T(8,128)(2,1)}, u32[]{:S(2)}, u32[]{:S(2)}) collective-permute-start(bf16[2,2,2,1,32,2624]{5,4,3,2,1,0:T(8,128)(2,1)} %constant_dynamic-slice_fusion.17), channel_id=1, source_target_pairs={{0,2},{2,0},{1,3},{3,1},{4,6},{6,4},{5,7},{7,5},{8,10},{10,8},{9,1... | collective-permute-start | bytes 4030472 | tf_op jit(solution)/shard_map/ppermute | solution.py:43
  242.5 73.2 %collective-permute-start.81 = (bf16[2,2,1,2,32,2624]{5,4,3,2,1,0:T(8,128)(2,1)}, bf16[2,2,1,2,32,2624]{5,4,3,2,1,0:T(8,128)(2,1)}, u32[]{:S(2)}, u32[]{:S(2)}) collective-permute-start(bf16[2,2,1,2,32,2624]{5,4,3,2,1,0:T(8,128)(2,1)} %constant_dynamic-slice_fusion.12), channel_id=1, source_target_pairs={{0,4},{4,0},{8,12},{12,8},{16,20},{20,16},{24,28},{28,24},{1,5},{5... | collective-permute-start | bytes 4030472 | tf_op jit(solution)/shard_map/ppermute | solution.py:43
  246.3 35.6 %collective-permute-start.88 = (bf16[2,2,1,1,32,1312]{5,4,3,2,1,0:T(8,128)(2,1)S(1)}, bf16[2,2,1,1,32,1312]{5,4,3,2,1,0:T(8,128)(2,1)S(1)}, u32[]{:S(2)}, u32[]{:S(2)}) collective-permute-start(bf16[2,2,1,1,32,1312]{5,4,3,2,1,0:T(8,128)(2,1)S(1)} %constant_dynamic-slice_fusion.6), channel_id=1, source_target_pairs={{0,4},{4,0},{8,12},{12,8},{16,20},{20,16},{24,28},{28,24},{1,5},{5... | collective-permute-start | bytes 1007624 | tf_op jit(solution)/shard_map/ppermute | solution.py:43
  249.2 36.9 %collective-permute-start.93 = (bf16[2,2,1,1,32,1312]{5,4,3,2,1,0:T(8,128)(2,1)S(1)}, bf16[2,2,1,1,32,1312]{5,4,3,2,1,0:T(8,128)(2,1)S(1)}, u32[]{:S(2)}, u32[]{:S(2)}) collective-permute-start(bf16[2,2,1,1,32,1312]{5,4,3,2,1,0:T(8,128)(2,1)S(1)} %constant_dynamic-slice_fusion.1), channel_id=1, source_target_pairs={{0,2},{2,0},{1,3},{3,1},{4,6},{6,4},{5,7},{7,5},{8,10},{10,8},{9,1... | collective-permute-start | bytes 1007624 | tf_op jit(solution)/shard_map/ppermute | solution.py:43
  282.0 17.5 %collective-permute-start.89 = (bf16[1,2,1,1,32,1312]{5,4,3,2,1,0:T(8,128)(2,1)S(1)}, bf16[1,2,1,1,32,1312]{5,4,3,2,1,0:T(8,128)(2,1)S(1)}, u32[]{:S(2)}, u32[]{:S(2)}) collective-permute-start(bf16[1,2,1,1,32,1312]{5,4,3,2,1,0:T(8,128)(2,1)S(1)} %constant_dynamic-slice_fusion.5), channel_id=1, source_target_pairs={{0,8},{4,12},{24,16},{28,20},{1,9},{5,13},{25,17},{29,21},{2,10},{... | collective-permute-start | bytes 503816 | tf_op jit(solution)/shard_map/ppermute | solution.py:81
  286.3 14.6 %collective-permute-start.94 = (bf16[1,2,1,1,32,1312]{5,4,3,2,1,0:T(8,128)(2,1)S(1)}, bf16[1,2,1,1,32,1312]{5,4,3,2,1,0:T(8,128)(2,1)S(1)}, u32[]{:S(2)}, u32[]{:S(2)}) collective-permute-start(bf16[1,2,1,1,32,1312]{5,4,3,2,1,0:T(8,128)(2,1)S(1)} %constant_dynamic-slice_fusion), channel_id=1, source_target_pairs={{0,8},{4,12},{24,16},{28,20},{1,9},{5,13},{25,17},{29,21},{2,10},{... | collective-permute-start | bytes 503816 | tf_op jit(solution)/shard_map/ppermute | solution.py:81
  300.9 23.3 %collective-permute-start.65 = (bf16[8,32,1024]{2,1,0:T(8,128)(2,1)S(1)}, bf16[8,32,1024]{2,1,0:T(8,128)(2,1)S(1)}, u32[]{:S(2)}, u32[]{:S(2)}) collective-permute-start(bf16[8,32,1024]{2,1,0:T(8,128)(2,1)S(1)} %dynamic-slice_bitcast_fusion), channel_id=1, source_target_pairs={{0,1},{1,0},{2,3},{3,2},{4,5},{5,4},{6,7},{7,6},{8,9},{9,8},{10,11... | collective-permute-start | bytes 1572872 | tf_op jit(solution)/shard_map/ppermute | solution.py:100
  310.1 21.1 %collective-permute-start.53 = (f32[128,1024]{1,0:T(8,128)S(1)}, f32[128,1024]{1,0:T(8,128)S(1)}, u32[]{:S(2)}, u32[]{:S(2)}) collective-permute-start(f32[128,1024]{1,0:T(8,128)S(1)} %constant_dynamic-slice_fusion.37), channel_id=1, source_target_pairs={{0,1},{1,0},{2,3},{3,2},{4,5},{5,4},{6,7},{7,6},{8,9},{9,8},{10,11... | collective-permute-start | bytes 1572872 | tf_op jit(solution)/shard_map/ppermute | solution.py:100
  310.3 64.4 %collective-permute-start.54 = (bf16[2,2,2,1,32,1536]{5,4,3,2,1,0:T(8,128)(2,1)S(1)}, bf16[2,2,2,1,32,1536]{5,4,3,2,1,0:T(8,128)(2,1)S(1)}, u32[]{:S(2)}, u32[]{:S(2)}) collective-permute-start(bf16[2,2,2,1,32,1536]{5,4,3,2,1,0:T(8,128)(2,1)S(1)} %constant_dynamic-slice_fusion.35), channel_id=1, source_target_pairs={{0,2},{2,0},{1,3},{3,1},{4,6},{6,4},{5,7},{7,5},{8,10},{10,8},{9,1... | collective-permute-start | bytes 2359304 | tf_op jit(solution)/shard_map/ppermute | solution.py:43
  313.1 63.2 %collective-permute-start.59 = (bf16[2,2,1,2,32,1536]{5,4,3,2,1,0:T(8,128)(2,1)S(1)}, bf16[2,2,1,2,32,1536]{5,4,3,2,1,0:T(8,128)(2,1)S(1)}, u32[]{:S(2)}, u32[]{:S(2)}) collective-permute-start(bf16[2,2,1,2,32,1536]{5,4,3,2,1,0:T(8,128)(2,1)S(1)} %constant_dynamic-slice_fusion.30), channel_id=1, source_target_pairs={{0,4},{4,0},{8,12},{12,8},{16,20},{20,16},{24,28},{28,24},{1,5},{5... | collective-permute-start | bytes 2359304 | tf_op jit(solution)/shard_map/ppermute | solution.py:43
  326.7 49.9 %collective-permute-start.77 = (bf16[2,2,1,1,32,2624]{5,4,3,2,1,0:T(8,128)(2,1)S(1)}, bf16[2,2,1,1,32,2624]{5,4,3,2,1,0:T(8,128)(2,1)S(1)}, u32[]{:S(2)}, u32[]{:S(2)}) collective-permute-start(bf16[2,2,1,1,32,2624]{5,4,3,2,1,0:T(8,128)(2,1)S(1)} %constant_dynamic-slice_fusion.16), channel_id=1, source_target_pairs={{0,4},{4,0},{8,12},{12,8},{16,20},{20,16},{24,28},{28,24},{1,5},{5... | collective-permute-start | bytes 2015240 | tf_op jit(solution)/shard_map/ppermute | solution.py:43
  328.2 50.1 %collective-permute-start.82 = (bf16[2,2,1,1,32,2624]{5,4,3,2,1,0:T(8,128)(2,1)S(1)}, bf16[2,2,1,1,32,2624]{5,4,3,2,1,0:T(8,128)(2,1)S(1)}, u32[]{:S(2)}, u32[]{:S(2)}) collective-permute-start(bf16[2,2,1,1,32,2624]{5,4,3,2,1,0:T(8,128)(2,1)S(1)} %constant_dynamic-slice_fusion.11), channel_id=1, source_target_pairs={{0,2},{2,0},{1,3},{3,1},{4,6},{6,4},{5,7},{7,5},{8,10},{10,8},{9,1... | collective-permute-start | bytes 2015240 | tf_op jit(solution)/shard_map/ppermute | solution.py:43
  331.2 20.3 %collective-permute-start.66 = (bf16[2,2,2,1,32,512]{5,4,3,2,1,0:T(8,128)(2,1)S(1)}, bf16[2,2,2,1,32,512]{5,4,3,2,1,0:T(8,128)(2,1)S(1)}, u32[]{:S(2)}, u32[]{:S(2)}) collective-permute-start(bf16[2,2,2,1,32,512]{5,4,3,2,1,0:T(8,128)(2,1)S(1)} %constant_dynamic-slice_fusion.26), channel_id=1, source_target_pairs={{0,2},{2,0},{1,3},{3,1},{4,6},{6,4},{5,7},{7,5},{8,10},{10,8},{9,1... | collective-permute-start | bytes 786440 | tf_op jit(solution)/shard_map/ppermute | solution.py:43
  376.2 25.1 %collective-permute-start.55 = (bf16[2,2,1,1,32,1536]{5,4,3,2,1,0:T(8,128)(2,1)S(1)}, bf16[2,2,1,1,32,1536]{5,4,3,2,1,0:T(8,128)(2,1)S(1)}, u32[]{:S(2)}, u32[]{:S(2)}) collective-permute-start(bf16[2,2,1,1,32,1536]{5,4,3,2,1,0:T(8,128)(2,1)S(1)} %constant_dynamic-slice_fusion.34), channel_id=1, source_target_pairs={{0,4},{4,0},{8,12},{12,8},{16,20},{20,16},{24,28},{28,24},{1,5},{5... | collective-permute-start | bytes 1179656 | tf_op jit(solution)/shard_map/ppermute | solution.py:43
  376.6 33.3 %collective-permute-start.60 = (bf16[2,2,1,1,32,1536]{5,4,3,2,1,0:T(8,128)(2,1)S(1)}, bf16[2,2,1,1,32,1536]{5,4,3,2,1,0:T(8,128)(2,1)S(1)}, u32[]{:S(2)}, u32[]{:S(2)}) collective-permute-start(bf16[2,2,1,1,32,1536]{5,4,3,2,1,0:T(8,128)(2,1)S(1)} %constant_dynamic-slice_fusion.29), channel_id=1, source_target_pairs={{0,2},{2,0},{1,3},{3,1},{4,6},{6,4},{5,7},{7,5},{8,10},{10,8},{9,1... | collective-permute-start | bytes 1179656 | tf_op jit(solution)/shard_map/ppermute | solution.py:43
  378.4 21.4 %collective-permute-start.78 = (bf16[1,2,1,1,32,2624]{5,4,3,2,1,0:T(8,128)(2,1)S(1)}, bf16[1,2,1,1,32,2624]{5,4,3,2,1,0:T(8,128)(2,1)S(1)}, u32[]{:S(2)}, u32[]{:S(2)}) collective-permute-start(bf16[1,2,1,1,32,2624]{5,4,3,2,1,0:T(8,128)(2,1)S(1)} %constant_dynamic-slice_fusion.15), channel_id=1, source_target_pairs={{0,8},{4,12},{24,16},{28,20},{1,9},{5,13},{25,17},{29,21},{2,10},{... | collective-permute-start | bytes 1007624 | tf_op jit(solution)/shard_map/ppermute | solution.py:81
  379.9 20.6 %collective-permute-start.83 = (bf16[1,2,1,1,32,2624]{5,4,3,2,1,0:T(8,128)(2,1)S(1)}, bf16[1,2,1,1,32,2624]{5,4,3,2,1,0:T(8,128)(2,1)S(1)}, u32[]{:S(2)}, u32[]{:S(2)}) collective-permute-start(bf16[1,2,1,1,32,2624]{5,4,3,2,1,0:T(8,128)(2,1)S(1)} %constant_dynamic-slice_fusion.10), channel_id=1, source_target_pairs={{0,8},{4,12},{24,16},{28,20},{1,9},{5,13},{25,17},{29,21},{2,10},{... | collective-permute-start | bytes 1007624 | tf_op jit(solution)/shard_map/ppermute | solution.py:81
  399.9 19.6 %collective-permute-start.79 = (bf16[1,2,1,1,32,2624]{5,4,3,2,1,0:T(8,128)(2,1)S(1)}, bf16[1,2,1,1,32,2624]{5,4,3,2,1,0:T(8,128)(2,1)S(1)}, u32[]{:S(2)}, u32[]{:S(2)}) collective-permute-start(bf16[1,2,1,1,32,2624]{5,4,3,2,1,0:T(8,128)(2,1)S(1)} %add_convert_fusion.16), channel_id=1, source_target_pairs={{8,16},{12,20},{16,8},{20,12},{9,17},{13,21},{17,9},{21,13},{10,18... | collective-permute-start | bytes 1007624 | tf_op jit(solution)/shard_map/ppermute | solution.py:82
  400.7 22.8 %collective-permute-start.84 = (bf16[1,2,1,1,32,2624]{5,4,3,2,1,0:T(8,128)(2,1)S(1)}, bf16[1,2,1,1,32,2624]{5,4,3,2,1,0:T(8,128)(2,1)S(1)}, u32[]{:S(2)}, u32[]{:S(2)}) collective-permute-start(bf16[1,2,1,1,32,2624]{5,4,3,2,1,0:T(8,128)(2,1)S(1)} %add_convert_fusion.14), channel_id=1, source_target_pairs={{8,16},{12,20},{16,8},{20,12},{9,17},{13,21},{17,9},{21,13},{10,18... | collective-permute-start | bytes 1007624 | tf_op jit(solution)/shard_map/ppermute | solution.py:82
  401.5 13.0 %collective-permute-start.56 = (bf16[1,2,1,1,32,1536]{5,4,3,2,1,0:T(8,128)(2,1)S(1)}, bf16[1,2,1,1,32,1536]{5,4,3,2,1,0:T(8,128)(2,1)S(1)}, u32[]{:S(2)}, u32[]{:S(2)}) collective-permute-start(bf16[1,2,1,1,32,1536]{5,4,3,2,1,0:T(8,128)(2,1)S(1)} %constant_dynamic-slice_fusion.33), channel_id=1, source_target_pairs={{0,8},{4,12},{24,16},{28,20},{1,9},{5,13},{25,17},{29,21},{2,10},{... | collective-permute-start | bytes 589832 | tf_op jit(solution)/shard_map/ppermute | solution.py:81
  414.6 14.4 %collective-permute-start.57 = (bf16[1,2,1,1,32,1536]{5,4,3,2,1,0:T(8,128)(2,1)S(1)}, bf16[1,2,1,1,32,1536]{5,4,3,2,1,0:T(8,128)(2,1)S(1)}, u32[]{:S(2)}, u32[]{:S(2)}) collective-permute-start(bf16[1,2,1,1,32,1536]{5,4,3,2,1,0:T(8,128)(2,1)S(1)} %add_convert_fusion.23), channel_id=1, source_target_pairs={{8,16},{12,20},{16,8},{20,12},{9,17},{13,21},{17,9},{21,13},{10,18... | collective-permute-start | bytes 589832 | tf_op jit(solution)/shard_map/ppermute | solution.py:82
  419.6 15.8 %collective-permute-start.80 = (bf16[1,1,1,1,32,2624]{5,4,3,2,1,0:T(8,128)(2,1)S(1)}, bf16[1,1,1,1,32,2624]{5,4,3,2,1,0:T(8,128)(2,1)S(1)}, u32[]{:S(2)}, u32[]{:S(2)}) collective-permute-start(bf16[1,1,1,1,32,2624]{5,4,3,2,1,0:T(8,128)(2,1)S(1)} %constant_dynamic-slice_fusion.14), channel_id=1, source_target_pairs={{0,8},{4,12},{8,0},{12,4},{16,24},{20,28},{24,16},{28,20},{1,9},{5... | collective-permute-start | bytes 503816 | tf_op jit(solution)/shard_map/ppermute | solution.py:43
  (74 other events, 587.9 us)

commit v2 on v1

v2 whole, which is shorter than its diff:
```python
import jax
import jax.numpy as jnp
from jax import lax
from jax.experimental import pallas as pl
from jax.experimental.pallas import tpu as pltpu
from jax.sharding import Mesh, PartitionSpec as P

D = 1024
HEADS = 16
HDIM = 64
FF = 2624
HALF = 64
GROUP = 4
OWN_HEADS = HEADS // GROUP
OWN = OWN_HEADS * HDIM
OWN_FF = FF // GROUP

EPSILON = 1e-05
MASKED = -1e30
ALL = ("seq", "fy", "core")
BF16 = jnp.bfloat16
F32 = jnp.float32


def flat_pairs(change):
    count = lax.axis_size(ALL)
    return [(i, change(i)) for i in range(count)]


def send_seq(cells, flip):
    return lax.ppermute(cells, ALL, flat_pairs(lambda i: i ^ (flip * GROUP)))


def trade(cells, axis, dim):
    me = lax.axis_index(axis)
    kept = lax.dynamic_slice_in_dim(cells, me, 1, axis=dim)
    sent = lax.dynamic_slice_in_dim(cells, 1 - me, 1, axis=dim)
    got = lax.ppermute(sent, axis, [(0, 1), (1, 0)])
    low = me == 0
    return jnp.concatenate([jnp.where(low, kept, got), jnp.where(low, got, kept)], axis=dim)


def join(cells, axis, dim):
    me = lax.axis_index(axis)
    got = lax.ppermute(cells, axis, [(0, 1), (1, 0)])
    low = me == 0
    return jnp.stack([jnp.where(low, cells, got), jnp.where(low, got, cells)], axis=dim)


def reduce_pair(cells, axis, dim):
    me = lax.axis_index(axis)
    kept = lax.dynamic_index_in_dim(cells, me, dim, keepdims=False)
    sent = lax.dynamic_index_in_dim(cells, 1 - me, dim, keepdims=False).astype(BF16)
    got = lax.ppermute(sent, axis, [(0, 1), (1, 0)])
    return kept.astype(F32) + got.astype(F32)


def group_rows(cells):
    both = join(join(cells, "fy", 0), "core", 1)
    return both.reshape((-1,) + cells.shape[1:])


def group_sum(part, rows):
    cells = part.reshape(2, 2, rows, part.shape[-1])
    return reduce_pair(reduce_pair(cells, "core", 1), "fy", 0)


def depth_of():
    return lax.axis_size("seq") // 2


def z_stage(cells):
    z, x = depth_of(), lax.axis_index("seq") & 1
    me = lax.axis_index("seq") >> 1
    if z == 4:
        got = [cells] + [send_seq(cells, 2 * d) for d in range(1, 4)]
        odd, up = (me & 1) == 1, (me >> 1) == 1
        pairs = [
            (jnp.where(odd, got[i + 1], got[i]), jnp.where(odd, got[i], got[i + 1])) for i in (0, 2)
        ]
        return jnp.stack(
            [jnp.where(up, pairs[1][i], pairs[0][i]) for i in (0, 1)]
            + [jnp.where(up, pairs[0][i], pairs[1][i]) for i in (0, 1)]
        )
    cells = cells[None]
    flip = 1
    while flip < z:
        got = send_seq(cells, 2 * flip)
        high = (me & flip) != 0
        cells = jnp.concatenate([jnp.where(high, got, cells), jnp.where(high, cells, got)])
        flip *= 2
    return cells


def x_stage(cells):
    got = send_seq(cells, 1)
    high = (lax.axis_index("seq") & 1) == 1
    return jnp.stack([jnp.where(high, got, cells), jnp.where(high, cells, got)], axis=1)


def x_sum(cells):
    me = lax.axis_index("seq") & 1
    kept = lax.dynamic_index_in_dim(cells, me, 1, keepdims=False)
    got = send_seq(lax.dynamic_index_in_dim(cells, 1 - me, 1, keepdims=False), 1)
    return (kept.astype(F32) + got.astype(F32)).astype(BF16)


def z_sum(cells):
    z, me = depth_of(), lax.axis_index("seq") >> 1
    if z == 4:
        total = lax.dynamic_index_in_dim(cells, me, 0, keepdims=False).astype(F32)
        for d in range(1, 4):
            sent = lax.dynamic_index_in_dim(cells, me ^ d, 0, keepdims=False)
            total = total + send_seq(sent, 2 * d).astype(F32)
        return total
    flip = z // 2
    while flip:
        high = ((me & flip) != 0).astype(jnp.int32)
        kept = lax.dynamic_slice_in_dim(cells, high * flip, flip, 0)
        sent = lax.dynamic_slice_in_dim(cells, (1 - high) * flip, flip, 0)
        cells = kept.astype(F32) + send_seq(sent.astype(BF16), 2 * flip).astype(F32)
        flip //= 2
    return cells[0]


def place(index, seq_lengths):
    count = seq_lengths.shape[0]
    ids = jnp.arange(count, dtype=jnp.int32)
    ends = jnp.sum(jnp.where(ids[None, :] <= ids[:, None], seq_lengths[None, :], 0), axis=1)
    starts = ends - seq_lengths
    segment = jnp.sum((index[:, None] >= ends[None, :]).astype(jnp.int32), axis=1)
    begins = jnp.sum(jnp.where(segment[:, None] == ids[None, :], starts[None, :], 0), axis=1)
    return segment, index - begins


def angles(position):
    freqs = 10000.0 ** (-(jnp.arange(HDIM // 2, dtype=F32) * 2.0) / HDIM)
    freqs = jnp.concatenate([freqs] * 4)
    turns = position.astype(F32)[:, None] * freqs[None, :]
    sign = jnp.where(jnp.arange(128) % HDIM < HDIM // 2, -1.0, 1.0)
    return jnp.cos(turns), jnp.sin(turns) * sign[None, :]


def normalize(values):
    average = jnp.mean(values, axis=-1, keepdims=True)
    centered = values - average
    variance = jnp.mean(centered * centered, axis=-1, keepdims=True)
    inverse = lax.rsqrt(variance + EPSILON)
    return centered * inverse, inverse


def norm_back(grad_hat, normed, inverse):
    return inverse * (
        grad_hat
        - jnp.mean(grad_hat, axis=-1, keepdims=True)
        - normed * jnp.mean(grad_hat * normed, axis=-1, keepdims=True)
    )


def geglu(gate_in, up_in):
    return jax.nn.gelu(gate_in, approximate=False) * up_in


def contract(left, right, dims, out=F32):
    return lax.dot_general(left, right, ((dims[0], dims[1]), ((), ())), preferred_element_type=out)


def rows_dot(left, right):
    return contract(left, right, ((0,), (0,)))


def cols_dot(left, right):
    return contract(left, right, ((1,), (1,)))


def half_swap(values):
    lane = lax.broadcasted_iota(jnp.int32, values.shape, 1)
    left = pltpu.roll(values, 128 - HDIM // 2, 1)
    right = pltpu.roll(values, HDIM // 2, 1)
    return jnp.where(lane % HDIM < HDIM // 2, left, right)


def bias_of(q_seg, k_seg, block):
    row = lax.broadcasted_iota(jnp.int32, (128, 256), 0)
    col = lax.broadcasted_iota(jnp.int32, (128, 256), 1)
    near = jnp.abs(row + HALF - col) <= HALF
    same = q_seg[pl.ds(block * 128, 128), :] == k_seg[:, pl.ds(block * 128, 256)]
    return jnp.where(near & same, 0.0, MASKED)


def softmax_of(scores):
    exponent = jnp.exp(scores - jnp.max(scores, axis=-1, keepdims=True))
    return exponent * (1.0 / jnp.sum(exponent, axis=-1, keepdims=True))


def attend_kernel(packed, cosine, sine, q_seg, k_seg, query, keys, values, attended, bias):
    rows = query.shape[0]
    blocks = rows // 128
    for b in range(blocks):
        bias[b] = bias_of(q_seg, k_seg, b)
    first = lax.broadcasted_iota(jnp.int32, (1, 128), 1) < HDIM
    for p in range(OWN_HEADS // 2):
        at = slice(p * 128, (p + 1) * 128)
        u = packed[HALF : HALF + rows, at]
        q_cos, q_sin = cosine[HALF : HALF + rows, :], sine[HALF : HALF + rows, :]
        query[:, at] = (u * q_cos + half_swap(u) * q_sin).astype(BF16)
        u = packed[:, OWN + p * 128 : OWN + (p + 1) * 128]
        keys[:, at] = (u * cosine[...] + half_swap(u) * sine[...]).astype(BF16)
        values[:, at] = packed[:, 2 * OWN + p * 128 : 2 * OWN + (p + 1) * 128].astype(BF16)
        for b in range(blocks):
            q = query[b * 128 : (b + 1) * 128, at]
            k = keys[b * 128 : b * 128 + 256, at]
            v = values[b * 128 : b * 128 + 256, at]
            outs = []
            for side in (first, ~first):
                q_one = jnp.where(side, q, jnp.zeros_like(q))
                scores = contract(q_one, k, ((1,), (1,))) * (HDIM**-0.5) + bias[b]
                prob = softmax_of(scores).astype(BF16)
                outs.append(contract(prob, v, ((1,), (0,))))
            attended[b * 128 : (b + 1) * 128, at] = jnp.where(first, outs[0], outs[1]).astype(BF16)


def attend_back_kernel(
    query, keys, values, grad, cosine, sine, q_seg, k_seg, grad_q, grad_k, grad_v, bias
):
    rows = query.shape[0]
    blocks = rows // 128
    scale = HDIM**-0.5
    for b in range(blocks):
        bias[b] = bias_of(q_seg, k_seg, b)
    first = lax.broadcasted_iota(jnp.int32, (1, 128), 1) < HDIM
    grad_k[...] = jnp.zeros_like(grad_k)
    grad_v[...] = jnp.zeros_like(grad_v)
    for p in range(OWN_HEADS // 2):
        at = slice(p * 128, (p + 1) * 128)
        for b in range(blocks):
            here, span = slice(b * 128, (b + 1) * 128), slice(b * 128, b * 128 + 256)
            q, go = query[here, at], grad[here, at]
            k, v = keys[span, at], values[span, at]
            d_q = jnp.zeros((128, 128), F32)
            d_k = jnp.zeros((256, 128), F32)
            d_v = jnp.zeros((256, 128), F32)
            for side in (first, ~first):
                q_one = jnp.where(side, q, jnp.zeros_like(q))
                k_one = jnp.where(side, k, jnp.zeros_like(k))
                go_one = jnp.where(side, go, jnp.zeros_like(go))
                scores = contract(q_one, k, ((1,), (1,))) * scale + bias[b]
                prob = softmax_of(scores)
                grad_prob = contract(go_one, v, ((1,), (1,)))
                inner = jnp.sum(grad_prob * prob, axis=-1, keepdims=True)
                grad_scores = (prob * (grad_prob - inner)).astype(BF16)
                d_q = d_q + contract(grad_scores, k_one, ((1,), (0,)))
                d_k = d_k + contract(grad_scores, q_one, ((0,), (0,)))
                d_v = d_v + contract(prob.astype(BF16), go_one, ((0,), (0,)))
            d_q = d_q * scale
            at_q = slice(HALF + b * 128, HALF + (b + 1) * 128)
            turned = d_q * cosine[at_q, :] - half_swap(d_q) * sine[at_q, :]
            grad_q[here, at] = turned.astype(BF16)
            grad_k[span, at] += d_k * scale
            grad_v[span, at] += d_v
        d_k = grad_k[:, at]
        grad_k[:, at] = d_k * cosine[...] - half_swap(d_k) * sine[...]


VMEM_LIMIT = 48 * 1024 * 1024


def call_kernel(kernel, outs, blocks, flops, args):
    moved = sum(a.size * a.dtype.itemsize for a in args) + sum(
        o.size * o.dtype.itemsize for o in outs
    )
    return pl.pallas_call(
        kernel,
        out_shape=outs,
        in_specs=[pl.BlockSpec(memory_space=pltpu.VMEM)] * len(args),
        out_specs=[pl.BlockSpec(memory_space=pltpu.VMEM)] * len(outs),
        scratch_shapes=[pltpu.VMEM((blocks, 128, 256), F32)],
        compiler_params=pltpu.CompilerParams(vmem_limit_bytes=VMEM_LIMIT),
        cost_estimate=pl.CostEstimate(flops=flops, bytes_accessed=moved, transcendentals=0),
    )(*args)


def like(shape, dtype):
    return jax.ShapeDtypeStruct(shape, dtype)


def on_device(
    tokens, cotangent, seq_lengths, w_qkv, w_attn_out, w_in, w_mlp_out, gain_attn, gain_mlp
):
    share = tokens.shape[0]
    rows = GROUP * share
    seq, seqs = lax.axis_index("seq"), lax.axis_size("seq")
    total = seqs * rows
    shard = w_qkv.shape[0]
    tie = lax.optimization_barrier

    gain_a = gain_attn.astype(F32)[:, None]
    gain_m = gain_mlp.astype(F32)[:, None]

    def columns(w, parts, width):
        cells = w.reshape(shard, parts, 2, 2, width).transpose(2, 3, 0, 1, 4)
        return cells.reshape(2, 2, shard, parts * width)

    def regroup(cells):
        return trade(trade(cells, "fy", 0), "core", 1).reshape(GROUP * shard, -1)

    ours = tokens.astype(F32)
    normed, inverse = normalize(ours)
    hidden = group_rows(normed.astype(BF16))

    qkv = regroup(columns((w_qkv.astype(F32) * gain_a).astype(BF16), 3, OWN))
    attn = z_stage(w_attn_out)
    rest = regroup(
        jnp.concatenate(
            [
                columns(w_mlp_out, 1, OWN_FF),
                columns((w_in.astype(F32) * gain_m).astype(BF16), 2, OWN_FF),
            ],
            axis=-1,
        )
    )
    mlp, gate_w, up_w = (rest[:, i * OWN_FF : (i + 1) * OWN_FF] for i in range(3))
    qkv, attn, mlp, gate_w, up_w, hidden = tie((qkv, attn, mlp, gate_w, up_w, hidden))

    ahead = [(i, i + 1) for i in range(seqs - 1)]
    behind = [(i + 1, i) for i in range(seqs - 1)]
    before = lax.ppermute(hidden[rows - HALF :], "seq", ahead)
    after = lax.ppermute(hidden[:HALF], "seq", behind)
    qkv, attn = z_stage(qkv), x_stage(attn)
    qkv, attn, before, after, mlp = tie((qkv, attn, before, after, mlp))
    qkv, mlp = x_stage(qkv), z_stage(mlp)
    attn = trade(attn.reshape(2, 2, seqs // 4, shard, D), "fy", 0)
    attn = trade(attn, "core", 1)
    attn_full = attn.transpose(2, 0, 1, 3, 4).reshape(OWN, D)
    cot = group_rows(cotangent)
    qkv, mlp, gate_w, cot, attn_full = tie((qkv, mlp, gate_w, cot, attn_full))
    qkv_full = qkv.reshape(D, 3 * OWN)
    mlp, gate_w = x_stage(mlp), z_stage(gate_w)

    wide = jnp.concatenate([before, hidden, after], axis=0)
    index = seq * rows - HALF + jnp.arange(rows + 2 * HALF, dtype=jnp.int32)
    segment, position = place(jnp.clip(index, 0, total - 1), seq_lengths)
    segment = jnp.where((index >= 0) & (index < total), segment, -1)
    q_seg = segment[HALF : HALF + rows][:, None]
    k_seg = segment[None, :]
    cosine, sine = angles(position)

    packed = jnp.dot(wide, qkv_full, preferred_element_type=F32)
    blocks = rows // 128
    flops = blocks * OWN_HEADS * 128 * 256 * 128 * 4
    query, keys, values, attended = call_kernel(
        attend_kernel,
        [
            like((rows, OWN), BF16),
            like((rows + 2 * HALF, OWN), BF16),
            like((rows + 2 * HALF, OWN), BF16),
            like((rows, OWN), BF16),
        ],
        blocks,
        flops,
        (packed, cosine, sine, q_seg, k_seg),
    )
    part = jnp.dot(attended, attn_full, preferred_element_type=F32)
    middle = ours + group_sum(part, share)
    mlp, gate_w, up_w, middle = tie((mlp, gate_w, up_w, middle))
    gate_w, up_w = x_stage(gate_w), z_stage(up_w)
    normed_mid, inverse_mid = normalize(middle)
    lifted = group_rows(normed_mid.astype(BF16))
    mlp_full = mlp.reshape(D, OWN_FF)
    grad_mixed = jnp.dot(cot, mlp_full, preferred_element_type=F32)
    gate_w, up_w, lifted, grad_mixed = tie((gate_w, up_w, lifted, grad_mixed))
    up_full = x_stage(up_w).reshape(D, OWN_FF)
    gate_full = gate_w.reshape(D, OWN_FF)
    gate = jnp.dot(lifted, gate_full, preferred_element_type=F32)
    up_full, gate = tie((up_full, gate))
    up = jnp.dot(lifted, up_full, preferred_element_type=F32)
    mixed = geglu(gate, up).astype(BF16)

    unused, gelu_back = jax.vjp(geglu, gate, up)
    grad_gate, grad_up = gelu_back(grad_mixed)
    grad_gate, grad_up = grad_gate.astype(BF16), grad_up.astype(BF16)

    def stacked(grad):
        return grad.astype(BF16).reshape(seqs // 2, 2, -1, grad.shape[-1])

    mlp_g = stacked(rows_dot(cot, mixed))
    mixed, grad_gate, grad_up, mlp_g = tie((mixed, grad_gate, grad_up, mlp_g))
    mlp_g = x_sum(mlp_g)
    part_lifted = cols_dot(grad_gate, gate_full) + cols_dot(grad_up, up_full)
    gate_g = stacked(rows_dot(lifted, grad_gate))
    up_g = stacked(rows_dot(lifted, grad_up))
    grad_hat = group_sum(part_lifted, share)
    mlp_g, gate_g, up_g, grad_hat = tie((mlp_g, gate_g, up_g, grad_hat))
    mlp_g, gate_g = z_sum(mlp_g), x_sum(gate_g)
    grad_middle = cotangent.astype(F32) + norm_back(grad_hat, normed_mid, inverse_mid)
    grad_attn = group_rows(grad_middle.astype(BF16))
    grad_attended = cols_dot(grad_attn, attn_full).astype(BF16)
    attn_g = rows_dot(attended, grad_attn).astype(BF16)
    grad_q, grad_k, grad_v = call_kernel(
        attend_back_kernel,
        [
            like((rows, OWN), BF16),
            like((rows + 2 * HALF, OWN), F32),
            like((rows + 2 * HALF, OWN), F32),
        ],
        blocks,
        flops * 3,
        (query, keys, values, grad_attended, cosine, sine, q_seg, k_seg),
    )
    grad_kv = jnp.concatenate([grad_k, grad_v], axis=1)
    mlp_g, gate_g, up_g, grad_kv, grad_q, attn_g = tie((mlp_g, gate_g, up_g, grad_kv, grad_q, attn_g))
    low_edge = lax.ppermute(grad_kv[:HALF].astype(BF16), "seq", behind)
    high_edge = lax.ppermute(grad_kv[HALF + rows :].astype(BF16), "seq", ahead)
    gate_g, up_g = z_sum(gate_g), x_sum(up_g)
    attn_g = attn_g.reshape(seqs // 4, 2, 2, shard, D).transpose(1, 2, 0, 3, 4)
    attn_g = trade(trade(attn_g, "core", 1), "fy", 0).reshape(seqs // 2, 2, shard, D)
    middle_kv = grad_kv[HALF : HALF + rows]
    gap = jnp.zeros((rows - 2 * HALF, 2 * OWN), F32)
    edges = jnp.concatenate([high_edge.astype(F32), gap, low_edge.astype(F32)], axis=0)
    grad_packed = jnp.concatenate([grad_q, (middle_kv + edges).astype(BF16)], axis=1)
    qkv_g = stacked(rows_dot(hidden, grad_packed))
    gate_g, up_g, attn_g, qkv_g, grad_packed = tie((gate_g, up_g, attn_g, qkv_g, grad_packed))
    up_g, attn_g, qkv_g = z_sum(up_g), x_sum(attn_g), x_sum(qkv_g)
    part_hidden = cols_dot(grad_packed, qkv_full)
    grad_hidden = group_sum(part_hidden, share)
    part_out = cols_dot(mixed, mlp_full)
    output = middle + group_sum(part_out, share)

    def regroup_back(cells):
        cells = cells.astype(BF16).reshape(2, 2, shard, -1)
        return trade(trade(cells, "fy", 0), "core", 1)

    def back_columns(cells, parts, width):
        cells = cells.reshape(2, 2, shard, parts, width).transpose(2, 3, 0, 1, 4)
        return cells.reshape(shard, parts * 2 * 2 * width).astype(F32)

    up_g, attn_g, qkv_g, mlp_g, gate_g, grad_hidden, output = tie(
        (up_g, attn_g, qkv_g, mlp_g, gate_g, grad_hidden, output)
    )
    grad_qkv, grad_attn_out = z_sum(qkv_g), z_sum(attn_g)
    rest_g = regroup_back(jnp.concatenate([mlp_g, gate_g, up_g], axis=-1))
    raw_mlp = back_columns(rest_g[..., :OWN_FF], 1, OWN_FF)
    raw_in = back_columns(rest_g[..., OWN_FF:], 2, OWN_FF)
    raw_qkv = back_columns(regroup_back(grad_qkv), 3, OWN)
    input_grad = grad_middle + norm_back(grad_hidden, normed, inverse)
    grad_gain_attn = jnp.sum(raw_qkv * w_qkv.astype(F32), axis=1)
    grad_gain_mlp = jnp.sum(raw_in * w_in.astype(F32), axis=1)
    return (
        output.astype(BF16),
        input_grad,
        raw_qkv * gain_a,
        grad_attn_out,
        raw_in * gain_m,
        raw_mlp,
        grad_gain_attn,
        grad_gain_mlp,
    )


def solution(mesh):
    split = Mesh(mesh.devices.reshape(mesh.shape["seq"], -1, 2), ALL)
    two, one = P(ALL, None), P(ALL)
    return jax.shard_map(
        on_device,
        mesh=split,
        in_specs=(two, two, P(), two, two, two, two, one, one),
        out_specs=(two, two, two, two, two, two, one, one),
        check_vma=False,
    )
```

time: 447 us -> 378 us (0.85)
  the two profiles are of different devices: /device:TPU:0 before, /device:TPU:11 now
where the time goes in v2:
time: 378 us; the launch traced here: 371 us
  waiting for transfers between devices  108 us (29%)
  starting transfers between devices  91.6 us (24%)
  local copies, waits for them, and re-layouts  89.7 us (24%)
  other arithmetic  43.9 us (12%)
  matrix products  26.1 us (7%)
  Pallas kernels  8.6 us (2%)
    ppermute x40, waiting for transfers between devices, send_seq(): return lax.ppermute(cells, ALL, flat_pairs(lambda i: i ^ flip * GROUP))  96.2 us
    ppermute x40, starting transfers between devices, send_seq(): return lax.ppermute(cells, ALL, flat_pairs(lambda i: i ^ flip * GROUP))  40.8 us
    ppermute x12, starting transfers between devices, trade(): got = lax.ppermute(sent, axis, [(0, 1), (1, 0)])  17.5 us
    reshape x3, local copies, waits for them, and re-layouts, stacked(): return grad.astype(BF16).reshape(seqs // 2, 2, -1, grad.shape[-1])  13.6 us
    dot_general x10, matrix products, contract(): lax.dot_general(left, right, ((dims[0], dims[1]), ((), ())), preferred_el...  13.6 us
    ppermute x8, starting transfers between devices, reduce_pair(): got = lax.ppermute(sent, axis, [(0, 1), (1, 0)])  11.3 us
    ppermute x8, starting transfers between devices, join(): got = lax.ppermute(cells, axis, [(0, 1), (1, 0)])  11.1 us
    unnamed x92, local copies, waits for them, and re-layouts  9.82 us
  transfers between devices with their start and end apart: 72, of which 29 were waited for; matrix products, arithmetic and copies ran while one was open for 27% of the time, Pallas kernels for 1%

profile of v2, /device:TPU:11, one launch (start us, length us, event | category | flops | bytes accessed | tf_op | source)
XLA Modules:
  0.0 370.9 jit_solution(316551657994195310)
XLA Ops:
  16.5 4.0 %collective-permute-start.1 = (bf16[2,1,32,768]{3,2,1,0:T(8,128)(2,1)S(1)}, bf16[2,1,32,768]{3,2,1,0:T(8,128)(2,1)S(1)}, u32[]{:S(2)}, u32[]{:S(2)}) collective-permute-start(bf16[2,1,32,768]{3,2,1,0:T(8,128)(2,1)S(1)} %fusion.72), channel_id=1, source_target_pairs={{0,1},{1,0},{2,3},{3,2},{4,5},{5,4},{6,7},{7,6},{8,9},{9,8},{10,11... | collective-permute-start | bytes 294920 | tf_op jit(solution)/shard_map/ppermute | solution.py:38
  22.5 3.9 %collective-permute-start.8 = (bf16[2,128,1024]{2,1,0:T(8,128)(2,1)S(1)}, bf16[2,128,1024]{2,1,0:T(8,128)(2,1)S(1)}, u32[]{:S(2)}, u32[]{:S(2)}) collective-permute-start(bf16[2,128,1024]{2,1,0:T(8,128)(2,1)S(1)} %pad_maximum_fusion.15), channel_id=1, source_target_pairs={{0,1},{1,0},{2,3},{3,2},{4,5},{5,4},{6,7},{7,6},{8,9},{9,8},{10,11... | collective-permute-start | bytes 1572872 | tf_op jit(solution)/shard_map/ppermute | solution.py:45
  33.7 7.9 %collective-permute-done.10 = bf16[128,768]{1,0:T(8,128)(2,1)S(1)} collective-permute-done((bf16[128,768]{1,0:T(8,128)(2,1)S(1)}, bf16[128,768]{1,0:T(8,128)(2,1)S(1)}, u32[]{:S(2)}, u32[]{:S(2)}) %collective-permute-start.10) | collective-permute-done | bytes 196640 | tf_op jit(solution)/shard_map/ppermute | solution.py:31
  43.5 3.6 collective-permute-start.14
  47.1 3.0 collective-permute-done.9
  50.4 2.5 collective-permute-done.13
  60.4 2.5 collective-permute-start.22
  62.9 6.8 %collective-permute-done.16 = bf16[128,656]{1,0:T(8,128)(2,1)S(1)} collective-permute-done((bf16[128,656]{1,0:T(8,128)(2,1)S(1)}, bf16[128,656]{1,0:T(8,128)(2,1)S(1)}, u32[]{:S(2)}, u32[]{:S(2)}) %collective-permute-start.16) | collective-permute-done | bytes 167968 | tf_op jit(solution)/shard_map/ppermute | solution.py:31
  69.7 4.2 %collective-permute-done.17 = bf16[128,656]{1,0:T(8,128)(2,1)S(1)} collective-permute-done((bf16[128,656]{1,0:T(8,128)(2,1)S(1)}, bf16[128,656]{1,0:T(8,128)(2,1)S(1)}, u32[]{:S(2)}, u32[]{:S(2)}) %collective-permute-start.17) | collective-permute-done | bytes 167968 | tf_op jit(solution)/shard_map/ppermute | solution.py:31
  81.0 3.8 %shard_map.152 = (bf16[512,256]{1,0:T(8,128)(2,1)S(1)}, bf16[640,256]{1,0:T(8,128)(2,1)S(1)}, bf16[640,256]{1,0:T(8,128)(2,1)S(1)}, bf16[512,256]{1,0:T(8,128)(2,1)S(1)}) custom-call(f32[640,768]{1,0:T(8,128)S(1)} %fusion.12.packed, f32[640,128]{1,0:T(8,128)S(1)} %get-tuple-element.233.cosine, f32[640,128]{1,0:T(8,128)S(1)} %get-tuple-element.232.sine, ...), custom_call_target="tpu_custom_call" | custom-call | flops 268435456 | bytes 3805696 | tf_op jit(solution)/shard_map/pallas_call | solution.py:272
  87.4 2.8 collective-permute-start.27
  98.7 10.9 %collective-permute-done.23 = bf16[4,128,656]{1,2,0:T(8,128)(2,1)} collective-permute-done((bf16[4,128,656]{1,2,0:T(8,128)(2,1)}, bf16[4,128,656]{1,2,0:T(8,128)(2,1)}, u32[]{:S(2)}, u32[]{:S(2)}) %collective-permute-start.23) | collective-permute-done | bytes 671776 | tf_op jit(solution)/shard_map/ppermute | solution.py:31
  118.7 5.2 %copy.156 = bf16[4,2,128,656]{2,1,0,3:T(2,128)(2,1)} copy(bf16[4,2,128,656]{3,2,0,1:T(8,128)(2,1)} %pad_maximum_fusion.1) | data formatting | bytes 2686976 | tf_op jit(solution)/shard_map/optimization_barrier | solution.py:365
  123.9 4.3 %reshape.261 = bf16[1024,656]{0,1:T(8,128)(2,1)} reshape(bf16[4,2,128,656]{2,1,0,3:T(2,128)(2,1)} %copy.156) | data formatting | bytes 2686976 | tf_op jit(solution)/shard_map/reshape | solution.py:369
  132.7 3.6 fusion.88
  142.4 4.1 %collective-permute-done.29 = bf16[4,128,656]{1,2,0:T(8,128)(2,1)} collective-permute-done((bf16[4,128,656]{1,2,0:T(8,128)(2,1)}, bf16[4,128,656]{1,2,0:T(8,128)(2,1)}, u32[]{:S(2)}, u32[]{:S(2)}) %collective-permute-start.29) | collective-permute-done | bytes 671776 | tf_op jit(solution)/shard_map/ppermute | solution.py:31
  157.6 4.3 %reshape.290 = bf16[1024,656,1,1]{0,1,2,3:T(8,128)(2,1)} reshape(bf16[4,2,128,656]{2,1,0,3:T(2,128)(2,1)} %copy.156) | data formatting | bytes 2686976 | tf_op jit(solution)/shard_map/reshape | solution.py:369
  161.9 4.8 %copy.161 = bf16[4,2,128,656]{2,1,0,3:T(2,128)(2,1)} copy(bf16[4,2,128,656]{3,2,0,1:T(8,128)(2,1)} %pad_maximum_fusion.2) | data formatting | bytes 2686976 | tf_op jit(solution)/shard_map/optimization_barrier | solution.py:371
  166.7 4.3 %reshape.263 = bf16[1024,656]{0,1:T(8,128)(2,1)} reshape(bf16[4,2,128,656]{2,1,0,3:T(2,128)(2,1)} %copy.161) | data formatting | bytes 2686976 | tf_op jit(solution)/shard_map/reshape | solution.py:373
  171.1 3.6 fusion.89
  179.7 4.8 %copy.160 = bf16[4,2,128,656]{2,1,0,3:T(2,128)(2,1)} copy(bf16[4,2,128,656]{3,2,0,1:T(8,128)(2,1)} %pad_maximum_fusion.3) | data formatting | bytes 2686976 | tf_op jit(solution)/shard_map/stack | solution.py:98
  184.6 4.3 %reshape.262 = bf16[1024,656]{0,1:T(8,128)(2,1)} reshape(bf16[4,2,128,656]{2,1,0,3:T(2,128)(2,1)} %copy.160) | data formatting | bytes 2686976 | tf_op jit(solution)/shard_map/reshape | solution.py:372
  188.9 5.3 %multiply_convert_fusion = (bf16[512,656]{0,1:T(8,128)(2,1)}, f32[512,656]{0,1:T(8,128)S(1)}) fusion(f32[512,656]{0,1:T(8,128)} %fusion.88, f32[512,656]{0,1:T(8,128)} %fusion.89), kind=kLoop, calls=%fused_computation.21 | loop fusion | flops 22167552 | bytes 4702208 | tf_op jit(solution)/shard_map/convert_element_type | solution.py:381
  194.2 3.6 add_convert_fusion
  200.6 4.5 %reshape.264 = bf16[4,2,128,656]{2,1,0,3:T(2,128)(2,1)} reshape(bf16[1024,656]{0,1:T(8,128)(2,1)} %convolution_convert_fusion.3) | data formatting | bytes 2686976 | tf_op jit(solution)/shard_map/reshape | solution.py:384
  205.1 2.7 dot_general.64
  207.8 2.7 fusion.90
  211.6 2.9 collective-permute-start.37
  226.4 4.7 %reshape.266 = bf16[4,2,128,656]{2,1,0,3:T(2,128)(2,1)} reshape(bf16[1024,656]{0,1:T(8,128)(2,1)} %convolution_convert_fusion.1) | data formatting | bytes 2686976 | tf_op jit(solution)/shard_map/reshape | solution.py:384
  231.1 4.5 %reshape.265 = bf16[4,2,128,656]{2,1,0,3:T(2,128)(2,1)} reshape(bf16[1024,656]{0,1:T(8,128)(2,1)} %convolution_convert_fusion.2) | data formatting | bytes 2686976 | tf_op jit(solution)/shard_map/reshape | solution.py:384
  248.6 2.9 collective-permute-done.40
  251.5 7.2 %collective-permute-done.41 = bf16[128,656]{0,1:T(8,128)(2,1)S(1)} collective-permute-done((bf16[128,656]{0,1:T(8,128)(2,1)S(1)}, bf16[128,656]{0,1:T(8,128)(2,1)S(1)}, u32[]{:S(2)}, u32[]{:S(2)}) %collective-permute-start.41) | collective-permute-done | bytes 167968 | tf_op jit(solution)/shard_map/ppermute | solution.py:31
  261.5 4.8 %shard_map.153 = (bf16[512,256]{1,0:T(8,128)(2,1)S(1)}, f32[640,256]{1,0:T(8,128)S(1)}, f32[640,256]{1,0:T(8,128)S(1)}) custom-call(bf16[512,256]{1,0:T(8,128)(2,1)S(1)} %get-tuple-element.100.query, bf16[640,256]{1,0:T(8,128)(2,1)S(1)} %get-tuple-element.101.keys, bf16[640,256]{1,0:T(8,128)(2,1)S(1)} %get-tuple-element.102.values, ...), custom_call_target="tpu_custom_call" | custom-call | flops 805306368 | bytes 3412480 | tf_op jit(solution)/shard_map/pallas_call | solution.py:272
  268.1 3.3 collective-permute-start.51
  277.4 2.4 collective-permute-start.46
  284.7 2.9 collective-permute-done.46
  287.5 7.1 %collective-permute-done.47 = bf16[128,656]{0,1:T(8,128)(2,1)S(1)} collective-permute-done((bf16[128,656]{0,1:T(8,128)(2,1)S(1)}, bf16[128,656]{0,1:T(8,128)(2,1)S(1)}, u32[]{:S(2)}, u32[]{:S(2)}) %collective-permute-start.47) | collective-permute-done | bytes 167968 | tf_op jit(solution)/shard_map/ppermute | solution.py:31
  302.1 2.4 collective-permute-start.54
  304.9 2.7 collective-permute-done.53
  308.7 3.3 collective-permute-done.54
  311.9 7.1 %collective-permute-done.55 = bf16[128,656]{0,1:T(8,128)(2,1)S(1)} collective-permute-done((bf16[128,656]{0,1:T(8,128)(2,1)S(1)}, bf16[128,656]{0,1:T(8,128)(2,1)S(1)}, u32[]{:S(2)}, u32[]{:S(2)}) %collective-permute-start.55) | collective-permute-done | bytes 167968 | tf_op jit(solution)/shard_map/ppermute | solution.py:31
  319.2 6.0 %collective-permute-done.56 = bf16[4,32,1024]{2,1,0:T(8,128)(2,1)S(1)} collective-permute-done((bf16[4,32,1024]{2,1,0:T(8,128)(2,1)S(1)}, bf16[4,32,1024]{2,1,0:T(8,128)(2,1)S(1)}, u32[]{:S(2)}, u32[]{:S(2)}) %collective-permute-start.56) | collective-permute-done | bytes 262176 | tf_op jit(solution)/shard_map/ppermute | solution.py:31
  329.9 2.4 collective-permute-start.68
  338.0 3.1 collective-permute-done.62
  341.1 8.4 %collective-permute-done.63 = bf16[128,768]{1,0:T(8,128)(2,1)S(1)} collective-permute-done((bf16[128,768]{1,0:T(8,128)(2,1)S(1)}, bf16[128,768]{1,0:T(8,128)(2,1)S(1)}, u32[]{:S(2)}, u32[]{:S(2)}) %collective-permute-start.63) | collective-permute-done | bytes 196640 | tf_op jit(solution)/shard_map/ppermute | solution.py:31
  349.5 5.6 %collective-permute-done.64 = bf16[128,768]{1,0:T(8,128)(2,1)S(1)} collective-permute-done((bf16[128,768]{1,0:T(8,128)(2,1)S(1)}, bf16[128,768]{1,0:T(8,128)(2,1)S(1)}, u32[]{:S(2)}, u32[]{:S(2)}) %collective-permute-start.64) | collective-permute-done | bytes 196640 | tf_op jit(solution)/shard_map/ppermute | solution.py:31
  355.8 3.0 collective-permute-done.65
  358.8 2.8 collective-permute-start.66
  (404 shorter events, 160.7 us)
Async XLA Ops:
  0.6 12.0 %collective-permute-start.2 = (bf16[32,1024]{1,0:T(8,128)(2,1)}, bf16[32,1024]{1,0:T(8,128)(2,1)S(1)}, u32[]{:S(2)}, u32[]{:S(2)}) collective-permute-start(bf16[32,1024]{1,0:T(8,128)(2,1)} %param.13), channel_id=1, source_target_pairs={{0,24},{1,25},{2,26},{3,27},{4,28},{5,29},{6,30},{7,31},{8,16},{9,... | collective-permute-start | bytes 196616 | tf_op jit(solution)/shard_map/ppermute | solution.py:31
  2.0 11.9 %collective-permute-start.3 = (bf16[32,1024]{1,0:T(8,128)(2,1)}, bf16[32,1024]{1,0:T(8,128)(2,1)S(1)}, u32[]{:S(2)}, u32[]{:S(2)}) collective-permute-start(bf16[32,1024]{1,0:T(8,128)(2,1)} %param.13), channel_id=1, source_target_pairs={{0,16},{1,17},{2,18},{3,19},{4,20},{5,21},{6,22},{7,23},{8,24},{9,... | collective-permute-start | bytes 196616 | tf_op jit(solution)/shard_map/ppermute | solution.py:31
  3.1 11.1 %collective-permute-start.4 = (bf16[32,1024]{1,0:T(8,128)(2,1)}, bf16[32,1024]{1,0:T(8,128)(2,1)}, u32[]{:S(2)}, u32[]{:S(2)}) collective-permute-start(bf16[32,1024]{1,0:T(8,128)(2,1)} %param.13), channel_id=1, source_target_pairs={{0,8},{1,9},{2,10},{3,11},{4,12},{5,13},{6,14},{7,15},{8,0},{9,1},... | collective-permute-start | bytes 196616 | tf_op jit(solution)/shard_map/ppermute | solution.py:31
  7.7 13.8 %collective-permute-start.5 = (bf16[1,2,32,1968]{3,2,1,0:T(8,128)(2,1)S(1)}, bf16[1,2,32,1968]{3,2,1,0:T(8,128)(2,1)S(1)}, u32[]{:S(2)}, u32[]{:S(2)}) collective-permute-start(bf16[1,2,32,1968]{3,2,1,0:T(8,128)(2,1)S(1)} %fusion.57), channel_id=1, source_target_pairs={{0,2},{2,0},{1,3},{3,1},{4,6},{6,4},{5,7},{7,5},{8,10},{10,8},{9,1... | collective-permute-start | bytes 755720 | tf_op jit(solution)/shard_map/ppermute | solution.py:38
  12.6 9.6 %collective-permute-start.7 = (bf16[128,1024]{1,0:T(8,128)(2,1)S(1)}, bf16[128,1024]{1,0:T(8,128)(2,1)S(1)}, u32[]{:S(2)}, u32[]{:S(2)}) collective-permute-start(bf16[128,1024]{1,0:T(8,128)(2,1)S(1)} %fusion.26), channel_id=1, source_target_pairs={{0,2},{2,0},{1,3},{3,1},{4,6},{6,4},{5,7},{7,5},{8,10},{10,8},{9,1... | collective-permute-start | bytes 786440 | tf_op jit(solution)/shard_map/ppermute | solution.py:45
  13.9 13.8 %collective-permute-start.19 = (bf16[128,1024]{1,0:T(8,128)(2,1)S(1)}, bf16[128,1024]{1,0:T(8,128)(2,1)S(1)}, u32[]{:S(2)}, u32[]{:S(2)}) collective-permute-start(bf16[128,1024]{1,0:T(8,128)(2,1)S(1)} %copy-done.28), channel_id=1, source_target_pairs={{0,2},{2,0},{1,3},{3,1},{4,6},{6,4},{5,7},{7,5},{8,10},{10,8},{9,1... | collective-permute-start | bytes 786440 | tf_op jit(solution)/shard_map/ppermute | solution.py:45
  27.8 26.5 %collective-permute-start.20 = (bf16[2,128,1024]{2,1,0:T(8,128)(2,1)S(1)}, bf16[2,128,1024]{2,1,0:T(8,128)(2,1)S(1)}, u32[]{:S(2)}, u32[]{:S(2)}) collective-permute-start(bf16[2,128,1024]{2,1,0:T(8,128)(2,1)S(1)} %pad_maximum_fusion.17), channel_id=1, source_target_pairs={{0,1},{1,0},{2,3},{3,2},{4,5},{5,4},{6,7},{7,6},{8,9},{9,8},{10,11... | collective-permute-start | bytes 1572872 | tf_op jit(solution)/shard_map/ppermute | solution.py:45
  30.6 10.9 %collective-permute-start.10 = (bf16[128,768]{1,0:T(8,128)(2,1)S(1)}, bf16[128,768]{1,0:T(8,128)(2,1)S(1)}, u32[]{:S(2)}, u32[]{:S(2)}) collective-permute-start(bf16[128,768]{1,0:T(8,128)(2,1)S(1)} %bitcast.346), channel_id=1, source_target_pairs={{0,16},{1,17},{2,18},{3,19},{4,20},{5,21},{6,22},{7,23},{8,24},{9,... | collective-permute-start | bytes 589832 | tf_op jit(solution)/shard_map/ppermute | solution.py:31
  33.0 10.4 %collective-permute-start.11 = (bf16[128,768]{1,0:T(8,128)(2,1)S(1)}, bf16[128,768]{1,0:T(8,128)(2,1)S(1)}, u32[]{:S(2)}, u32[]{:S(2)}) collective-permute-start(bf16[128,768]{1,0:T(8,128)(2,1)S(1)} %bitcast.347), channel_id=1, source_target_pairs={{0,8},{1,9},{2,10},{3,11},{4,12},{5,13},{6,14},{7,15},{8,0},{9,1},... | collective-permute-start | bytes 589832 | tf_op jit(solution)/shard_map/ppermute | solution.py:31
  33.1 17.0 %collective-permute-start.9 = (bf16[128,768]{1,0:T(8,128)(2,1)S(1)}, bf16[128,768]{1,0:T(8,128)(2,1)S(1)}, u32[]{:S(2)}, u32[]{:S(2)}) collective-permute-start(bf16[128,768]{1,0:T(8,128)(2,1)S(1)} %bitcast.348), channel_id=1, source_target_pairs={{0,24},{1,25},{2,26},{3,27},{4,28},{5,29},{6,30},{7,31},{8,16},{9,... | collective-permute-start | bytes 589832 | tf_op jit(solution)/shard_map/ppermute | solution.py:31
  33.4 16.9 %collective-permute-start.12 = (bf16[4,32,1024]{2,1,0:T(8,128)(2,1)S(1)}, bf16[4,32,1024]{2,1,0:T(8,128)(2,1)S(1)}, u32[]{:S(2)}, u32[]{:S(2)}) collective-permute-start(bf16[4,32,1024]{2,1,0:T(8,128)(2,1)S(1)} %pad_maximum_fusion.22), channel_id=1, source_target_pairs={{0,4},{1,5},{2,6},{3,7},{4,0},{5,1},{6,2},{7,3},{8,12},{9,13},{10,... | collective-permute-start | bytes 786440 | tf_op jit(solution)/shard_map/ppermute | solution.py:31
  41.5 11.4 %collective-permute-start.13 = (bf16[64,1024]{1,0:T(8,128)(2,1)S(1)}, bf16[64,1024]{1,0:T(8,128)(2,1)S(1)}, u32[]{:S(2)}, u32[]{:S(2)}) collective-permute-start(bf16[64,1024]{1,0:T(8,128)(2,1)S(1)} %get-tuple-element.151), channel_id=1, source_target_pairs={{0,4},{4,8},{8,12},{12,16},{16,20},{20,24},{24,28},{1,5},{5,9},{9,... | collective-permute-start | bytes 393224 | tf_op jit(solution)/shard_map/ppermute | solution.py:327
  55.5 14.2 %collective-permute-start.16 = (bf16[128,656]{1,0:T(8,128)(2,1)S(1)}, bf16[128,656]{1,0:T(8,128)(2,1)S(1)}, u32[]{:S(2)}, u32[]{:S(2)}) collective-permute-start(bf16[128,656]{1,0:T(8,128)(2,1)S(1)} %get-tuple-element.72), channel_id=1, source_target_pairs={{0,24},{1,25},{2,26},{3,27},{4,28},{5,29},{6,30},{7,31},{8,16},{9,... | collective-permute-start | bytes 503816 | tf_op jit(solution)/shard_map/ppermute | solution.py:31
  56.8 17.1 %collective-permute-start.17 = (bf16[128,656]{1,0:T(8,128)(2,1)S(1)}, bf16[128,656]{1,0:T(8,128)(2,1)S(1)}, u32[]{:S(2)}, u32[]{:S(2)}) collective-permute-start(bf16[128,656]{1,0:T(8,128)(2,1)S(1)} %get-tuple-element.72), channel_id=1, source_target_pairs={{0,16},{1,17},{2,18},{3,19},{4,20},{5,21},{6,22},{7,23},{8,24},{9,... | collective-permute-start | bytes 503816 | tf_op jit(solution)/shard_map/ppermute | solution.py:31
  56.8 17.1 %collective-permute-start.18 = (bf16[128,656]{1,0:T(8,128)(2,1)S(1)}, bf16[128,656]{1,0:T(8,128)(2,1)S(1)}, u32[]{:S(2)}, u32[]{:S(2)}) collective-permute-start(bf16[128,656]{1,0:T(8,128)(2,1)S(1)} %get-tuple-element.72), channel_id=1, source_target_pairs={{0,8},{1,9},{2,10},{3,11},{4,12},{5,13},{6,14},{7,15},{8,0},{9,1},... | collective-permute-start | bytes 503816 | tf_op jit(solution)/shard_map/ppermute | solution.py:31
  58.2 17.7 %collective-permute-start.15 = (bf16[4,128,768]{2,1,0:T(8,128)(2,1)S(1)}, bf16[4,128,768]{2,1,0:T(8,128)(2,1)S(1)}, u32[]{:S(2)}, u32[]{:S(2)}) collective-permute-start(bf16[4,128,768]{2,1,0:T(8,128)(2,1)S(1)} %pad_maximum_fusion.9), channel_id=1, source_target_pairs={{0,4},{1,5},{2,6},{3,7},{4,0},{5,1},{6,2},{7,3},{8,12},{9,13},{10,... | collective-permute-start | bytes 2359304 | tf_op jit(solution)/shard_map/ppermute | solution.py:31
  60.4 14.6 %collective-permute-start.22 = (bf16[2,1,2,32,1024]{4,3,1,0,2:T(8,128)(2,1)S(1)}, bf16[2,1,2,32,1024]{4,3,1,0,2:T(8,128)(2,1)S(1)}, u32[]{:S(2)}, u32[]{:S(2)}) collective-permute-start(bf16[2,1,2,32,1024]{4,3,1,0,2:T(8,128)(2,1)S(1)} %fusion.63), channel_id=1, source_target_pairs={{0,1},{1,0},{2,3},{3,2},{4,5},{5,4},{6,7},{7,6},{8,9},{9,8},{10,11... | collective-permute-start | bytes 786440 | tf_op jit(solution)/shard_map/ppermute | solution.py:38
  76.1 17.9 %collective-permute-start.24 = (bf16[128,656]{1,0:T(8,128)(2,1)S(1)}, bf16[128,656]{1,0:T(8,128)(2,1)S(1)}, u32[]{:S(2)}, u32[]{:S(2)}) collective-permute-start(bf16[128,656]{1,0:T(8,128)(2,1)S(1)} %get-tuple-element.76), channel_id=1, source_target_pairs={{0,24},{1,25},{2,26},{3,27},{4,28},{5,29},{6,30},{7,31},{8,16},{9,... | collective-permute-start | bytes 503816 | tf_op jit(solution)/shard_map/ppermute | solution.py:31
  77.3 16.7 %collective-permute-start.25 = (bf16[128,656]{1,0:T(8,128)(2,1)S(1)}, bf16[128,656]{1,0:T(8,128)(2,1)}, u32[]{:S(2)}, u32[]{:S(2)}) collective-permute-start(bf16[128,656]{1,0:T(8,128)(2,1)S(1)} %get-tuple-element.76), channel_id=1, source_target_pairs={{0,16},{1,17},{2,18},{3,19},{4,20},{5,21},{6,22},{7,23},{8,24},{9,... | collective-permute-start | bytes 503816 | tf_op jit(solution)/shard_map/ppermute | solution.py:31
  78.6 15.4 %collective-permute-start.26 = (bf16[128,656]{1,0:T(8,128)(2,1)S(1)}, bf16[128,656]{1,0:T(8,128)(2,1)}, u32[]{:S(2)}, u32[]{:S(2)}) collective-permute-start(bf16[128,656]{1,0:T(8,128)(2,1)S(1)} %get-tuple-element.76), channel_id=1, source_target_pairs={{0,8},{1,9},{2,10},{3,11},{4,12},{5,13},{6,14},{7,15},{8,0},{9,1},... | collective-permute-start | bytes 503816 | tf_op jit(solution)/shard_map/ppermute | solution.py:31
  92.5 17.0 %collective-permute-start.23 = (bf16[4,128,656]{1,2,0:T(8,128)(2,1)}, bf16[4,128,656]{1,2,0:T(8,128)(2,1)}, u32[]{:S(2)}, u32[]{:S(2)}) collective-permute-start(bf16[4,128,656]{1,2,0:T(8,128)(2,1)} %copy.144), channel_id=1, source_target_pairs={{0,4},{1,5},{2,6},{3,7},{4,0},{5,1},{6,2},{7,3},{8,12},{9,13},{10,... | collective-permute-start | bytes 2015240 | tf_op jit(solution)/shard_map/ppermute | solution.py:31
  98.4 16.2 %collective-permute-start.28 = (bf16[128,1024]{1,0:T(8,128)(2,1)S(1)}, bf16[128,1024]{1,0:T(8,128)(2,1)S(1)}, u32[]{:S(2)}, u32[]{:S(2)}) collective-permute-start(bf16[128,1024]{1,0:T(8,128)(2,1)S(1)} %fusion.53), channel_id=1, source_target_pairs={{0,2},{2,0},{1,3},{3,1},{4,6},{6,4},{5,7},{7,5},{8,10},{10,8},{9,1... | collective-permute-start | bytes 786440 | tf_op jit(solution)/shard_map/ppermute | solution.py:54
  114.9 21.4 %collective-permute-start.30 = (bf16[128,656]{1,0:T(8,128)(2,1)S(1)}, bf16[128,656]{1,0:T(8,128)(2,1)S(1)}, u32[]{:S(2)}, u32[]{:S(2)}) collective-permute-start(bf16[128,656]{1,0:T(8,128)(2,1)S(1)} %get-tuple-element.84), channel_id=1, source_target_pairs={{0,24},{1,25},{2,26},{3,27},{4,28},{5,29},{6,30},{7,31},{8,16},{9,... | collective-permute-start | bytes 503816 | tf_op jit(solution)/shard_map/ppermute | solution.py:31
  116.5 19.9 %collective-permute-start.31 = (bf16[128,656]{1,0:T(8,128)(2,1)S(1)}, bf16[128,656]{1,0:T(8,128)(2,1)}, u32[]{:S(2)}, u32[]{:S(2)}) collective-permute-start(bf16[128,656]{1,0:T(8,128)(2,1)S(1)} %get-tuple-element.84), channel_id=1, source_target_pairs={{0,16},{1,17},{2,18},{3,19},{4,20},{5,21},{6,22},{7,23},{8,24},{9,... | collective-permute-start | bytes 503816 | tf_op jit(solution)/shard_map/ppermute | solution.py:31
  118.3 18.1 %collective-permute-start.32 = (bf16[128,656]{1,0:T(8,128)(2,1)S(1)}, bf16[128,656]{1,0:T(8,128)(2,1)}, u32[]{:S(2)}, u32[]{:S(2)}) collective-permute-start(bf16[128,656]{1,0:T(8,128)(2,1)S(1)} %get-tuple-element.84), channel_id=1, source_target_pairs={{0,8},{1,9},{2,10},{3,11},{4,12},{5,13},{6,14},{7,15},{8,0},{9,1},... | collective-permute-start | bytes 503816 | tf_op jit(solution)/shard_map/ppermute | solution.py:31
  131.2 15.3 %collective-permute-start.29 = (bf16[4,128,656]{1,2,0:T(8,128)(2,1)}, bf16[4,128,656]{1,2,0:T(8,128)(2,1)}, u32[]{:S(2)}, u32[]{:S(2)}) collective-permute-start(bf16[4,128,656]{1,2,0:T(8,128)(2,1)} %copy.152), channel_id=1, source_target_pairs={{0,4},{1,5},{2,6},{3,7},{4,0},{5,1},{6,2},{7,3},{8,12},{9,13},{10,... | collective-permute-start | bytes 2015240 | tf_op jit(solution)/shard_map/ppermute | solution.py:31
  139.5 12.0 %collective-permute-start.34 = (bf16[2,128,1024]{2,1,0:T(8,128)(2,1)}, bf16[2,128,1024]{2,1,0:T(8,128)(2,1)}, u32[]{:S(2)}, u32[]{:S(2)}) collective-permute-start(bf16[2,128,1024]{2,1,0:T(8,128)(2,1)} %pad_maximum_fusion.19), channel_id=1, source_target_pairs={{0,1},{1,0},{2,3},{3,2},{4,5},{5,4},{6,7},{7,6},{8,9},{9,8},{10,11... | collective-permute-start | bytes 1572872 | tf_op jit(solution)/shard_map/ppermute | solution.py:45
  156.1 18.6 %collective-permute-start.35 = (bf16[4,128,656]{1,2,0:T(8,128)(2,1)}, bf16[4,128,656]{1,2,0:T(8,128)(2,1)}, u32[]{:S(2)}, u32[]{:S(2)}) collective-permute-start(bf16[4,128,656]{1,2,0:T(8,128)(2,1)} %copy.157), channel_id=1, source_target_pairs={{0,4},{1,5},{2,6},{3,7},{4,0},{5,1},{6,2},{7,3},{8,12},{9,13},{10,... | collective-permute-start | bytes 2015240 | tf_op jit(solution)/shard_map/ppermute | solution.py:31
  211.6 9.8 %collective-permute-start.37 = (bf16[2,128,1024]{2,1,0:T(8,128)(2,1)S(1)}, bf16[2,128,1024]{2,1,0:T(8,128)(2,1)S(1)}, u32[]{:S(2)}, u32[]{:S(2)}) collective-permute-start(bf16[2,128,1024]{2,1,0:T(8,128)(2,1)S(1)} %fusion.34), channel_id=1, source_target_pairs={{0,1},{1,0},{2,3},{3,2},{4,5},{5,4},{6,7},{7,6},{8,9},{9,8},{10,11... | collective-permute-start | bytes 1572872 | tf_op jit(solution)/shard_map/ppermute | solution.py:54
  215.6 20.0 %collective-permute-start.36 = (bf16[4,128,656]{1,2,0:T(8,128)(2,1)}, bf16[4,128,656]{1,2,0:T(8,128)(2,1)}, u32[]{:S(2)}, u32[]{:S(2)}) collective-permute-start(bf16[4,128,656]{1,2,0:T(8,128)(2,1)} %dynamic-slice_bitcast_fusion.3), channel_id=1, source_target_pairs={{0,4},{1,5},{2,6},{3,7},{4,0},{5,1},{6,2},{7,3},{8,12},{9,13},{10,... | collective-permute-start | bytes 2015240 | tf_op jit(solution)/shard_map/ppermute | solution.py:31
  222.5 14.6 %collective-permute-start.38 = (bf16[128,1024]{1,0:T(8,128)(2,1)S(1)}, bf16[128,1024]{1,0:T(8,128)(2,1)S(1)}, u32[]{:S(2)}, u32[]{:S(2)}) collective-permute-start(bf16[128,1024]{1,0:T(8,128)(2,1)S(1)} %fusion.54), channel_id=1, source_target_pairs={{0,2},{2,0},{1,3},{3,1},{4,6},{6,4},{5,7},{7,5},{8,10},{10,8},{9,1... | collective-permute-start | bytes 786440 | tf_op jit(solution)/shard_map/ppermute | solution.py:54
  226.0 12.6 %collective-permute-start.60 = (bf16[2,128,1024]{2,1,0:T(8,128)(2,1)}, bf16[2,128,1024]{2,1,0:T(8,128)(2,1)}, u32[]{:S(2)}, u32[]{:S(2)}) collective-permute-start(bf16[2,128,1024]{2,1,0:T(8,128)(2,1)} %fusion.35), channel_id=1, source_target_pairs={{0,1},{1,0},{2,3},{3,2},{4,5},{5,4},{6,7},{7,6},{8,9},{9,8},{10,11... | collective-permute-start | bytes 1572872 | tf_op jit(solution)/shard_map/ppermute | solution.py:54
  240.3 19.2 %collective-permute-start.42 = (bf16[4,128,656]{1,2,0:T(8,128)(2,1)S(1)}, bf16[4,128,656]{1,2,0:T(8,128)(2,1)S(1)}, u32[]{:S(2)}, u32[]{:S(2)}) collective-permute-start(bf16[4,128,656]{1,2,0:T(8,128)(2,1)S(1)} %dynamic-slice_bitcast_fusion.2), channel_id=1, source_target_pairs={{0,4},{1,5},{2,6},{3,7},{4,0},{5,1},{6,2},{7,3},{8,12},{9,13},{10,... | collective-permute-start | bytes 2015240 | tf_op jit(solution)/shard_map/ppermute | solution.py:31
  243.9 14.8 %collective-permute-start.41 = (bf16[128,656]{0,1:T(8,128)(2,1)S(1)}, bf16[128,656]{0,1:T(8,128)(2,1)S(1)}, u32[]{:S(2)}, u32[]{:S(2)}) collective-permute-start(bf16[128,656]{0,1:T(8,128)(2,1)S(1)} %get-tuple-element.198), channel_id=1, source_target_pairs={{0,24},{1,25},{2,26},{3,27},{4,28},{5,29},{6,30},{7,31},{8,16},{9,... | collective-permute-start | bytes 503816 | tf_op jit(solution)/shard_map/ppermute | solution.py:31
  246.4 13.3 %collective-permute-start.44 = (bf16[2,128,1024]{2,1,0:T(8,128)(2,1)S(1)}, bf16[2,128,1024]{2,1,0:T(8,128)(2,1)S(1)}, u32[]{:S(2)}, u32[]{:S(2)}) collective-permute-start(bf16[2,128,1024]{2,1,0:T(8,128)(2,1)S(1)} %pad_maximum_fusion.20), channel_id=1, source_target_pairs={{0,1},{1,0},{2,3},{3,2},{4,5},{5,4},{6,7},{7,6},{8,9},{9,8},{10,11... | collective-permute-start | bytes 1572872 | tf_op jit(solution)/shard_map/ppermute | solution.py:45
  275.8 19.7 %collective-permute-start.48 = (bf16[4,128,656]{1,2,0:T(8,128)(2,1)S(1)}, bf16[4,128,656]{1,2,0:T(8,128)(2,1)S(1)}, u32[]{:S(2)}, u32[]{:S(2)}) collective-permute-start(bf16[4,128,656]{1,2,0:T(8,128)(2,1)S(1)} %dynamic-slice_bitcast_fusion.1), channel_id=1, source_target_pairs={{0,4},{1,5},{2,6},{3,7},{4,0},{5,1},{6,2},{7,3},{8,12},{9,13},{10,... | collective-permute-start | bytes 2015240 | tf_op jit(solution)/shard_map/ppermute | solution.py:31
  277.4 10.2 %collective-permute-start.46 = (bf16[128,656]{0,1:T(8,128)(2,1)S(1)}, bf16[128,656]{0,1:T(8,128)(2,1)S(1)}, u32[]{:S(2)}, u32[]{:S(2)}) collective-permute-start(bf16[128,656]{0,1:T(8,128)(2,1)S(1)} %get-tuple-element.196), channel_id=1, source_target_pairs={{0,16},{1,17},{2,18},{3,19},{4,20},{5,21},{6,22},{7,23},{8,24},{9,... | collective-permute-start | bytes 503816 | tf_op jit(solution)/shard_map/ppermute | solution.py:31
  279.8 14.8 %collective-permute-start.47 = (bf16[128,656]{0,1:T(8,128)(2,1)S(1)}, bf16[128,656]{0,1:T(8,128)(2,1)S(1)}, u32[]{:S(2)}, u32[]{:S(2)}) collective-permute-start(bf16[128,656]{0,1:T(8,128)(2,1)S(1)} %get-tuple-element.195), channel_id=1, source_target_pairs={{0,24},{1,25},{2,26},{3,27},{4,28},{5,29},{6,30},{7,31},{8,16},{9,... | collective-permute-start | bytes 503816 | tf_op jit(solution)/shard_map/ppermute | solution.py:31
  281.4 14.0 %collective-permute-start.50 = (bf16[1,2,2,32,1024]{4,3,1,0,2:T(8,128)(2,1)S(1)}, bf16[1,2,2,32,1024]{4,3,1,0,2:T(8,128)(2,1)S(1)}, u32[]{:S(2)}, u32[]{:S(2)}) collective-permute-start(bf16[1,2,2,32,1024]{4,3,1,0,2:T(8,128)(2,1)S(1)} %fusion.61), channel_id=1, source_target_pairs={{0,2},{2,0},{1,3},{3,1},{4,6},{6,4},{5,7},{7,5},{8,10},{10,8},{9,1... | collective-permute-start | bytes 786440 | tf_op jit(solution)/shard_map/ppermute | solution.py:38
  283.6 15.8 %collective-permute-start.61 = (bf16[128,1024]{1,0:T(8,128)(2,1)}, bf16[128,1024]{1,0:T(8,128)(2,1)S(1)}, u32[]{:S(2)}, u32[]{:S(2)}) collective-permute-start(bf16[128,1024]{1,0:T(8,128)(2,1)} %fusion.56), channel_id=1, source_target_pairs={{0,2},{2,0},{1,3},{3,1},{4,6},{6,4},{5,7},{7,5},{8,10},{10,8},{9,1... | collective-permute-start | bytes 786440 | tf_op jit(solution)/shard_map/ppermute | solution.py:54
  300.3 25.0 %collective-permute-start.57 = (bf16[4,128,768]{2,1,0:T(8,128)(2,1)S(1)}, bf16[4,128,768]{2,1,0:T(8,128)(2,1)S(1)}, u32[]{:S(2)}, u32[]{:S(2)}) collective-permute-start(bf16[4,128,768]{2,1,0:T(8,128)(2,1)S(1)} %dynamic-slice_bitcast_fusion), channel_id=1, source_target_pairs={{0,4},{1,5},{2,6},{3,7},{4,0},{5,1},{6,2},{7,3},{8,12},{9,13},{10,... | collective-permute-start | bytes 2359304 | tf_op jit(solution)/shard_map/ppermute | solution.py:31
  300.5 24.6 %collective-permute-start.56 = (bf16[4,32,1024]{2,1,0:T(8,128)(2,1)S(1)}, bf16[4,32,1024]{2,1,0:T(8,128)(2,1)S(1)}, u32[]{:S(2)}, u32[]{:S(2)}) collective-permute-start(bf16[4,32,1024]{2,1,0:T(8,128)(2,1)S(1)} %dynamic-slice_bitcast_fusion.4), channel_id=1, source_target_pairs={{0,4},{1,5},{2,6},{3,7},{4,0},{5,1},{6,2},{7,3},{8,12},{9,13},{10,... | collective-permute-start | bytes 786440 | tf_op jit(solution)/shard_map/ppermute | solution.py:31
  302.1 9.9 %collective-permute-start.54 = (bf16[128,656]{0,1:T(8,128)(2,1)S(1)}, bf16[128,656]{0,1:T(8,128)(2,1)S(1)}, u32[]{:S(2)}, u32[]{:S(2)}) collective-permute-start(bf16[128,656]{0,1:T(8,128)(2,1)S(1)} %get-tuple-element.193), channel_id=1, source_target_pairs={{0,16},{1,17},{2,18},{3,19},{4,20},{5,21},{6,22},{7,23},{8,24},{9,... | collective-permute-start | bytes 503816 | tf_op jit(solution)/shard_map/ppermute | solution.py:31
  304.5 14.6 %collective-permute-start.55 = (bf16[128,656]{0,1:T(8,128)(2,1)S(1)}, bf16[128,656]{0,1:T(8,128)(2,1)S(1)}, u32[]{:S(2)}, u32[]{:S(2)}) collective-permute-start(bf16[128,656]{0,1:T(8,128)(2,1)S(1)} %get-tuple-element.192), channel_id=1, source_target_pairs={{0,24},{1,25},{2,26},{3,27},{4,28},{5,29},{6,30},{7,31},{8,16},{9,... | collective-permute-start | bytes 503816 | tf_op jit(solution)/shard_map/ppermute | solution.py:31
  307.6 17.6 %collective-permute-start.59 = (bf16[128,1024]{1,0:T(8,128)(2,1)S(1)}, bf16[128,1024]{1,0:T(8,128)(2,1)S(1)}, u32[]{:S(2)}, u32[]{:S(2)}) collective-permute-start(bf16[128,1024]{1,0:T(8,128)(2,1)S(1)} %fusion.55), channel_id=1, source_target_pairs={{0,2},{2,0},{1,3},{3,1},{4,6},{6,4},{5,7},{7,5},{8,10},{10,8},{9,1... | collective-permute-start | bytes 786440 | tf_op jit(solution)/shard_map/ppermute | solution.py:54
  328.7 27.0 %collective-permute-start.70 = (bf16[1,2,32,1968]{3,2,1,0:T(8,128)(2,1)S(1)}, bf16[1,2,32,1968]{3,2,1,0:T(8,128)(2,1)S(1)}, u32[]{:S(2)}, u32[]{:S(2)}) collective-permute-start(bf16[1,2,32,1968]{3,2,1,0:T(8,128)(2,1)S(1)} %constant_dynamic-slice_fusion), channel_id=1, source_target_pairs={{0,2},{2,0},{1,3},{3,1},{4,6},{6,4},{5,7},{7,5},{8,10},{10,8},{9,1... | collective-permute-start | bytes 755720 | tf_op jit(solution)/shard_map/ppermute | solution.py:38
  334.9 14.6 %collective-permute-start.63 = (bf16[128,768]{1,0:T(8,128)(2,1)S(1)}, bf16[128,768]{1,0:T(8,128)(2,1)S(1)}, u32[]{:S(2)}, u32[]{:S(2)}) collective-permute-start(bf16[128,768]{1,0:T(8,128)(2,1)S(1)} %get-tuple-element.162), channel_id=1, source_target_pairs={{0,16},{1,17},{2,18},{3,19},{4,20},{5,21},{6,22},{7,23},{8,24},{9,... | collective-permute-start | bytes 589832 | tf_op jit(solution)/shard_map/ppermute | solution.py:31
  336.4 18.7 %collective-permute-start.64 = (bf16[128,768]{1,0:T(8,128)(2,1)S(1)}, bf16[128,768]{1,0:T(8,128)(2,1)S(1)}, u32[]{:S(2)}, u32[]{:S(2)}) collective-permute-start(bf16[128,768]{1,0:T(8,128)(2,1)S(1)} %get-tuple-element.161), channel_id=1, source_target_pairs={{0,24},{1,25},{2,26},{3,27},{4,28},{5,29},{6,30},{7,31},{8,16},{9,... | collective-permute-start | bytes 589832 | tf_op jit(solution)/shard_map/ppermute | solution.py:31
  (70 other events, 337.3 us)

commit v3 on v2

--- a/solution.py
+++ b/solution.py
@@ -69,11 +69,15 @@
     return lax.axis_size("seq") // 2
 
 
-def z_stage(cells):
-    z, x = depth_of(), lax.axis_index("seq") & 1
-    me = lax.axis_index("seq") >> 1
+def z_send(cells):
+    if depth_of() == 4:
+        return [cells] + [send_seq(cells, 2 * d) for d in range(1, 4)]
+    return [cells]
+
+
+def z_order(got):
+    z, me = depth_of(), lax.axis_index("seq") >> 1
     if z == 4:
-        got = [cells] + [send_seq(cells, 2 * d) for d in range(1, 4)]
         odd, up = (me & 1) == 1, (me >> 1) == 1
         pairs = [
             (jnp.where(odd, got[i + 1], got[i]), jnp.where(odd, got[i], got[i + 1])) for i in (0, 2)
@@ -82,37 +86,47 @@
             [jnp.where(up, pairs[1][i], pairs[0][i]) for i in (0, 1)]
             + [jnp.where(up, pairs[0][i], pairs[1][i]) for i in (0, 1)]
         )
-    cells = cells[None]
+    cells = got[0][None]
     flip = 1
     while flip < z:
-        got = send_seq(cells, 2 * flip)
+        other = send_seq(cells, 2 * flip)
         high = (me & flip) != 0
-        cells = jnp.concatenate([jnp.where(high, got, cells), jnp.where(high, cells, got)])
+        cells = jnp.concatenate([jnp.where(high, other, cells), jnp.where(high, cells, other)])
         flip *= 2
     return cells
 
 
-def x_stage(cells):
-    got = send_seq(cells, 1)
+def x_order(cells, got):
     high = (lax.axis_index("seq") & 1) == 1
-    return jnp.stack([jnp.where(high, got, cells), jnp.where(high, cells, got)], axis=1)
-
-
-def x_sum(cells):
-    me = lax.axis_index("seq") & 1
-    kept = lax.dynamic_index_in_dim(cells, me, 1, keepdims=False)
-    got = send_seq(lax.dynamic_index_in_dim(cells, 1 - me, 1, keepdims=False), 1)
+    blocks = []
+    for i in range(cells.shape[0]):
+        blocks += [jnp.where(high, got[i], cells[i]), jnp.where(high, cells[i], got[i])]
+    return blocks
+
+
+def x_split(blocks):
+    high = (lax.axis_index("seq") & 1) == 1
+    pairs = list(zip(blocks[::2], blocks[1::2]))
+    kept = jnp.stack([jnp.where(high, b, a) for a, b in pairs])
+    sent = jnp.stack([jnp.where(high, a, b) for a, b in pairs])
+    return kept, sent
+
+
+def lane_blocks(grad):
+    count = lax.axis_size("seq")
+    size = grad.shape[1] // count
+    return [grad[:, i * size : (i + 1) * size] for i in range(count)]
+
+
+def x_sum(kept, got):
     return (kept.astype(F32) + got.astype(F32)).astype(BF16)
 
 
-def z_sum(cells):
+def z_spread(cells):
     z, me = depth_of(), lax.axis_index("seq") >> 1
     if z == 4:
-        total = lax.dynamic_index_in_dim(cells, me, 0, keepdims=False).astype(F32)
-        for d in range(1, 4):
-            sent = lax.dynamic_index_in_dim(cells, me ^ d, 0, keepdims=False)
-            total = total + send_seq(sent, 2 * d).astype(F32)
-        return total
+        blocks = [lax.dynamic_index_in_dim(cells, me ^ d, 0, keepdims=False) for d in range(4)]
+        return [blocks[0]] + [send_seq(blocks[d], 2 * d) for d in range(1, 4)]
     flip = z // 2
     while flip:
         high = ((me & flip) != 0).astype(jnp.int32)
@@ -120,7 +134,11 @@
         sent = lax.dynamic_slice_in_dim(cells, (1 - high) * flip, flip, 0)
         cells = kept.astype(F32) + send_seq(sent.astype(BF16), 2 * flip).astype(F32)
         flip //= 2
-    return cells[0]
+    return [cells[0]]
+
+
+def z_total(got):
+    return sum(cells.astype(F32) for cells in got)
 
 
 def place(index, seq_lengths):
@@ -302,14 +320,14 @@
         return cells.reshape(2, 2, shard, parts * width)
 
     def regroup(cells):
-        return trade(trade(cells, "fy", 0), "core", 1).reshape(GROUP * shard, -1)
-
-    ours = tokens.astype(F32)
-    normed, inverse = normalize(ours)
-    hidden = group_rows(normed.astype(BF16))
-
-    qkv = regroup(columns((w_qkv.astype(F32) * gain_a).astype(BF16), 3, OWN))
-    attn = z_stage(w_attn_out)
+        cells = trade(trade(cells, "fy", 0), "core", 1)
+        return cells.reshape(GROUP * shard, -1).T
+
+    def whole(cells, got):
+        return jnp.concatenate(x_order(cells, got), axis=-1)
+
+    attn_got = z_send(w_attn_out)
+    qkv_got = z_send(regroup(columns((w_qkv.astype(F32) * gain_a).astype(BF16), 3, OWN)))
     rest = regroup(
         jnp.concatenate(
             [
@@ -319,23 +337,33 @@
             axis=-1,
         )
     )
-    mlp, gate_w, up_w = (rest[:, i * OWN_FF : (i + 1) * OWN_FF] for i in range(3))
-    qkv, attn, mlp, gate_w, up_w, hidden = tie((qkv, attn, mlp, gate_w, up_w, hidden))
-
+    mlp_got, gate_got, up_got = (
+        z_send(rest[i * OWN_FF : (i + 1) * OWN_FF]) for i in range(3)
+    )
+    ours = tokens.astype(F32)
+    normed, inverse = normalize(ours)
+    hidden = group_rows(normed.astype(BF16))
+    cot = group_rows(cotangent)
+
+    attn_z = z_order(attn_got)
+    attn_x = send_seq(attn_z, 1)
+    qkv_got, attn_z = tie((qkv_got, attn_z))
+    qkv_z = z_order(qkv_got)
+    qkv_x = send_seq(qkv_z, 1)
+    hidden, qkv_z = tie((hidden, qkv_z))
     ahead = [(i, i + 1) for i in range(seqs - 1)]
     behind = [(i + 1, i) for i in range(seqs - 1)]
     before = lax.ppermute(hidden[rows - HALF :], "seq", ahead)
     after = lax.ppermute(hidden[:HALF], "seq", behind)
-    qkv, attn = z_stage(qkv), x_stage(attn)
-    qkv, attn, before, after, mlp = tie((qkv, attn, before, after, mlp))
-    qkv, mlp = x_stage(qkv), z_stage(mlp)
+    attn = jnp.stack(x_order(attn_z, attn_x))
     attn = trade(attn.reshape(2, 2, seqs // 4, shard, D), "fy", 0)
     attn = trade(attn, "core", 1)
     attn_full = attn.transpose(2, 0, 1, 3, 4).reshape(OWN, D)
-    cot = group_rows(cotangent)
-    qkv, mlp, gate_w, cot, attn_full = tie((qkv, mlp, gate_w, cot, attn_full))
-    qkv_full = qkv.reshape(D, 3 * OWN)
-    mlp, gate_w = x_stage(mlp), z_stage(gate_w)
+    mlp_got, qkv_z = tie((mlp_got, qkv_z))
+    mlp_z = z_order(mlp_got)
+    mlp_x = send_seq(mlp_z, 1)
+    qkv_x, mlp_z, attn_full = tie((qkv_x, mlp_z, attn_full))
+    qkv_full = whole(qkv_z, qkv_x)
 
     wide = jnp.concatenate([before, hidden, after], axis=0)
     index = seq * rows - HALF + jnp.arange(rows + 2 * HALF, dtype=jnp.int32)
@@ -345,7 +373,7 @@
     k_seg = segment[None, :]
     cosine, sine = angles(position)
 
-    packed = jnp.dot(wide, qkv_full, preferred_element_type=F32)
+    packed = cols_dot(wide, qkv_full)
     blocks = rows // 128
     flops = blocks * OWN_HEADS * 128 * 256 * 128 * 4
     query, keys, values, attended = call_kernel(
@@ -362,40 +390,51 @@
     )
     part = jnp.dot(attended, attn_full, preferred_element_type=F32)
     middle = ours + group_sum(part, share)
-    mlp, gate_w, up_w, middle = tie((mlp, gate_w, up_w, middle))
-    gate_w, up_w = x_stage(gate_w), z_stage(up_w)
+    gate_got, part = tie((gate_got, part))
+    gate_z = z_order(gate_got)
+    gate_x = send_seq(gate_z, 1)
+    gate_z, middle = tie((gate_z, middle))
     normed_mid, inverse_mid = normalize(middle)
     lifted = group_rows(normed_mid.astype(BF16))
-    mlp_full = mlp.reshape(D, OWN_FF)
-    grad_mixed = jnp.dot(cot, mlp_full, preferred_element_type=F32)
-    gate_w, up_w, lifted, grad_mixed = tie((gate_w, up_w, lifted, grad_mixed))
-    up_full = x_stage(up_w).reshape(D, OWN_FF)
-    gate_full = gate_w.reshape(D, OWN_FF)
-    gate = jnp.dot(lifted, gate_full, preferred_element_type=F32)
-    up_full, gate = tie((up_full, gate))
-    up = jnp.dot(lifted, up_full, preferred_element_type=F32)
+    mlp_x, gate_z = tie((mlp_x, gate_z))
+    mlp_full = whole(mlp_z, mlp_x)
+    grad_mixed = cols_dot(cot, mlp_full)
+    up_got, grad_mixed, lifted = tie((up_got, grad_mixed, lifted))
+    up_z = z_order(up_got)
+    up_x = send_seq(up_z, 1)
+    gate_x, up_z = tie((gate_x, up_z))
+    gate_full = whole(gate_z, gate_x)
+    gate = cols_dot(lifted, gate_full)
+    up_x, gate = tie((up_x, gate))
+    up_full = whole(up_z, up_x)
+    up = cols_dot(lifted, up_full)
     mixed = geglu(gate, up).astype(BF16)
 
     unused, gelu_back = jax.vjp(geglu, gate, up)
     grad_gate, grad_up = gelu_back(grad_mixed)
     grad_gate, grad_up = grad_gate.astype(BF16), grad_up.astype(BF16)
 
-    def stacked(grad):
-        return grad.astype(BF16).reshape(seqs // 2, 2, -1, grad.shape[-1])
-
-    mlp_g = stacked(rows_dot(cot, mixed))
-    mixed, grad_gate, grad_up, mlp_g = tie((mixed, grad_gate, grad_up, mlp_g))
-    mlp_g = x_sum(mlp_g)
-    part_lifted = cols_dot(grad_gate, gate_full) + cols_dot(grad_up, up_full)
-    gate_g = stacked(rows_dot(lifted, grad_gate))
-    up_g = stacked(rows_dot(lifted, grad_up))
-    grad_hat = group_sum(part_lifted, share)
-    mlp_g, gate_g, up_g, grad_hat = tie((mlp_g, gate_g, up_g, grad_hat))
-    mlp_g, gate_g = z_sum(mlp_g), x_sum(gate_g)
+    def grad_split(left, right):
+        return x_split(lane_blocks(rows_dot(left, right).astype(BF16)))
+
+    mlp_kept, mlp_sent = grad_split(mixed, cot)
+    mlp_x = send_seq(mlp_sent, 1)
+    mlp_sent, grad_gate, grad_up = tie((mlp_sent, grad_gate, grad_up))
+    part_lifted = jnp.dot(grad_gate, gate_full, preferred_element_type=F32) + jnp.dot(
+        grad_up, up_full, preferred_element_type=F32
+    )
+    half_hat = reduce_pair(part_lifted.reshape(2, 2, share, D), "core", 1)
+    part_lifted, grad_gate, grad_up = tie((part_lifted, grad_gate, grad_up))
+    gate_kept, gate_sent = grad_split(grad_gate, lifted)
+    gate_x = send_seq(gate_sent, 1)
+    half_hat, gate_sent = tie((half_hat, gate_sent))
+    grad_hat = reduce_pair(half_hat, "fy", 0)
+    up_kept, up_sent = grad_split(grad_up, lifted)
+    up_x = send_seq(up_sent, 1)
+    grad_hat, up_sent = tie((grad_hat, up_sent))
     grad_middle = cotangent.astype(F32) + norm_back(grad_hat, normed_mid, inverse_mid)
     grad_attn = group_rows(grad_middle.astype(BF16))
     grad_attended = cols_dot(grad_attn, attn_full).astype(BF16)
-    attn_g = rows_dot(attended, grad_attn).astype(BF16)
     grad_q, grad_k, grad_v = call_kernel(
         attend_back_kernel,
         [
@@ -408,37 +447,48 @@
         (query, keys, values, grad_attended, cosine, sine, q_seg, k_seg),
     )
     grad_kv = jnp.concatenate([grad_k, grad_v], axis=1)
-    mlp_g, gate_g, up_g, grad_kv, grad_q, attn_g = tie((mlp_g, gate_g, up_g, grad_kv, grad_q, attn_g))
-    low_edge = lax.ppermute(grad_kv[:HALF].astype(BF16), "seq", behind)
-    high_edge = lax.ppermute(grad_kv[HALF + rows :].astype(BF16), "seq", ahead)
-    gate_g, up_g = z_sum(gate_g), x_sum(up_g)
+    low_sent = grad_kv[:HALF].astype(BF16)
+    high_sent = grad_kv[HALF + rows :].astype(BF16)
+    low_edge = lax.ppermute(low_sent, "seq", behind)
+    high_edge = lax.ppermute(high_sent, "seq", ahead)
+    mlp_x, gate_x, low_sent, attended = tie((mlp_x, gate_x, low_sent, attended))
+    mlp_got = z_spread(x_sum(mlp_kept, mlp_x))
+    attn_g = rows_dot(attended, grad_attn).astype(BF16)
     attn_g = attn_g.reshape(seqs // 4, 2, 2, shard, D).transpose(1, 2, 0, 3, 4)
-    attn_g = trade(trade(attn_g, "core", 1), "fy", 0).reshape(seqs // 2, 2, shard, D)
+    attn_g = trade(trade(attn_g, "core", 1), "fy", 0).reshape(seqs, shard, D)
+    low_edge, high_edge, mlp_got = tie((low_edge, high_edge, mlp_got))
     middle_kv = grad_kv[HALF : HALF + rows]
     gap = jnp.zeros((rows - 2 * HALF, 2 * OWN), F32)
     edges = jnp.concatenate([high_edge.astype(F32), gap, low_edge.astype(F32)], axis=0)
     grad_packed = jnp.concatenate([grad_q, (middle_kv + edges).astype(BF16)], axis=1)
-    qkv_g = stacked(rows_dot(hidden, grad_packed))
-    gate_g, up_g, attn_g, qkv_g, grad_packed = tie((gate_g, up_g, attn_g, qkv_g, grad_packed))
-    up_g, attn_g, qkv_g = z_sum(up_g), x_sum(attn_g), x_sum(qkv_g)
-    part_hidden = cols_dot(grad_packed, qkv_full)
+    qkv_kept, qkv_sent = grad_split(grad_packed, hidden)
+    qkv_x = send_seq(qkv_sent, 1)
+    gate_x, qkv_sent = tie((gate_x, qkv_sent))
+    gate_got = z_spread(x_sum(gate_kept, gate_x))
+    attn_kept, attn_sent = x_split([attn_g[i] for i in range(seqs)])
+    attn_x = send_seq(attn_sent, 1)
+    up_x, gate_got, attn_sent = tie((up_x, gate_got, attn_sent))
+    up_got = z_spread(x_sum(up_kept, up_x))
+    part_hidden = jnp.dot(grad_packed, qkv_full, preferred_element_type=F32)
     grad_hidden = group_sum(part_hidden, share)
-    part_out = cols_dot(mixed, mlp_full)
+    part_out = jnp.dot(mixed, mlp_full, preferred_element_type=F32)
     output = middle + group_sum(part_out, share)
+    qkv_x, up_got, grad_hidden, output = tie((qkv_x, up_got, grad_hidden, output))
+    qkv_got = z_spread(x_sum(qkv_kept, qkv_x))
+    attn_x, qkv_got = tie((attn_x, qkv_got))
+    grad_attn_out = z_total(z_spread(x_sum(attn_kept, attn_x)))
+    mlp_g, gate_g, up_g = z_total(mlp_got), z_total(gate_got), z_total(up_got)
+    grad_qkv = z_total(qkv_got)
 
     def regroup_back(cells):
-        cells = cells.astype(BF16).reshape(2, 2, shard, -1)
+        cells = cells.T.astype(BF16).reshape(2, 2, shard, -1)
         return trade(trade(cells, "fy", 0), "core", 1)
 
     def back_columns(cells, parts, width):
         cells = cells.reshape(2, 2, shard, parts, width).transpose(2, 3, 0, 1, 4)
         return cells.reshape(shard, parts * 2 * 2 * width).astype(F32)
 
-    up_g, attn_g, qkv_g, mlp_g, gate_g, grad_hidden, output = tie(
-        (up_g, attn_g, qkv_g, mlp_g, gate_g, grad_hidden, output)
-    )
-    grad_qkv, grad_attn_out = z_sum(qkv_g), z_sum(attn_g)
-    rest_g = regroup_back(jnp.concatenate([mlp_g, gate_g, up_g], axis=-1))
+    rest_g = regroup_back(jnp.concatenate([mlp_g, gate_g, up_g], axis=0))
     raw_mlp = back_columns(rest_g[..., :OWN_FF], 1, OWN_FF)
     raw_in = back_columns(rest_g[..., OWN_FF:], 2, OWN_FF)
     raw_qkv = back_columns(regroup_back(grad_qkv), 3, OWN)

time: 378 us -> 363 us (0.960)
  the two profiles are of different devices: /device:TPU:11 before, /device:TPU:0 now
where the time goes in v3:
time: 363 us; the launch traced here: 356 us
  waiting for transfers between devices  135 us (37%)
  starting transfers between devices  106 us (29%)
  other arithmetic  55.2 us (15%)
  local copies, waits for them, and re-layouts  33.1 us (9%)
  matrix products  15.3 us (4%)
  Pallas kernels  8.78 us (2%)
    ppermute x40, waiting for transfers between devices, send_seq(): return lax.ppermute(cells, ALL, flat_pairs(lambda i: i ^ flip * GROUP))  88.1 us
    ppermute x40, starting transfers between devices, send_seq(): return lax.ppermute(cells, ALL, flat_pairs(lambda i: i ^ flip * GROUP))  81.5 us
    ppermute x8, waiting for transfers between devices, reduce_pair(): got = lax.ppermute(sent, axis, [(0, 1), (1, 0)])  18.5 us
    ppermute x12, waiting for transfers between devices, trade(): got = lax.ppermute(sent, axis, [(0, 1), (1, 0)])  12.2 us
    unnamed x35, other arithmetic  11.1 us
    dot_general x10, matrix products, contract(): lax.dot_general(left, right, ((dims[0], dims[1]), ((), ())), preferred_el...  10.7 us
    pallas_call x2, Pallas kernels, call_kernel(): pl.pallas_call(kernel, out_shape=outs, in_specs=[pl.BlockSpec(memory_spac...  8.78 us
    ppermute x8, waiting for transfers between devices, join(): got = lax.ppermute(cells, axis, [(0, 1), (1, 0)])  7.95 us
  transfers between devices with their start and end apart: 72, of which 27 were waited for; matrix products, arithmetic and copies ran while one was open for 18% of the time, Pallas kernels for 2%

profile of v3, /device:TPU:0, one launch (start us, length us, event | category | flops | bytes accessed | tf_op | source)
XLA Modules:
  0.0 356.2 jit_solution(13282457145525951647)
XLA Ops:
  0.7 5.1 %collective-permute-start.7 = (bf16[32,1024]{1,0:T(8,128)(2,1)}, bf16[32,1024]{1,0:T(8,128)(2,1)S(1)}, u32[]{:S(2)}, u32[]{:S(2)}) collective-permute-start(bf16[32,1024]{1,0:T(8,128)(2,1)} %param.13), channel_id=1, source_target_pairs={{0,24},{1,25},{2,26},{3,27},{4,28},{5,29},{6,30},{7,31},{8,16},{9,... | collective-permute-start | bytes 196616 | tf_op jit(solution)/shard_map/ppermute | solution.py:31
  22.5 2.9 collective-permute-start.5
  27.1 3.6 %collective-permute-start.6 = (bf16[768,128]{0,1:T(8,128)(2,1)S(1)}, bf16[768,128]{0,1:T(8,128)(2,1)S(1)}, u32[]{:S(2)}, u32[]{:S(2)}) collective-permute-start(bf16[768,128]{0,1:T(8,128)(2,1)S(1)} %bitcast.414), channel_id=1, source_target_pairs={{0,24},{1,25},{2,26},{3,27},{4,28},{5,29},{6,30},{7,31},{8,16},{9,... | collective-permute-start | bytes 589832 | tf_op jit(solution)/shard_map/ppermute | solution.py:31
  32.0 7.6 %collective-permute-done.5 = bf16[768,128]{0,1:T(8,128)(2,1)S(1)} collective-permute-done((bf16[768,128]{0,1:T(8,128)(2,1)S(1)}, bf16[768,128]{0,1:T(8,128)(2,1)S(1)}, u32[]{:S(2)}, u32[]{:S(2)}) %collective-permute-start.5) | collective-permute-done | bytes 196640 | tf_op jit(solution)/shard_map/ppermute | solution.py:31
  43.9 4.0 %collective-permute-start.15 = (bf16[656,128]{0,1:T(8,128)(2,1)S(1)}, bf16[656,128]{0,1:T(8,128)(2,1)S(1)}, u32[]{:S(2)}, u32[]{:S(2)}) collective-permute-start(bf16[656,128]{0,1:T(8,128)(2,1)S(1)} %get-tuple-element.90), channel_id=1, source_target_pairs={{0,8},{1,9},{2,10},{3,11},{4,12},{5,13},{6,14},{7,15},{8,0},{9,1},... | collective-permute-start | bytes 503816 | tf_op jit(solution)/shard_map/ppermute | solution.py:31
  48.7 3.7 %collective-permute-start.16 = (bf16[656,128]{0,1:T(8,128)(2,1)S(1)}, bf16[656,128]{0,1:T(8,128)(2,1)S(1)}, u32[]{:S(2)}, u32[]{:S(2)}) collective-permute-start(bf16[656,128]{0,1:T(8,128)(2,1)S(1)} %get-tuple-element.90), channel_id=1, source_target_pairs={{0,16},{1,17},{2,18},{3,19},{4,20},{5,21},{6,22},{7,23},{8,24},{9,... | collective-permute-start | bytes 503816 | tf_op jit(solution)/shard_map/ppermute | solution.py:31
  54.5 11.7 %collective-permute-done.16 = bf16[656,128]{0,1:T(8,128)(2,1)S(1)} collective-permute-done((bf16[656,128]{0,1:T(8,128)(2,1)S(1)}, bf16[656,128]{0,1:T(8,128)(2,1)S(1)}, u32[]{:S(2)}, u32[]{:S(2)}) %collective-permute-start.16) | collective-permute-done | bytes 167968 | tf_op jit(solution)/shard_map/ppermute | solution.py:31
  66.2 2.9 collective-permute-start.10
  71.6 5.9 %collective-permute-done.11 = bf16[64,1024]{1,0:T(8,128)(2,1)S(1)} collective-permute-done((bf16[64,1024]{1,0:T(8,128)(2,1)S(1)}, bf16[64,1024]{1,0:T(8,128)(2,1)S(1)}, u32[]{:S(2)}, u32[]{:S(2)}) %collective-permute-start.11) | collective-permute-done | bytes 131104 | tf_op jit(solution)/shard_map/ppermute | solution.py:357
  78.7 3.8 %shard_map.152 = (bf16[512,256]{1,0:T(8,128)(2,1)S(1)}, bf16[640,256]{1,0:T(8,128)(2,1)S(1)}, bf16[640,256]{1,0:T(8,128)(2,1)S(1)}, bf16[512,256]{1,0:T(8,128)(2,1)S(1)}) custom-call(f32[640,768]{1,0:T(8,128)S(1)} %fusion.6.packed, f32[640,128]{1,0:T(8,128)S(1)} %get-tuple-element.297.cosine, f32[640,128]{1,0:T(8,128)S(1)} %get-tuple-element.296.sine, ...), custom_call_target="tpu_custom_call" | custom-call | flops 268435456 | bytes 3805696 | tf_op jit(solution)/shard_map/pallas_call | solution.py:290
  85.2 2.3 collective-permute-start.21
  95.5 2.0 collective-permute-done.21
  97.6 7.4 %collective-permute-done.22 = bf16[656,128]{0,1:T(8,128)(2,1)} collective-permute-done((bf16[656,128]{0,1:T(8,128)(2,1)}, bf16[656,128]{0,1:T(8,128)(2,1)}, u32[]{:S(2)}, u32[]{:S(2)}) %collective-permute-start.22) | collective-permute-done | bytes 167968 | tf_op jit(solution)/shard_map/ppermute | solution.py:31
  105.0 2.7 collective-permute-start.28
  113.6 3.6 %collective-permute-done.25 = bf16[128,1024]{1,0:T(8,128)(2,1)} collective-permute-done((bf16[128,1024]{1,0:T(8,128)(2,1)}, bf16[128,1024]{1,0:T(8,128)(2,1)}, u32[]{:S(2)}, u32[]{:S(2)}) %collective-permute-start.25) | collective-permute-done | bytes 262176 | tf_op jit(solution)/shard_map/ppermute | solution.py:54
  120.1 5.9 %collective-permute-done.31 = bf16[4,656,128]{2,1,0:T(8,128)(2,1)} collective-permute-done((bf16[4,656,128]{2,1,0:T(8,128)(2,1)}, bf16[4,656,128]{2,1,0:T(8,128)(2,1)}, u32[]{:S(2)}, u32[]{:S(2)}) %collective-permute-start.31) | collective-permute-done | bytes 671776 | tf_op jit(solution)/shard_map/ppermute | solution.py:31
  127.2 2.3 copy.109
  134.6 2.1 fusion.75
  140.3 2.2 copy.114
  142.5 2.3 copy.116
  149.4 2.0 fusion.76
  151.5 14.6 %collective-permute-done.34 = bf16[4,656,128]{2,1,0:T(8,128)(2,1)} collective-permute-done((bf16[4,656,128]{2,1,0:T(8,128)(2,1)S(1)}, bf16[4,656,128]{2,1,0:T(8,128)(2,1)}, u32[]{:S(2)}, u32[]{:S(2)}) %collective-permute-start.34) | collective-permute-done | bytes 671776 | tf_op jit(solution)/shard_map/ppermute | solution.py:31
  166.1 2.6 copy.120
  175.0 2.9 multiply_convert_fusion
  193.0 5.6 %collective-permute-done.37 = bf16[128,1024]{1,0:T(8,128)(2,1)S(1)} collective-permute-done((bf16[128,1024]{1,0:T(8,128)(2,1)S(1)}, bf16[128,1024]{1,0:T(8,128)(2,1)S(1)}, u32[]{:S(2)}, u32[]{:S(2)}) %collective-permute-start.37) | collective-permute-done | bytes 262176 | tf_op jit(solution)/shard_map/ppermute | solution.py:54
  200.9 6.5 %collective-permute-done.38 = bf16[128,1024]{1,0:T(8,128)(2,1)S(1)} collective-permute-done((bf16[128,1024]{1,0:T(8,128)(2,1)S(1)}, bf16[128,1024]{1,0:T(8,128)(2,1)S(1)}, u32[]{:S(2)}, u32[]{:S(2)}) %collective-permute-start.38) | collective-permute-done | bytes 262176 | tf_op jit(solution)/shard_map/ppermute | solution.py:45
  211.9 6.2 %collective-permute-done.60 = bf16[128,1024]{1,0:T(8,128)(2,1)} collective-permute-done((bf16[128,1024]{1,0:T(8,128)(2,1)}, bf16[128,1024]{1,0:T(8,128)(2,1)}, u32[]{:S(2)}, u32[]{:S(2)}) %collective-permute-start.60) | collective-permute-done | bytes 262176 | tf_op jit(solution)/shard_map/ppermute | solution.py:54
  218.0 2.0 fusion.29
  222.8 5.0 %shard_map.153 = (bf16[512,256]{1,0:T(8,128)(2,1)S(1)}, f32[640,256]{1,0:T(8,128)S(1)}, f32[640,256]{1,0:T(8,128)S(1)}) custom-call(bf16[512,256]{1,0:T(8,128)(2,1)S(1)} %get-tuple-element.94.query, bf16[640,256]{1,0:T(8,128)(2,1)S(1)} %get-tuple-element.95.keys, bf16[640,256]{1,0:T(8,128)(2,1)S(1)} %get-tuple-element.96.values, ...), custom_call_target="tpu_custom_call" | custom-call | flops 805306368 | bytes 3412480 | tf_op jit(solution)/shard_map/pallas_call | solution.py:290
  229.6 12.8 %collective-permute-done.42 = bf16[4,656,128]{2,1,0:T(8,128)(2,1)S(1)} collective-permute-done((bf16[4,656,128]{2,1,0:T(8,128)(2,1)}, bf16[4,656,128]{2,1,0:T(8,128)(2,1)S(1)}, u32[]{:S(2)}, u32[]{:S(2)}) %collective-permute-start.42) | collective-permute-done | bytes 671776 | tf_op jit(solution)/shard_map/ppermute | solution.py:31
  242.7 11.3 %collective-permute-start.44 = (bf16[656,128]{1,0:T(8,128)(2,1)S(1)}, bf16[656,128]{1,0:T(8,128)(2,1)S(1)}, u32[]{:S(2)}, u32[]{:S(2)}) collective-permute-start(bf16[656,128]{1,0:T(8,128)(2,1)S(1)} %get-tuple-element.252), channel_id=1, source_target_pairs={{0,8},{1,9},{2,10},{3,11},{4,12},{5,13},{6,14},{7,15},{8,0},{9,1},... | collective-permute-start | bytes 503816 | tf_op jit(solution)/shard_map/ppermute | solution.py:31
  256.4 4.3 %collective-permute-start.41 = (bf16[64,512]{1,0:T(8,128)(2,1)S(1)}, bf16[64,512]{1,0:T(8,128)(2,1)S(1)}, u32[]{:S(2)}, u32[]{:S(2)}) collective-permute-start(bf16[64,512]{1,0:T(8,128)(2,1)S(1)} %get-tuple-element.254), channel_id=1, source_target_pairs={{0,4},{4,8},{8,12},{12,16},{16,20},{20,24},{24,28},{1,5},{5,9},{9,... | collective-permute-start | bytes 196616 | tf_op jit(solution)/shard_map/ppermute | solution.py:453
  263.2 5.1 %collective-permute-done.45 = bf16[656,128]{1,0:T(8,128)(2,1)S(1)} collective-permute-done((bf16[656,128]{1,0:T(8,128)(2,1)S(1)}, bf16[656,128]{1,0:T(8,128)(2,1)S(1)}, u32[]{:S(2)}, u32[]{:S(2)}) %collective-permute-start.45) | collective-permute-done | bytes 167968 | tf_op jit(solution)/shard_map/ppermute | solution.py:31
  271.8 3.3 collective-permute-start.49
  275.1 3.1 collective-permute-start.50
  281.8 7.2 %collective-permute-done.53 = bf16[1,2,2,32,1024]{4,3,1,0,2:T(8,128)(2,1)S(1)} collective-permute-done((bf16[1,2,2,32,1024]{4,3,1,0,2:T(8,128)(2,1)S(1)}, bf16[1,2,2,32,1024]{4,3,1,0,2:T(8,128)(2,1)S(1)}, u32[]{:S(2)}, u32[]{:S(2)}) %collective-permute-start.53) | collective-permute-done | bytes 262176 | tf_op jit(solution)/shard_map/ppermute | solution.py:38
  290.6 2.0 collective-permute-start.61
  294.0 2.1 collective-permute-start.54
  296.1 2.0 collective-permute-start.55
  298.2 3.1 collective-permute-done.58
  301.3 2.4 collective-permute-start.56
  303.9 6.8 %collective-permute-done.56 = bf16[656,128]{1,0:T(8,128)(2,1)S(1)} collective-permute-done((bf16[656,128]{1,0:T(8,128)(2,1)S(1)}, bf16[656,128]{1,0:T(8,128)(2,1)S(1)}, u32[]{:S(2)}, u32[]{:S(2)}) %collective-permute-start.56) | collective-permute-done | bytes 167968 | tf_op jit(solution)/shard_map/ppermute | solution.py:31
  313.4 4.1 %collective-permute-start.62 = (bf16[768,128]{1,0:T(8,128)(2,1)S(1)}, bf16[768,128]{1,0:T(8,128)(2,1)S(1)}, u32[]{:S(2)}, u32[]{:S(2)}) collective-permute-start(bf16[768,128]{1,0:T(8,128)(2,1)S(1)} %get-tuple-element.214), channel_id=1, source_target_pairs={{0,8},{1,9},{2,10},{3,11},{4,12},{5,13},{6,14},{7,15},{8,0},{9,1},... | collective-permute-start | bytes 589832 | tf_op jit(solution)/shard_map/ppermute | solution.py:31
  321.5 3.9 %collective-permute-done.62 = bf16[768,128]{1,0:T(8,128)(2,1)S(1)} collective-permute-done((bf16[768,128]{1,0:T(8,128)(2,1)S(1)}, bf16[768,128]{1,0:T(8,128)(2,1)S(1)}, u32[]{:S(2)}, u32[]{:S(2)}) %collective-permute-start.62) | collective-permute-done | bytes 196640 | tf_op jit(solution)/shard_map/ppermute | solution.py:31
  325.4 9.3 %collective-permute-done.63 = bf16[768,128]{1,0:T(8,128)(2,1)S(1)} collective-permute-done((bf16[768,128]{1,0:T(8,128)(2,1)S(1)}, bf16[768,128]{1,0:T(8,128)(2,1)S(1)}, u32[]{:S(2)}, u32[]{:S(2)}) %collective-permute-start.63) | collective-permute-done | bytes 196640 | tf_op jit(solution)/shard_map/ppermute | solution.py:31
  335.8 3.4 collective-permute-start.67
  339.7 2.0 collective-permute-start.69
  342.9 3.7 %collective-permute-done.65 = bf16[1,2,32,768]{3,2,1,0:T(8,128)(2,1)S(1)} collective-permute-done((bf16[1,2,32,768]{3,2,1,0:T(8,128)(2,1)S(1)}, bf16[1,2,32,768]{3,2,1,0:T(8,128)(2,1)S(1)}, u32[]{:S(2)}, u32[]{:S(2)}) %collective-permute-start.65) | collective-permute-done | bytes 98336 | tf_op jit(solution)/shard_map/ppermute | solution.py:38
  (444 shorter events, 130.2 us)
Async XLA Ops:
  0.7 14.5 %collective-permute-start.7 = (bf16[32,1024]{1,0:T(8,128)(2,1)}, bf16[32,1024]{1,0:T(8,128)(2,1)S(1)}, u32[]{:S(2)}, u32[]{:S(2)}) collective-permute-start(bf16[32,1024]{1,0:T(8,128)(2,1)} %param.13), channel_id=1, source_target_pairs={{0,24},{1,25},{2,26},{3,27},{4,28},{5,29},{6,30},{7,31},{8,16},{9,... | collective-permute-start | bytes 196616 | tf_op jit(solution)/shard_map/ppermute | solution.py:31
  5.8 11.1 %collective-permute-start.8 = (bf16[32,1024]{1,0:T(8,128)(2,1)}, bf16[32,1024]{1,0:T(8,128)(2,1)S(1)}, u32[]{:S(2)}, u32[]{:S(2)}) collective-permute-start(bf16[32,1024]{1,0:T(8,128)(2,1)} %param.13), channel_id=1, source_target_pairs={{0,16},{1,17},{2,18},{3,19},{4,20},{5,21},{6,22},{7,23},{8,24},{9,... | collective-permute-start | bytes 196616 | tf_op jit(solution)/shard_map/ppermute | solution.py:31
  5.8 11.7 %collective-permute-start.9 = (bf16[32,1024]{1,0:T(8,128)(2,1)}, bf16[32,1024]{1,0:T(8,128)(2,1)}, u32[]{:S(2)}, u32[]{:S(2)}) collective-permute-start(bf16[32,1024]{1,0:T(8,128)(2,1)} %param.13), channel_id=1, source_target_pairs={{0,8},{1,9},{2,10},{3,11},{4,12},{5,13},{6,14},{7,15},{8,0},{9,1},... | collective-permute-start | bytes 196616 | tf_op jit(solution)/shard_map/ppermute | solution.py:31
  12.2 10.3 %collective-permute-start.13 = (bf16[1,2,32,1968]{3,2,1,0:T(8,128)(2,1)S(1)}, bf16[1,2,32,1968]{3,2,1,0:T(8,128)(2,1)S(1)}, u32[]{:S(2)}, u32[]{:S(2)}) collective-permute-start(bf16[1,2,32,1968]{3,2,1,0:T(8,128)(2,1)S(1)} %fusion.41), channel_id=1, source_target_pairs={{0,2},{2,0},{1,3},{3,1},{4,6},{6,4},{5,7},{7,5},{8,10},{10,8},{9,1... | collective-permute-start | bytes 755720 | tf_op jit(solution)/shard_map/ppermute | solution.py:38
  15.1 12.0 %collective-permute-start = (bf16[128,1024]{1,0:T(8,128)(2,1)S(1)}, bf16[128,1024]{1,0:T(8,128)(2,1)S(1)}, u32[]{:S(2)}, u32[]{:S(2)}) collective-permute-start(bf16[128,1024]{1,0:T(8,128)(2,1)S(1)} %fusion.19), channel_id=1, source_target_pairs={{0,2},{2,0},{1,3},{3,1},{4,6},{6,4},{5,7},{7,5},{8,10},{10,8},{9,1... | collective-permute-start | bytes 786440 | tf_op jit(solution)/shard_map/ppermute | solution.py:45
  16.9 14.1 %collective-permute-start.29 = (bf16[128,1024]{1,0:T(8,128)(2,1)S(1)}, bf16[128,1024]{1,0:T(8,128)(2,1)S(1)}, u32[]{:S(2)}, u32[]{:S(2)}) collective-permute-start(bf16[128,1024]{1,0:T(8,128)(2,1)S(1)} %copy-done.26), channel_id=1, source_target_pairs={{0,2},{2,0},{1,3},{3,1},{4,6},{6,4},{5,7},{7,5},{8,10},{10,8},{9,1... | collective-permute-start | bytes 786440 | tf_op jit(solution)/shard_map/ppermute | solution.py:45
  19.6 20.0 %collective-permute-start.18 = (bf16[4,32,1024]{2,1,0:T(8,128)(2,1)S(1)}, bf16[4,32,1024]{2,1,0:T(8,128)(2,1)S(1)}, u32[]{:S(2)}, u32[]{:S(2)}) collective-permute-start(bf16[4,32,1024]{2,1,0:T(8,128)(2,1)S(1)} %pad_maximum_fusion.22), channel_id=1, source_target_pairs={{0,4},{1,5},{2,6},{3,7},{4,0},{5,1},{6,2},{7,3},{8,12},{9,13},{10,... | collective-permute-start | bytes 786440 | tf_op jit(solution)/shard_map/ppermute | solution.py:31
  21.2 10.8 %collective-permute-start.4 = (bf16[768,128]{0,1:T(8,128)(2,1)S(1)}, bf16[768,128]{0,1:T(8,128)(2,1)S(1)}, u32[]{:S(2)}, u32[]{:S(2)}) collective-permute-start(bf16[768,128]{0,1:T(8,128)(2,1)S(1)} %bitcast.412), channel_id=1, source_target_pairs={{0,8},{1,9},{2,10},{3,11},{4,12},{5,13},{6,14},{7,15},{8,0},{9,1},... | collective-permute-start | bytes 589832 | tf_op jit(solution)/shard_map/ppermute | solution.py:31
  22.5 17.1 %collective-permute-start.5 = (bf16[768,128]{0,1:T(8,128)(2,1)S(1)}, bf16[768,128]{0,1:T(8,128)(2,1)S(1)}, u32[]{:S(2)}, u32[]{:S(2)}) collective-permute-start(bf16[768,128]{0,1:T(8,128)(2,1)S(1)} %bitcast.413), channel_id=1, source_target_pairs={{0,16},{1,17},{2,18},{3,19},{4,20},{5,21},{6,22},{7,23},{8,24},{9,... | collective-permute-start | bytes 589832 | tf_op jit(solution)/shard_map/ppermute | solution.py:31
  27.1 12.5 %collective-permute-start.6 = (bf16[768,128]{0,1:T(8,128)(2,1)S(1)}, bf16[768,128]{0,1:T(8,128)(2,1)S(1)}, u32[]{:S(2)}, u32[]{:S(2)}) collective-permute-start(bf16[768,128]{0,1:T(8,128)(2,1)S(1)} %bitcast.414), channel_id=1, source_target_pairs={{0,24},{1,25},{2,26},{3,27},{4,28},{5,29},{6,30},{7,31},{8,16},{9,... | collective-permute-start | bytes 589832 | tf_op jit(solution)/shard_map/ppermute | solution.py:31
  31.0 11.9 %collective-permute-start.14 = (bf16[2,1,32,1968]{3,2,1,0:T(8,128)(2,1)S(1)}, bf16[2,1,32,1968]{3,2,1,0:T(8,128)(2,1)S(1)}, u32[]{:S(2)}, u32[]{:S(2)}) collective-permute-start(bf16[2,1,32,1968]{3,2,1,0:T(8,128)(2,1)S(1)} %fusion.49), channel_id=1, source_target_pairs={{0,1},{1,0},{2,3},{3,2},{4,5},{5,4},{6,7},{7,6},{8,9},{9,8},{10,11... | collective-permute-start | bytes 755720 | tf_op jit(solution)/shard_map/ppermute | solution.py:38
  32.0 20.5 %collective-permute-start.1 = (bf16[2,128,1024]{2,1,0:T(8,128)(2,1)S(1)}, bf16[2,128,1024]{2,1,0:T(8,128)(2,1)S(1)}, u32[]{:S(2)}, u32[]{:S(2)}) collective-permute-start(bf16[2,128,1024]{2,1,0:T(8,128)(2,1)S(1)} %pad_maximum_fusion.13), channel_id=1, source_target_pairs={{0,1},{1,0},{2,3},{3,2},{4,5},{5,4},{6,7},{7,6},{8,9},{9,8},{10,11... | collective-permute-start | bytes 1572872 | tf_op jit(solution)/shard_map/ppermute | solution.py:45
  39.6 50.6 %collective-permute-start.30 = (bf16[2,128,1024]{2,1,0:T(8,128)(2,1)S(1)}, bf16[2,128,1024]{2,1,0:T(8,128)(2,1)S(1)}, u32[]{:S(2)}, u32[]{:S(2)}) collective-permute-start(bf16[2,128,1024]{2,1,0:T(8,128)(2,1)S(1)} %pad_maximum_fusion.16), channel_id=1, source_target_pairs={{0,1},{1,0},{2,3},{3,2},{4,5},{5,4},{6,7},{7,6},{8,9},{9,8},{10,11... | collective-permute-start | bytes 1572872 | tf_op jit(solution)/shard_map/ppermute | solution.py:45
  41.6 29.3 %collective-permute-start.12 = (bf16[4,768,128]{1,2,0:T(8,128)(2,1)S(1)}, bf16[4,768,128]{1,2,0:T(8,128)(2,1)S(1)}, u32[]{:S(2)}, u32[]{:S(2)}) collective-permute-start(bf16[4,768,128]{1,2,0:T(8,128)(2,1)S(1)} %pad_maximum_fusion.4), channel_id=1, source_target_pairs={{0,4},{1,5},{2,6},{3,7},{4,0},{5,1},{6,2},{7,3},{8,12},{9,13},{10,... | collective-permute-start | bytes 2359304 | tf_op jit(solution)/shard_map/ppermute | solution.py:31
  43.9 10.5 %collective-permute-start.15 = (bf16[656,128]{0,1:T(8,128)(2,1)S(1)}, bf16[656,128]{0,1:T(8,128)(2,1)S(1)}, u32[]{:S(2)}, u32[]{:S(2)}) collective-permute-start(bf16[656,128]{0,1:T(8,128)(2,1)S(1)} %get-tuple-element.90), channel_id=1, source_target_pairs={{0,8},{1,9},{2,10},{3,11},{4,12},{5,13},{6,14},{7,15},{8,0},{9,1},... | collective-permute-start | bytes 503816 | tf_op jit(solution)/shard_map/ppermute | solution.py:31
  48.7 17.5 %collective-permute-start.16 = (bf16[656,128]{0,1:T(8,128)(2,1)S(1)}, bf16[656,128]{0,1:T(8,128)(2,1)S(1)}, u32[]{:S(2)}, u32[]{:S(2)}) collective-permute-start(bf16[656,128]{0,1:T(8,128)(2,1)S(1)} %get-tuple-element.90), channel_id=1, source_target_pairs={{0,16},{1,17},{2,18},{3,19},{4,20},{5,21},{6,22},{7,23},{8,24},{9,... | collective-permute-start | bytes 503816 | tf_op jit(solution)/shard_map/ppermute | solution.py:31
  52.5 13.7 %collective-permute-start.17 = (bf16[656,128]{0,1:T(8,128)(2,1)S(1)}, bf16[656,128]{0,1:T(8,128)(2,1)S(1)}, u32[]{:S(2)}, u32[]{:S(2)}) collective-permute-start(bf16[656,128]{0,1:T(8,128)(2,1)S(1)} %get-tuple-element.90), channel_id=1, source_target_pairs={{0,24},{1,25},{2,26},{3,27},{4,28},{5,29},{6,30},{7,31},{8,16},{9,... | collective-permute-start | bytes 503816 | tf_op jit(solution)/shard_map/ppermute | solution.py:31
  54.4 16.4 %collective-permute-start.20 = (bf16[2,1,2,32,1024]{4,3,1,0,2:T(8,128)(2,1)S(1)}, bf16[2,1,2,32,1024]{4,3,1,0,2:T(8,128)(2,1)S(1)}, u32[]{:S(2)}, u32[]{:S(2)}) collective-permute-start(bf16[2,1,2,32,1024]{4,3,1,0,2:T(8,128)(2,1)S(1)} %fusion.47), channel_id=1, source_target_pairs={{0,1},{1,0},{2,3},{3,2},{4,5},{5,4},{6,7},{7,6},{8,9},{9,8},{10,11... | collective-permute-start | bytes 786440 | tf_op jit(solution)/shard_map/ppermute | solution.py:38
  85.2 23.3 %collective-permute-start.24 = (bf16[2,128,1024]{2,1,0:T(8,128)(2,1)}, bf16[2,128,1024]{2,1,0:T(8,128)(2,1)}, u32[]{:S(2)}, u32[]{:S(2)}) collective-permute-start(bf16[2,128,1024]{2,1,0:T(8,128)(2,1)} %fusion.25), channel_id=1, source_target_pairs={{0,1},{1,0},{2,3},{3,2},{4,5},{5,4},{6,7},{7,6},{8,9},{9,8},{10,11... | collective-permute-start | bytes 1572872 | tf_op jit(solution)/shard_map/ppermute | solution.py:54
  85.2 12.3 %collective-permute-start.21 = (bf16[656,128]{0,1:T(8,128)(2,1)}, bf16[656,128]{0,1:T(8,128)(2,1)}, u32[]{:S(2)}, u32[]{:S(2)}) collective-permute-start(bf16[656,128]{0,1:T(8,128)(2,1)} %get-tuple-element.102), channel_id=1, source_target_pairs={{0,8},{1,9},{2,10},{3,11},{4,12},{5,13},{6,14},{7,15},{8,0},{9,1},... | collective-permute-start | bytes 503816 | tf_op jit(solution)/shard_map/ppermute | solution.py:31
  87.5 17.5 %collective-permute-start.22 = (bf16[656,128]{0,1:T(8,128)(2,1)}, bf16[656,128]{0,1:T(8,128)(2,1)}, u32[]{:S(2)}, u32[]{:S(2)}) collective-permute-start(bf16[656,128]{0,1:T(8,128)(2,1)} %get-tuple-element.102), channel_id=1, source_target_pairs={{0,16},{1,17},{2,18},{3,19},{4,20},{5,21},{6,22},{7,23},{8,24},{9,... | collective-permute-start | bytes 503816 | tf_op jit(solution)/shard_map/ppermute | solution.py:31
  88.7 18.9 %collective-permute-start.23 = (bf16[656,128]{0,1:T(8,128)(2,1)}, bf16[656,128]{0,1:T(8,128)(2,1)}, u32[]{:S(2)}, u32[]{:S(2)}) collective-permute-start(bf16[656,128]{0,1:T(8,128)(2,1)} %get-tuple-element.102), channel_id=1, source_target_pairs={{0,24},{1,25},{2,26},{3,27},{4,28},{5,29},{6,30},{7,31},{8,16},{9,... | collective-permute-start | bytes 503816 | tf_op jit(solution)/shard_map/ppermute | solution.py:31
  90.2 47.8 %collective-permute-start.26 = (bf16[656,128]{0,1:T(8,128)(2,1)}, bf16[656,128]{0,1:T(8,128)(2,1)}, u32[]{:S(2)}, u32[]{:S(2)}) collective-permute-start(bf16[656,128]{0,1:T(8,128)(2,1)} %get-tuple-element.110), channel_id=1, source_target_pairs={{0,8},{1,9},{2,10},{3,11},{4,12},{5,13},{6,14},{7,15},{8,0},{9,1},... | collective-permute-start | bytes 503816 | tf_op jit(solution)/shard_map/ppermute | solution.py:31
  97.5 40.5 %collective-permute-start.27 = (bf16[656,128]{0,1:T(8,128)(2,1)}, bf16[656,128]{0,1:T(8,128)(2,1)}, u32[]{:S(2)}, u32[]{:S(2)}) collective-permute-start(bf16[656,128]{0,1:T(8,128)(2,1)} %get-tuple-element.110), channel_id=1, source_target_pairs={{0,16},{1,17},{2,18},{3,19},{4,20},{5,21},{6,22},{7,23},{8,24},{9,... | collective-permute-start | bytes 503816 | tf_op jit(solution)/shard_map/ppermute | solution.py:31
  105.0 33.0 %collective-permute-start.28 = (bf16[656,128]{0,1:T(8,128)(2,1)}, bf16[656,128]{0,1:T(8,128)(2,1)}, u32[]{:S(2)}, u32[]{:S(2)}) collective-permute-start(bf16[656,128]{0,1:T(8,128)(2,1)} %get-tuple-element.110), channel_id=1, source_target_pairs={{0,24},{1,25},{2,26},{3,27},{4,28},{5,29},{6,30},{7,31},{8,16},{9,... | collective-permute-start | bytes 503816 | tf_op jit(solution)/shard_map/ppermute | solution.py:31
  107.6 18.3 %collective-permute-start.31 = (bf16[4,656,128]{2,1,0:T(8,128)(2,1)}, bf16[4,656,128]{2,1,0:T(8,128)(2,1)}, u32[]{:S(2)}, u32[]{:S(2)}) collective-permute-start(bf16[4,656,128]{2,1,0:T(8,128)(2,1)} %copy.108), channel_id=1, source_target_pairs={{0,4},{1,5},{2,6},{3,7},{4,0},{5,1},{6,2},{7,3},{8,12},{9,13},{10,... | collective-permute-start | bytes 2015240 | tf_op jit(solution)/shard_map/ppermute | solution.py:31
  117.2 25.3 %collective-permute-start.35 = (bf16[4,656,128]{2,1,0:T(8,128)(2,1)}, bf16[4,656,128]{2,1,0:T(8,128)(2,1)}, u32[]{:S(2)}, u32[]{:S(2)}) collective-permute-start(bf16[4,656,128]{2,1,0:T(8,128)(2,1)} %copy.115), channel_id=1, source_target_pairs={{0,4},{1,5},{2,6},{3,7},{4,0},{5,1},{6,2},{7,3},{8,12},{9,13},{10,... | collective-permute-start | bytes 2015240 | tf_op jit(solution)/shard_map/ppermute | solution.py:31
  148.4 17.7 %collective-permute-start.34 = (bf16[4,656,128]{2,1,0:T(8,128)(2,1)S(1)}, bf16[4,656,128]{2,1,0:T(8,128)(2,1)}, u32[]{:S(2)}, u32[]{:S(2)}) collective-permute-start(bf16[4,656,128]{2,1,0:T(8,128)(2,1)S(1)} %copy-done.43), channel_id=1, source_target_pairs={{0,4},{1,5},{2,6},{3,7},{4,0},{5,1},{6,2},{7,3},{8,12},{9,13},{10,... | collective-permute-start | bytes 2015240 | tf_op jit(solution)/shard_map/ppermute | solution.py:31
  187.8 13.0 %collective-permute-start.59 = (bf16[2,128,1024]{2,1,0:T(8,128)(2,1)S(1)}, bf16[2,128,1024]{2,1,0:T(8,128)(2,1)S(1)}, u32[]{:S(2)}, u32[]{:S(2)}) collective-permute-start(bf16[2,128,1024]{2,1,0:T(8,128)(2,1)S(1)} %fusion.28), channel_id=1, source_target_pairs={{0,1},{1,0},{2,3},{3,2},{4,5},{5,4},{6,7},{7,6},{8,9},{9,8},{10,11... | collective-permute-start | bytes 1572872 | tf_op jit(solution)/shard_map/ppermute | solution.py:54
  208.3 11.7 %collective-permute-start.39 = (bf16[2,128,1024]{2,1,0:T(8,128)(2,1)}, bf16[2,128,1024]{2,1,0:T(8,128)(2,1)}, u32[]{:S(2)}, u32[]{:S(2)}) collective-permute-start(bf16[2,128,1024]{2,1,0:T(8,128)(2,1)} %pad_maximum_fusion.18), channel_id=1, source_target_pairs={{0,1},{1,0},{2,3},{3,2},{4,5},{5,4},{6,7},{7,6},{8,9},{9,8},{10,11... | collective-permute-start | bytes 1572872 | tf_op jit(solution)/shard_map/ppermute | solution.py:45
  209.9 19.7 %collective-permute-start.43 = (bf16[4,656,128]{2,1,0:T(8,128)(2,1)}, bf16[4,656,128]{2,1,0:T(8,128)(2,1)S(1)}, u32[]{:S(2)}, u32[]{:S(2)}) collective-permute-start(bf16[4,656,128]{2,1,0:T(8,128)(2,1)} %pad_maximum_fusion.11), channel_id=1, source_target_pairs={{0,4},{1,5},{2,6},{3,7},{4,0},{5,1},{6,2},{7,3},{8,12},{9,13},{10,... | collective-permute-start | bytes 2015240 | tf_op jit(solution)/shard_map/ppermute | solution.py:31
  210.6 31.8 %collective-permute-start.42 = (bf16[4,656,128]{2,1,0:T(8,128)(2,1)}, bf16[4,656,128]{2,1,0:T(8,128)(2,1)S(1)}, u32[]{:S(2)}, u32[]{:S(2)}) collective-permute-start(bf16[4,656,128]{2,1,0:T(8,128)(2,1)} %pad_maximum_fusion.10), channel_id=1, source_target_pairs={{0,4},{1,5},{2,6},{3,7},{4,0},{5,1},{6,2},{7,3},{8,12},{9,13},{10,... | collective-permute-start | bytes 2015240 | tf_op jit(solution)/shard_map/ppermute | solution.py:31
  228.1 33.0 %collective-permute-start.40 = (bf16[64,512]{1,0:T(8,128)(2,1)S(1)}, bf16[64,512]{1,0:T(8,128)(2,1)S(1)}, u32[]{:S(2)}, u32[]{:S(2)}) collective-permute-start(bf16[64,512]{1,0:T(8,128)(2,1)S(1)} %get-tuple-element.255), channel_id=1, source_target_pairs={{4,0},{8,4},{12,8},{16,12},{20,16},{24,20},{28,24},{5,1},{9,5},{13... | collective-permute-start | bytes 196616 | tf_op jit(solution)/shard_map/ppermute | solution.py:452
  242.7 20.5 %collective-permute-start.44 = (bf16[656,128]{1,0:T(8,128)(2,1)S(1)}, bf16[656,128]{1,0:T(8,128)(2,1)S(1)}, u32[]{:S(2)}, u32[]{:S(2)}) collective-permute-start(bf16[656,128]{1,0:T(8,128)(2,1)S(1)} %get-tuple-element.252), channel_id=1, source_target_pairs={{0,8},{1,9},{2,10},{3,11},{4,12},{5,13},{6,14},{7,15},{8,0},{9,1},... | collective-permute-start | bytes 503816 | tf_op jit(solution)/shard_map/ppermute | solution.py:31
  253.9 14.4 %collective-permute-start.45 = (bf16[656,128]{1,0:T(8,128)(2,1)S(1)}, bf16[656,128]{1,0:T(8,128)(2,1)S(1)}, u32[]{:S(2)}, u32[]{:S(2)}) collective-permute-start(bf16[656,128]{1,0:T(8,128)(2,1)S(1)} %get-tuple-element.251), channel_id=1, source_target_pairs={{0,16},{1,17},{2,18},{3,19},{4,20},{5,21},{6,22},{7,23},{8,24},{9,... | collective-permute-start | bytes 503816 | tf_op jit(solution)/shard_map/ppermute | solution.py:31
  254.5 13.7 %collective-permute-start.46 = (bf16[656,128]{1,0:T(8,128)(2,1)S(1)}, bf16[656,128]{1,0:T(8,128)(2,1)S(1)}, u32[]{:S(2)}, u32[]{:S(2)}) collective-permute-start(bf16[656,128]{1,0:T(8,128)(2,1)S(1)} %get-tuple-element.250), channel_id=1, source_target_pairs={{0,24},{1,25},{2,26},{3,27},{4,28},{5,29},{6,30},{7,31},{8,16},{9,... | collective-permute-start | bytes 503816 | tf_op jit(solution)/shard_map/ppermute | solution.py:31
  261.2 29.4 %collective-permute-start.48 = (bf16[4,656,128]{2,1,0:T(8,128)(2,1)S(1)}, bf16[4,656,128]{2,1,0:T(8,128)(2,1)S(1)}, u32[]{:S(2)}, u32[]{:S(2)}) collective-permute-start(bf16[4,656,128]{2,1,0:T(8,128)(2,1)S(1)} %copy-done.42), channel_id=1, source_target_pairs={{0,4},{1,5},{2,6},{3,7},{4,0},{5,1},{6,2},{7,3},{8,12},{9,13},{10,... | collective-permute-start | bytes 2015240 | tf_op jit(solution)/shard_map/ppermute | solution.py:31
  263.2 17.5 %collective-permute-start.52 = (bf16[2,1,2,32,1024]{4,3,1,0,2:T(8,128)(2,1)S(1)}, bf16[2,1,2,32,1024]{4,3,1,0,2:T(8,128)(2,1)S(1)}, u32[]{:S(2)}, u32[]{:S(2)}) collective-permute-start(bf16[2,1,2,32,1024]{4,3,1,0,2:T(8,128)(2,1)S(1)} %dynamic-slice_bitcast_fusion), channel_id=1, source_target_pairs={{0,1},{1,0},{2,3},{3,2},{4,5},{5,4},{6,7},{7,6},{8,9},{9,8},{10,11... | collective-permute-start | bytes 786440 | tf_op jit(solution)/shard_map/ppermute | solution.py:38
  271.8 18.8 %collective-permute-start.49 = (bf16[656,128]{1,0:T(8,128)(2,1)S(1)}, bf16[656,128]{1,0:T(8,128)(2,1)S(1)}, u32[]{:S(2)}, u32[]{:S(2)}) collective-permute-start(bf16[656,128]{1,0:T(8,128)(2,1)S(1)} %get-tuple-element.248), channel_id=1, source_target_pairs={{0,8},{1,9},{2,10},{3,11},{4,12},{5,13},{6,14},{7,15},{8,0},{9,1},... | collective-permute-start | bytes 503816 | tf_op jit(solution)/shard_map/ppermute | solution.py:31
  275.1 17.5 %collective-permute-start.50 = (bf16[656,128]{1,0:T(8,128)(2,1)S(1)}, bf16[656,128]{1,0:T(8,128)(2,1)S(1)}, u32[]{:S(2)}, u32[]{:S(2)}) collective-permute-start(bf16[656,128]{1,0:T(8,128)(2,1)S(1)} %get-tuple-element.247), channel_id=1, source_target_pairs={{0,16},{1,17},{2,18},{3,19},{4,20},{5,21},{6,22},{7,23},{8,24},{9,... | collective-permute-start | bytes 503816 | tf_op jit(solution)/shard_map/ppermute | solution.py:31
  278.2 14.4 %collective-permute-start.51 = (bf16[656,128]{1,0:T(8,128)(2,1)S(1)}, bf16[656,128]{1,0:T(8,128)(2,1)S(1)}, u32[]{:S(2)}, u32[]{:S(2)}) collective-permute-start(bf16[656,128]{1,0:T(8,128)(2,1)S(1)} %get-tuple-element.246), channel_id=1, source_target_pairs={{0,24},{1,25},{2,26},{3,27},{4,28},{5,29},{6,30},{7,31},{8,16},{9,... | collective-permute-start | bytes 503816 | tf_op jit(solution)/shard_map/ppermute | solution.py:31
  290.6 20.3 %collective-permute-start.47 = (bf16[4,768,128]{2,1,0:T(8,128)(2,1)S(1)}, bf16[4,768,128]{2,1,0:T(8,128)(2,1)S(1)}, u32[]{:S(2)}, u32[]{:S(2)}) collective-permute-start(bf16[4,768,128]{2,1,0:T(8,128)(2,1)S(1)} %pad_maximum_fusion.9), channel_id=1, source_target_pairs={{0,4},{1,5},{2,6},{3,7},{4,0},{5,1},{6,2},{7,3},{8,12},{9,13},{10,... | collective-permute-start | bytes 2359304 | tf_op jit(solution)/shard_map/ppermute | solution.py:31
  290.6 30.9 %collective-permute-start.61 = (bf16[4,32,1024]{2,1,0:T(8,128)(2,1)}, bf16[4,32,1024]{2,1,0:T(8,128)(2,1)}, u32[]{:S(2)}, u32[]{:S(2)}) collective-permute-start(bf16[4,32,1024]{2,1,0:T(8,128)(2,1)} %pad_maximum_fusion.23), channel_id=1, source_target_pairs={{0,4},{1,5},{2,6},{3,7},{4,0},{5,1},{6,2},{7,3},{8,12},{9,13},{10,... | collective-permute-start | bytes 786440 | tf_op jit(solution)/shard_map/ppermute | solution.py:31
  312.0 30.7 %collective-permute-start.70 = (bf16[1,2,32,1968]{3,2,1,0:T(8,128)(2,1)}, bf16[1,2,32,1968]{3,2,1,0:T(8,128)(2,1)S(1)}, u32[]{:S(2)}, u32[]{:S(2)}) collective-permute-start(bf16[1,2,32,1968]{3,2,1,0:T(8,128)(2,1)} %constant_dynamic-slice_fusion), channel_id=1, source_target_pairs={{0,2},{2,0},{1,3},{3,1},{4,6},{6,4},{5,7},{7,5},{8,10},{10,8},{9,1... | collective-permute-start | bytes 755720 | tf_op jit(solution)/shard_map/ppermute | solution.py:38
  313.4 12.0 %collective-permute-start.62 = (bf16[768,128]{1,0:T(8,128)(2,1)S(1)}, bf16[768,128]{1,0:T(8,128)(2,1)S(1)}, u32[]{:S(2)}, u32[]{:S(2)}) collective-permute-start(bf16[768,128]{1,0:T(8,128)(2,1)S(1)} %get-tuple-element.214), channel_id=1, source_target_pairs={{0,8},{1,9},{2,10},{3,11},{4,12},{5,13},{6,14},{7,15},{8,0},{9,1},... | collective-permute-start | bytes 589832 | tf_op jit(solution)/shard_map/ppermute | solution.py:31
  317.5 17.2 %collective-permute-start.63 = (bf16[768,128]{1,0:T(8,128)(2,1)S(1)}, bf16[768,128]{1,0:T(8,128)(2,1)S(1)}, u32[]{:S(2)}, u32[]{:S(2)}) collective-permute-start(bf16[768,128]{1,0:T(8,128)(2,1)S(1)} %get-tuple-element.213), channel_id=1, source_target_pairs={{0,16},{1,17},{2,18},{3,19},{4,20},{5,21},{6,22},{7,23},{8,24},{9,... | collective-permute-start | bytes 589832 | tf_op jit(solution)/shard_map/ppermute | solution.py:31
  318.8 15.9 %collective-permute-start.64 = (bf16[768,128]{1,0:T(8,128)(2,1)S(1)}, bf16[768,128]{1,0:T(8,128)(2,1)S(1)}, u32[]{:S(2)}, u32[]{:S(2)}) collective-permute-start(bf16[768,128]{1,0:T(8,128)(2,1)S(1)} %get-tuple-element.212), channel_id=1, source_target_pairs={{0,24},{1,25},{2,26},{3,27},{4,28},{5,29},{6,30},{7,31},{8,16},{9,... | collective-permute-start | bytes 589832 | tf_op jit(solution)/shard_map/ppermute | solution.py:31
  335.8 11.0 %collective-permute-start.67 = (bf16[32,1024]{1,0:T(8,128)(2,1)S(1)}, bf16[32,1024]{1,0:T(8,128)(2,1)S(1)}, u32[]{:S(2)}, u32[]{:S(2)}) collective-permute-start(bf16[32,1024]{1,0:T(8,128)(2,1)S(1)} %get-tuple-element.289), channel_id=1, source_target_pairs={{0,8},{1,9},{2,10},{3,11},{4,12},{5,13},{6,14},{7,15},{8,0},{9,1},... | collective-permute-start | bytes 196616 | tf_op jit(solution)/shard_map/ppermute | solution.py:31
  (81 other events, 493.4 us)

commit v4 on v3

--- a/solution.py
+++ b/solution.py
@@ -14,6 +14,8 @@
 OWN_HEADS = HEADS // GROUP
 OWN = OWN_HEADS * HDIM
 OWN_FF = FF // GROUP
+WIDE = 2048
+VMEM_LIMIT = 48 * 1024 * 1024
 
 EPSILON = 1e-05
 MASKED = -1e30
@@ -69,26 +71,21 @@
     return lax.axis_size("seq") // 2
 
 
-def z_send(cells):
-    if depth_of() == 4:
-        return [cells] + [send_seq(cells, 2 * d) for d in range(1, 4)]
-    return [cells]
-
-
-def z_order(got):
-    z, me = depth_of(), lax.axis_index("seq") >> 1
-    if z == 4:
-        odd, up = (me & 1) == 1, (me >> 1) == 1
-        pairs = [
-            (jnp.where(odd, got[i + 1], got[i]), jnp.where(odd, got[i], got[i + 1])) for i in (0, 2)
-        ]
-        return jnp.stack(
-            [jnp.where(up, pairs[1][i], pairs[0][i]) for i in (0, 1)]
-            + [jnp.where(up, pairs[0][i], pairs[1][i]) for i in (0, 1)]
-        )
-    cells = got[0][None]
+def direct():
+    return lax.axis_size("seq") == 8
+
+
+def place_of_device():
+    seq = lax.axis_index("seq")
+    return jnp.stack([seq >> 1, seq & 1]).astype(jnp.int32)
+
+
+def z_gather(cells):
+    if direct():
+        return jnp.stack([cells] + [send_seq(cells, 2 * d) for d in range(1, 4)])
+    cells, me = cells[None], lax.axis_index("seq") >> 1
     flip = 1
-    while flip < z:
+    while flip < depth_of():
         other = send_seq(cells, 2 * flip)
         high = (me & flip) != 0
         cells = jnp.concatenate([jnp.where(high, other, cells), jnp.where(high, cells, other)])
@@ -96,38 +93,14 @@
     return cells
 
 
-def x_order(cells, got):
-    high = (lax.axis_index("seq") & 1) == 1
-    blocks = []
-    for i in range(cells.shape[0]):
-        blocks += [jnp.where(high, got[i], cells[i]), jnp.where(high, cells[i], got[i])]
-    return blocks
-
-
-def x_split(blocks):
-    high = (lax.axis_index("seq") & 1) == 1
-    pairs = list(zip(blocks[::2], blocks[1::2]))
-    kept = jnp.stack([jnp.where(high, b, a) for a, b in pairs])
-    sent = jnp.stack([jnp.where(high, a, b) for a, b in pairs])
-    return kept, sent
-
-
-def lane_blocks(grad):
-    count = lax.axis_size("seq")
-    size = grad.shape[1] // count
-    return [grad[:, i * size : (i + 1) * size] for i in range(count)]
-
-
 def x_sum(kept, got):
     return (kept.astype(F32) + got.astype(F32)).astype(BF16)
 
 
 def z_spread(cells):
-    z, me = depth_of(), lax.axis_index("seq") >> 1
-    if z == 4:
-        blocks = [lax.dynamic_index_in_dim(cells, me ^ d, 0, keepdims=False) for d in range(4)]
-        return [blocks[0]] + [send_seq(blocks[d], 2 * d) for d in range(1, 4)]
-    flip = z // 2
+    if direct():
+        return [cells[0]] + [send_seq(cells[d], 2 * d) for d in range(1, 4)]
+    flip, me = depth_of() // 2, lax.axis_index("seq") >> 1
     while flip:
         high = ((me & flip) != 0).astype(jnp.int32)
         kept = lax.dynamic_slice_in_dim(cells, high * flip, flip, 0)
@@ -137,8 +110,146 @@
     return [cells[0]]
 
 
-def z_total(got):
+def total_of(got):
     return sum(cells.astype(F32) for cells in got)
+
+
+def local_kernel(kernel, outs, args, scratch=()):
+    spaces = [
+        pltpu.SMEM if a.dtype == jnp.int32 and a.size == 2 else pltpu.VMEM for a in args
+    ]
+    moved = sum(a.size * a.dtype.itemsize for a in args)
+    return pl.pallas_call(
+        kernel,
+        out_shape=outs,
+        in_specs=[pl.BlockSpec(memory_space=s) for s in spaces],
+        out_specs=[pl.BlockSpec(memory_space=pltpu.VMEM)] * len(outs),
+        scratch_shapes=list(scratch),
+        compiler_params=pltpu.CompilerParams(vmem_limit_bytes=VMEM_LIMIT),
+        cost_estimate=pl.CostEstimate(flops=0, bytes_accessed=moved, transcendentals=0),
+    )(*args)
+
+
+def lane_assemble_kernel(cells, got, where, full):
+    for d in range(4):
+        z = where[0] ^ d
+        mine = pl.multiple_of((2 * z + where[1]) * 128, 128)
+        theirs = pl.multiple_of((2 * z + 1 - where[1]) * 128, 128)
+        full[:, pl.ds(mine, 128)] = cells[d]
+        full[:, pl.ds(theirs, 128)] = got[d]
+
+
+def lane_split_kernel(full, where, kept, sent):
+    for d in range(4):
+        z = where[0] ^ d
+        mine = pl.multiple_of((2 * z + where[1]) * 128, 128)
+        theirs = pl.multiple_of((2 * z + 1 - where[1]) * 128, 128)
+        kept[d] = full[:, pl.ds(mine, 128)]
+        sent[d] = full[:, pl.ds(theirs, 128)]
+
+
+def row_assemble_kernel(cells, got, where, full):
+    for d in range(4):
+        z = where[0] ^ d
+        full[2 * z + where[1]] = cells[d]
+        full[2 * z + 1 - where[1]] = got[d]
+
+
+def row_split_kernel(full, where, kept, sent):
+    for d in range(4):
+        z = where[0] ^ d
+        kept[d] = full[2 * z + where[1]]
+        sent[d] = full[2 * z + 1 - where[1]]
+
+
+def turn_kernel(cells, *outs):
+    turned = cells[...].astype(F32).T.astype(BF16)
+    at = 0
+    for out in outs:
+        out[...] = turned[at : at + out.shape[0]]
+        at += out.shape[0]
+
+
+def turn_back_kernel(*refs):
+    *parts, out, full = refs
+    at = 0
+    full[...] = jnp.zeros_like(full)
+    for i in range(0, len(parts), 4):
+        total = parts[i][...].astype(F32)
+        for j in range(1, 4):
+            total = total + parts[i + j][...].astype(F32)
+        full[at : at + total.shape[0], :] = total
+        at += total.shape[0]
+    out[...] = full[...].T.astype(out.dtype)
+
+
+def x_blocks(cells, got):
+    high = (lax.axis_index("seq") & 1) == 1
+    blocks = []
+    for i in range(cells.shape[0]):
+        blocks += [jnp.where(high, got[i], cells[i]), jnp.where(high, cells[i], got[i])]
+    return blocks
+
+
+def x_parts(blocks):
+    high = (lax.axis_index("seq") & 1) == 1
+    pairs = list(zip(blocks[::2], blocks[1::2]))
+    kept = jnp.stack([jnp.where(high, b, a) for a, b in pairs])
+    sent = jnp.stack([jnp.where(high, a, b) for a, b in pairs])
+    return kept, sent
+
+
+def assemble(cells, got):
+    if direct():
+        shape = like((cells.shape[1], D), BF16)
+        return local_kernel(lane_assemble_kernel, [shape], (cells, got, place_of_device()))[0]
+    return jnp.concatenate(x_blocks(cells, got), axis=-1)
+
+
+def split(grad):
+    count = lax.axis_size("seq")
+    size = D // count
+    if direct():
+        shape = like((4, grad.shape[0], size), BF16)
+        return local_kernel(lane_split_kernel, [shape, shape], (grad, place_of_device()))
+    return x_parts([grad[:, i * size : (i + 1) * size] for i in range(count)])
+
+
+def assemble_rows(cells, got):
+    if direct():
+        shape = like((8,) + cells.shape[1:], BF16)
+        return local_kernel(row_assemble_kernel, [shape], (cells, got, place_of_device()))[0]
+    return jnp.stack(x_blocks(cells, got))
+
+
+def split_rows(cells):
+    if direct():
+        shape = like((4,) + cells.shape[1:], BF16)
+        return local_kernel(row_split_kernel, [shape, shape], (cells, place_of_device()))
+    return x_parts([cells[i] for i in range(cells.shape[0])])
+
+
+def turn(cells, sizes):
+    if direct():
+        return local_kernel(turn_kernel, [like((n, cells.shape[0]), BF16) for n in sizes], (cells,))
+    turned, outs, at = cells.T, [], 0
+    for n in sizes:
+        outs.append(turned[at : at + n])
+        at += n
+    return outs
+
+
+def turn_back(chunks, width):
+    if direct():
+        lanes = chunks[0][0].shape[1]
+        return local_kernel(
+            turn_back_kernel,
+            [like((lanes, width), BF16)],
+            tuple(c for chunk in chunks for c in chunk),
+            [pltpu.VMEM((width, lanes), F32)],
+        )[0]
+    turned = jnp.concatenate([total_of(c) for c in chunks], axis=0).T.astype(BF16)
+    return jnp.pad(turned, ((0, 0), (0, width - turned.shape[1])))
 
 
 def place(index, seq_lengths):
@@ -280,9 +391,6 @@
         grad_k[:, at] = d_k * cosine[...] - half_swap(d_k) * sine[...]
 
 
-VMEM_LIMIT = 48 * 1024 * 1024
-
-
 def call_kernel(kernel, outs, blocks, flops, args):
     moved = sum(a.size * a.dtype.itemsize for a in args) + sum(
         o.size * o.dtype.itemsize for o in outs
@@ -321,50 +429,40 @@
 
     def regroup(cells):
         cells = trade(trade(cells, "fy", 0), "core", 1)
-        return cells.reshape(GROUP * shard, -1).T
-
-    def whole(cells, got):
-        return jnp.concatenate(x_order(cells, got), axis=-1)
-
-    attn_got = z_send(w_attn_out)
-    qkv_got = z_send(regroup(columns((w_qkv.astype(F32) * gain_a).astype(BF16), 3, OWN)))
-    rest = regroup(
-        jnp.concatenate(
-            [
-                columns(w_mlp_out, 1, OWN_FF),
-                columns((w_in.astype(F32) * gain_m).astype(BF16), 2, OWN_FF),
-            ],
-            axis=-1,
-        )
-    )
-    mlp_got, gate_got, up_got = (
-        z_send(rest[i * OWN_FF : (i + 1) * OWN_FF]) for i in range(3)
+        return cells.reshape(GROUP * shard, -1)
+
+    attn_z = z_gather(w_attn_out)
+    qkv = regroup(columns((w_qkv.astype(F32) * gain_a).astype(BF16), 3, OWN))
+    (qkv,) = turn(qkv, (3 * OWN,))
+    rest = jnp.concatenate(
+        [
+            columns(w_mlp_out, 1, OWN_FF),
+            columns((w_in.astype(F32) * gain_m).astype(BF16), 2, OWN_FF),
+            jnp.zeros((2, 2, shard, WIDE - 3 * OWN_FF), BF16),
+        ],
+        axis=-1,
     )
     ours = tokens.astype(F32)
     normed, inverse = normalize(ours)
+    attn_z, qkv, rest, normed = tie((attn_z, qkv, rest, normed))
+    qkv_z = z_gather(qkv)
+    attn_x = send_seq(attn_z, 1)
     hidden = group_rows(normed.astype(BF16))
-    cot = group_rows(cotangent)
-
-    attn_z = z_order(attn_got)
-    attn_x = send_seq(attn_z, 1)
-    qkv_got, attn_z = tie((qkv_got, attn_z))
-    qkv_z = z_order(qkv_got)
+    mlp, gate, up = turn(regroup(rest), (OWN_FF,) * 3)
+    qkv_z, attn_x, hidden, mlp, gate, up = tie((qkv_z, attn_x, hidden, mlp, gate, up))
+    mlp_z = z_gather(mlp)
     qkv_x = send_seq(qkv_z, 1)
-    hidden, qkv_z = tie((hidden, qkv_z))
     ahead = [(i, i + 1) for i in range(seqs - 1)]
     behind = [(i + 1, i) for i in range(seqs - 1)]
     before = lax.ppermute(hidden[rows - HALF :], "seq", ahead)
     after = lax.ppermute(hidden[:HALF], "seq", behind)
-    attn = jnp.stack(x_order(attn_z, attn_x))
-    attn = trade(attn.reshape(2, 2, seqs // 4, shard, D), "fy", 0)
-    attn = trade(attn, "core", 1)
+    attn = assemble_rows(attn_z, attn_x).reshape(2, 2, seqs // 4, shard, D)
+    attn = trade(trade(attn, "fy", 0), "core", 1)
     attn_full = attn.transpose(2, 0, 1, 3, 4).reshape(OWN, D)
-    mlp_got, qkv_z = tie((mlp_got, qkv_z))
-    mlp_z = z_order(mlp_got)
+    mlp_z, qkv_x, before, after, attn_full, gate = tie((mlp_z, qkv_x, before, after, attn_full, gate))
+    gate_z = z_gather(gate)
     mlp_x = send_seq(mlp_z, 1)
-    qkv_x, mlp_z, attn_full = tie((qkv_x, mlp_z, attn_full))
-    qkv_full = whole(qkv_z, qkv_x)
-
+    qkv_full = assemble(qkv_z, qkv_x)
     wide = jnp.concatenate([before, hidden, after], axis=0)
     index = seq * rows - HALF + jnp.arange(rows + 2 * HALF, dtype=jnp.int32)
     segment, position = place(jnp.clip(index, 0, total - 1), seq_lengths)
@@ -372,7 +470,6 @@
     q_seg = segment[HALF : HALF + rows][:, None]
     k_seg = segment[None, :]
     cosine, sine = angles(position)
-
     packed = cols_dot(wide, qkv_full)
     blocks = rows // 128
     flops = blocks * OWN_HEADS * 128 * 256 * 128 * 4
@@ -390,50 +487,40 @@
     )
     part = jnp.dot(attended, attn_full, preferred_element_type=F32)
     middle = ours + group_sum(part, share)
-    gate_got, part = tie((gate_got, part))
-    gate_z = z_order(gate_got)
+    gate_z, mlp_x, middle, up = tie((gate_z, mlp_x, middle, up))
+    up_z = z_gather(up)
     gate_x = send_seq(gate_z, 1)
-    gate_z, middle = tie((gate_z, middle))
     normed_mid, inverse_mid = normalize(middle)
     lifted = group_rows(normed_mid.astype(BF16))
-    mlp_x, gate_z = tie((mlp_x, gate_z))
-    mlp_full = whole(mlp_z, mlp_x)
+    cot = group_rows(cotangent)
+    mlp_full = assemble(mlp_z, mlp_x)
     grad_mixed = cols_dot(cot, mlp_full)
-    up_got, grad_mixed, lifted = tie((up_got, grad_mixed, lifted))
-    up_z = z_order(up_got)
+    up_z, gate_x, lifted, grad_mixed = tie((up_z, gate_x, lifted, grad_mixed))
     up_x = send_seq(up_z, 1)
-    gate_x, up_z = tie((gate_x, up_z))
-    gate_full = whole(gate_z, gate_x)
+    gate_full = assemble(gate_z, gate_x)
     gate = cols_dot(lifted, gate_full)
     up_x, gate = tie((up_x, gate))
-    up_full = whole(up_z, up_x)
+    up_full = assemble(up_z, up_x)
     up = cols_dot(lifted, up_full)
     mixed = geglu(gate, up).astype(BF16)
 
     unused, gelu_back = jax.vjp(geglu, gate, up)
     grad_gate, grad_up = gelu_back(grad_mixed)
     grad_gate, grad_up = grad_gate.astype(BF16), grad_up.astype(BF16)
-
-    def grad_split(left, right):
-        return x_split(lane_blocks(rows_dot(left, right).astype(BF16)))
-
-    mlp_kept, mlp_sent = grad_split(mixed, cot)
+    mlp_kept, mlp_sent = split(rows_dot(mixed, cot).astype(BF16))
+    mlp_kept, mlp_sent, grad_gate, grad_up = tie((mlp_kept, mlp_sent, grad_gate, grad_up))
     mlp_x = send_seq(mlp_sent, 1)
-    mlp_sent, grad_gate, grad_up = tie((mlp_sent, grad_gate, grad_up))
     part_lifted = jnp.dot(grad_gate, gate_full, preferred_element_type=F32) + jnp.dot(
         grad_up, up_full, preferred_element_type=F32
     )
-    half_hat = reduce_pair(part_lifted.reshape(2, 2, share, D), "core", 1)
-    part_lifted, grad_gate, grad_up = tie((part_lifted, grad_gate, grad_up))
-    gate_kept, gate_sent = grad_split(grad_gate, lifted)
+    grad_hat = group_sum(part_lifted, share)
+    gate_kept, gate_sent = split(rows_dot(grad_gate, lifted).astype(BF16))
+    mlp_x, gate_sent, grad_hat = tie((mlp_x, gate_sent, grad_hat))
+    mlp_got = z_spread(x_sum(mlp_kept, mlp_x))
     gate_x = send_seq(gate_sent, 1)
-    half_hat, gate_sent = tie((half_hat, gate_sent))
-    grad_hat = reduce_pair(half_hat, "fy", 0)
-    up_kept, up_sent = grad_split(grad_up, lifted)
-    up_x = send_seq(up_sent, 1)
-    grad_hat, up_sent = tie((grad_hat, up_sent))
     grad_middle = cotangent.astype(F32) + norm_back(grad_hat, normed_mid, inverse_mid)
     grad_attn = group_rows(grad_middle.astype(BF16))
+    up_kept, up_sent = split(rows_dot(grad_up, lifted).astype(BF16))
     grad_attended = cols_dot(grad_attn, attn_full).astype(BF16)
     grad_q, grad_k, grad_v = call_kernel(
         attend_back_kernel,
@@ -447,51 +534,44 @@
         (query, keys, values, grad_attended, cosine, sine, q_seg, k_seg),
     )
     grad_kv = jnp.concatenate([grad_k, grad_v], axis=1)
-    low_sent = grad_kv[:HALF].astype(BF16)
-    high_sent = grad_kv[HALF + rows :].astype(BF16)
-    low_edge = lax.ppermute(low_sent, "seq", behind)
-    high_edge = lax.ppermute(high_sent, "seq", ahead)
-    mlp_x, gate_x, low_sent, attended = tie((mlp_x, gate_x, low_sent, attended))
-    mlp_got = z_spread(x_sum(mlp_kept, mlp_x))
+    mlp_got, gate_x, up_sent, grad_kv, attended = tie((mlp_got, gate_x, up_sent, grad_kv, attended))
+    low_edge = lax.ppermute(grad_kv[:HALF].astype(BF16), "seq", behind)
+    high_edge = lax.ppermute(grad_kv[HALF + rows :].astype(BF16), "seq", ahead)
+    gate_got = z_spread(x_sum(gate_kept, gate_x))
+    up_x = send_seq(up_sent, 1)
     attn_g = rows_dot(attended, grad_attn).astype(BF16)
     attn_g = attn_g.reshape(seqs // 4, 2, 2, shard, D).transpose(1, 2, 0, 3, 4)
     attn_g = trade(trade(attn_g, "core", 1), "fy", 0).reshape(seqs, shard, D)
-    low_edge, high_edge, mlp_got = tie((low_edge, high_edge, mlp_got))
+    attn_kept, attn_sent = split_rows(attn_g)
     middle_kv = grad_kv[HALF : HALF + rows]
     gap = jnp.zeros((rows - 2 * HALF, 2 * OWN), F32)
     edges = jnp.concatenate([high_edge.astype(F32), gap, low_edge.astype(F32)], axis=0)
     grad_packed = jnp.concatenate([grad_q, (middle_kv + edges).astype(BF16)], axis=1)
-    qkv_kept, qkv_sent = grad_split(grad_packed, hidden)
+    qkv_kept, qkv_sent = split(rows_dot(grad_packed, hidden).astype(BF16))
+    gate_got, up_x, attn_sent, qkv_sent, mixed = tie((gate_got, up_x, attn_sent, qkv_sent, mixed))
+    up_got = z_spread(x_sum(up_kept, up_x))
     qkv_x = send_seq(qkv_sent, 1)
-    gate_x, qkv_sent = tie((gate_x, qkv_sent))
-    gate_got = z_spread(x_sum(gate_kept, gate_x))
-    attn_kept, attn_sent = x_split([attn_g[i] for i in range(seqs)])
     attn_x = send_seq(attn_sent, 1)
-    up_x, gate_got, attn_sent = tie((up_x, gate_got, attn_sent))
-    up_got = z_spread(x_sum(up_kept, up_x))
     part_hidden = jnp.dot(grad_packed, qkv_full, preferred_element_type=F32)
     grad_hidden = group_sum(part_hidden, share)
     part_out = jnp.dot(mixed, mlp_full, preferred_element_type=F32)
     output = middle + group_sum(part_out, share)
-    qkv_x, up_got, grad_hidden, output = tie((qkv_x, up_got, grad_hidden, output))
+    up_got, qkv_x, attn_x, grad_hidden, output = tie((up_got, qkv_x, attn_x, grad_hidden, output))
     qkv_got = z_spread(x_sum(qkv_kept, qkv_x))
-    attn_x, qkv_got = tie((attn_x, qkv_got))
-    grad_attn_out = z_total(z_spread(x_sum(attn_kept, attn_x)))
-    mlp_g, gate_g, up_g = z_total(mlp_got), z_total(gate_got), z_total(up_got)
-    grad_qkv = z_total(qkv_got)
+    grad_attn_out = total_of(z_spread(x_sum(attn_kept, attn_x)))
 
     def regroup_back(cells):
-        cells = cells.T.astype(BF16).reshape(2, 2, shard, -1)
+        cells = cells.reshape(2, 2, shard, -1)
         return trade(trade(cells, "fy", 0), "core", 1)
 
     def back_columns(cells, parts, width):
         cells = cells.reshape(2, 2, shard, parts, width).transpose(2, 3, 0, 1, 4)
         return cells.reshape(shard, parts * 2 * 2 * width).astype(F32)
 
-    rest_g = regroup_back(jnp.concatenate([mlp_g, gate_g, up_g], axis=0))
+    rest_g = regroup_back(turn_back([mlp_got, gate_got, up_got], WIDE))
     raw_mlp = back_columns(rest_g[..., :OWN_FF], 1, OWN_FF)
-    raw_in = back_columns(rest_g[..., OWN_FF:], 2, OWN_FF)
-    raw_qkv = back_columns(regroup_back(grad_qkv), 3, OWN)
+    raw_in = back_columns(rest_g[..., OWN_FF : 3 * OWN_FF], 2, OWN_FF)
+    raw_qkv = back_columns(regroup_back(turn_back([qkv_got], 3 * OWN)), 3, OWN)
     input_grad = grad_middle + norm_back(grad_hidden, normed, inverse)
     grad_gain_attn = jnp.sum(raw_qkv * w_qkv.astype(F32), axis=1)
     grad_gain_mlp = jnp.sum(raw_in * w_in.astype(F32), axis=1)

time: 363 us -> 313 us (0.86)
  the two profiles are of different devices: /device:TPU:0 before, /device:TPU:17 now
where the time goes in v4:
time: 313 us; the launch traced here: 307 us
  waiting for transfers between devices  145 us (46%)
  starting transfers between devices  90.1 us (29%)
  other arithmetic  26.4 us (8%)
  Pallas kernels  18.1 us (6%)
  matrix products  13 us (4%)
  local copies, waits for them, and re-layouts  11.9 us (4%)
    ppermute x40, waiting for transfers between devices, send_seq(): return lax.ppermute(cells, ALL, flat_pairs(lambda i: i ^ flip * GROUP))  101 us
    ppermute x40, starting transfers between devices, send_seq(): return lax.ppermute(cells, ALL, flat_pairs(lambda i: i ^ flip * GROUP))  38.8 us
    ppermute x12, starting transfers between devices, trade(): got = lax.ppermute(sent, axis, [(0, 1), (1, 0)])  16.1 us
    ppermute x8, waiting for transfers between devices, reduce_pair(): got = lax.ppermute(sent, axis, [(0, 1), (1, 0)])  13.8 us
    ppermute x8, waiting for transfers between devices, join(): got = lax.ppermute(cells, axis, [(0, 1), (1, 0)])  13.4 us
    ppermute x8, starting transfers between devices, reduce_pair(): got = lax.ppermute(sent, axis, [(0, 1), (1, 0)])  12.6 us
    pallas_call x14, Pallas kernels, local_kernel(): pl.pallas_call(kernel, out_shape=outs, in_specs=[pl.BlockSpec(memory_spac...  9.43 us
    ppermute x8, starting transfers between devices, join(): got = lax.ppermute(cells, axis, [(0, 1), (1, 0)])  9.06 us
  transfers between devices with their start and end apart: 72, of which 37 were waited for; matrix products, arithmetic and copies ran while one was open for 10% of the time, Pallas kernels for 3%

profile of v4, /device:TPU:17, one launch (start us, length us, event | category | flops | bytes accessed | tf_op | source)
XLA Modules:
  0.0 306.9 jit_solution(17161793894722200914)
XLA Ops:
  10.1 1.9 collective-permute-start.4
  13.1 2.3 collective-permute-start.5
  18.4 3.1 %collective-permute-done.5 = bf16[768,128]{1,0:T(8,128)(2,1)S(1)} collective-permute-done((bf16[768,128]{1,0:T(8,128)(2,1)S(1)}, bf16[768,128]{1,0:T(8,128)(2,1)S(1)}, u32[]{:S(2)}, u32[]{:S(2)}) %collective-permute-start.5) | collective-permute-done | bytes 196640 | tf_op jit(solution)/shard_map/ppermute | solution.py:33
  23.4 10.5 %collective-permute-done.7 = bf16[768,128]{1,0:T(8,128)(2,1)S(1)} collective-permute-done((bf16[768,128]{1,0:T(8,128)(2,1)S(1)}, bf16[768,128]{1,0:T(8,128)(2,1)S(1)}, u32[]{:S(2)}, u32[]{:S(2)}) %collective-permute-start.7) | collective-permute-done | bytes 196640 | tf_op jit(solution)/shard_map/ppermute | solution.py:33
  48.5 2.9 collective-permute-start.17
  51.8 4.3 %collective-permute-start.18 = (bf16[64,1024]{1,0:T(8,128)(2,1)S(1)}, bf16[64,1024]{1,0:T(8,128)(2,1)S(1)}, u32[]{:S(2)}, u32[]{:S(2)}) collective-permute-start(bf16[64,1024]{1,0:T(8,128)(2,1)S(1)} %get-tuple-element.178), channel_id=1, source_target_pairs={{4,0},{8,4},{12,8},{16,12},{20,16},{24,20},{28,24},{5,1},{9,5},{13... | collective-permute-start | bytes 393224 | tf_op jit(solution)/shard_map/ppermute | solution.py:458
  56.1 3.9 %collective-permute-done.15 = bf16[656,128]{1,0:T(8,128)(2,1)S(1)} collective-permute-done((bf16[656,128]{1,0:T(8,128)(2,1)S(1)}, bf16[656,128]{1,0:T(8,128)(2,1)S(1)}, u32[]{:S(2)}, u32[]{:S(2)}) %collective-permute-start.15) | collective-permute-done | bytes 167968 | tf_op jit(solution)/shard_map/ppermute | solution.py:33
  60.3 7.6 %collective-permute-done.17 = bf16[64,1024]{1,0:T(8,128)(2,1)S(1)} collective-permute-done((bf16[64,1024]{1,0:T(8,128)(2,1)S(1)}, bf16[64,1024]{1,0:T(8,128)(2,1)S(1)}, u32[]{:S(2)}, u32[]{:S(2)}) %collective-permute-start.17) | collective-permute-done | bytes 131104 | tf_op jit(solution)/shard_map/ppermute | solution.py:457
  71.2 3.8 %shard_map.156 = (bf16[512,256]{1,0:T(8,128)(2,1)S(1)}, bf16[640,256]{1,0:T(8,128)(2,1)S(1)}, bf16[640,256]{1,0:T(8,128)(2,1)S(1)}, bf16[512,256]{1,0:T(8,128)(2,1)S(1)}) custom-call(f32[640,768]{1,0:T(8,128)S(1)} %fusion.6.packed, f32[640,128]{1,0:T(8,128)S(1)} %get-tuple-element.242.cosine, f32[640,128]{1,0:T(8,128)S(1)} %get-tuple-element.241.sine, ...), custom_call_target="tpu_custom_call" | custom-call | flops 268435456 | bytes 3805696 | tf_op jit(solution)/shard_map/pallas_call | solution.py:398
  76.1 2.3 collective-permute-start.25
  82.8 3.4 %collective-permute-done.33 = bf16[128,1024]{1,0:T(8,128)(2,1)S(1)} collective-permute-done((bf16[128,1024]{1,0:T(8,128)(2,1)S(1)}, bf16[128,1024]{1,0:T(8,128)(2,1)S(1)}, u32[]{:S(2)}, u32[]{:S(2)}) %collective-permute-start.33) | collective-permute-done | bytes 262176 | tf_op jit(solution)/shard_map/ppermute | solution.py:47
  88.6 7.3 %collective-permute-done.23 = bf16[656,128]{1,0:T(8,128)(2,1)S(1)} collective-permute-done((bf16[656,128]{1,0:T(8,128)(2,1)S(1)}, bf16[656,128]{1,0:T(8,128)(2,1)S(1)}, u32[]{:S(2)}, u32[]{:S(2)}) %collective-permute-start.23) | collective-permute-done | bytes 167968 | tf_op jit(solution)/shard_map/ppermute | solution.py:33
  104.0 3.6 %collective-permute-done.31 = bf16[128,1024]{1,0:T(8,128)(2,1)S(1)} collective-permute-done((bf16[128,1024]{1,0:T(8,128)(2,1)S(1)}, bf16[128,1024]{1,0:T(8,128)(2,1)S(1)}, u32[]{:S(2)}, u32[]{:S(2)}) %collective-permute-start.31) | collective-permute-done | bytes 262176 | tf_op jit(solution)/shard_map/ppermute | solution.py:47
  107.8 2.9 collective-permute-start.32
  110.9 1.7 collective-permute-start.27
  116.7 1.9 collective-permute-done.27
  118.6 2.1 collective-permute-done.28
  120.8 8.3 %collective-permute-done.29 = bf16[656,128]{1,0:T(8,128)(2,1)S(1)} collective-permute-done((bf16[656,128]{1,0:T(8,128)(2,1)S(1)}, bf16[656,128]{1,0:T(8,128)(2,1)S(1)}, u32[]{:S(2)}, u32[]{:S(2)}) %collective-permute-start.29) | collective-permute-done | bytes 167968 | tf_op jit(solution)/shard_map/ppermute | solution.py:33
  133.4 12.6 %collective-permute-done.35.got = bf16[4,656,128]{2,1,0:T(8,128)(2,1)S(1)} collective-permute-done((bf16[4,656,128]{2,1,0:T(8,128)(2,1)S(1)}, bf16[4,656,128]{2,1,0:T(8,128)(2,1)S(1)}, u32[]{:S(2)}, u32[]{:S(2)}) %collective-permute-start.35) | collective-permute-done | bytes 671776 | tf_op jit(solution)/shard_map/ppermute | solution.py:33
  147.8 3.4 %multiply_convert_fusion = (bf16[512,656]{0,1:T(8,128)(2,1)S(1)}, f32[512,656]{0,1:T(8,128)S(1)}) fusion(f32[512,656]{0,1:T(8,128)S(1)} %fusion.64, f32[512,656]{0,1:T(8,128)S(1)} %fusion.65), kind=kLoop, calls=%fused_computation.11 | loop fusion | flops 22167552 | bytes 4702208 | tf_op jit(solution)/shard_map/convert_element_type | solution.py:509
  156.3 2.5 collective-permute-start.37
  163.6 4.6 %collective-permute-done.38 = bf16[128,1024]{1,0:T(8,128)(2,1)S(1)} collective-permute-done((bf16[128,1024]{1,0:T(8,128)(2,1)S(1)}, bf16[128,1024]{1,0:T(8,128)(2,1)S(1)}, u32[]{:S(2)}, u32[]{:S(2)}) %collective-permute-start.38) | collective-permute-done | bytes 262176 | tf_op jit(solution)/shard_map/ppermute | solution.py:56
  168.2 7.2 %collective-permute-done.36 = bf16[4,656,128]{2,1,0:T(8,128)(2,1)S(1)} collective-permute-done((bf16[4,656,128]{2,1,0:T(8,128)(2,1)S(1)}, bf16[4,656,128]{2,1,0:T(8,128)(2,1)S(1)}, u32[]{:S(2)}, u32[]{:S(2)}) %collective-permute-start.36) | collective-permute-done | bytes 671776 | tf_op jit(solution)/shard_map/ppermute | solution.py:33
  177.2 5.7 %collective-permute-done.43 = bf16[128,1024]{1,0:T(8,128)(2,1)S(1)} collective-permute-done((bf16[128,1024]{1,0:T(8,128)(2,1)S(1)}, bf16[128,1024]{1,0:T(8,128)(2,1)S(1)}, u32[]{:S(2)}, u32[]{:S(2)}) %collective-permute-start.43) | collective-permute-done | bytes 262176 | tf_op jit(solution)/shard_map/ppermute | solution.py:47
  183.1 1.8 collective-permute-start.44
  186.9 2.1 collective-permute-start.39
  192.6 4.8 %shard_map.163 = (bf16[512,256]{1,0:T(8,128)(2,1)S(1)}, f32[640,256]{1,0:T(8,128)S(1)}, f32[640,256]{1,0:T(8,128)S(1)}) custom-call(bf16[512,256]{1,0:T(8,128)(2,1)S(1)} %copy-done.15, bf16[640,256]{1,0:T(8,128)(2,1)S(1)} %copy-done.11, bf16[640,256]{1,0:T(8,128)(2,1)S(1)} %copy-done.13, bf16[512,256]{1,0:T(8,128)(2,1)S(1)} %convolution_convert_fusion.5.grad, ...), custom_call_target="tpu_custom_call" | custom-call | flops 805306368 | bytes 3412480 | tf_op jit(solution)/shard_map/pallas_call | solution.py:398
  197.6 7.9 %collective-permute-done.41.refs_3_ = bf16[656,128]{1,0:T(8,128)(2,1)S(1)} collective-permute-done((bf16[656,128]{1,0:T(8,128)(2,1)S(1)}, bf16[656,128]{1,0:T(8,128)(2,1)S(1)}, u32[]{:S(2)}, u32[]{:S(2)}) %collective-permute-start.41) | collective-permute-done | bytes 167968 | tf_op jit(solution)/shard_map/ppermute | solution.py:33
  206.4 2.4 collective-permute-start.51
  208.9 3.9 %collective-permute-start.52 = (bf16[64,512]{1,0:T(8,128)(2,1)S(1)}, bf16[64,512]{1,0:T(8,128)(2,1)S(1)}, u32[]{:S(2)}, u32[]{:S(2)}) collective-permute-start(bf16[64,512]{1,0:T(8,128)(2,1)S(1)} %get-tuple-element.215), channel_id=1, source_target_pairs={{4,0},{8,4},{12,8},{16,12},{20,16},{24,20},{28,24},{5,1},{9,5},{13... | collective-permute-start | bytes 196616 | tf_op jit(solution)/shard_map/ppermute | solution.py:538
  213.3 2.1 collective-permute-start.49
  215.6 2.4 collective-permute-start.45
  223.9 3.1 collective-permute-done.50
  226.9 2.5 collective-permute-start.58
  230.2 4.3 %collective-permute-done.47.refs_7_ = bf16[656,128]{1,0:T(8,128)(2,1)S(1)} collective-permute-done((bf16[656,128]{1,0:T(8,128)(2,1)S(1)}, bf16[656,128]{1,0:T(8,128)(2,1)S(1)}, u32[]{:S(2)}, u32[]{:S(2)}) %collective-permute-start.47) | collective-permute-done | bytes 167968 | tf_op jit(solution)/shard_map/ppermute | solution.py:33
  241.0 2.4 collective-permute-start.53
  243.4 2.8 collective-permute-done.59
  246.2 5.5 %collective-permute-done.61 = bf16[128,1024]{1,0:T(8,128)(2,1)S(1)} collective-permute-done((bf16[128,1024]{1,0:T(8,128)(2,1)S(1)}, bf16[128,1024]{1,0:T(8,128)(2,1)S(1)}, u32[]{:S(2)}, u32[]{:S(2)}) %collective-permute-start.61) | collective-permute-done | bytes 262176 | tf_op jit(solution)/shard_map/ppermute | solution.py:56
  252.8 5.5 %collective-permute-done.55.refs_11_ = bf16[656,128]{1,0:T(8,128)(2,1)S(1)} collective-permute-done((bf16[656,128]{1,0:T(8,128)(2,1)S(1)}, bf16[656,128]{1,0:T(8,128)(2,1)S(1)}, u32[]{:S(2)}, u32[]{:S(2)}) %collective-permute-start.55) | collective-permute-done | bytes 167968 | tf_op jit(solution)/shard_map/ppermute | solution.py:33
  258.2 5.6 %collective-permute-done.57 = bf16[4,32,1024]{2,1,0:T(8,128)(2,1)S(1)} collective-permute-done((bf16[4,32,1024]{2,1,0:T(8,128)(2,1)S(1)}, bf16[4,32,1024]{2,1,0:T(8,128)(2,1)S(1)}, u32[]{:S(2)}, u32[]{:S(2)}) %collective-permute-start.57) | collective-permute-done | bytes 262176 | tf_op jit(solution)/shard_map/ppermute | solution.py:33
  264.7 2.4 collective-permute-start.67
  268.6 2.4 collective-permute-start.62
  272.1 2.1 collective-permute-start.64
  275.6 4.4 %collective-permute-done.63.refs_2_ = bf16[768,128]{1,0:T(8,128)(2,1)S(1)} collective-permute-done((bf16[768,128]{1,0:T(8,128)(2,1)S(1)}, bf16[768,128]{1,0:T(8,128)(2,1)S(1)}, u32[]{:S(2)}, u32[]{:S(2)}) %collective-permute-start.63) | collective-permute-done | bytes 196640 | tf_op jit(solution)/shard_map/ppermute | solution.py:33
  280.0 11.0 %collective-permute-done.64.refs_3_ = bf16[768,128]{1,0:T(8,128)(2,1)S(1)} collective-permute-done((bf16[768,128]{1,0:T(8,128)(2,1)S(1)}, bf16[768,128]{1,0:T(8,128)(2,1)S(1)}, u32[]{:S(2)}, u32[]{:S(2)}) %collective-permute-start.64) | collective-permute-done | bytes 196640 | tf_op jit(solution)/shard_map/ppermute | solution.py:33
  292.4 2.3 collective-permute-done.65
  294.7 3.1 %collective-permute-start.66 = (bf16[2,1,32,768]{3,2,1,0:T(8,128)(2,1)S(1)}, bf16[2,1,32,768]{3,2,1,0:T(8,128)(2,1)S(1)}, u32[]{:S(2)}, u32[]{:S(2)}) collective-permute-start(bf16[2,1,32,768]{3,2,1,0:T(8,128)(2,1)S(1)} %fusion.45), channel_id=1, source_target_pairs={{0,1},{1,0},{2,3},{3,2},{4,5},{5,4},{6,7},{7,6},{8,9},{9,8},{10,11... | collective-permute-start | bytes 294920 | tf_op jit(solution)/shard_map/ppermute | solution.py:40
  305.1 1.6 fusion.14
  (362 shorter events, 106.5 us)
Async XLA Ops:
  0.6 11.3 %collective-permute-start = (bf16[32,1024]{1,0:T(8,128)(2,1)}, bf16[32,1024]{1,0:T(8,128)(2,1)S(1)}, u32[]{:S(2)}, u32[]{:S(2)}) collective-permute-start(bf16[32,1024]{1,0:T(8,128)(2,1)} %param.13), channel_id=1, source_target_pairs={{0,8},{1,9},{2,10},{3,11},{4,12},{5,13},{6,14},{7,15},{8,0},{9,1},... | collective-permute-start | bytes 196616 | tf_op jit(solution)/shard_map/ppermute | solution.py:33
  2.0 10.0 %collective-permute-start.1 = (bf16[32,1024]{1,0:T(8,128)(2,1)}, bf16[32,1024]{1,0:T(8,128)(2,1)S(1)}, u32[]{:S(2)}, u32[]{:S(2)}) collective-permute-start(bf16[32,1024]{1,0:T(8,128)(2,1)} %param.13), channel_id=1, source_target_pairs={{0,16},{1,17},{2,18},{3,19},{4,20},{5,21},{6,22},{7,23},{8,24},{9,... | collective-permute-start | bytes 196616 | tf_op jit(solution)/shard_map/ppermute | solution.py:33
  2.1 9.9 %collective-permute-start.2 = (bf16[32,1024]{1,0:T(8,128)(2,1)}, bf16[32,1024]{1,0:T(8,128)(2,1)S(1)}, u32[]{:S(2)}, u32[]{:S(2)}) collective-permute-start(bf16[32,1024]{1,0:T(8,128)(2,1)} %param.13), channel_id=1, source_target_pairs={{0,24},{1,25},{2,26},{3,27},{4,28},{5,29},{6,30},{7,31},{8,16},{9,... | collective-permute-start | bytes 196616 | tf_op jit(solution)/shard_map/ppermute | solution.py:33
  13.1 8.4 %collective-permute-start.5 = (bf16[768,128]{1,0:T(8,128)(2,1)S(1)}, bf16[768,128]{1,0:T(8,128)(2,1)S(1)}, u32[]{:S(2)}, u32[]{:S(2)}) collective-permute-start(bf16[768,128]{1,0:T(8,128)(2,1)S(1)} %shard_map.152), channel_id=1, source_target_pairs={{0,8},{1,9},{2,10},{3,11},{4,12},{5,13},{6,14},{7,15},{8,0},{9,1},... | collective-permute-start | bytes 589832 | tf_op jit(solution)/shard_map/ppermute | solution.py:33
  15.4 8.1 %collective-permute-start.6 = (bf16[768,128]{1,0:T(8,128)(2,1)S(1)}, bf16[768,128]{1,0:T(8,128)(2,1)S(1)}, u32[]{:S(2)}, u32[]{:S(2)}) collective-permute-start(bf16[768,128]{1,0:T(8,128)(2,1)S(1)} %shard_map.152), channel_id=1, source_target_pairs={{0,16},{1,17},{2,18},{3,19},{4,20},{5,21},{6,22},{7,23},{8,24},{9,... | collective-permute-start | bytes 589832 | tf_op jit(solution)/shard_map/ppermute | solution.py:33
  15.4 18.6 %collective-permute-start.7 = (bf16[768,128]{1,0:T(8,128)(2,1)S(1)}, bf16[768,128]{1,0:T(8,128)(2,1)S(1)}, u32[]{:S(2)}, u32[]{:S(2)}) collective-permute-start(bf16[768,128]{1,0:T(8,128)(2,1)S(1)} %shard_map.152), channel_id=1, source_target_pairs={{0,24},{1,25},{2,26},{3,27},{4,28},{5,29},{6,30},{7,31},{8,16},{9,... | collective-permute-start | bytes 589832 | tf_op jit(solution)/shard_map/ppermute | solution.py:33
  16.6 17.4 %collective-permute-start.11 = (bf16[1,2,32,2048]{3,2,1,0:T(8,128)(2,1)S(1)}, bf16[1,2,32,2048]{3,2,1,0:T(8,128)(2,1)S(1)}, u32[]{:S(2)}, u32[]{:S(2)}) collective-permute-start(bf16[1,2,32,2048]{3,2,1,0:T(8,128)(2,1)S(1)} %constant_dynamic-slice_fusion.4), channel_id=1, source_target_pairs={{0,2},{2,0},{1,3},{3,1},{4,6},{6,4},{5,7},{7,5},{8,10},{10,8},{9,1... | collective-permute-start | bytes 786440 | tf_op jit(solution)/shard_map/ppermute | solution.py:40
  18.0 17.5 %collective-permute-start.9 = (bf16[128,1024]{1,0:T(8,128)(2,1)S(1)}, bf16[128,1024]{1,0:T(8,128)(2,1)S(1)}, u32[]{:S(2)}, u32[]{:S(2)}) collective-permute-start(bf16[128,1024]{1,0:T(8,128)(2,1)S(1)} %convert_element_type.261), channel_id=1, source_target_pairs={{0,2},{2,0},{1,3},{3,1},{4,6},{6,4},{5,7},{7,5},{8,10},{10,8},{9,1... | collective-permute-start | bytes 786440 | tf_op jit(solution)/shard_map/ppermute | solution.py:47
  21.5 17.2 %collective-permute-start.8 = (bf16[4,32,1024]{2,1,0:T(8,128)(2,1)S(1)}, bf16[4,32,1024]{2,1,0:T(8,128)(2,1)S(1)}, u32[]{:S(2)}, u32[]{:S(2)}) collective-permute-start(bf16[4,32,1024]{2,1,0:T(8,128)(2,1)S(1)} %pad_maximum_fusion.19.cells), channel_id=1, source_target_pairs={{0,4},{1,5},{2,6},{3,7},{4,0},{5,1},{6,2},{7,3},{8,12},{9,13},{10,... | collective-permute-start | bytes 786440 | tf_op jit(solution)/shard_map/ppermute | solution.py:33
  42.9 8.9 %collective-permute-start.14 = (bf16[656,128]{1,0:T(8,128)(2,1)S(1)}, bf16[656,128]{1,0:T(8,128)(2,1)S(1)}, u32[]{:S(2)}, u32[]{:S(2)}) collective-permute-start(bf16[656,128]{1,0:T(8,128)(2,1)S(1)} %get-tuple-element.92), channel_id=1, source_target_pairs={{0,16},{1,17},{2,18},{3,19},{4,20},{5,21},{6,22},{7,23},{8,24},{9,... | collective-permute-start | bytes 503816 | tf_op jit(solution)/shard_map/ppermute | solution.py:33
  44.3 15.8 %collective-permute-start.15 = (bf16[656,128]{1,0:T(8,128)(2,1)S(1)}, bf16[656,128]{1,0:T(8,128)(2,1)S(1)}, u32[]{:S(2)}, u32[]{:S(2)}) collective-permute-start(bf16[656,128]{1,0:T(8,128)(2,1)S(1)} %get-tuple-element.92), channel_id=1, source_target_pairs={{0,24},{1,25},{2,26},{3,27},{4,28},{5,29},{6,30},{7,31},{8,16},{9,... | collective-permute-start | bytes 503816 | tf_op jit(solution)/shard_map/ppermute | solution.py:33
  45.5 23.4 %collective-permute-start.16 = (bf16[4,768,128]{2,1,0:T(8,128)(2,1)S(1)}, bf16[4,768,128]{2,1,0:T(8,128)(2,1)S(1)}, u32[]{:S(2)}, u32[]{:S(2)}) collective-permute-start(bf16[4,768,128]{2,1,0:T(8,128)(2,1)S(1)} %pad_maximum_fusion.5.cells), channel_id=1, source_target_pairs={{0,4},{1,5},{2,6},{3,7},{4,0},{5,1},{6,2},{7,3},{8,12},{9,13},{10,... | collective-permute-start | bytes 2359304 | tf_op jit(solution)/shard_map/ppermute | solution.py:33
  47.2 12.9 %collective-permute-start.20 = (bf16[2,1,2,32,1024]{4,3,1,0,2:T(8,128)(2,1)S(1)}, bf16[2,1,2,32,1024]{4,3,1,0,2:T(8,128)(2,1)S(1)}, u32[]{:S(2)}, u32[]{:S(2)}) collective-permute-start(bf16[2,1,2,32,1024]{4,3,1,0,2:T(8,128)(2,1)S(1)} %fusion.38), channel_id=1, source_target_pairs={{0,1},{1,0},{2,3},{3,2},{4,5},{5,4},{6,7},{7,6},{8,9},{9,8},{10,11... | collective-permute-start | bytes 786440 | tf_op jit(solution)/shard_map/ppermute | solution.py:40
  48.5 19.4 %collective-permute-start.17 = (bf16[64,1024]{1,0:T(8,128)(2,1)S(1)}, bf16[64,1024]{1,0:T(8,128)(2,1)S(1)}, u32[]{:S(2)}, u32[]{:S(2)}) collective-permute-start(bf16[64,1024]{1,0:T(8,128)(2,1)S(1)} %get-tuple-element.179), channel_id=1, source_target_pairs={{0,4},{4,8},{8,12},{12,16},{16,20},{20,24},{24,28},{1,5},{5,9},{9,... | collective-permute-start | bytes 393224 | tf_op jit(solution)/shard_map/ppermute | solution.py:457
  51.8 17.0 %collective-permute-start.18 = (bf16[64,1024]{1,0:T(8,128)(2,1)S(1)}, bf16[64,1024]{1,0:T(8,128)(2,1)S(1)}, u32[]{:S(2)}, u32[]{:S(2)}) collective-permute-start(bf16[64,1024]{1,0:T(8,128)(2,1)S(1)} %get-tuple-element.178), channel_id=1, source_target_pairs={{4,0},{8,4},{12,8},{16,12},{20,16},{24,20},{28,24},{5,1},{9,5},{13... | collective-permute-start | bytes 393224 | tf_op jit(solution)/shard_map/ppermute | solution.py:458
  78.4 7.9 %collective-permute-start.33 = (bf16[128,1024]{1,0:T(8,128)(2,1)S(1)}, bf16[128,1024]{1,0:T(8,128)(2,1)S(1)}, u32[]{:S(2)}, u32[]{:S(2)}) collective-permute-start(bf16[128,1024]{1,0:T(8,128)(2,1)S(1)} %copy-done.35), channel_id=1, source_target_pairs={{0,2},{2,0},{1,3},{3,1},{4,6},{6,4},{5,7},{7,5},{8,10},{10,8},{9,1... | collective-permute-start | bytes 786440 | tf_op jit(solution)/shard_map/ppermute | solution.py:47
  78.7 8.8 %collective-permute-start.21 = (bf16[656,128]{1,0:T(8,128)(2,1)S(1)}, bf16[656,128]{1,0:T(8,128)(2,1)S(1)}, u32[]{:S(2)}, u32[]{:S(2)}) collective-permute-start(bf16[656,128]{1,0:T(8,128)(2,1)S(1)} %copy-done.9), channel_id=1, source_target_pairs={{0,8},{1,9},{2,10},{3,11},{4,12},{5,13},{6,14},{7,15},{8,0},{9,1},... | collective-permute-start | bytes 503816 | tf_op jit(solution)/shard_map/ppermute | solution.py:33
  79.7 8.9 %collective-permute-start.22 = (bf16[656,128]{1,0:T(8,128)(2,1)S(1)}, bf16[656,128]{1,0:T(8,128)(2,1)S(1)}, u32[]{:S(2)}, u32[]{:S(2)}) collective-permute-start(bf16[656,128]{1,0:T(8,128)(2,1)S(1)} %copy-done.9), channel_id=1, source_target_pairs={{0,16},{1,17},{2,18},{3,19},{4,20},{5,21},{6,22},{7,23},{8,24},{9,... | collective-permute-start | bytes 503816 | tf_op jit(solution)/shard_map/ppermute | solution.py:33
  80.1 15.9 %collective-permute-start.23 = (bf16[656,128]{1,0:T(8,128)(2,1)S(1)}, bf16[656,128]{1,0:T(8,128)(2,1)S(1)}, u32[]{:S(2)}, u32[]{:S(2)}) collective-permute-start(bf16[656,128]{1,0:T(8,128)(2,1)S(1)} %copy-done.9), channel_id=1, source_target_pairs={{0,24},{1,25},{2,26},{3,27},{4,28},{5,29},{6,30},{7,31},{8,16},{9,... | collective-permute-start | bytes 503816 | tf_op jit(solution)/shard_map/ppermute | solution.py:33
  81.3 15.6 %collective-permute-start.24 = (bf16[4,656,128]{2,1,0:T(8,128)(2,1)S(1)}, bf16[4,656,128]{2,1,0:T(8,128)(2,1)S(1)}, u32[]{:S(2)}, u32[]{:S(2)}) collective-permute-start(bf16[4,656,128]{2,1,0:T(8,128)(2,1)S(1)} %pad_maximum_fusion.7.cells), channel_id=1, source_target_pairs={{0,4},{1,5},{2,6},{3,7},{4,0},{5,1},{6,2},{7,3},{8,12},{9,13},{10,... | collective-permute-start | bytes 2015240 | tf_op jit(solution)/shard_map/ppermute | solution.py:33
  86.2 9.8 %collective-permute-start.26 = (bf16[128,1024]{1,0:T(8,128)(2,1)S(1)}, bf16[128,1024]{1,0:T(8,128)(2,1)S(1)}, u32[]{:S(2)}, u32[]{:S(2)}) collective-permute-start(bf16[128,1024]{1,0:T(8,128)(2,1)S(1)} %fusion.30), channel_id=1, source_target_pairs={{0,2},{2,0},{1,3},{3,1},{4,6},{6,4},{5,7},{7,5},{8,10},{10,8},{9,1... | collective-permute-start | bytes 786440 | tf_op jit(solution)/shard_map/ppermute | solution.py:56
  87.5 15.3 %collective-permute-start.34 = (bf16[2,128,1024]{2,1,0:T(8,128)(2,1)}, bf16[2,128,1024]{2,1,0:T(8,128)(2,1)}, u32[]{:S(2)}, u32[]{:S(2)}) collective-permute-start(bf16[2,128,1024]{2,1,0:T(8,128)(2,1)} %pad_maximum_fusion.14), channel_id=1, source_target_pairs={{0,1},{1,0},{2,3},{3,2},{4,5},{5,4},{6,7},{7,6},{8,9},{9,8},{10,11... | collective-permute-start | bytes 1572872 | tf_op jit(solution)/shard_map/ppermute | solution.py:47
  107.8 21.4 %collective-permute-start.32 = (bf16[2,128,1024]{2,1,0:T(8,128)(2,1)S(1)}, bf16[2,128,1024]{2,1,0:T(8,128)(2,1)S(1)}, u32[]{:S(2)}, u32[]{:S(2)}) collective-permute-start(bf16[2,128,1024]{2,1,0:T(8,128)(2,1)S(1)} %pad_maximum_fusion.13), channel_id=1, source_target_pairs={{0,1},{1,0},{2,3},{3,2},{4,5},{5,4},{6,7},{7,6},{8,9},{9,8},{10,11... | collective-permute-start | bytes 1572872 | tf_op jit(solution)/shard_map/ppermute | solution.py:47
  112.6 8.2 %collective-permute-start.28 = (bf16[656,128]{1,0:T(8,128)(2,1)S(1)}, bf16[656,128]{1,0:T(8,128)(2,1)S(1)}, u32[]{:S(2)}, u32[]{:S(2)}) collective-permute-start(bf16[656,128]{1,0:T(8,128)(2,1)S(1)} %get-tuple-element.105), channel_id=1, source_target_pairs={{0,16},{1,17},{2,18},{3,19},{4,20},{5,21},{6,22},{7,23},{8,24},{9,... | collective-permute-start | bytes 503816 | tf_op jit(solution)/shard_map/ppermute | solution.py:33
  112.6 16.5 %collective-permute-start.29 = (bf16[656,128]{1,0:T(8,128)(2,1)S(1)}, bf16[656,128]{1,0:T(8,128)(2,1)S(1)}, u32[]{:S(2)}, u32[]{:S(2)}) collective-permute-start(bf16[656,128]{1,0:T(8,128)(2,1)S(1)} %get-tuple-element.105), channel_id=1, source_target_pairs={{0,24},{1,25},{2,26},{3,27},{4,28},{5,29},{6,30},{7,31},{8,16},{9,... | collective-permute-start | bytes 503816 | tf_op jit(solution)/shard_map/ppermute | solution.py:33
  114.8 16.1 %collective-permute-start.30 = (bf16[4,656,128]{2,1,0:T(8,128)(2,1)S(1)}, bf16[4,656,128]{2,1,0:T(8,128)(2,1)S(1)}, u32[]{:S(2)}, u32[]{:S(2)}) collective-permute-start(bf16[4,656,128]{2,1,0:T(8,128)(2,1)S(1)} %pad_maximum_fusion.8.cells), channel_id=1, source_target_pairs={{0,4},{1,5},{2,6},{3,7},{4,0},{5,1},{6,2},{7,3},{8,12},{9,13},{10,... | collective-permute-start | bytes 2015240 | tf_op jit(solution)/shard_map/ppermute | solution.py:33
  130.9 15.1 %collective-permute-start.35 = (bf16[4,656,128]{2,1,0:T(8,128)(2,1)S(1)}, bf16[4,656,128]{2,1,0:T(8,128)(2,1)S(1)}, u32[]{:S(2)}, u32[]{:S(2)}) collective-permute-start(bf16[4,656,128]{2,1,0:T(8,128)(2,1)S(1)} %pad_maximum_fusion.9.cells), channel_id=1, source_target_pairs={{0,4},{1,5},{2,6},{3,7},{4,0},{5,1},{6,2},{7,3},{8,12},{9,13},{10,... | collective-permute-start | bytes 2015240 | tf_op jit(solution)/shard_map/ppermute | solution.py:33
  158.8 16.7 %collective-permute-start.36 = (bf16[4,656,128]{2,1,0:T(8,128)(2,1)S(1)}, bf16[4,656,128]{2,1,0:T(8,128)(2,1)S(1)}, u32[]{:S(2)}, u32[]{:S(2)}) collective-permute-start(bf16[4,656,128]{2,1,0:T(8,128)(2,1)S(1)} %get-tuple-element.122), channel_id=1, source_target_pairs={{0,4},{1,5},{2,6},{3,7},{4,0},{5,1},{6,2},{7,3},{8,12},{9,13},{10,... | collective-permute-start | bytes 2015240 | tf_op jit(solution)/shard_map/ppermute | solution.py:33
  186.9 10.7 %collective-permute-start.39 = (bf16[656,128]{1,0:T(8,128)(2,1)S(1)}, bf16[656,128]{1,0:T(8,128)(2,1)S(1)}, u32[]{:S(2)}, u32[]{:S(2)}) collective-permute-start(bf16[656,128]{1,0:T(8,128)(2,1)S(1)} %get-tuple-element.212), channel_id=1, source_target_pairs={{0,8},{1,9},{2,10},{3,11},{4,12},{5,13},{6,14},{7,15},{8,0},{9,1},... | collective-permute-start | bytes 503816 | tf_op jit(solution)/shard_map/ppermute | solution.py:33
  189.0 8.6 %collective-permute-start.40 = (bf16[656,128]{1,0:T(8,128)(2,1)S(1)}, bf16[656,128]{1,0:T(8,128)(2,1)S(1)}, u32[]{:S(2)}, u32[]{:S(2)}) collective-permute-start(bf16[656,128]{1,0:T(8,128)(2,1)S(1)} %get-tuple-element.211), channel_id=1, source_target_pairs={{0,16},{1,17},{2,18},{3,19},{4,20},{5,21},{6,22},{7,23},{8,24},{9,... | collective-permute-start | bytes 503816 | tf_op jit(solution)/shard_map/ppermute | solution.py:33
  189.0 16.5 %collective-permute-start.41 = (bf16[656,128]{1,0:T(8,128)(2,1)S(1)}, bf16[656,128]{1,0:T(8,128)(2,1)S(1)}, u32[]{:S(2)}, u32[]{:S(2)}) collective-permute-start(bf16[656,128]{1,0:T(8,128)(2,1)S(1)} %get-tuple-element.210), channel_id=1, source_target_pairs={{0,24},{1,25},{2,26},{3,27},{4,28},{5,29},{6,30},{7,31},{8,16},{9,... | collective-permute-start | bytes 503816 | tf_op jit(solution)/shard_map/ppermute | solution.py:33
  190.3 16.1 %collective-permute-start.42 = (bf16[4,656,128]{2,1,0:T(8,128)(2,1)S(1)}, bf16[4,656,128]{2,1,0:T(8,128)(2,1)S(1)}, u32[]{:S(2)}, u32[]{:S(2)}) collective-permute-start(bf16[4,656,128]{2,1,0:T(8,128)(2,1)S(1)} %get-tuple-element.125), channel_id=1, source_target_pairs={{0,4},{1,5},{2,6},{3,7},{4,0},{5,1},{6,2},{7,3},{8,12},{9,13},{10,... | collective-permute-start | bytes 2015240 | tf_op jit(solution)/shard_map/ppermute | solution.py:33
  206.4 11.5 %collective-permute-start.51 = (bf16[64,512]{1,0:T(8,128)(2,1)S(1)}, bf16[64,512]{1,0:T(8,128)(2,1)S(1)}, u32[]{:S(2)}, u32[]{:S(2)}) collective-permute-start(bf16[64,512]{1,0:T(8,128)(2,1)S(1)} %get-tuple-element.214), channel_id=1, source_target_pairs={{0,4},{4,8},{8,12},{12,16},{16,20},{20,24},{24,28},{1,5},{5,9},{9,... | collective-permute-start | bytes 196616 | tf_op jit(solution)/shard_map/ppermute | solution.py:539
  208.9 10.4 %collective-permute-start.52 = (bf16[64,512]{1,0:T(8,128)(2,1)S(1)}, bf16[64,512]{1,0:T(8,128)(2,1)S(1)}, u32[]{:S(2)}, u32[]{:S(2)}) collective-permute-start(bf16[64,512]{1,0:T(8,128)(2,1)S(1)} %get-tuple-element.215), channel_id=1, source_target_pairs={{4,0},{8,4},{12,8},{16,12},{20,16},{24,20},{28,24},{5,1},{9,5},{13... | collective-permute-start | bytes 196616 | tf_op jit(solution)/shard_map/ppermute | solution.py:538
  215.6 14.5 %collective-permute-start.45 = (bf16[656,128]{1,0:T(8,128)(2,1)S(1)}, bf16[656,128]{1,0:T(8,128)(2,1)S(1)}, u32[]{:S(2)}, u32[]{:S(2)}) collective-permute-start(bf16[656,128]{1,0:T(8,128)(2,1)S(1)} %get-tuple-element.208), channel_id=1, source_target_pairs={{0,8},{1,9},{2,10},{3,11},{4,12},{5,13},{6,14},{7,15},{8,0},{9,1},... | collective-permute-start | bytes 503816 | tf_op jit(solution)/shard_map/ppermute | solution.py:33
  218.0 12.2 %collective-permute-start.46 = (bf16[656,128]{1,0:T(8,128)(2,1)S(1)}, bf16[656,128]{1,0:T(8,128)(2,1)S(1)}, u32[]{:S(2)}, u32[]{:S(2)}) collective-permute-start(bf16[656,128]{1,0:T(8,128)(2,1)S(1)} %get-tuple-element.207), channel_id=1, source_target_pairs={{0,16},{1,17},{2,18},{3,19},{4,20},{5,21},{6,22},{7,23},{8,24},{9,... | collective-permute-start | bytes 503816 | tf_op jit(solution)/shard_map/ppermute | solution.py:33
  218.0 16.5 %collective-permute-start.47 = (bf16[656,128]{1,0:T(8,128)(2,1)S(1)}, bf16[656,128]{1,0:T(8,128)(2,1)S(1)}, u32[]{:S(2)}, u32[]{:S(2)}) collective-permute-start(bf16[656,128]{1,0:T(8,128)(2,1)S(1)} %get-tuple-element.206), channel_id=1, source_target_pairs={{0,24},{1,25},{2,26},{3,27},{4,28},{5,29},{6,30},{7,31},{8,16},{9,... | collective-permute-start | bytes 503816 | tf_op jit(solution)/shard_map/ppermute | solution.py:33
  219.3 16.1 %collective-permute-start.48 = (bf16[4,656,128]{2,1,0:T(8,128)(2,1)S(1)}, bf16[4,656,128]{2,1,0:T(8,128)(2,1)S(1)}, u32[]{:S(2)}, u32[]{:S(2)}) collective-permute-start(bf16[4,656,128]{2,1,0:T(8,128)(2,1)S(1)} %get-tuple-element.134), channel_id=1, source_target_pairs={{0,4},{1,5},{2,6},{3,7},{4,0},{5,1},{6,2},{7,3},{8,12},{9,13},{10,... | collective-permute-start | bytes 2015240 | tf_op jit(solution)/shard_map/ppermute | solution.py:33
  226.9 11.0 %collective-permute-start.58 = (bf16[2,128,1024]{2,1,0:T(8,128)(2,1)S(1)}, bf16[2,128,1024]{2,1,0:T(8,128)(2,1)S(1)}, u32[]{:S(2)}, u32[]{:S(2)}) collective-permute-start(bf16[2,128,1024]{2,1,0:T(8,128)(2,1)S(1)} %fusion.20), channel_id=1, source_target_pairs={{0,1},{1,0},{2,3},{3,2},{4,5},{5,4},{6,7},{7,6},{8,9},{9,8},{10,11... | collective-permute-start | bytes 1572872 | tf_op jit(solution)/shard_map/ppermute | solution.py:56
  238.2 8.0 %collective-permute-start.59 = (bf16[128,1024]{1,0:T(8,128)(2,1)S(1)}, bf16[128,1024]{1,0:T(8,128)(2,1)S(1)}, u32[]{:S(2)}, u32[]{:S(2)}) collective-permute-start(bf16[128,1024]{1,0:T(8,128)(2,1)S(1)} %fusion.32), channel_id=1, source_target_pairs={{0,2},{2,0},{1,3},{3,1},{4,6},{6,4},{5,7},{7,5},{8,10},{10,8},{9,1... | collective-permute-start | bytes 786440 | tf_op jit(solution)/shard_map/ppermute | solution.py:56
  239.4 24.4 %collective-permute-start.56 = (bf16[4,768,128]{2,1,0:T(8,128)(2,1)S(1)}, bf16[4,768,128]{2,1,0:T(8,128)(2,1)S(1)}, u32[]{:S(2)}, u32[]{:S(2)}) collective-permute-start(bf16[4,768,128]{2,1,0:T(8,128)(2,1)S(1)} %get-tuple-element.141), channel_id=1, source_target_pairs={{0,4},{1,5},{2,6},{3,7},{4,0},{5,1},{6,2},{7,3},{8,12},{9,13},{10,... | collective-permute-start | bytes 2359304 | tf_op jit(solution)/shard_map/ppermute | solution.py:33
  239.8 12.0 %collective-permute-start.61 = (bf16[128,1024]{1,0:T(8,128)(2,1)S(1)}, bf16[128,1024]{1,0:T(8,128)(2,1)S(1)}, u32[]{:S(2)}, u32[]{:S(2)}) collective-permute-start(bf16[128,1024]{1,0:T(8,128)(2,1)S(1)} %fusion.33), channel_id=1, source_target_pairs={{0,2},{2,0},{1,3},{3,1},{4,6},{6,4},{5,7},{7,5},{8,10},{10,8},{9,1... | collective-permute-start | bytes 786440 | tf_op jit(solution)/shard_map/ppermute | solution.py:56
  241.0 11.8 %collective-permute-start.53 = (bf16[656,128]{1,0:T(8,128)(2,1)S(1)}, bf16[656,128]{1,0:T(8,128)(2,1)S(1)}, u32[]{:S(2)}, u32[]{:S(2)}) collective-permute-start(bf16[656,128]{1,0:T(8,128)(2,1)S(1)} %get-tuple-element.204), channel_id=1, source_target_pairs={{0,8},{1,9},{2,10},{3,11},{4,12},{5,13},{6,14},{7,15},{8,0},{9,1},... | collective-permute-start | bytes 503816 | tf_op jit(solution)/shard_map/ppermute | solution.py:33
  243.4 9.4 %collective-permute-start.54 = (bf16[656,128]{1,0:T(8,128)(2,1)S(1)}, bf16[656,128]{1,0:T(8,128)(2,1)S(1)}, u32[]{:S(2)}, u32[]{:S(2)}) collective-permute-start(bf16[656,128]{1,0:T(8,128)(2,1)S(1)} %get-tuple-element.203), channel_id=1, source_target_pairs={{0,16},{1,17},{2,18},{3,19},{4,20},{5,21},{6,22},{7,23},{8,24},{9,... | collective-permute-start | bytes 503816 | tf_op jit(solution)/shard_map/ppermute | solution.py:33
  246.2 17.7 %collective-permute-start.57 = (bf16[4,32,1024]{2,1,0:T(8,128)(2,1)S(1)}, bf16[4,32,1024]{2,1,0:T(8,128)(2,1)S(1)}, u32[]{:S(2)}, u32[]{:S(2)}) collective-permute-start(bf16[4,32,1024]{2,1,0:T(8,128)(2,1)S(1)} %get-tuple-element.142), channel_id=1, source_target_pairs={{0,4},{1,5},{2,6},{3,7},{4,0},{5,1},{6,2},{7,3},{8,12},{9,13},{10,... | collective-permute-start | bytes 786440 | tf_op jit(solution)/shard_map/ppermute | solution.py:33
  264.2 28.1 %collective-permute-start.70 = (bf16[1,2,32,2048]{3,2,1,0:T(8,128)(2,1)S(1)}, bf16[1,2,32,2048]{3,2,1,0:T(8,128)(2,1)S(1)}, u32[]{:S(2)}, u32[]{:S(2)}) collective-permute-start(bf16[1,2,32,2048]{3,2,1,0:T(8,128)(2,1)S(1)} %constant_dynamic-slice_fusion), channel_id=1, source_target_pairs={{0,2},{2,0},{1,3},{3,1},{4,6},{6,4},{5,7},{7,5},{8,10},{10,8},{9,1... | collective-permute-start | bytes 786440 | tf_op jit(solution)/shard_map/ppermute | solution.py:40
  272.1 7.9 %collective-permute-start.63 = (bf16[768,128]{1,0:T(8,128)(2,1)S(1)}, bf16[768,128]{1,0:T(8,128)(2,1)S(1)}, u32[]{:S(2)}, u32[]{:S(2)}) collective-permute-start(bf16[768,128]{1,0:T(8,128)(2,1)S(1)} %get-tuple-element.187), channel_id=1, source_target_pairs={{0,16},{1,17},{2,18},{3,19},{4,20},{5,21},{6,22},{7,23},{8,24},{9,... | collective-permute-start | bytes 589832 | tf_op jit(solution)/shard_map/ppermute | solution.py:33
  272.1 18.8 %collective-permute-start.64 = (bf16[768,128]{1,0:T(8,128)(2,1)S(1)}, bf16[768,128]{1,0:T(8,128)(2,1)S(1)}, u32[]{:S(2)}, u32[]{:S(2)}) collective-permute-start(bf16[768,128]{1,0:T(8,128)(2,1)S(1)} %get-tuple-element.186), channel_id=1, source_target_pairs={{0,24},{1,25},{2,26},{3,27},{4,28},{5,29},{6,30},{7,31},{8,16},{9,... | collective-permute-start | bytes 589832 | tf_op jit(solution)/shard_map/ppermute | solution.py:33
  (66 other events, 357.4 us)

commit v5 on v4

--- a/solution.py
+++ b/solution.py
@@ -57,9 +57,12 @@
     return kept.astype(F32) + got.astype(F32)
 
 
+def core_rows(cells):
+    return join(cells, "core", 1).reshape((-1,) + cells.shape[2:])
+
+
 def group_rows(cells):
-    both = join(join(cells, "fy", 0), "core", 1)
-    return both.reshape((-1,) + cells.shape[1:])
+    return core_rows(join(cells, "fy", 0))
 
 
 def group_sum(part, rows):
@@ -444,26 +447,32 @@
     )
     ours = tokens.astype(F32)
     normed, inverse = normalize(ours)
-    attn_z, qkv, rest, normed = tie((attn_z, qkv, rest, normed))
+    hidden = normed.astype(BF16)
+    devices = lax.axis_size(ALL)
+    ahead = [(i, i + 1) for i in range(GROUP - 1, devices - 1, GROUP)]
+    behind = [(i + 1, i) for i in range(GROUP - 1, devices - 1, GROUP)]
+    edge = lax.ppermute(hidden[share - HALF :], ALL, ahead)
+    edge = edge + lax.ppermute(hidden[:HALF], ALL, behind)
+    attn_z, qkv, rest, hidden, edge = tie((attn_z, qkv, rest, hidden, edge))
     qkv_z = z_gather(qkv)
     attn_x = send_seq(attn_z, 1)
-    hidden = group_rows(normed.astype(BF16))
+    hidden = group_rows(jnp.concatenate([hidden, edge], axis=0)).reshape(GROUP, share + HALF, D)
+    before, after = hidden[0, share:], hidden[GROUP - 1, share:]
+    hidden = hidden[:, :share].reshape(rows, D)
     mlp, gate, up = turn(regroup(rest), (OWN_FF,) * 3)
-    qkv_z, attn_x, hidden, mlp, gate, up = tie((qkv_z, attn_x, hidden, mlp, gate, up))
+    wide = jnp.concatenate([before, hidden, after], axis=0)
+    qkv_z, attn_x, wide, mlp, gate, up = tie((qkv_z, attn_x, wide, mlp, gate, up))
+    hidden = wide[HALF : HALF + rows]
     mlp_z = z_gather(mlp)
     qkv_x = send_seq(qkv_z, 1)
-    ahead = [(i, i + 1) for i in range(seqs - 1)]
-    behind = [(i + 1, i) for i in range(seqs - 1)]
-    before = lax.ppermute(hidden[rows - HALF :], "seq", ahead)
-    after = lax.ppermute(hidden[:HALF], "seq", behind)
+    cot = group_rows(cotangent)
     attn = assemble_rows(attn_z, attn_x).reshape(2, 2, seqs // 4, shard, D)
     attn = trade(trade(attn, "fy", 0), "core", 1)
     attn_full = attn.transpose(2, 0, 1, 3, 4).reshape(OWN, D)
-    mlp_z, qkv_x, before, after, attn_full, gate = tie((mlp_z, qkv_x, before, after, attn_full, gate))
+    mlp_z, qkv_x, attn_full, gate, cot = tie((mlp_z, qkv_x, attn_full, gate, cot))
     gate_z = z_gather(gate)
     mlp_x = send_seq(mlp_z, 1)
     qkv_full = assemble(qkv_z, qkv_x)
-    wide = jnp.concatenate([before, hidden, after], axis=0)
     index = seq * rows - HALF + jnp.arange(rows + 2 * HALF, dtype=jnp.int32)
     segment, position = place(jnp.clip(index, 0, total - 1), seq_lengths)
     segment = jnp.where((index >= 0) & (index < total), segment, -1)
@@ -486,20 +495,20 @@
         (packed, cosine, sine, q_seg, k_seg),
     )
     part = jnp.dot(attended, attn_full, preferred_element_type=F32)
-    middle = ours + group_sum(part, share)
-    gate_z, mlp_x, middle, up = tie((gate_z, mlp_x, middle, up))
+    gate_z, mlp_x, part, up = tie((gate_z, mlp_x, part, up))
     up_z = z_gather(up)
     gate_x = send_seq(gate_z, 1)
-    normed_mid, inverse_mid = normalize(middle)
-    lifted = group_rows(normed_mid.astype(BF16))
-    cot = group_rows(cotangent)
+    middle = ours + group_sum(part, share)
     mlp_full = assemble(mlp_z, mlp_x)
     grad_mixed = cols_dot(cot, mlp_full)
-    up_z, gate_x, lifted, grad_mixed = tie((up_z, gate_x, lifted, grad_mixed))
+    up_z, gate_x, middle, grad_mixed = tie((up_z, gate_x, middle, grad_mixed))
     up_x = send_seq(up_z, 1)
+    normed_mid, inverse_mid = normalize(middle)
+    lifted = join(normed_mid.astype(BF16), "fy", 0)
     gate_full = assemble(gate_z, gate_x)
+    up_x, lifted, gate_full = tie((up_x, lifted, gate_full))
+    lifted = core_rows(lifted)
     gate = cols_dot(lifted, gate_full)
-    up_x, gate = tie((up_x, gate))
     up_full = assemble(up_z, up_x)
     up = cols_dot(lifted, up_full)
     mixed = geglu(gate, up).astype(BF16)
@@ -515,12 +524,16 @@
     )
     grad_hat = group_sum(part_lifted, share)
     gate_kept, gate_sent = split(rows_dot(grad_gate, lifted).astype(BF16))
-    mlp_x, gate_sent, grad_hat = tie((mlp_x, gate_sent, grad_hat))
+    up_kept, up_sent = split(rows_dot(grad_up, lifted).astype(BF16))
+    mlp_x, gate_sent, up_sent, grad_hat = tie((mlp_x, gate_sent, up_sent, grad_hat))
     mlp_got = z_spread(x_sum(mlp_kept, mlp_x))
     gate_x = send_seq(gate_sent, 1)
     grad_middle = cotangent.astype(F32) + norm_back(grad_hat, normed_mid, inverse_mid)
-    grad_attn = group_rows(grad_middle.astype(BF16))
-    up_kept, up_sent = split(rows_dot(grad_up, lifted).astype(BF16))
+    grad_attn = join(grad_middle.astype(BF16), "fy", 0)
+    mlp_got, gate_x, grad_attn, grad_up, attended = tie((mlp_got, gate_x, grad_attn, grad_up, attended))
+    gate_got = z_spread(x_sum(gate_kept, gate_x))
+    up_x = send_seq(up_sent, 1)
+    grad_attn = core_rows(grad_attn)
     grad_attended = cols_dot(grad_attn, attn_full).astype(BF16)
     grad_q, grad_k, grad_v = call_kernel(
         attend_back_kernel,
@@ -534,13 +547,15 @@
         (query, keys, values, grad_attended, cosine, sine, q_seg, k_seg),
     )
     grad_kv = jnp.concatenate([grad_k, grad_v], axis=1)
-    mlp_got, gate_x, up_sent, grad_kv, attended = tie((mlp_got, gate_x, up_sent, grad_kv, attended))
+    attn_g = rows_dot(attended, grad_attn).astype(BF16)
+    attn_g = attn_g.reshape(seqs // 4, 2, 2, shard, D).transpose(1, 2, 0, 3, 4)
+    part_out = jnp.dot(mixed, mlp_full, preferred_element_type=F32)
+    gate_got, up_x, grad_kv, attn_g, part_out = tie((gate_got, up_x, grad_kv, attn_g, part_out))
+    up_got = z_spread(x_sum(up_kept, up_x))
+    ahead = [(i, i + 1) for i in range(seqs - 1)]
+    behind = [(i + 1, i) for i in range(seqs - 1)]
     low_edge = lax.ppermute(grad_kv[:HALF].astype(BF16), "seq", behind)
     high_edge = lax.ppermute(grad_kv[HALF + rows :].astype(BF16), "seq", ahead)
-    gate_got = z_spread(x_sum(gate_kept, gate_x))
-    up_x = send_seq(up_sent, 1)
-    attn_g = rows_dot(attended, grad_attn).astype(BF16)
-    attn_g = attn_g.reshape(seqs // 4, 2, 2, shard, D).transpose(1, 2, 0, 3, 4)
     attn_g = trade(trade(attn_g, "core", 1), "fy", 0).reshape(seqs, shard, D)
     attn_kept, attn_sent = split_rows(attn_g)
     middle_kv = grad_kv[HALF : HALF + rows]
@@ -548,17 +563,17 @@
     edges = jnp.concatenate([high_edge.astype(F32), gap, low_edge.astype(F32)], axis=0)
     grad_packed = jnp.concatenate([grad_q, (middle_kv + edges).astype(BF16)], axis=1)
     qkv_kept, qkv_sent = split(rows_dot(grad_packed, hidden).astype(BF16))
-    gate_got, up_x, attn_sent, qkv_sent, mixed = tie((gate_got, up_x, attn_sent, qkv_sent, mixed))
-    up_got = z_spread(x_sum(up_kept, up_x))
+    attn_sent, qkv_sent, grad_packed = tie((attn_sent, qkv_sent, grad_packed))
     qkv_x = send_seq(qkv_sent, 1)
     attn_x = send_seq(attn_sent, 1)
     part_hidden = jnp.dot(grad_packed, qkv_full, preferred_element_type=F32)
-    grad_hidden = group_sum(part_hidden, share)
-    part_out = jnp.dot(mixed, mlp_full, preferred_element_type=F32)
-    output = middle + group_sum(part_out, share)
-    up_got, qkv_x, attn_x, grad_hidden, output = tie((up_got, qkv_x, attn_x, grad_hidden, output))
+    parts = jnp.stack([part_hidden, part_out]).reshape(2, 2, 2, share, D)
+    parts = reduce_pair(parts, "core", 2)
+    up_got, qkv_x, attn_x, parts = tie((up_got, qkv_x, attn_x, parts))
     qkv_got = z_spread(x_sum(qkv_kept, qkv_x))
     grad_attn_out = total_of(z_spread(x_sum(attn_kept, attn_x)))
+    grad_hidden, sum_out = reduce_pair(parts, "fy", 1)
+    output = middle + sum_out
 
     def regroup_back(cells):
         cells = cells.reshape(2, 2, shard, -1)
@@ -571,6 +586,7 @@
     rest_g = regroup_back(turn_back([mlp_got, gate_got, up_got], WIDE))
     raw_mlp = back_columns(rest_g[..., :OWN_FF], 1, OWN_FF)
     raw_in = back_columns(rest_g[..., OWN_FF : 3 * OWN_FF], 2, OWN_FF)
+    output, rest_g, raw_in, raw_mlp, qkv_got = tie((output, rest_g, raw_in, raw_mlp, qkv_got))
     raw_qkv = back_columns(regroup_back(turn_back([qkv_got], 3 * OWN)), 3, OWN)
     input_grad = grad_middle + norm_back(grad_hidden, normed, inverse)
     grad_gain_attn = jnp.sum(raw_qkv * w_qkv.astype(F32), axis=1)

time: 313 us -> 306 us (0.978)
  the two profiles are of different devices: /device:TPU:17 before, /device:TPU:0 now
where the time goes in v5:
time: 306 us; the launch traced here: 302 us
  waiting for transfers between devices  135 us (44%)
  starting transfers between devices  86 us (28%)
  other arithmetic  22.6 us (7%)
  matrix products  20.4 us (7%)
  Pallas kernels  18.2 us (6%)
  local copies, waits for them, and re-layouts  17 us (6%)
    ppermute x40, waiting for transfers between devices, send_seq(): return lax.ppermute(cells, ALL, flat_pairs(lambda i: i ^ flip * GROUP))  81.8 us
    ppermute x40, starting transfers between devices, send_seq(): return lax.ppermute(cells, ALL, flat_pairs(lambda i: i ^ flip * GROUP))  60.1 us
    ppermute x8, waiting for transfers between devices, join(): got = lax.ppermute(cells, axis, [(0, 1), (1, 0)])  16.7 us
    dot_general x10, matrix products, contract(): lax.dot_general(left, right, ((dims[0], dims[1]), ((), ())), preferred_el...  16 us
    ppermute x6, waiting for transfers between devices, reduce_pair(): got = lax.ppermute(sent, axis, [(0, 1), (1, 0)])  16 us
    ppermute x12, waiting for transfers between devices, trade(): got = lax.ppermute(sent, axis, [(0, 1), (1, 0)])  14.8 us
    ppermute x12, starting transfers between devices, trade(): got = lax.ppermute(sent, axis, [(0, 1), (1, 0)])  14.7 us
    pallas_call x14, Pallas kernels, local_kernel(): pl.pallas_call(kernel, out_shape=outs, in_specs=[pl.BlockSpec(memory_spac...  9.43 us
  transfers between devices with their start and end apart: 70, of which 33 were waited for; matrix products, arithmetic and copies ran while one was open for 12% of the time, Pallas kernels for 5%

profile of v5, /device:TPU:0, one launch (start us, length us, event | category | flops | bytes accessed | tf_op | source)
XLA Modules:
  0.0 302.1 jit_solution(9181673036462245578)
XLA Ops:
  0.6 3.1 %collective-permute-start = (bf16[32,1024]{1,0:T(8,128)(2,1)}, bf16[32,1024]{1,0:T(8,128)(2,1)S(1)}, u32[]{:S(2)}, u32[]{:S(2)}) collective-permute-start(bf16[32,1024]{1,0:T(8,128)(2,1)} %param.13), channel_id=1, source_target_pairs={{0,8},{1,9},{2,10},{3,11},{4,12},{5,13},{6,14},{7,15},{8,0},{9,1},... | collective-permute-start | bytes 196616 | tf_op jit(solution)/shard_map/ppermute | solution.py:33
  3.7 2.6 collective-permute-start.1
  8.5 1.8 collective-permute-start.3
  17.1 4.4 %collective-permute-start.4 = (bf16[2,1,32,768]{3,2,1,0:T(8,128)(2,1)S(1)}, bf16[2,1,32,768]{3,2,1,0:T(8,128)(2,1)S(1)}, u32[]{:S(2)}, u32[]{:S(2)}) collective-permute-start(bf16[2,1,32,768]{3,2,1,0:T(8,128)(2,1)S(1)} %fusion.50), channel_id=1, source_target_pairs={{0,1},{1,0},{2,3},{3,2},{4,5},{5,4},{6,7},{7,6},{8,9},{9,8},{10,11... | collective-permute-start | bytes 294920 | tf_op jit(solution)/shard_map/ppermute | solution.py:40
  22.6 3.4 %collective-permute-start.7 = (bf16[768,128]{1,0:T(8,128)(2,1)S(1)}, bf16[768,128]{1,0:T(8,128)(2,1)S(1)}, u32[]{:S(2)}, u32[]{:S(2)}) collective-permute-start(bf16[768,128]{1,0:T(8,128)(2,1)S(1)} %shard_map.152), channel_id=1, source_target_pairs={{0,8},{1,9},{2,10},{3,11},{4,12},{5,13},{6,14},{7,15},{8,0},{9,1},... | collective-permute-start | bytes 589832 | tf_op jit(solution)/shard_map/ppermute | solution.py:33
  26.0 3.5 %collective-permute-start.8 = (bf16[768,128]{1,0:T(8,128)(2,1)S(1)}, bf16[768,128]{1,0:T(8,128)(2,1)S(1)}, u32[]{:S(2)}, u32[]{:S(2)}) collective-permute-start(bf16[768,128]{1,0:T(8,128)(2,1)S(1)} %shard_map.152), channel_id=1, source_target_pairs={{0,16},{1,17},{2,18},{3,19},{4,20},{5,21},{6,22},{7,23},{8,24},{9,... | collective-permute-start | bytes 589832 | tf_op jit(solution)/shard_map/ppermute | solution.py:33
  31.9 6.9 %collective-permute-done.13 = bf16[1,2,32,2048]{3,2,1,0:T(8,128)(2,1)S(1)} collective-permute-done((bf16[1,2,32,2048]{3,2,1,0:T(8,128)(2,1)S(1)}, bf16[1,2,32,2048]{3,2,1,0:T(8,128)(2,1)S(1)}, u32[]{:S(2)}, u32[]{:S(2)}) %collective-permute-start.13) | collective-permute-done | bytes 262176 | tf_op jit(solution)/shard_map/ppermute | solution.py:40
  39.1 7.2 %collective-permute-done.11 = bf16[192,1024]{1,0:T(8,128)(2,1)S(1)} collective-permute-done((bf16[192,1024]{1,0:T(8,128)(2,1)S(1)}, bf16[192,1024]{1,0:T(8,128)(2,1)S(1)}, u32[]{:S(2)}, u32[]{:S(2)}) %collective-permute-start.11) | collective-permute-done | bytes 393248 | tf_op jit(solution)/shard_map/ppermute | solution.py:47
  50.9 1.8 collective-permute-start.19
  53.5 3.5 %collective-permute-start.16 = (bf16[656,128]{1,0:T(8,128)(2,1)S(1)}, bf16[656,128]{1,0:T(8,128)(2,1)S(1)}, u32[]{:S(2)}, u32[]{:S(2)}) collective-permute-start(bf16[656,128]{1,0:T(8,128)(2,1)S(1)} %get-tuple-element.103), channel_id=1, source_target_pairs={{0,16},{1,17},{2,18},{3,19},{4,20},{5,21},{6,22},{7,23},{8,24},{9,... | collective-permute-start | bytes 503816 | tf_op jit(solution)/shard_map/ppermute | solution.py:33
  59.9 2.3 collective-permute-done.15
  62.2 7.2 %collective-permute-done.16 = bf16[656,128]{1,0:T(8,128)(2,1)S(1)} collective-permute-done((bf16[656,128]{1,0:T(8,128)(2,1)S(1)}, bf16[656,128]{1,0:T(8,128)(2,1)S(1)}, u32[]{:S(2)}, u32[]{:S(2)}) %collective-permute-start.16) | collective-permute-done | bytes 167968 | tf_op jit(solution)/shard_map/ppermute | solution.py:33
  69.6 6.4 %collective-permute-done.18.got = bf16[4,768,128]{2,1,0:T(8,128)(2,1)S(1)} collective-permute-done((bf16[4,768,128]{2,1,0:T(8,128)(2,1)S(1)}, bf16[4,768,128]{2,1,0:T(8,128)(2,1)S(1)}, u32[]{:S(2)}, u32[]{:S(2)}) %collective-permute-start.18) | collective-permute-done | bytes 786464 | tf_op jit(solution)/shard_map/ppermute | solution.py:33
  76.5 3.5 %collective-permute-start.24 = (bf16[656,128]{1,0:T(8,128)(2,1)S(1)}, bf16[656,128]{1,0:T(8,128)(2,1)S(1)}, u32[]{:S(2)}, u32[]{:S(2)}) collective-permute-start(bf16[656,128]{1,0:T(8,128)(2,1)S(1)} %get-tuple-element.107), channel_id=1, source_target_pairs={{0,16},{1,17},{2,18},{3,19},{4,20},{5,21},{6,22},{7,23},{8,24},{9,... | collective-permute-start | bytes 503816 | tf_op jit(solution)/shard_map/ppermute | solution.py:33
  83.6 3.8 %shard_map.156 = (bf16[512,256]{1,0:T(8,128)(2,1)S(1)}, bf16[640,256]{1,0:T(8,128)(2,1)S(1)}, bf16[640,256]{1,0:T(8,128)(2,1)S(1)}, bf16[512,256]{1,0:T(8,128)(2,1)S(1)}) custom-call(f32[640,768]{1,0:T(8,128)S(1)} %fusion.62.packed, f32[640,128]{1,0:T(8,128)S(1)} %get-tuple-element.262.cosine, f32[640,128]{1,0:T(8,128)S(1)} %get-tuple-element.261.sine, ...), custom_call_target="tpu_custom_call" | custom-call | flops 268435456 | bytes 3805696 | tf_op jit(solution)/shard_map/pallas_call | solution.py:401
  88.3 3.2 %collective-permute-done.24 = bf16[656,128]{1,0:T(8,128)(2,1)S(1)} collective-permute-done((bf16[656,128]{1,0:T(8,128)(2,1)S(1)}, bf16[656,128]{1,0:T(8,128)(2,1)S(1)}, u32[]{:S(2)}, u32[]{:S(2)}) %collective-permute-start.24) | collective-permute-done | bytes 167968 | tf_op jit(solution)/shard_map/ppermute | solution.py:33
  91.6 4.2 %collective-permute-done.26.got = bf16[4,656,128]{2,1,0:T(8,128)(2,1)S(1)} collective-permute-done((bf16[4,656,128]{2,1,0:T(8,128)(2,1)S(1)}, bf16[4,656,128]{2,1,0:T(8,128)(2,1)S(1)}, u32[]{:S(2)}, u32[]{:S(2)}) %collective-permute-start.26) | collective-permute-done | bytes 671776 | tf_op jit(solution)/shard_map/ppermute | solution.py:33
  96.7 3.5 %collective-permute-start.28 = (bf16[656,128]{1,0:T(8,128)(2,1)S(1)}, bf16[656,128]{1,0:T(8,128)(2,1)S(1)}, u32[]{:S(2)}, u32[]{:S(2)}) collective-permute-start(bf16[656,128]{1,0:T(8,128)(2,1)S(1)} %get-tuple-element.114), channel_id=1, source_target_pairs={{0,16},{1,17},{2,18},{3,19},{4,20},{5,21},{6,22},{7,23},{8,24},{9,... | collective-permute-start | bytes 503816 | tf_op jit(solution)/shard_map/ppermute | solution.py:33
  103.3 2.0 fusion.64
  106.0 6.5 %collective-permute-done.28 = bf16[656,128]{1,0:T(8,128)(2,1)S(1)} collective-permute-done((bf16[656,128]{1,0:T(8,128)(2,1)S(1)}, bf16[656,128]{1,0:T(8,128)(2,1)S(1)}, u32[]{:S(2)}, u32[]{:S(2)}) %collective-permute-start.28) | collective-permute-done | bytes 167968 | tf_op jit(solution)/shard_map/ppermute | solution.py:33
  113.5 4.6 %collective-permute-done.30.got = bf16[4,656,128]{2,1,0:T(8,128)(2,1)S(1)} collective-permute-done((bf16[4,656,128]{2,1,0:T(8,128)(2,1)S(1)}, bf16[4,656,128]{2,1,0:T(8,128)(2,1)S(1)}, u32[]{:S(2)}, u32[]{:S(2)}) %collective-permute-start.30) | collective-permute-done | bytes 671776 | tf_op jit(solution)/shard_map/ppermute | solution.py:33
  125.2 5.3 %collective-permute-done.34 = bf16[128,1024]{1,0:T(8,128)(2,1)S(1)} collective-permute-done((bf16[128,1024]{1,0:T(8,128)(2,1)S(1)}, bf16[128,1024]{1,0:T(8,128)(2,1)S(1)}, u32[]{:S(2)}, u32[]{:S(2)}) %collective-permute-start.34) | collective-permute-done | bytes 262176 | tf_op jit(solution)/shard_map/ppermute | solution.py:47
  130.8 6.4 %collective-permute-done.33.got = bf16[4,656,128]{2,1,0:T(8,128)(2,1)S(1)} collective-permute-done((bf16[4,656,128]{2,1,0:T(8,128)(2,1)S(1)}, bf16[4,656,128]{2,1,0:T(8,128)(2,1)S(1)}, u32[]{:S(2)}, u32[]{:S(2)}) %collective-permute-start.33) | collective-permute-done | bytes 671776 | tf_op jit(solution)/shard_map/ppermute | solution.py:33
  141.1 7.3 %multiply_convert_fusion = (bf16[512,656]{0,1:T(8,128)(2,1)S(1)}, f32[512,656]{0,1:T(8,128)S(1)}, f32[512,656]{0,1:T(8,128)S(1)}) fusion(f32[512,656]{0,1:T(8,128)S(1)} %copy-done.23, bf16[512,1024]{1,0:T(8,128)(2,1)S(1)} %bitcast.260, bf16[656,1024]{1,0:T(8,128)(2,1)S(1)} %shard_map.158), kind=kOutput, calls=%fused_computation.21 | convolution fusion | flops 710033408 | bytes 7094272 | tf_op jit(solution)/shard_map/dot_general | solution.py:297
  159.7 6.1 %collective-permute-done.38 = bf16[128,1024]{1,0:T(8,128)(2,1)S(1)} collective-permute-done((bf16[128,1024]{1,0:T(8,128)(2,1)S(1)}, bf16[128,1024]{1,0:T(8,128)(2,1)S(1)}, u32[]{:S(2)}, u32[]{:S(2)}) %collective-permute-start.38) | collective-permute-done | bytes 262176 | tf_op jit(solution)/shard_map/ppermute | solution.py:56
  165.9 7.5 %collective-permute-done.36 = bf16[4,656,128]{2,1,0:T(8,128)(2,1)S(1)} collective-permute-done((bf16[4,656,128]{2,1,0:T(8,128)(2,1)S(1)}, bf16[4,656,128]{2,1,0:T(8,128)(2,1)S(1)}, u32[]{:S(2)}, u32[]{:S(2)}) %collective-permute-start.36) | collective-permute-done | bytes 671776 | tf_op jit(solution)/shard_map/ppermute | solution.py:33
  177.4 3.2 %collective-permute-start.40 = (bf16[656,128]{1,0:T(8,128)(2,1)S(1)}, bf16[656,128]{1,0:T(8,128)(2,1)S(1)}, u32[]{:S(2)}, u32[]{:S(2)}) collective-permute-start(bf16[656,128]{1,0:T(8,128)(2,1)S(1)} %get-tuple-element.231), channel_id=1, source_target_pairs={{0,16},{1,17},{2,18},{3,19},{4,20},{5,21},{6,22},{7,23},{8,24},{9,... | collective-permute-start | bytes 503816 | tf_op jit(solution)/shard_map/ppermute | solution.py:33
  184.2 8.7 %collective-permute-done.40.refs_2_ = bf16[656,128]{1,0:T(8,128)(2,1)S(1)} collective-permute-done((bf16[656,128]{1,0:T(8,128)(2,1)S(1)}, bf16[656,128]{1,0:T(8,128)(2,1)S(1)}, u32[]{:S(2)}, u32[]{:S(2)}) %collective-permute-start.40) | collective-permute-done | bytes 167968 | tf_op jit(solution)/shard_map/ppermute | solution.py:33
  195.0 2.4 collective-permute-start.44
  202.9 5.0 %shard_map.163 = (bf16[512,256]{1,0:T(8,128)(2,1)S(1)}, f32[640,256]{1,0:T(8,128)S(1)}, f32[640,256]{1,0:T(8,128)S(1)}) custom-call(bf16[512,256]{1,0:T(8,128)(2,1)S(1)} %copy-done.13, bf16[640,256]{1,0:T(8,128)(2,1)S(1)} %copy-done.9, bf16[640,256]{1,0:T(8,128)(2,1)S(1)} %copy-done.11, bf16[512,256]{1,0:T(8,128)(2,1)S(1)} %convolution_convert_fusion.5.grad, ...), custom_call_target="tpu_custom_call" | custom-call | flops 805306368 | bytes 3412480 | tf_op jit(solution)/shard_map/pallas_call | solution.py:401
  208.1 3.3 %collective-permute-done.47 = bf16[4,656,128]{2,1,0:T(8,128)(2,1)S(1)} collective-permute-done((bf16[4,656,128]{2,1,0:T(8,128)(2,1)S(1)}, bf16[4,656,128]{2,1,0:T(8,128)(2,1)S(1)}, u32[]{:S(2)}, u32[]{:S(2)}) %collective-permute-start.47) | collective-permute-done | bytes 671776 | tf_op jit(solution)/shard_map/ppermute | solution.py:33
  212.8 3.1 %collective-permute-start.54 = (bf16[64,512]{1,0:T(8,128)(2,1)S(1)}, bf16[64,512]{1,0:T(8,128)(2,1)S(1)}, u32[]{:S(2)}, u32[]{:S(2)}) collective-permute-start(bf16[64,512]{1,0:T(8,128)(2,1)S(1)} %get-tuple-element.234), channel_id=1, source_target_pairs={{0,4},{4,8},{8,12},{12,16},{16,20},{20,24},{24,28},{1,5},{5,9},{9,... | collective-permute-start | bytes 196616 | tf_op jit(solution)/shard_map/ppermute | solution.py:558
  217.8 5.7 %collective-permute-done.55 = bf16[64,512]{1,0:T(8,128)(2,1)S(1)} collective-permute-done((bf16[64,512]{1,0:T(8,128)(2,1)S(1)}, bf16[64,512]{1,0:T(8,128)(2,1)S(1)}, u32[]{:S(2)}, u32[]{:S(2)}) %collective-permute-start.55) | collective-permute-done | bytes 65568 | tf_op jit(solution)/shard_map/ppermute | solution.py:557
  227.6 2.6 collective-permute-done.53
  232.2 3.0 collective-permute-start.56
  237.1 2.8 collective-permute-start.51
  241.1 2.8 collective-permute-done.49.refs_9_
  243.9 8.2 %collective-permute-done.50.refs_10_ = bf16[656,128]{1,0:T(8,128)(2,1)S(1)} collective-permute-done((bf16[656,128]{1,0:T(8,128)(2,1)S(1)}, bf16[656,128]{1,0:T(8,128)(2,1)S(1)}, u32[]{:S(2)}, u32[]{:S(2)}) %collective-permute-start.50) | collective-permute-done | bytes 167968 | tf_op jit(solution)/shard_map/ppermute | solution.py:33
  252.1 6.9 %collective-permute-done.57 = bf16[4,32,1024]{2,1,0:T(8,128)(2,1)S(1)} collective-permute-done((bf16[4,32,1024]{2,1,0:T(8,128)(2,1)S(1)}, bf16[4,32,1024]{2,1,0:T(8,128)(2,1)S(1)}, u32[]{:S(2)}, u32[]{:S(2)}) %collective-permute-start.57) | collective-permute-done | bytes 262176 | tf_op jit(solution)/shard_map/ppermute | solution.py:33
  261.7 1.8 collective-permute-start.69
  265.5 1.8 collective-permute-start.60
  267.4 2.0 collective-permute-start.63
  269.3 1.8 collective-permute-start.64
  273.8 9.8 %collective-permute-done.59 = bf16[2,128,1024]{2,1,0:T(8,128)(2,1)S(1)} collective-permute-done((bf16[2,128,1024]{2,1,0:T(8,128)(2,1)S(1)}, bf16[2,128,1024]{2,1,0:T(8,128)(2,1)S(1)}, u32[]{:S(2)}, u32[]{:S(2)}) %collective-permute-start.59) | collective-permute-done | bytes 524320 | tf_op jit(solution)/shard_map/ppermute | solution.py:56
  287.2 1.8 reshape.223
  290.5 2.0 reshape.219
  293.0 1.8 collective-permute-start.65
  295.8 1.9 collective-permute-done.65
  (359 shorter events, 99.0 us)
Async XLA Ops:
  0.6 16.1 %collective-permute-start = (bf16[32,1024]{1,0:T(8,128)(2,1)}, bf16[32,1024]{1,0:T(8,128)(2,1)S(1)}, u32[]{:S(2)}, u32[]{:S(2)}) collective-permute-start(bf16[32,1024]{1,0:T(8,128)(2,1)} %param.13), channel_id=1, source_target_pairs={{0,8},{1,9},{2,10},{3,11},{4,12},{5,13},{6,14},{7,15},{8,0},{9,1},... | collective-permute-start | bytes 196616 | tf_op jit(solution)/shard_map/ppermute | solution.py:33
  3.7 13.4 %collective-permute-start.1 = (bf16[32,1024]{1,0:T(8,128)(2,1)}, bf16[32,1024]{1,0:T(8,128)(2,1)S(1)}, u32[]{:S(2)}, u32[]{:S(2)}) collective-permute-start(bf16[32,1024]{1,0:T(8,128)(2,1)} %param.13), channel_id=1, source_target_pairs={{0,16},{1,17},{2,18},{3,19},{4,20},{5,21},{6,22},{7,23},{8,24},{9,... | collective-permute-start | bytes 196616 | tf_op jit(solution)/shard_map/ppermute | solution.py:33
  6.3 15.2 %collective-permute-start.2 = (bf16[32,1024]{1,0:T(8,128)(2,1)}, bf16[32,1024]{1,0:T(8,128)(2,1)S(1)}, u32[]{:S(2)}, u32[]{:S(2)}) collective-permute-start(bf16[32,1024]{1,0:T(8,128)(2,1)} %param.13), channel_id=1, source_target_pairs={{0,24},{1,25},{2,26},{3,27},{4,28},{5,29},{6,30},{7,31},{8,16},{9,... | collective-permute-start | bytes 196616 | tf_op jit(solution)/shard_map/ppermute | solution.py:33
  10.9 10.6 %collective-permute-start.5 = (bf16[64,1024]{1,0:T(8,128)(2,1)S(1)}, bf16[64,1024]{1,0:T(8,128)(2,1)S(1)}, u32[]{:S(2)}, u32[]{:S(2)}) collective-permute-start(bf16[64,1024]{1,0:T(8,128)(2,1)S(1)} %get-tuple-element.260), channel_id=1, source_target_pairs={{3,4},{7,8},{11,12},{15,16},{19,20},{23,24},{27,28}} | collective-permute-start | bytes 393224 | tf_op jit(solution)/shard_map/ppermute | solution.py:454
  16.8 14.0 %collective-permute-start.21 = (bf16[128,1024]{1,0:T(8,128)(2,1)S(1)}, bf16[128,1024]{1,0:T(8,128)(2,1)S(1)}, u32[]{:S(2)}, u32[]{:S(2)}) collective-permute-start(bf16[128,1024]{1,0:T(8,128)(2,1)S(1)} %copy-done.30), channel_id=1, source_target_pairs={{0,2},{2,0},{1,3},{3,1},{4,6},{6,4},{5,7},{7,5},{8,10},{10,8},{9,1... | collective-permute-start | bytes 786440 | tf_op jit(solution)/shard_map/ppermute | solution.py:47
  22.6 23.9 %collective-permute-start.7 = (bf16[768,128]{1,0:T(8,128)(2,1)S(1)}, bf16[768,128]{1,0:T(8,128)(2,1)S(1)}, u32[]{:S(2)}, u32[]{:S(2)}) collective-permute-start(bf16[768,128]{1,0:T(8,128)(2,1)S(1)} %shard_map.152), channel_id=1, source_target_pairs={{0,8},{1,9},{2,10},{3,11},{4,12},{5,13},{6,14},{7,15},{8,0},{9,1},... | collective-permute-start | bytes 589832 | tf_op jit(solution)/shard_map/ppermute | solution.py:33
  26.0 21.1 %collective-permute-start.8 = (bf16[768,128]{1,0:T(8,128)(2,1)S(1)}, bf16[768,128]{1,0:T(8,128)(2,1)S(1)}, u32[]{:S(2)}, u32[]{:S(2)}) collective-permute-start(bf16[768,128]{1,0:T(8,128)(2,1)S(1)} %shard_map.152), channel_id=1, source_target_pairs={{0,16},{1,17},{2,18},{3,19},{4,20},{5,21},{6,22},{7,23},{8,24},{9,... | collective-permute-start | bytes 589832 | tf_op jit(solution)/shard_map/ppermute | solution.py:33
  29.5 17.7 %collective-permute-start.9 = (bf16[768,128]{1,0:T(8,128)(2,1)S(1)}, bf16[768,128]{1,0:T(8,128)(2,1)S(1)}, u32[]{:S(2)}, u32[]{:S(2)}) collective-permute-start(bf16[768,128]{1,0:T(8,128)(2,1)S(1)} %shard_map.152), channel_id=1, source_target_pairs={{0,24},{1,25},{2,26},{3,27},{4,28},{5,29},{6,30},{7,31},{8,16},{9,... | collective-permute-start | bytes 589832 | tf_op jit(solution)/shard_map/ppermute | solution.py:33
  29.6 9.2 %collective-permute-start.13 = (bf16[1,2,32,2048]{3,2,1,0:T(8,128)(2,1)S(1)}, bf16[1,2,32,2048]{3,2,1,0:T(8,128)(2,1)S(1)}, u32[]{:S(2)}, u32[]{:S(2)}) collective-permute-start(bf16[1,2,32,2048]{3,2,1,0:T(8,128)(2,1)S(1)} %constant_dynamic-slice_fusion.5), channel_id=1, source_target_pairs={{0,2},{2,0},{1,3},{3,1},{4,6},{6,4},{5,7},{7,5},{8,10},{10,8},{9,1... | collective-permute-start | bytes 786440 | tf_op jit(solution)/shard_map/ppermute | solution.py:40
  30.8 15.6 %collective-permute-start.11 = (bf16[192,1024]{1,0:T(8,128)(2,1)S(1)}, bf16[192,1024]{1,0:T(8,128)(2,1)S(1)}, u32[]{:S(2)}, u32[]{:S(2)}) collective-permute-start(bf16[192,1024]{1,0:T(8,128)(2,1)S(1)} %constant_dynamic-update-slice_fusion), channel_id=1, source_target_pairs={{0,2},{2,0},{1,3},{3,1},{4,6},{6,4},{5,7},{7,5},{8,10},{10,8},{9,1... | collective-permute-start | bytes 1179656 | tf_op jit(solution)/shard_map/ppermute | solution.py:47
  38.8 11.5 %collective-permute-start.10 = (bf16[4,32,1024]{2,1,0:T(8,128)(2,1)S(1)}, bf16[4,32,1024]{2,1,0:T(8,128)(2,1)S(1)}, u32[]{:S(2)}, u32[]{:S(2)}) collective-permute-start(bf16[4,32,1024]{2,1,0:T(8,128)(2,1)S(1)} %pad_maximum_fusion.19.cells), channel_id=1, source_target_pairs={{0,4},{1,5},{2,6},{3,7},{4,0},{5,1},{6,2},{7,3},{8,12},{9,13},{10,... | collective-permute-start | bytes 786440 | tf_op jit(solution)/shard_map/ppermute | solution.py:33
  50.9 8.6 %collective-permute-start.19 = (bf16[1,2,2,32,1024]{4,3,1,0,2:T(8,128)(2,1)S(1)}, bf16[1,2,2,32,1024]{4,3,1,0,2:T(8,128)(2,1)S(1)}, u32[]{:S(2)}, u32[]{:S(2)}) collective-permute-start(bf16[1,2,2,32,1024]{4,3,1,0,2:T(8,128)(2,1)S(1)} %copy.86), channel_id=1, source_target_pairs={{0,2},{2,0},{1,3},{3,1},{4,6},{6,4},{5,7},{7,5},{8,10},{10,8},{9,1... | collective-permute-start | bytes 786440 | tf_op jit(solution)/shard_map/ppermute | solution.py:40
  52.8 9.4 %collective-permute-start.15 = (bf16[656,128]{1,0:T(8,128)(2,1)S(1)}, bf16[656,128]{1,0:T(8,128)(2,1)S(1)}, u32[]{:S(2)}, u32[]{:S(2)}) collective-permute-start(bf16[656,128]{1,0:T(8,128)(2,1)S(1)} %get-tuple-element.103), channel_id=1, source_target_pairs={{0,8},{1,9},{2,10},{3,11},{4,12},{5,13},{6,14},{7,15},{8,0},{9,1},... | collective-permute-start | bytes 503816 | tf_op jit(solution)/shard_map/ppermute | solution.py:33
  53.5 15.9 %collective-permute-start.16 = (bf16[656,128]{1,0:T(8,128)(2,1)S(1)}, bf16[656,128]{1,0:T(8,128)(2,1)S(1)}, u32[]{:S(2)}, u32[]{:S(2)}) collective-permute-start(bf16[656,128]{1,0:T(8,128)(2,1)S(1)} %get-tuple-element.103), channel_id=1, source_target_pairs={{0,16},{1,17},{2,18},{3,19},{4,20},{5,21},{6,22},{7,23},{8,24},{9,... | collective-permute-start | bytes 503816 | tf_op jit(solution)/shard_map/ppermute | solution.py:33
  57.0 12.4 %collective-permute-start.17 = (bf16[656,128]{1,0:T(8,128)(2,1)S(1)}, bf16[656,128]{1,0:T(8,128)(2,1)S(1)}, u32[]{:S(2)}, u32[]{:S(2)}) collective-permute-start(bf16[656,128]{1,0:T(8,128)(2,1)S(1)} %get-tuple-element.103), channel_id=1, source_target_pairs={{0,24},{1,25},{2,26},{3,27},{4,28},{5,29},{6,30},{7,31},{8,16},{9,... | collective-permute-start | bytes 503816 | tf_op jit(solution)/shard_map/ppermute | solution.py:33
  57.3 18.7 %collective-permute-start.18 = (bf16[4,768,128]{2,1,0:T(8,128)(2,1)S(1)}, bf16[4,768,128]{2,1,0:T(8,128)(2,1)S(1)}, u32[]{:S(2)}, u32[]{:S(2)}) collective-permute-start(bf16[4,768,128]{2,1,0:T(8,128)(2,1)S(1)} %pad_maximum_fusion.6.cells), channel_id=1, source_target_pairs={{0,4},{1,5},{2,6},{3,7},{4,0},{5,1},{6,2},{7,3},{8,12},{9,13},{10,... | collective-permute-start | bytes 2359304 | tf_op jit(solution)/shard_map/ppermute | solution.py:33
  59.7 9.8 %collective-permute-start.20 = (bf16[2,1,2,32,1024]{4,3,1,0,2:T(8,128)(2,1)S(1)}, bf16[2,1,2,32,1024]{4,3,1,0,2:T(8,128)(2,1)S(1)}, u32[]{:S(2)}, u32[]{:S(2)}) collective-permute-start(bf16[2,1,2,32,1024]{4,3,1,0,2:T(8,128)(2,1)S(1)} %fusion.40), channel_id=1, source_target_pairs={{0,1},{1,0},{2,3},{3,2},{4,5},{5,4},{6,7},{7,6},{8,9},{9,8},{10,11... | collective-permute-start | bytes 786440 | tf_op jit(solution)/shard_map/ppermute | solution.py:40
  76.0 12.4 %collective-permute-start.23 = (bf16[656,128]{1,0:T(8,128)(2,1)S(1)}, bf16[656,128]{1,0:T(8,128)(2,1)S(1)}, u32[]{:S(2)}, u32[]{:S(2)}) collective-permute-start(bf16[656,128]{1,0:T(8,128)(2,1)S(1)} %get-tuple-element.107), channel_id=1, source_target_pairs={{0,8},{1,9},{2,10},{3,11},{4,12},{5,13},{6,14},{7,15},{8,0},{9,1},... | collective-permute-start | bytes 503816 | tf_op jit(solution)/shard_map/ppermute | solution.py:33
  76.5 15.0 %collective-permute-start.24 = (bf16[656,128]{1,0:T(8,128)(2,1)S(1)}, bf16[656,128]{1,0:T(8,128)(2,1)S(1)}, u32[]{:S(2)}, u32[]{:S(2)}) collective-permute-start(bf16[656,128]{1,0:T(8,128)(2,1)S(1)} %get-tuple-element.107), channel_id=1, source_target_pairs={{0,16},{1,17},{2,18},{3,19},{4,20},{5,21},{6,22},{7,23},{8,24},{9,... | collective-permute-start | bytes 503816 | tf_op jit(solution)/shard_map/ppermute | solution.py:33
  80.1 11.5 %collective-permute-start.25 = (bf16[656,128]{1,0:T(8,128)(2,1)S(1)}, bf16[656,128]{1,0:T(8,128)(2,1)S(1)}, u32[]{:S(2)}, u32[]{:S(2)}) collective-permute-start(bf16[656,128]{1,0:T(8,128)(2,1)S(1)} %get-tuple-element.107), channel_id=1, source_target_pairs={{0,24},{1,25},{2,26},{3,27},{4,28},{5,29},{6,30},{7,31},{8,16},{9,... | collective-permute-start | bytes 503816 | tf_op jit(solution)/shard_map/ppermute | solution.py:33
  81.3 14.5 %collective-permute-start.26 = (bf16[4,656,128]{2,1,0:T(8,128)(2,1)S(1)}, bf16[4,656,128]{2,1,0:T(8,128)(2,1)S(1)}, u32[]{:S(2)}, u32[]{:S(2)}) collective-permute-start(bf16[4,656,128]{2,1,0:T(8,128)(2,1)S(1)} %pad_maximum_fusion.9.cells), channel_id=1, source_target_pairs={{0,4},{1,5},{2,6},{3,7},{4,0},{5,1},{6,2},{7,3},{8,12},{9,13},{10,... | collective-permute-start | bytes 2015240 | tf_op jit(solution)/shard_map/ppermute | solution.py:33
  96.0 10.0 %collective-permute-start.27 = (bf16[656,128]{1,0:T(8,128)(2,1)S(1)}, bf16[656,128]{1,0:T(8,128)(2,1)S(1)}, u32[]{:S(2)}, u32[]{:S(2)}) collective-permute-start(bf16[656,128]{1,0:T(8,128)(2,1)S(1)} %get-tuple-element.114), channel_id=1, source_target_pairs={{0,8},{1,9},{2,10},{3,11},{4,12},{5,13},{6,14},{7,15},{8,0},{9,1},... | collective-permute-start | bytes 503816 | tf_op jit(solution)/shard_map/ppermute | solution.py:33
  96.7 15.8 %collective-permute-start.28 = (bf16[656,128]{1,0:T(8,128)(2,1)S(1)}, bf16[656,128]{1,0:T(8,128)(2,1)S(1)}, u32[]{:S(2)}, u32[]{:S(2)}) collective-permute-start(bf16[656,128]{1,0:T(8,128)(2,1)S(1)} %get-tuple-element.114), channel_id=1, source_target_pairs={{0,16},{1,17},{2,18},{3,19},{4,20},{5,21},{6,22},{7,23},{8,24},{9,... | collective-permute-start | bytes 503816 | tf_op jit(solution)/shard_map/ppermute | solution.py:33
  100.2 12.3 %collective-permute-start.29 = (bf16[656,128]{1,0:T(8,128)(2,1)S(1)}, bf16[656,128]{1,0:T(8,128)(2,1)S(1)}, u32[]{:S(2)}, u32[]{:S(2)}) collective-permute-start(bf16[656,128]{1,0:T(8,128)(2,1)S(1)} %get-tuple-element.114), channel_id=1, source_target_pairs={{0,24},{1,25},{2,26},{3,27},{4,28},{5,29},{6,30},{7,31},{8,16},{9,... | collective-permute-start | bytes 503816 | tf_op jit(solution)/shard_map/ppermute | solution.py:33
  101.4 16.7 %collective-permute-start.30 = (bf16[4,656,128]{2,1,0:T(8,128)(2,1)S(1)}, bf16[4,656,128]{2,1,0:T(8,128)(2,1)S(1)}, u32[]{:S(2)}, u32[]{:S(2)}) collective-permute-start(bf16[4,656,128]{2,1,0:T(8,128)(2,1)S(1)} %pad_maximum_fusion.10.cells), channel_id=1, source_target_pairs={{0,4},{1,5},{2,6},{3,7},{4,0},{5,1},{6,2},{7,3},{8,12},{9,13},{10,... | collective-permute-start | bytes 2015240 | tf_op jit(solution)/shard_map/ppermute | solution.py:33
  102.8 9.8 %collective-permute-start.32 = (bf16[128,1024]{1,0:T(8,128)(2,1)S(1)}, bf16[128,1024]{1,0:T(8,128)(2,1)S(1)}, u32[]{:S(2)}, u32[]{:S(2)}) collective-permute-start(bf16[128,1024]{1,0:T(8,128)(2,1)S(1)} %fusion.34), channel_id=1, source_target_pairs={{0,2},{2,0},{1,3},{3,1},{4,6},{6,4},{5,7},{7,5},{8,10},{10,8},{9,1... | collective-permute-start | bytes 786440 | tf_op jit(solution)/shard_map/ppermute | solution.py:56
  121.4 15.8 %collective-permute-start.33 = (bf16[4,656,128]{2,1,0:T(8,128)(2,1)S(1)}, bf16[4,656,128]{2,1,0:T(8,128)(2,1)S(1)}, u32[]{:S(2)}, u32[]{:S(2)}) collective-permute-start(bf16[4,656,128]{2,1,0:T(8,128)(2,1)S(1)} %pad_maximum_fusion.11.cells), channel_id=1, source_target_pairs={{0,4},{1,5},{2,6},{3,7},{4,0},{5,1},{6,2},{7,3},{8,12},{9,13},{10,... | collective-permute-start | bytes 2015240 | tf_op jit(solution)/shard_map/ppermute | solution.py:33
  156.0 17.4 %collective-permute-start.36 = (bf16[4,656,128]{2,1,0:T(8,128)(2,1)S(1)}, bf16[4,656,128]{2,1,0:T(8,128)(2,1)S(1)}, u32[]{:S(2)}, u32[]{:S(2)}) collective-permute-start(bf16[4,656,128]{2,1,0:T(8,128)(2,1)S(1)} %get-tuple-element.133), channel_id=1, source_target_pairs={{0,4},{1,5},{2,6},{3,7},{4,0},{5,1},{6,2},{7,3},{8,12},{9,13},{10,... | collective-permute-start | bytes 2015240 | tf_op jit(solution)/shard_map/ppermute | solution.py:33
  157.4 8.4 %collective-permute-start.38 = (bf16[128,1024]{1,0:T(8,128)(2,1)S(1)}, bf16[128,1024]{1,0:T(8,128)(2,1)S(1)}, u32[]{:S(2)}, u32[]{:S(2)}) collective-permute-start(bf16[128,1024]{1,0:T(8,128)(2,1)S(1)} %fusion.35), channel_id=1, source_target_pairs={{0,2},{2,0},{1,3},{3,1},{4,6},{6,4},{5,7},{7,5},{8,10},{10,8},{9,1... | collective-permute-start | bytes 786440 | tf_op jit(solution)/shard_map/ppermute | solution.py:56
  175.0 17.8 %collective-permute-start.42 = (bf16[4,656,128]{2,1,0:T(8,128)(2,1)S(1)}, bf16[4,656,128]{2,1,0:T(8,128)(2,1)S(1)}, u32[]{:S(2)}, u32[]{:S(2)}) collective-permute-start(bf16[4,656,128]{2,1,0:T(8,128)(2,1)S(1)} %get-tuple-element.137), channel_id=1, source_target_pairs={{0,4},{1,5},{2,6},{3,7},{4,0},{5,1},{6,2},{7,3},{8,12},{9,13},{10,... | collective-permute-start | bytes 2015240 | tf_op jit(solution)/shard_map/ppermute | solution.py:33
  177.4 15.4 %collective-permute-start.40 = (bf16[656,128]{1,0:T(8,128)(2,1)S(1)}, bf16[656,128]{1,0:T(8,128)(2,1)S(1)}, u32[]{:S(2)}, u32[]{:S(2)}) collective-permute-start(bf16[656,128]{1,0:T(8,128)(2,1)S(1)} %get-tuple-element.231), channel_id=1, source_target_pairs={{0,16},{1,17},{2,18},{3,19},{4,20},{5,21},{6,22},{7,23},{8,24},{9,... | collective-permute-start | bytes 503816 | tf_op jit(solution)/shard_map/ppermute | solution.py:33
  180.6 12.2 %collective-permute-start.41 = (bf16[656,128]{1,0:T(8,128)(2,1)S(1)}, bf16[656,128]{1,0:T(8,128)(2,1)S(1)}, u32[]{:S(2)}, u32[]{:S(2)}) collective-permute-start(bf16[656,128]{1,0:T(8,128)(2,1)S(1)} %get-tuple-element.230), channel_id=1, source_target_pairs={{0,24},{1,25},{2,26},{3,27},{4,28},{5,29},{6,30},{7,31},{8,16},{9,... | collective-permute-start | bytes 503816 | tf_op jit(solution)/shard_map/ppermute | solution.py:33
  193.9 17.5 %collective-permute-start.47 = (bf16[4,656,128]{2,1,0:T(8,128)(2,1)S(1)}, bf16[4,656,128]{2,1,0:T(8,128)(2,1)S(1)}, u32[]{:S(2)}, u32[]{:S(2)}) collective-permute-start(bf16[4,656,128]{2,1,0:T(8,128)(2,1)S(1)} %get-tuple-element.140), channel_id=1, source_target_pairs={{0,4},{1,5},{2,6},{3,7},{4,0},{5,1},{6,2},{7,3},{8,12},{9,13},{10,... | collective-permute-start | bytes 2015240 | tf_op jit(solution)/shard_map/ppermute | solution.py:33
  195.0 16.4 %collective-permute-start.44 = (bf16[656,128]{1,0:T(8,128)(2,1)S(1)}, bf16[656,128]{1,0:T(8,128)(2,1)S(1)}, u32[]{:S(2)}, u32[]{:S(2)}) collective-permute-start(bf16[656,128]{1,0:T(8,128)(2,1)S(1)} %get-tuple-element.228), channel_id=1, source_target_pairs={{0,8},{1,9},{2,10},{3,11},{4,12},{5,13},{6,14},{7,15},{8,0},{9,1},... | collective-permute-start | bytes 503816 | tf_op jit(solution)/shard_map/ppermute | solution.py:33
  197.4 15.3 %collective-permute-start.45 = (bf16[656,128]{1,0:T(8,128)(2,1)S(1)}, bf16[656,128]{1,0:T(8,128)(2,1)S(1)}, u32[]{:S(2)}, u32[]{:S(2)}) collective-permute-start(bf16[656,128]{1,0:T(8,128)(2,1)S(1)} %get-tuple-element.227), channel_id=1, source_target_pairs={{0,16},{1,17},{2,18},{3,19},{4,20},{5,21},{6,22},{7,23},{8,24},{9,... | collective-permute-start | bytes 503816 | tf_op jit(solution)/shard_map/ppermute | solution.py:33
  198.5 14.2 %collective-permute-start.46 = (bf16[656,128]{1,0:T(8,128)(2,1)S(1)}, bf16[656,128]{1,0:T(8,128)(2,1)S(1)}, u32[]{:S(2)}, u32[]{:S(2)}) collective-permute-start(bf16[656,128]{1,0:T(8,128)(2,1)S(1)} %get-tuple-element.226), channel_id=1, source_target_pairs={{0,24},{1,25},{2,26},{3,27},{4,28},{5,29},{6,30},{7,31},{8,16},{9,... | collective-permute-start | bytes 503816 | tf_op jit(solution)/shard_map/ppermute | solution.py:33
  232.2 26.7 %collective-permute-start.56 = (bf16[4,768,128]{2,1,0:T(8,128)(2,1)S(1)}, bf16[4,768,128]{2,1,0:T(8,128)(2,1)S(1)}, u32[]{:S(2)}, u32[]{:S(2)}) collective-permute-start(bf16[4,768,128]{2,1,0:T(8,128)(2,1)S(1)} %get-tuple-element.154), channel_id=1, source_target_pairs={{0,4},{1,5},{2,6},{3,7},{4,0},{5,1},{6,2},{7,3},{8,12},{9,13},{10,... | collective-permute-start | bytes 2359304 | tf_op jit(solution)/shard_map/ppermute | solution.py:33
  235.5 8.4 %collective-permute-start.49 = (bf16[656,128]{1,0:T(8,128)(2,1)S(1)}, bf16[656,128]{1,0:T(8,128)(2,1)S(1)}, u32[]{:S(2)}, u32[]{:S(2)}) collective-permute-start(bf16[656,128]{1,0:T(8,128)(2,1)S(1)} %get-tuple-element.224), channel_id=1, source_target_pairs={{0,8},{1,9},{2,10},{3,11},{4,12},{5,13},{6,14},{7,15},{8,0},{9,1},... | collective-permute-start | bytes 503816 | tf_op jit(solution)/shard_map/ppermute | solution.py:33
  237.1 15.0 %collective-permute-start.50 = (bf16[656,128]{1,0:T(8,128)(2,1)S(1)}, bf16[656,128]{1,0:T(8,128)(2,1)S(1)}, u32[]{:S(2)}, u32[]{:S(2)}) collective-permute-start(bf16[656,128]{1,0:T(8,128)(2,1)S(1)} %get-tuple-element.223), channel_id=1, source_target_pairs={{0,16},{1,17},{2,18},{3,19},{4,20},{5,21},{6,22},{7,23},{8,24},{9,... | collective-permute-start | bytes 503816 | tf_op jit(solution)/shard_map/ppermute | solution.py:33
  237.1 15.0 %collective-permute-start.51 = (bf16[656,128]{1,0:T(8,128)(2,1)S(1)}, bf16[656,128]{1,0:T(8,128)(2,1)S(1)}, u32[]{:S(2)}, u32[]{:S(2)}) collective-permute-start(bf16[656,128]{1,0:T(8,128)(2,1)S(1)} %get-tuple-element.222), channel_id=1, source_target_pairs={{0,24},{1,25},{2,26},{3,27},{4,28},{5,29},{6,30},{7,31},{8,16},{9,... | collective-permute-start | bytes 503816 | tf_op jit(solution)/shard_map/ppermute | solution.py:33
  239.9 19.0 %collective-permute-start.57 = (bf16[4,32,1024]{2,1,0:T(8,128)(2,1)S(1)}, bf16[4,32,1024]{2,1,0:T(8,128)(2,1)S(1)}, u32[]{:S(2)}, u32[]{:S(2)}) collective-permute-start(bf16[4,32,1024]{2,1,0:T(8,128)(2,1)S(1)} %get-tuple-element.155), channel_id=1, source_target_pairs={{0,4},{1,5},{2,6},{3,7},{4,0},{5,1},{6,2},{7,3},{8,12},{9,13},{10,... | collective-permute-start | bytes 786440 | tf_op jit(solution)/shard_map/ppermute | solution.py:33
  260.7 8.7 %collective-permute-start.68 = (bf16[32,1024]{1,0:T(8,128)(2,1)S(1)}, bf16[32,1024]{1,0:T(8,128)(2,1)S(1)}, u32[]{:S(2)}, u32[]{:S(2)}) collective-permute-start(bf16[32,1024]{1,0:T(8,128)(2,1)S(1)} %get-tuple-element.258), channel_id=1, source_target_pairs={{0,16},{1,17},{2,18},{3,19},{4,20},{5,21},{6,22},{7,23},{8,24},{9,... | collective-permute-start | bytes 196616 | tf_op jit(solution)/shard_map/ppermute | solution.py:33
  261.7 9.5 %collective-permute-start.69 = (bf16[32,1024]{1,0:T(8,128)(2,1)S(1)}, bf16[32,1024]{1,0:T(8,128)(2,1)S(1)}, u32[]{:S(2)}, u32[]{:S(2)}) collective-permute-start(bf16[32,1024]{1,0:T(8,128)(2,1)S(1)} %get-tuple-element.257), channel_id=1, source_target_pairs={{0,24},{1,25},{2,26},{3,27},{4,28},{5,29},{6,30},{7,31},{8,16},{9,... | collective-permute-start | bytes 196616 | tf_op jit(solution)/shard_map/ppermute | solution.py:33
  264.5 28.3 %collective-permute-start.62 = (bf16[768,128]{1,0:T(8,128)(2,1)}, bf16[768,128]{1,0:T(8,128)(2,1)S(1)}, u32[]{:S(2)}, u32[]{:S(2)}) collective-permute-start(bf16[768,128]{1,0:T(8,128)(2,1)} %get-tuple-element.202), channel_id=1, source_target_pairs={{0,8},{1,9},{2,10},{3,11},{4,12},{5,13},{6,14},{7,15},{8,0},{9,1},... | collective-permute-start | bytes 589832 | tf_op jit(solution)/shard_map/ppermute | solution.py:33
  267.4 25.4 %collective-permute-start.63 = (bf16[768,128]{1,0:T(8,128)(2,1)S(1)}, bf16[768,128]{1,0:T(8,128)(2,1)S(1)}, u32[]{:S(2)}, u32[]{:S(2)}) collective-permute-start(bf16[768,128]{1,0:T(8,128)(2,1)S(1)} %get-tuple-element.201), channel_id=1, source_target_pairs={{0,16},{1,17},{2,18},{3,19},{4,20},{5,21},{6,22},{7,23},{8,24},{9,... | collective-permute-start | bytes 589832 | tf_op jit(solution)/shard_map/ppermute | solution.py:33
  269.3 23.4 %collective-permute-start.64 = (bf16[768,128]{1,0:T(8,128)(2,1)S(1)}, bf16[768,128]{1,0:T(8,128)(2,1)S(1)}, u32[]{:S(2)}, u32[]{:S(2)}) collective-permute-start(bf16[768,128]{1,0:T(8,128)(2,1)S(1)} %get-tuple-element.200), channel_id=1, source_target_pairs={{0,24},{1,25},{2,26},{3,27},{4,28},{5,29},{6,30},{7,31},{8,16},{9,... | collective-permute-start | bytes 589832 | tf_op jit(solution)/shard_map/ppermute | solution.py:33
  271.2 12.4 %collective-permute-start.59 = (bf16[2,128,1024]{2,1,0:T(8,128)(2,1)S(1)}, bf16[2,128,1024]{2,1,0:T(8,128)(2,1)S(1)}, u32[]{:S(2)}, u32[]{:S(2)}) collective-permute-start(bf16[2,128,1024]{2,1,0:T(8,128)(2,1)S(1)} %fusion.24), channel_id=1, source_target_pairs={{0,2},{2,0},{1,3},{3,1},{4,6},{6,4},{5,7},{7,5},{8,10},{10,8},{9,1... | collective-permute-start | bytes 1572872 | tf_op jit(solution)/shard_map/ppermute | solution.py:56
  273.7 10.9 %collective-permute-start.61 = (bf16[2,1,32,2048]{3,2,1,0:T(8,128)(2,1)S(1)}, bf16[2,1,32,2048]{3,2,1,0:T(8,128)(2,1)S(1)}, u32[]{:S(2)}, u32[]{:S(2)}) collective-permute-start(bf16[2,1,32,2048]{3,2,1,0:T(8,128)(2,1)S(1)} %fusion.36), channel_id=1, source_target_pairs={{0,1},{1,0},{2,3},{3,2},{4,5},{5,4},{6,7},{7,6},{8,9},{9,8},{10,11... | collective-permute-start | bytes 786440 | tf_op jit(solution)/shard_map/ppermute | solution.py:40
  (63 other events, 532.4 us)

commit v6 on v5

--- a/solution.py
+++ b/solution.py
@@ -423,6 +423,11 @@
     shard = w_qkv.shape[0]
     tie = lax.optimization_barrier
 
+    def close(first, last):
+        first = tie(first)
+        return tie((first, last))
+
+
     gain_a = gain_attn.astype(F32)[:, None]
     gain_m = gain_mlp.astype(F32)[:, None]
 
@@ -430,12 +435,14 @@
         cells = w.reshape(shard, parts, 2, 2, width).transpose(2, 3, 0, 1, 4)
         return cells.reshape(2, 2, shard, parts * width)
 
-    def regroup(cells):
-        cells = trade(trade(cells, "fy", 0), "core", 1)
-        return cells.reshape(GROUP * shard, -1)
-
+    devices = lax.axis_size(ALL)
+    ahead = [(i, i + 1) for i in range(GROUP - 1, devices - 1, GROUP)]
+    behind = [(i + 1, i) for i in range(GROUP - 1, devices - 1, GROUP)]
+    edge = lax.ppermute(tokens[share - HALF :], ALL, ahead)
+    edge = edge + lax.ppermute(tokens[:HALF], ALL, behind)
     attn_z = z_gather(w_attn_out)
-    qkv = regroup(columns((w_qkv.astype(F32) * gain_a).astype(BF16), 3, OWN))
+    qkv = trade(columns((w_qkv.astype(F32) * gain_a).astype(BF16), 3, OWN), "fy", 0)
+    qkv = trade(qkv, "core", 1).reshape(GROUP * shard, -1)
     (qkv,) = turn(qkv, (3 * OWN,))
     rest = jnp.concatenate(
         [
@@ -445,31 +452,28 @@
         ],
         axis=-1,
     )
+    rest = trade(rest, "fy", 0)
+    attn_z, qkv, rest, edge, cotangent_in = tie((attn_z, qkv, rest, edge, cotangent))
+    qkv_z = z_gather(qkv)
+    attn_x = send_seq(attn_z, 1)
     ours = tokens.astype(F32)
     normed, inverse = normalize(ours)
-    hidden = normed.astype(BF16)
-    devices = lax.axis_size(ALL)
-    ahead = [(i, i + 1) for i in range(GROUP - 1, devices - 1, GROUP)]
-    behind = [(i + 1, i) for i in range(GROUP - 1, devices - 1, GROUP)]
-    edge = lax.ppermute(hidden[share - HALF :], ALL, ahead)
-    edge = edge + lax.ppermute(hidden[:HALF], ALL, behind)
-    attn_z, qkv, rest, hidden, edge = tie((attn_z, qkv, rest, hidden, edge))
-    qkv_z = z_gather(qkv)
-    attn_x = send_seq(attn_z, 1)
-    hidden = group_rows(jnp.concatenate([hidden, edge], axis=0)).reshape(GROUP, share + HALF, D)
+    hidden = jnp.concatenate([normed, normalize(edge.astype(F32))[0]], axis=0).astype(BF16)
+    hidden = group_rows(hidden).reshape(GROUP, share + HALF, D)
     before, after = hidden[0, share:], hidden[GROUP - 1, share:]
     hidden = hidden[:, :share].reshape(rows, D)
-    mlp, gate, up = turn(regroup(rest), (OWN_FF,) * 3)
+    mlp, gate, up = turn(trade(rest, "core", 1).reshape(GROUP * shard, -1), (OWN_FF,) * 3)
     wide = jnp.concatenate([before, hidden, after], axis=0)
-    qkv_z, attn_x, wide, mlp, gate, up = tie((qkv_z, attn_x, wide, mlp, gate, up))
+    (attn_x, wide, mlp, gate, up), qkv_z = close((attn_x, wide, mlp, gate, up), qkv_z)
     hidden = wide[HALF : HALF + rows]
     mlp_z = z_gather(mlp)
     qkv_x = send_seq(qkv_z, 1)
-    cot = group_rows(cotangent)
     attn = assemble_rows(attn_z, attn_x).reshape(2, 2, seqs // 4, shard, D)
-    attn = trade(trade(attn, "fy", 0), "core", 1)
-    attn_full = attn.transpose(2, 0, 1, 3, 4).reshape(OWN, D)
-    mlp_z, qkv_x, attn_full, gate, cot = tie((mlp_z, qkv_x, attn_full, gate, cot))
+    attn_full = trade(trade(attn, "fy", 0), "core", 1)
+    attn_full = attn_full.transpose(2, 0, 1, 3, 4).reshape(OWN, D)
+    (qkv_x, attn_full, gate, cotangent_in), mlp_z = close(
+        (qkv_x, attn_full, gate, cotangent_in), mlp_z
+    )
     gate_z = z_gather(gate)
     mlp_x = send_seq(mlp_z, 1)
     qkv_full = assemble(qkv_z, qkv_x)
@@ -495,22 +499,24 @@
         (packed, cosine, sine, q_seg, k_seg),
     )
     part = jnp.dot(attended, attn_full, preferred_element_type=F32)
-    gate_z, mlp_x, part, up = tie((gate_z, mlp_x, part, up))
+    cot = join(cotangent_in, "fy", 0)
+    (mlp_x, part, up, cot), gate_z = close((mlp_x, part, up, cot), gate_z)
     up_z = z_gather(up)
     gate_x = send_seq(gate_z, 1)
     middle = ours + group_sum(part, share)
     mlp_full = assemble(mlp_z, mlp_x)
-    grad_mixed = cols_dot(cot, mlp_full)
-    up_z, gate_x, middle, grad_mixed = tie((up_z, gate_x, middle, grad_mixed))
+    (gate_x, middle, mlp_full), up_z = close((gate_x, middle, mlp_full), up_z)
     up_x = send_seq(up_z, 1)
     normed_mid, inverse_mid = normalize(middle)
     lifted = join(normed_mid.astype(BF16), "fy", 0)
     gate_full = assemble(gate_z, gate_x)
     up_x, lifted, gate_full = tie((up_x, lifted, gate_full))
-    lifted = core_rows(lifted)
+    lifted, cot = core_rows(lifted), core_rows(cot)
+    grad_mixed = cols_dot(cot, mlp_full)
     gate = cols_dot(lifted, gate_full)
     up_full = assemble(up_z, up_x)
     up = cols_dot(lifted, up_full)
+    gate, up = tie((gate, up))
     mixed = geglu(gate, up).astype(BF16)
 
     unused, gelu_back = jax.vjp(geglu, gate, up)
@@ -530,7 +536,7 @@
     gate_x = send_seq(gate_sent, 1)
     grad_middle = cotangent.astype(F32) + norm_back(grad_hat, normed_mid, inverse_mid)
     grad_attn = join(grad_middle.astype(BF16), "fy", 0)
-    mlp_got, gate_x, grad_attn, grad_up, attended = tie((mlp_got, gate_x, grad_attn, grad_up, attended))
+    (gate_x, grad_attn, attended), mlp_got = close((gate_x, grad_attn, attended), mlp_got)
     gate_got = z_spread(x_sum(gate_kept, gate_x))
     up_x = send_seq(up_sent, 1)
     grad_attn = core_rows(grad_attn)
@@ -549,54 +555,57 @@
     grad_kv = jnp.concatenate([grad_k, grad_v], axis=1)
     attn_g = rows_dot(attended, grad_attn).astype(BF16)
     attn_g = attn_g.reshape(seqs // 4, 2, 2, shard, D).transpose(1, 2, 0, 3, 4)
+    attn_g = trade(attn_g, "core", 1)
     part_out = jnp.dot(mixed, mlp_full, preferred_element_type=F32)
-    gate_got, up_x, grad_kv, attn_g, part_out = tie((gate_got, up_x, grad_kv, attn_g, part_out))
+    (up_x, grad_kv, attn_g, part_out), gate_got = close((up_x, grad_kv, attn_g, part_out), gate_got)
     up_got = z_spread(x_sum(up_kept, up_x))
     ahead = [(i, i + 1) for i in range(seqs - 1)]
     behind = [(i + 1, i) for i in range(seqs - 1)]
     low_edge = lax.ppermute(grad_kv[:HALF].astype(BF16), "seq", behind)
     high_edge = lax.ppermute(grad_kv[HALF + rows :].astype(BF16), "seq", ahead)
-    attn_g = trade(trade(attn_g, "core", 1), "fy", 0).reshape(seqs, shard, D)
-    attn_kept, attn_sent = split_rows(attn_g)
+    attn_g = trade(attn_g, "fy", 0).reshape(seqs, shard, D)
     middle_kv = grad_kv[HALF : HALF + rows]
     gap = jnp.zeros((rows - 2 * HALF, 2 * OWN), F32)
     edges = jnp.concatenate([high_edge.astype(F32), gap, low_edge.astype(F32)], axis=0)
     grad_packed = jnp.concatenate([grad_q, (middle_kv + edges).astype(BF16)], axis=1)
     qkv_kept, qkv_sent = split(rows_dot(grad_packed, hidden).astype(BF16))
-    attn_sent, qkv_sent, grad_packed = tie((attn_sent, qkv_sent, grad_packed))
+    (attn_g, qkv_sent, grad_packed), up_got = close((attn_g, qkv_sent, grad_packed), up_got)
     qkv_x = send_seq(qkv_sent, 1)
-    attn_x = send_seq(attn_sent, 1)
+    rest_g = turn_back([mlp_got, gate_got, up_got], WIDE).reshape(2, 2, shard, -1)
+    rest_g = trade(rest_g, "fy", 0)
+    attn_kept, attn_sent = split_rows(attn_g)
     part_hidden = jnp.dot(grad_packed, qkv_full, preferred_element_type=F32)
     parts = jnp.stack([part_hidden, part_out]).reshape(2, 2, 2, share, D)
-    parts = reduce_pair(parts, "core", 2)
-    up_got, qkv_x, attn_x, parts = tie((up_got, qkv_x, attn_x, parts))
+    qkv_x, rest_g, parts, attn_sent = tie((qkv_x, rest_g, parts, attn_sent))
     qkv_got = z_spread(x_sum(qkv_kept, qkv_x))
-    grad_attn_out = total_of(z_spread(x_sum(attn_kept, attn_x)))
-    grad_hidden, sum_out = reduce_pair(parts, "fy", 1)
-    output = middle + sum_out
-
-    def regroup_back(cells):
-        cells = cells.reshape(2, 2, shard, -1)
-        return trade(trade(cells, "fy", 0), "core", 1)
+    attn_x = send_seq(attn_sent, 1)
 
     def back_columns(cells, parts, width):
         cells = cells.reshape(2, 2, shard, parts, width).transpose(2, 3, 0, 1, 4)
         return cells.reshape(shard, parts * 2 * 2 * width).astype(F32)
 
-    rest_g = regroup_back(turn_back([mlp_got, gate_got, up_got], WIDE))
+    rest_g = trade(rest_g, "core", 1)
     raw_mlp = back_columns(rest_g[..., :OWN_FF], 1, OWN_FF)
     raw_in = back_columns(rest_g[..., OWN_FF : 3 * OWN_FF], 2, OWN_FF)
-    output, rest_g, raw_in, raw_mlp, qkv_got = tie((output, rest_g, raw_in, raw_mlp, qkv_got))
-    raw_qkv = back_columns(regroup_back(turn_back([qkv_got], 3 * OWN)), 3, OWN)
+    grad_w_in = raw_in * gain_m
+    grad_gain_mlp = jnp.sum(raw_in * w_in.astype(F32), axis=1)
+    grad_hidden, sum_out = reduce_pair(reduce_pair(parts, "core", 2), "fy", 1)
+    output = (middle + sum_out).astype(BF16)
     input_grad = grad_middle + norm_back(grad_hidden, normed, inverse)
+    attn_x, qkv_got, output, input_grad, raw_mlp, grad_w_in, grad_gain_mlp = tie(
+        (attn_x, qkv_got, output, input_grad, raw_mlp, grad_w_in, grad_gain_mlp)
+    )
+    attn_got = z_spread(x_sum(attn_kept, attn_x))
+    raw_qkv = turn_back([qkv_got], 3 * OWN).reshape(2, 2, shard, -1)
+    raw_qkv = back_columns(trade(trade(raw_qkv, "fy", 0), "core", 1), 3, OWN)
     grad_gain_attn = jnp.sum(raw_qkv * w_qkv.astype(F32), axis=1)
-    grad_gain_mlp = jnp.sum(raw_in * w_in.astype(F32), axis=1)
+    grad_attn_out = total_of(attn_got)
     return (
-        output.astype(BF16),
+        output,
         input_grad,
         raw_qkv * gain_a,
         grad_attn_out,
-        raw_in * gain_m,
+        grad_w_in,
         raw_mlp,
         grad_gain_attn,
         grad_gain_mlp,

time: 306 us -> 305 us (level)
  waiting for transfers between devices: 135 us -> 101 us
  starting transfers between devices: 86 us -> 106 us
  local copies, waits for them, and re-layouts: 17 us -> 25.6 us
  other arithmetic: 22.6 us -> 31.1 us
  matrix products: 20.4 us -> 15.7 us
    ppermute x40, starting transfers between devices: 60.1 us -> 82.4 us  [send_seq(): return lax.ppermute(cells, ALL, flat_pairs(lambda i: i ^ flip * GROUP))]
    ppermute x12, waiting for transfers between devices: 14.8 us -> 1.95 us  [trade(): got = lax.ppermute(sent, axis, [(0, 1), (1, 0)])]
    ppermute x8, waiting for transfers between devices: 16.7 us -> 5.68 us  [join(): got = lax.ppermute(cells, axis, [(0, 1), (1, 0)])]
    ppermute x6, waiting for transfers between devices: 16 us -> 5.56 us  [reduce_pair(): got = lax.ppermute(sent, axis, [(0, 1), (1, 0)])]
    dot_general x10, matrix products: 16 us -> 11.2 us  [contract(): lax.dot_general(left, right, ((dims[0], dims[1]), ((), ())), preferred_el...]
    convert_element_type x8, local copies, waits for them, and re-layouts: 7.6 us -> 12.2 us  [back_columns(): return cells.reshape(shard, parts * 2 * 2 * width).astype(F32)]
  transfers between devices with their start and end apart: 70 -> 70, of which waited for: 33 -> 24; matrix products, arithmetic and copies ran while one was open for 12% -> 17% of each run, Pallas kernels for 5% -> 6%
where the time goes in v6:
time: 305 us; the launch traced here: 301 us
  starting transfers between devices  106 us (35%)
  waiting for transfers between devices  101 us (33%)
  other arithmetic  31.1 us (10%)
  local copies, waits for them, and re-layouts  25.6 us (8%)
  Pallas kernels  18.8 us (6%)
  matrix products  15.7 us (5%)
    ppermute x40, waiting for transfers between devices, send_seq(): return lax.ppermute(cells, ALL, flat_pairs(lambda i: i ^ flip * GROUP))  84.4 us
    ppermute x40, starting transfers between devices, send_seq(): return lax.ppermute(cells, ALL, flat_pairs(lambda i: i ^ flip * GROUP))  82.4 us
    convert_element_type x8, local copies, waits for them, and re-layouts, back_columns(): return cells.reshape(shard, parts * 2 * 2 * width).astype(F32)  12.2 us
    ppermute x12, starting transfers between devices, trade(): got = lax.ppermute(sent, axis, [(0, 1), (1, 0)])  12 us
    dot_general x10, matrix products, contract(): lax.dot_general(left, right, ((dims[0], dims[1]), ((), ())), preferred_el...  11.2 us
    pallas_call x14, Pallas kernels, local_kernel(): pl.pallas_call(kernel, out_shape=outs, in_specs=[pl.BlockSpec(memory_spac...  10 us
    pallas_call x2, Pallas kernels, call_kernel(): pl.pallas_call(kernel, out_shape=outs, in_specs=[pl.BlockSpec(memory_spac...  8.8 us
  transfers between devices with their start and end apart: 70, of which 24 were waited for; matrix products, arithmetic and copies ran while one was open for 17% of the time, Pallas kernels for 6%

profile of v6, /device:TPU:0, one launch (start us, length us, event | category | flops | bytes accessed | tf_op | source)
XLA Modules:
  0.0 301.3 jit_solution(14400131358758299407)
XLA Ops:
  0.6 3.1 %collective-permute-start = (bf16[32,1024]{1,0:T(8,128)(2,1)}, bf16[32,1024]{1,0:T(8,128)(2,1)S(1)}, u32[]{:S(2)}, u32[]{:S(2)}) collective-permute-start(bf16[32,1024]{1,0:T(8,128)(2,1)} %param.13), channel_id=1, source_target_pairs={{0,8},{1,9},{2,10},{3,11},{4,12},{5,13},{6,14},{7,15},{8,0},{9,1},... | collective-permute-start | bytes 196616 | tf_op jit(solution)/shard_map/ppermute | solution.py:33
  3.7 2.6 collective-permute-start.1
  8.6 1.8 collective-permute-start.3
  16.0 4.2 %collective-permute-start.4 = (bf16[2,1,32,768]{3,2,1,0:T(8,128)(2,1)S(1)}, bf16[2,1,32,768]{3,2,1,0:T(8,128)(2,1)S(1)}, u32[]{:S(2)}, u32[]{:S(2)}) collective-permute-start(bf16[2,1,32,768]{3,2,1,0:T(8,128)(2,1)S(1)} %fusion.43), channel_id=1, source_target_pairs={{0,1},{1,0},{2,3},{3,2},{4,5},{5,4},{6,7},{7,6},{8,9},{9,8},{10,11... | collective-permute-start | bytes 294920 | tf_op jit(solution)/shard_map/ppermute | solution.py:40
  23.2 8.4 %collective-permute-start.12 = (bf16[768,128]{1,0:T(8,128)(2,1)S(1)}, bf16[768,128]{1,0:T(8,128)(2,1)S(1)}, u32[]{:S(2)}, u32[]{:S(2)}) collective-permute-start(bf16[768,128]{1,0:T(8,128)(2,1)S(1)} %shard_map.152), channel_id=1, source_target_pairs={{0,8},{1,9},{2,10},{3,11},{4,12},{5,13},{6,14},{7,15},{8,0},{9,1},... | collective-permute-start | bytes 589832 | tf_op jit(solution)/shard_map/ppermute | solution.py:33
  31.6 3.5 %collective-permute-start.13 = (bf16[768,128]{1,0:T(8,128)(2,1)S(1)}, bf16[768,128]{1,0:T(8,128)(2,1)S(1)}, u32[]{:S(2)}, u32[]{:S(2)}) collective-permute-start(bf16[768,128]{1,0:T(8,128)(2,1)S(1)} %shard_map.152), channel_id=1, source_target_pairs={{0,16},{1,17},{2,18},{3,19},{4,20},{5,21},{6,22},{7,23},{8,24},{9,... | collective-permute-start | bytes 589832 | tf_op jit(solution)/shard_map/ppermute | solution.py:33
  35.2 3.5 %collective-permute-start.8 = (bf16[4,32,1024]{2,1,0:T(8,128)(2,1)S(1)}, bf16[4,32,1024]{2,1,0:T(8,128)(2,1)S(1)}, u32[]{:S(2)}, u32[]{:S(2)}) collective-permute-start(bf16[4,32,1024]{2,1,0:T(8,128)(2,1)S(1)} %pad_maximum_fusion.24.cells), channel_id=1, source_target_pairs={{0,4},{1,5},{2,6},{3,7},{4,0},{5,1},{6,2},{7,3},{8,12},{9,13},{10,... | collective-permute-start | bytes 786440 | tf_op jit(solution)/shard_map/ppermute | solution.py:33
  39.0 9.3 %collective-permute-done.13 = bf16[768,128]{1,0:T(8,128)(2,1)S(1)} collective-permute-done((bf16[768,128]{1,0:T(8,128)(2,1)S(1)}, bf16[768,128]{1,0:T(8,128)(2,1)S(1)}, u32[]{:S(2)}, u32[]{:S(2)}) %collective-permute-start.13) | collective-permute-done | bytes 196640 | tf_op jit(solution)/shard_map/ppermute | solution.py:33
  52.6 2.7 collective-permute-start.18
  57.8 3.2 %collective-permute-start.15 = (bf16[4,768,128]{2,1,0:T(8,128)(2,1)S(1)}, bf16[4,768,128]{2,1,0:T(8,128)(2,1)S(1)}, u32[]{:S(2)}, u32[]{:S(2)}) collective-permute-start(bf16[4,768,128]{2,1,0:T(8,128)(2,1)S(1)} %pad_maximum_fusion.8.cells), channel_id=1, source_target_pairs={{0,4},{1,5},{2,6},{3,7},{4,0},{5,1},{6,2},{7,3},{8,12},{9,13},{10,... | collective-permute-start | bytes 2359304 | tf_op jit(solution)/shard_map/ppermute | solution.py:33
  63.3 5.7 %collective-permute-done.19 = bf16[656,128]{1,0:T(8,128)(2,1)} collective-permute-done((bf16[656,128]{1,0:T(8,128)(2,1)S(1)}, bf16[656,128]{1,0:T(8,128)(2,1)}, u32[]{:S(2)}, u32[]{:S(2)}) %collective-permute-start.19) | collective-permute-done | bytes 167968 | tf_op jit(solution)/shard_map/ppermute | solution.py:33
  70.3 6.9 %collective-permute-done.15.got = bf16[4,768,128]{2,1,0:T(8,128)(2,1)S(1)} collective-permute-done((bf16[4,768,128]{2,1,0:T(8,128)(2,1)S(1)}, bf16[4,768,128]{2,1,0:T(8,128)(2,1)S(1)}, u32[]{:S(2)}, u32[]{:S(2)}) %collective-permute-start.15) | collective-permute-done | bytes 786464 | tf_op jit(solution)/shard_map/ppermute | solution.py:33
  78.7 2.4 collective-permute-start.24
  82.5 1.6 collective-permute-start.22
  86.2 1.8 collective-permute-start.21
  89.3 3.8 %shard_map.156 = (bf16[512,256]{1,0:T(8,128)(2,1)S(1)}, bf16[640,256]{1,0:T(8,128)(2,1)S(1)}, bf16[640,256]{1,0:T(8,128)(2,1)S(1)}, bf16[512,256]{1,0:T(8,128)(2,1)S(1)}) custom-call(f32[640,768]{1,0:T(8,128)S(1)} %fusion.55.packed, f32[640,128]{1,0:T(8,128)S(1)} %get-tuple-element.330.cosine, f32[640,128]{1,0:T(8,128)S(1)} %get-tuple-element.329.sine, ...), custom_call_target="tpu_custom_call" | custom-call | flops 268435456 | bytes 3805696 | tf_op jit(solution)/shard_map/pallas_call | solution.py:401
  96.0 3.9 %collective-permute-done.21.got = bf16[4,656,128]{2,1,0:T(8,128)(2,1)S(1)} collective-permute-done((bf16[4,656,128]{2,1,0:T(8,128)(2,1)S(1)}, bf16[4,656,128]{2,1,0:T(8,128)(2,1)S(1)}, u32[]{:S(2)}, u32[]{:S(2)}) %collective-permute-start.21) | collective-permute-done | bytes 671776 | tf_op jit(solution)/shard_map/ppermute | solution.py:33
  100.1 3.0 collective-permute-start.30
  107.8 2.2 collective-permute-done.29
  110.0 5.4 %collective-permute-done.30 = bf16[656,128]{1,0:T(8,128)(2,1)S(1)} collective-permute-done((bf16[656,128]{1,0:T(8,128)(2,1)S(1)}, bf16[656,128]{1,0:T(8,128)(2,1)S(1)}, u32[]{:S(2)}, u32[]{:S(2)}) %collective-permute-start.30) | collective-permute-done | bytes 167968 | tf_op jit(solution)/shard_map/ppermute | solution.py:33
  116.4 4.7 %collective-permute-done.26.got = bf16[4,656,128]{2,1,0:T(8,128)(2,1)S(1)} collective-permute-done((bf16[4,656,128]{2,1,0:T(8,128)(2,1)S(1)}, bf16[4,656,128]{2,1,0:T(8,128)(2,1)S(1)}, u32[]{:S(2)}, u32[]{:S(2)}) %collective-permute-start.26) | collective-permute-done | bytes 671776 | tf_op jit(solution)/shard_map/ppermute | solution.py:33
  124.4 1.5 collective-permute-start.32
  128.8 5.1 %collective-permute-done.33 = bf16[128,1024]{1,0:T(8,128)(2,1)S(1)} collective-permute-done((bf16[128,1024]{1,0:T(8,128)(2,1)S(1)}, bf16[128,1024]{1,0:T(8,128)(2,1)S(1)}, u32[]{:S(2)}, u32[]{:S(2)}) %collective-permute-start.33) | collective-permute-done | bytes 262176 | tf_op jit(solution)/shard_map/ppermute | solution.py:47
  134.5 5.7 %collective-permute-done.32.got = bf16[4,656,128]{2,1,0:T(8,128)(2,1)S(1)} collective-permute-done((bf16[4,656,128]{2,1,0:T(8,128)(2,1)S(1)}, bf16[4,656,128]{2,1,0:T(8,128)(2,1)S(1)}, u32[]{:S(2)}, u32[]{:S(2)}) %collective-permute-start.32) | collective-permute-done | bytes 671776 | tf_op jit(solution)/shard_map/ppermute | solution.py:33
  145.2 3.6 %multiply_convert_fusion = (bf16[512,656]{0,1:T(8,128)(2,1)S(1)}, f32[512,656]{0,1:T(8,128)S(1)}, f32[512,656]{0,1:T(8,128)S(1)}) fusion(f32[512,656]{0,1:T(8,128)S(1)} %fusion.57, bf16[512,1024]{1,0:T(8,128)(2,1)S(1)} %bitcast.261, bf16[656,1024]{1,0:T(8,128)(2,1)S(1)} %copy-done.1), kind=kOutput, calls=%fused_computation.15 | convolution fusion | flops 710033408 | bytes 7094272 | tf_op jit(solution)/shard_map/dot_general | solution.py:297
  156.0 1.5 collective-permute-start.36
  160.2 5.6 %collective-permute-done.38 = bf16[128,1024]{1,0:T(8,128)(2,1)S(1)} collective-permute-done((bf16[128,1024]{1,0:T(8,128)(2,1)S(1)}, bf16[128,1024]{1,0:T(8,128)(2,1)S(1)}, u32[]{:S(2)}, u32[]{:S(2)}) %collective-permute-start.38) | collective-permute-done | bytes 262176 | tf_op jit(solution)/shard_map/ppermute | solution.py:56
  165.8 7.2 %collective-permute-done.36 = bf16[4,656,128]{2,1,0:T(8,128)(2,1)S(1)} collective-permute-done((bf16[4,656,128]{2,1,0:T(8,128)(2,1)S(1)}, bf16[4,656,128]{2,1,0:T(8,128)(2,1)S(1)}, u32[]{:S(2)}, u32[]{:S(2)}) %collective-permute-start.36) | collective-permute-done | bytes 671776 | tf_op jit(solution)/shard_map/ppermute | solution.py:33
  176.7 3.0 collective-permute-start.43
  181.8 9.0 %collective-permute-done.40 = bf16[4,656,128]{2,1,0:T(8,128)(2,1)S(1)} collective-permute-done((bf16[4,656,128]{2,1,0:T(8,128)(2,1)S(1)}, bf16[4,656,128]{2,1,0:T(8,128)(2,1)S(1)}, u32[]{:S(2)}, u32[]{:S(2)}) %collective-permute-start.40) | collective-permute-done | bytes 671776 | tf_op jit(solution)/shard_map/ppermute | solution.py:33
  193.7 2.2 collective-permute-start.47
  200.4 5.0 %shard_map.163 = (bf16[512,256]{1,0:T(8,128)(2,1)S(1)}, f32[640,256]{1,0:T(8,128)S(1)}, f32[640,256]{1,0:T(8,128)S(1)}) custom-call(bf16[512,256]{1,0:T(8,128)(2,1)S(1)} %copy-done.17, bf16[640,256]{1,0:T(8,128)(2,1)S(1)} %copy-done.13, bf16[640,256]{1,0:T(8,128)(2,1)S(1)} %copy-done.15, bf16[512,256]{1,0:T(8,128)(2,1)S(1)} %convolution_convert_fusion.5.grad, ...), custom_call_target="tpu_custom_call" | custom-call | flops 805306368 | bytes 3412480 | tf_op jit(solution)/shard_map/pallas_call | solution.py:401
  205.7 4.4 %collective-permute-done.39 = bf16[4,656,128]{2,1,0:T(8,128)(2,1)S(1)} collective-permute-done((bf16[4,656,128]{2,1,0:T(8,128)(2,1)S(1)}, bf16[4,656,128]{2,1,0:T(8,128)(2,1)S(1)}, u32[]{:S(2)}, u32[]{:S(2)}) %collective-permute-start.39) | collective-permute-done | bytes 671776 | tf_op jit(solution)/shard_map/ppermute | solution.py:33
  211.3 3.3 %collective-permute-start.53 = (bf16[656,128]{1,0:T(8,128)(2,1)S(1)}, bf16[656,128]{1,0:T(8,128)(2,1)S(1)}, u32[]{:S(2)}, u32[]{:S(2)}) collective-permute-start(bf16[656,128]{1,0:T(8,128)(2,1)S(1)} %get-tuple-element.292), channel_id=1, source_target_pairs={{0,8},{1,9},{2,10},{3,11},{4,12},{5,13},{6,14},{7,15},{8,0},{9,1},... | collective-permute-start | bytes 503816 | tf_op jit(solution)/shard_map/ppermute | solution.py:33
  217.1 3.4 %collective-permute-start.51 = (bf16[64,512]{1,0:T(8,128)(2,1)S(1)}, bf16[64,512]{1,0:T(8,128)(2,1)S(1)}, u32[]{:S(2)}, u32[]{:S(2)}) collective-permute-start(bf16[64,512]{1,0:T(8,128)(2,1)S(1)} %get-tuple-element.302), channel_id=1, source_target_pairs={{0,4},{4,8},{8,12},{12,16},{16,20},{20,24},{24,28},{1,5},{5,9},{9,... | collective-permute-start | bytes 196616 | tf_op jit(solution)/shard_map/ppermute | solution.py:565
  223.8 3.0 collective-permute-done.52
  232.5 4.6 %collective-permute-start.56 = (bf16[4,768,128]{2,1,0:T(8,128)(2,1)S(1)}, bf16[4,768,128]{2,1,0:T(8,128)(2,1)S(1)}, u32[]{:S(2)}, u32[]{:S(2)}) collective-permute-start(bf16[4,768,128]{2,1,0:T(8,128)(2,1)S(1)} %get-tuple-element.215), channel_id=1, source_target_pairs={{0,4},{1,5},{2,6},{3,7},{4,0},{5,1},{6,2},{7,3},{8,12},{9,13},{10,... | collective-permute-start | bytes 2359304 | tf_op jit(solution)/shard_map/ppermute | solution.py:33
  238.4 13.3 %collective-permute-done.56 = bf16[4,768,128]{2,1,0:T(8,128)(2,1)S(1)} collective-permute-done((bf16[4,768,128]{2,1,0:T(8,128)(2,1)S(1)}, bf16[4,768,128]{2,1,0:T(8,128)(2,1)S(1)}, u32[]{:S(2)}, u32[]{:S(2)}) %collective-permute-start.56) | collective-permute-done | bytes 786464 | tf_op jit(solution)/shard_map/ppermute | solution.py:33
  253.6 7.5 %collective-permute-start.59 = (bf16[768,128]{1,0:T(8,128)(2,1)}, bf16[768,128]{1,0:T(8,128)(2,1)S(1)}, u32[]{:S(2)}, u32[]{:S(2)}) collective-permute-start(bf16[768,128]{1,0:T(8,128)(2,1)} %get-tuple-element.272), channel_id=1, source_target_pairs={{0,8},{1,9},{2,10},{3,11},{4,12},{5,13},{6,14},{7,15},{8,0},{9,1},... | collective-permute-start | bytes 589832 | tf_op jit(solution)/shard_map/ppermute | solution.py:33
  261.0 2.5 collective-permute-start.60
  268.2 2.7 reshape.236
  271.0 2.6 copy.95
  273.6 2.8 reshape.232
  278.4 2.2 reshape.231
  280.6 2.8 fusion.10
  290.0 1.9 collective-permute-start.68
  293.5 3.0 collective-permute-done.68
  296.5 1.5 collective-permute-done.69
  (377 shorter events, 104.4 us)
Async XLA Ops:
  0.6 14.8 %collective-permute-start = (bf16[32,1024]{1,0:T(8,128)(2,1)}, bf16[32,1024]{1,0:T(8,128)(2,1)S(1)}, u32[]{:S(2)}, u32[]{:S(2)}) collective-permute-start(bf16[32,1024]{1,0:T(8,128)(2,1)} %param.13), channel_id=1, source_target_pairs={{0,8},{1,9},{2,10},{3,11},{4,12},{5,13},{6,14},{7,15},{8,0},{9,1},... | collective-permute-start | bytes 196616 | tf_op jit(solution)/shard_map/ppermute | solution.py:33
  3.7 12.2 %collective-permute-start.1 = (bf16[32,1024]{1,0:T(8,128)(2,1)}, bf16[32,1024]{1,0:T(8,128)(2,1)S(1)}, u32[]{:S(2)}, u32[]{:S(2)}) collective-permute-start(bf16[32,1024]{1,0:T(8,128)(2,1)} %param.13), channel_id=1, source_target_pairs={{0,16},{1,17},{2,18},{3,19},{4,20},{5,21},{6,22},{7,23},{8,24},{9,... | collective-permute-start | bytes 196616 | tf_op jit(solution)/shard_map/ppermute | solution.py:33
  6.3 13.8 %collective-permute-start.2 = (bf16[32,1024]{1,0:T(8,128)(2,1)}, bf16[32,1024]{1,0:T(8,128)(2,1)S(1)}, u32[]{:S(2)}, u32[]{:S(2)}) collective-permute-start(bf16[32,1024]{1,0:T(8,128)(2,1)} %param.13), channel_id=1, source_target_pairs={{0,24},{1,25},{2,26},{3,27},{4,28},{5,29},{6,30},{7,31},{8,16},{9,... | collective-permute-start | bytes 196616 | tf_op jit(solution)/shard_map/ppermute | solution.py:33
  10.4 9.8 %collective-permute-start.6 = (bf16[64,1024]{1,0:T(8,128)(2,1)S(1)}, bf16[64,1024]{1,0:T(8,128)(2,1)S(1)}, u32[]{:S(2)}, u32[]{:S(2)}) collective-permute-start(bf16[64,1024]{1,0:T(8,128)(2,1)S(1)} %get-tuple-element.328), channel_id=1, source_target_pairs={{3,4},{7,8},{11,12},{15,16},{19,20},{23,24},{27,28}} | collective-permute-start | bytes 393224 | tf_op jit(solution)/shard_map/ppermute | solution.py:441
  22.9 12.2 %collective-permute-start.9 = (bf16[192,1024]{1,0:T(8,128)(2,1)S(1)}, bf16[192,1024]{1,0:T(8,128)(2,1)S(1)}, u32[]{:S(2)}, u32[]{:S(2)}) collective-permute-start(bf16[192,1024]{1,0:T(8,128)(2,1)S(1)} %pad_maximum_fusion.22), channel_id=1, source_target_pairs={{0,2},{2,0},{1,3},{3,1},{4,6},{6,4},{5,7},{7,5},{8,10},{10,8},{9,1... | collective-permute-start | bytes 1179656 | tf_op jit(solution)/shard_map/ppermute | solution.py:47
  23.2 15.7 %collective-permute-start.12 = (bf16[768,128]{1,0:T(8,128)(2,1)S(1)}, bf16[768,128]{1,0:T(8,128)(2,1)S(1)}, u32[]{:S(2)}, u32[]{:S(2)}) collective-permute-start(bf16[768,128]{1,0:T(8,128)(2,1)S(1)} %shard_map.152), channel_id=1, source_target_pairs={{0,8},{1,9},{2,10},{3,11},{4,12},{5,13},{6,14},{7,15},{8,0},{9,1},... | collective-permute-start | bytes 589832 | tf_op jit(solution)/shard_map/ppermute | solution.py:33
  31.6 16.7 %collective-permute-start.13 = (bf16[768,128]{1,0:T(8,128)(2,1)S(1)}, bf16[768,128]{1,0:T(8,128)(2,1)S(1)}, u32[]{:S(2)}, u32[]{:S(2)}) collective-permute-start(bf16[768,128]{1,0:T(8,128)(2,1)S(1)} %shard_map.152), channel_id=1, source_target_pairs={{0,16},{1,17},{2,18},{3,19},{4,20},{5,21},{6,22},{7,23},{8,24},{9,... | collective-permute-start | bytes 589832 | tf_op jit(solution)/shard_map/ppermute | solution.py:33
  35.1 13.3 %collective-permute-start.14 = (bf16[768,128]{1,0:T(8,128)(2,1)S(1)}, bf16[768,128]{1,0:T(8,128)(2,1)S(1)}, u32[]{:S(2)}, u32[]{:S(2)}) collective-permute-start(bf16[768,128]{1,0:T(8,128)(2,1)S(1)} %shard_map.152), channel_id=1, source_target_pairs={{0,24},{1,25},{2,26},{3,27},{4,28},{5,29},{6,30},{7,31},{8,16},{9,... | collective-permute-start | bytes 589832 | tf_op jit(solution)/shard_map/ppermute | solution.py:33
  35.1 13.3 %collective-permute-start.11 = (bf16[2,1,32,2048]{3,2,1,0:T(8,128)(2,1)S(1)}, bf16[2,1,32,2048]{3,2,1,0:T(8,128)(2,1)S(1)}, u32[]{:S(2)}, u32[]{:S(2)}) collective-permute-start(bf16[2,1,32,2048]{3,2,1,0:T(8,128)(2,1)S(1)} %constant_dynamic-slice_fusion.6), channel_id=1, source_target_pairs={{0,1},{1,0},{2,3},{3,2},{4,5},{5,4},{6,7},{7,6},{8,9},{9,8},{10,11... | collective-permute-start | bytes 786440 | tf_op jit(solution)/shard_map/ppermute | solution.py:40
  35.2 16.3 %collective-permute-start.8 = (bf16[4,32,1024]{2,1,0:T(8,128)(2,1)S(1)}, bf16[4,32,1024]{2,1,0:T(8,128)(2,1)S(1)}, u32[]{:S(2)}, u32[]{:S(2)}) collective-permute-start(bf16[4,32,1024]{2,1,0:T(8,128)(2,1)S(1)} %pad_maximum_fusion.24.cells), channel_id=1, source_target_pairs={{0,4},{1,5},{2,6},{3,7},{4,0},{5,1},{6,2},{7,3},{8,12},{9,13},{10,... | collective-permute-start | bytes 786440 | tf_op jit(solution)/shard_map/ppermute | solution.py:33
  38.9 10.5 %collective-permute-start.10 = (bf16[2,192,1024]{2,1,0:T(8,128)(2,1)S(1)}, bf16[2,192,1024]{2,1,0:T(8,128)(2,1)S(1)}, u32[]{:S(2)}, u32[]{:S(2)}) collective-permute-start(bf16[2,192,1024]{2,1,0:T(8,128)(2,1)S(1)} %pad_maximum_fusion.7), channel_id=1, source_target_pairs={{0,1},{1,0},{2,3},{3,2},{4,5},{5,4},{6,7},{7,6},{8,9},{9,8},{10,11... | collective-permute-start | bytes 2359304 | tf_op jit(solution)/shard_map/ppermute | solution.py:47
  52.6 10.7 %collective-permute-start.18 = (bf16[656,128]{1,0:T(8,128)(2,1)S(1)}, bf16[656,128]{1,0:T(8,128)(2,1)}, u32[]{:S(2)}, u32[]{:S(2)}) collective-permute-start(bf16[656,128]{1,0:T(8,128)(2,1)S(1)} %get-tuple-element.148), channel_id=1, source_target_pairs={{0,8},{1,9},{2,10},{3,11},{4,12},{5,13},{6,14},{7,15},{8,0},{9,1},... | collective-permute-start | bytes 503816 | tf_op jit(solution)/shard_map/ppermute | solution.py:33
  55.4 13.7 %collective-permute-start.19 = (bf16[656,128]{1,0:T(8,128)(2,1)S(1)}, bf16[656,128]{1,0:T(8,128)(2,1)}, u32[]{:S(2)}, u32[]{:S(2)}) collective-permute-start(bf16[656,128]{1,0:T(8,128)(2,1)S(1)} %get-tuple-element.148), channel_id=1, source_target_pairs={{0,16},{1,17},{2,18},{3,19},{4,20},{5,21},{6,22},{7,23},{8,24},{9,... | collective-permute-start | bytes 503816 | tf_op jit(solution)/shard_map/ppermute | solution.py:33
  56.4 12.6 %collective-permute-start.20 = (bf16[656,128]{1,0:T(8,128)(2,1)S(1)}, bf16[656,128]{1,0:T(8,128)(2,1)}, u32[]{:S(2)}, u32[]{:S(2)}) collective-permute-start(bf16[656,128]{1,0:T(8,128)(2,1)S(1)} %get-tuple-element.148), channel_id=1, source_target_pairs={{0,24},{1,25},{2,26},{3,27},{4,28},{5,29},{6,30},{7,31},{8,16},{9,... | collective-permute-start | bytes 503816 | tf_op jit(solution)/shard_map/ppermute | solution.py:33
  57.8 19.4 %collective-permute-start.15 = (bf16[4,768,128]{2,1,0:T(8,128)(2,1)S(1)}, bf16[4,768,128]{2,1,0:T(8,128)(2,1)S(1)}, u32[]{:S(2)}, u32[]{:S(2)}) collective-permute-start(bf16[4,768,128]{2,1,0:T(8,128)(2,1)S(1)} %pad_maximum_fusion.8.cells), channel_id=1, source_target_pairs={{0,4},{1,5},{2,6},{3,7},{4,0},{5,1},{6,2},{7,3},{8,12},{9,13},{10,... | collective-permute-start | bytes 2359304 | tf_op jit(solution)/shard_map/ppermute | solution.py:33
  61.1 9.1 %collective-permute-start.17 = (bf16[2,1,2,32,1024]{4,3,1,0,2:T(8,128)(2,1)S(1)}, bf16[2,1,2,32,1024]{4,3,1,0,2:T(8,128)(2,1)S(1)}, u32[]{:S(2)}, u32[]{:S(2)}) collective-permute-start(bf16[2,1,2,32,1024]{4,3,1,0,2:T(8,128)(2,1)S(1)} %fusion.37), channel_id=1, source_target_pairs={{0,1},{1,0},{2,3},{3,2},{4,5},{5,4},{6,7},{7,6},{8,9},{9,8},{10,11... | collective-permute-start | bytes 786440 | tf_op jit(solution)/shard_map/ppermute | solution.py:40
  78.1 15.9 %collective-permute-start.23 = (bf16[656,128]{1,0:T(8,128)(2,1)}, bf16[656,128]{1,0:T(8,128)(2,1)S(1)}, u32[]{:S(2)}, u32[]{:S(2)}) collective-permute-start(bf16[656,128]{1,0:T(8,128)(2,1)} %get-tuple-element.160), channel_id=1, source_target_pairs={{0,8},{1,9},{2,10},{3,11},{4,12},{5,13},{6,14},{7,15},{8,0},{9,1},... | collective-permute-start | bytes 503816 | tf_op jit(solution)/shard_map/ppermute | solution.py:33
  78.7 15.3 %collective-permute-start.24 = (bf16[656,128]{1,0:T(8,128)(2,1)}, bf16[656,128]{1,0:T(8,128)(2,1)S(1)}, u32[]{:S(2)}, u32[]{:S(2)}) collective-permute-start(bf16[656,128]{1,0:T(8,128)(2,1)} %get-tuple-element.160), channel_id=1, source_target_pairs={{0,16},{1,17},{2,18},{3,19},{4,20},{5,21},{6,22},{7,23},{8,24},{9,... | collective-permute-start | bytes 503816 | tf_op jit(solution)/shard_map/ppermute | solution.py:33
  81.1 12.9 %collective-permute-start.25 = (bf16[656,128]{1,0:T(8,128)(2,1)}, bf16[656,128]{1,0:T(8,128)(2,1)S(1)}, u32[]{:S(2)}, u32[]{:S(2)}) collective-permute-start(bf16[656,128]{1,0:T(8,128)(2,1)} %get-tuple-element.160), channel_id=1, source_target_pairs={{0,24},{1,25},{2,26},{3,27},{4,28},{5,29},{6,30},{7,31},{8,16},{9,... | collective-permute-start | bytes 503816 | tf_op jit(solution)/shard_map/ppermute | solution.py:33
  82.5 12.5 %collective-permute-start.22 = (bf16[128,1024]{1,0:T(8,128)(2,1)S(1)}, bf16[128,1024]{1,0:T(8,128)(2,1)S(1)}, u32[]{:S(2)}, u32[]{:S(2)}) collective-permute-start(bf16[128,1024]{1,0:T(8,128)(2,1)S(1)} %copy-done.33), channel_id=1, source_target_pairs={{0,2},{2,0},{1,3},{3,1},{4,6},{6,4},{5,7},{7,5},{8,10},{10,8},{9,1... | collective-permute-start | bytes 786440 | tf_op jit(solution)/shard_map/ppermute | solution.py:47
  86.2 13.7 %collective-permute-start.21 = (bf16[4,656,128]{2,1,0:T(8,128)(2,1)S(1)}, bf16[4,656,128]{2,1,0:T(8,128)(2,1)S(1)}, u32[]{:S(2)}, u32[]{:S(2)}) collective-permute-start(bf16[4,656,128]{2,1,0:T(8,128)(2,1)S(1)} %pad_maximum_fusion.10.cells), channel_id=1, source_target_pairs={{0,4},{1,5},{2,6},{3,7},{4,0},{5,1},{6,2},{7,3},{8,12},{9,13},{10,... | collective-permute-start | bytes 2015240 | tf_op jit(solution)/shard_map/ppermute | solution.py:33
  100.1 9.9 %collective-permute-start.29 = (bf16[656,128]{1,0:T(8,128)(2,1)S(1)}, bf16[656,128]{1,0:T(8,128)(2,1)S(1)}, u32[]{:S(2)}, u32[]{:S(2)}) collective-permute-start(bf16[656,128]{1,0:T(8,128)(2,1)S(1)} %copy-done.11), channel_id=1, source_target_pairs={{0,8},{1,9},{2,10},{3,11},{4,12},{5,13},{6,14},{7,15},{8,0},{9,1},... | collective-permute-start | bytes 503816 | tf_op jit(solution)/shard_map/ppermute | solution.py:33
  100.1 15.3 %collective-permute-start.30 = (bf16[656,128]{1,0:T(8,128)(2,1)S(1)}, bf16[656,128]{1,0:T(8,128)(2,1)S(1)}, u32[]{:S(2)}, u32[]{:S(2)}) collective-permute-start(bf16[656,128]{1,0:T(8,128)(2,1)S(1)} %copy-done.11), channel_id=1, source_target_pairs={{0,16},{1,17},{2,18},{3,19},{4,20},{5,21},{6,22},{7,23},{8,24},{9,... | collective-permute-start | bytes 503816 | tf_op jit(solution)/shard_map/ppermute | solution.py:33
  103.1 12.3 %collective-permute-start.31 = (bf16[656,128]{1,0:T(8,128)(2,1)S(1)}, bf16[656,128]{1,0:T(8,128)(2,1)S(1)}, u32[]{:S(2)}, u32[]{:S(2)}) collective-permute-start(bf16[656,128]{1,0:T(8,128)(2,1)S(1)} %copy-done.11), channel_id=1, source_target_pairs={{0,24},{1,25},{2,26},{3,27},{4,28},{5,29},{6,30},{7,31},{8,16},{9,... | collective-permute-start | bytes 503816 | tf_op jit(solution)/shard_map/ppermute | solution.py:33
  104.5 16.6 %collective-permute-start.26 = (bf16[4,656,128]{2,1,0:T(8,128)(2,1)S(1)}, bf16[4,656,128]{2,1,0:T(8,128)(2,1)S(1)}, u32[]{:S(2)}, u32[]{:S(2)}) collective-permute-start(bf16[4,656,128]{2,1,0:T(8,128)(2,1)S(1)} %pad_maximum_fusion.11.cells), channel_id=1, source_target_pairs={{0,4},{1,5},{2,6},{3,7},{4,0},{5,1},{6,2},{7,3},{8,12},{9,13},{10,... | collective-permute-start | bytes 2015240 | tf_op jit(solution)/shard_map/ppermute | solution.py:33
  106.2 9.4 %collective-permute-start.28 = (bf16[128,1024]{1,0:T(8,128)(2,1)S(1)}, bf16[128,1024]{1,0:T(8,128)(2,1)S(1)}, u32[]{:S(2)}, u32[]{:S(2)}) collective-permute-start(bf16[128,1024]{1,0:T(8,128)(2,1)S(1)} %fusion.35), channel_id=1, source_target_pairs={{0,2},{2,0},{1,3},{3,1},{4,6},{6,4},{5,7},{7,5},{8,10},{10,8},{9,1... | collective-permute-start | bytes 786440 | tf_op jit(solution)/shard_map/ppermute | solution.py:56
  124.4 15.7 %collective-permute-start.32 = (bf16[4,656,128]{2,1,0:T(8,128)(2,1)S(1)}, bf16[4,656,128]{2,1,0:T(8,128)(2,1)S(1)}, u32[]{:S(2)}, u32[]{:S(2)}) collective-permute-start(bf16[4,656,128]{2,1,0:T(8,128)(2,1)S(1)} %pad_maximum_fusion.12.cells), channel_id=1, source_target_pairs={{0,4},{1,5},{2,6},{3,7},{4,0},{5,1},{6,2},{7,3},{8,12},{9,13},{10,... | collective-permute-start | bytes 2015240 | tf_op jit(solution)/shard_map/ppermute | solution.py:33
  127.8 12.4 %collective-permute-start.35 = (bf16[2,128,1024]{2,1,0:T(8,128)(2,1)}, bf16[2,128,1024]{2,1,0:T(8,128)(2,1)S(1)}, u32[]{:S(2)}, u32[]{:S(2)}) collective-permute-start(bf16[2,128,1024]{2,1,0:T(8,128)(2,1)} %pad_maximum_fusion.16), channel_id=1, source_target_pairs={{0,1},{1,0},{2,3},{3,2},{4,5},{5,4},{6,7},{7,6},{8,9},{9,8},{10,11... | collective-permute-start | bytes 1572872 | tf_op jit(solution)/shard_map/ppermute | solution.py:47
  156.0 17.1 %collective-permute-start.36 = (bf16[4,656,128]{2,1,0:T(8,128)(2,1)S(1)}, bf16[4,656,128]{2,1,0:T(8,128)(2,1)S(1)}, u32[]{:S(2)}, u32[]{:S(2)}) collective-permute-start(bf16[4,656,128]{2,1,0:T(8,128)(2,1)S(1)} %get-tuple-element.180), channel_id=1, source_target_pairs={{0,4},{1,5},{2,6},{3,7},{4,0},{5,1},{6,2},{7,3},{8,12},{9,13},{10,... | collective-permute-start | bytes 2015240 | tf_op jit(solution)/shard_map/ppermute | solution.py:33
  174.9 15.9 %collective-permute-start.40 = (bf16[4,656,128]{2,1,0:T(8,128)(2,1)S(1)}, bf16[4,656,128]{2,1,0:T(8,128)(2,1)S(1)}, u32[]{:S(2)}, u32[]{:S(2)}) collective-permute-start(bf16[4,656,128]{2,1,0:T(8,128)(2,1)S(1)} %get-tuple-element.189), channel_id=1, source_target_pairs={{0,4},{1,5},{2,6},{3,7},{4,0},{5,1},{6,2},{7,3},{8,12},{9,13},{10,... | collective-permute-start | bytes 2015240 | tf_op jit(solution)/shard_map/ppermute | solution.py:33
  176.6 14.2 %collective-permute-start.42 = (bf16[656,128]{1,0:T(8,128)(2,1)S(1)}, bf16[656,128]{1,0:T(8,128)(2,1)S(1)}, u32[]{:S(2)}, u32[]{:S(2)}) collective-permute-start(bf16[656,128]{1,0:T(8,128)(2,1)S(1)} %get-tuple-element.300), channel_id=1, source_target_pairs={{0,8},{1,9},{2,10},{3,11},{4,12},{5,13},{6,14},{7,15},{8,0},{9,1},... | collective-permute-start | bytes 503816 | tf_op jit(solution)/shard_map/ppermute | solution.py:33
  176.7 14.8 %collective-permute-start.43 = (bf16[656,128]{1,0:T(8,128)(2,1)S(1)}, bf16[656,128]{1,0:T(8,128)(2,1)S(1)}, u32[]{:S(2)}, u32[]{:S(2)}) collective-permute-start(bf16[656,128]{1,0:T(8,128)(2,1)S(1)} %get-tuple-element.299), channel_id=1, source_target_pairs={{0,16},{1,17},{2,18},{3,19},{4,20},{5,21},{6,22},{7,23},{8,24},{9,... | collective-permute-start | bytes 503816 | tf_op jit(solution)/shard_map/ppermute | solution.py:33
  179.7 11.8 %collective-permute-start.44 = (bf16[656,128]{1,0:T(8,128)(2,1)S(1)}, bf16[656,128]{1,0:T(8,128)(2,1)S(1)}, u32[]{:S(2)}, u32[]{:S(2)}) collective-permute-start(bf16[656,128]{1,0:T(8,128)(2,1)S(1)} %get-tuple-element.298), channel_id=1, source_target_pairs={{0,24},{1,25},{2,26},{3,27},{4,28},{5,29},{6,30},{7,31},{8,16},{9,... | collective-permute-start | bytes 503816 | tf_op jit(solution)/shard_map/ppermute | solution.py:33
  192.5 17.6 %collective-permute-start.39 = (bf16[4,656,128]{2,1,0:T(8,128)(2,1)S(1)}, bf16[4,656,128]{2,1,0:T(8,128)(2,1)S(1)}, u32[]{:S(2)}, u32[]{:S(2)}) collective-permute-start(bf16[4,656,128]{2,1,0:T(8,128)(2,1)S(1)} %get-tuple-element.185), channel_id=1, source_target_pairs={{0,4},{1,5},{2,6},{3,7},{4,0},{5,1},{6,2},{7,3},{8,12},{9,13},{10,... | collective-permute-start | bytes 2015240 | tf_op jit(solution)/shard_map/ppermute | solution.py:33
  193.7 16.4 %collective-permute-start.47 = (bf16[656,128]{1,0:T(8,128)(2,1)S(1)}, bf16[656,128]{1,0:T(8,128)(2,1)S(1)}, u32[]{:S(2)}, u32[]{:S(2)}) collective-permute-start(bf16[656,128]{1,0:T(8,128)(2,1)S(1)} %get-tuple-element.296), channel_id=1, source_target_pairs={{0,8},{1,9},{2,10},{3,11},{4,12},{5,13},{6,14},{7,15},{8,0},{9,1},... | collective-permute-start | bytes 503816 | tf_op jit(solution)/shard_map/ppermute | solution.py:33
  195.8 15.3 %collective-permute-start.48 = (bf16[656,128]{1,0:T(8,128)(2,1)S(1)}, bf16[656,128]{1,0:T(8,128)(2,1)S(1)}, u32[]{:S(2)}, u32[]{:S(2)}) collective-permute-start(bf16[656,128]{1,0:T(8,128)(2,1)S(1)} %get-tuple-element.295), channel_id=1, source_target_pairs={{0,16},{1,17},{2,18},{3,19},{4,20},{5,21},{6,22},{7,23},{8,24},{9,... | collective-permute-start | bytes 503816 | tf_op jit(solution)/shard_map/ppermute | solution.py:33
  196.9 14.2 %collective-permute-start.49 = (bf16[656,128]{1,0:T(8,128)(2,1)S(1)}, bf16[656,128]{1,0:T(8,128)(2,1)S(1)}, u32[]{:S(2)}, u32[]{:S(2)}) collective-permute-start(bf16[656,128]{1,0:T(8,128)(2,1)S(1)} %get-tuple-element.294), channel_id=1, source_target_pairs={{0,24},{1,25},{2,26},{3,27},{4,28},{5,29},{6,30},{7,31},{8,16},{9,... | collective-permute-start | bytes 503816 | tf_op jit(solution)/shard_map/ppermute | solution.py:33
  211.3 17.9 %collective-permute-start.53 = (bf16[656,128]{1,0:T(8,128)(2,1)S(1)}, bf16[656,128]{1,0:T(8,128)(2,1)S(1)}, u32[]{:S(2)}, u32[]{:S(2)}) collective-permute-start(bf16[656,128]{1,0:T(8,128)(2,1)S(1)} %get-tuple-element.292), channel_id=1, source_target_pairs={{0,8},{1,9},{2,10},{3,11},{4,12},{5,13},{6,14},{7,15},{8,0},{9,1},... | collective-permute-start | bytes 503816 | tf_op jit(solution)/shard_map/ppermute | solution.py:33
  214.6 15.0 %collective-permute-start.54 = (bf16[656,128]{1,0:T(8,128)(2,1)S(1)}, bf16[656,128]{1,0:T(8,128)(2,1)S(1)}, u32[]{:S(2)}, u32[]{:S(2)}) collective-permute-start(bf16[656,128]{1,0:T(8,128)(2,1)S(1)} %get-tuple-element.291), channel_id=1, source_target_pairs={{0,16},{1,17},{2,18},{3,19},{4,20},{5,21},{6,22},{7,23},{8,24},{9,... | collective-permute-start | bytes 503816 | tf_op jit(solution)/shard_map/ppermute | solution.py:33
  215.6 14.0 %collective-permute-start.55 = (bf16[656,128]{1,0:T(8,128)(2,1)S(1)}, bf16[656,128]{1,0:T(8,128)(2,1)S(1)}, u32[]{:S(2)}, u32[]{:S(2)}) collective-permute-start(bf16[656,128]{1,0:T(8,128)(2,1)S(1)} %get-tuple-element.290), channel_id=1, source_target_pairs={{0,24},{1,25},{2,26},{3,27},{4,28},{5,29},{6,30},{7,31},{8,16},{9,... | collective-permute-start | bytes 503816 | tf_op jit(solution)/shard_map/ppermute | solution.py:33
  232.5 19.2 %collective-permute-start.56 = (bf16[4,768,128]{2,1,0:T(8,128)(2,1)S(1)}, bf16[4,768,128]{2,1,0:T(8,128)(2,1)S(1)}, u32[]{:S(2)}, u32[]{:S(2)}) collective-permute-start(bf16[4,768,128]{2,1,0:T(8,128)(2,1)S(1)} %get-tuple-element.215), channel_id=1, source_target_pairs={{0,4},{1,5},{2,6},{3,7},{4,0},{5,1},{6,2},{7,3},{8,12},{9,13},{10,... | collective-permute-start | bytes 2359304 | tf_op jit(solution)/shard_map/ppermute | solution.py:33
  251.8 13.5 %collective-permute-start.62 = (bf16[2,2,128,1024]{3,2,0,1:T(8,128)(2,1)S(1)}, bf16[2,2,128,1024]{3,2,0,1:T(8,128)(2,1)S(1)}, u32[]{:S(2)}, u32[]{:S(2)}) collective-permute-start(bf16[2,2,128,1024]{3,2,0,1:T(8,128)(2,1)S(1)} %fusion.6), channel_id=1, source_target_pairs={{0,1},{1,0},{2,3},{3,2},{4,5},{5,4},{6,7},{7,6},{8,9},{9,8},{10,11... | collective-permute-start | bytes 3145736 | tf_op jit(solution)/shard_map/ppermute | solution.py:56
  252.0 13.1 %collective-permute-start.64 = (bf16[2,1,32,2048]{3,2,1,0:T(8,128)(2,1)S(1)}, bf16[2,1,32,2048]{3,2,1,0:T(8,128)(2,1)S(1)}, u32[]{:S(2)}, u32[]{:S(2)}) collective-permute-start(bf16[2,1,32,2048]{3,2,1,0:T(8,128)(2,1)S(1)} %constant_dynamic-slice_fusion.1), channel_id=1, source_target_pairs={{0,1},{1,0},{2,3},{3,2},{4,5},{5,4},{6,7},{7,6},{8,9},{9,8},{10,11... | collective-permute-start | bytes 786440 | tf_op jit(solution)/shard_map/ppermute | solution.py:40
  253.6 32.6 %collective-permute-start.59 = (bf16[768,128]{1,0:T(8,128)(2,1)}, bf16[768,128]{1,0:T(8,128)(2,1)S(1)}, u32[]{:S(2)}, u32[]{:S(2)}) collective-permute-start(bf16[768,128]{1,0:T(8,128)(2,1)} %get-tuple-element.272), channel_id=1, source_target_pairs={{0,8},{1,9},{2,10},{3,11},{4,12},{5,13},{6,14},{7,15},{8,0},{9,1},... | collective-permute-start | bytes 589832 | tf_op jit(solution)/shard_map/ppermute | solution.py:33
  261.0 25.2 %collective-permute-start.60 = (bf16[768,128]{1,0:T(8,128)(2,1)}, bf16[768,128]{1,0:T(8,128)(2,1)S(1)}, u32[]{:S(2)}, u32[]{:S(2)}) collective-permute-start(bf16[768,128]{1,0:T(8,128)(2,1)} %get-tuple-element.271), channel_id=1, source_target_pairs={{0,16},{1,17},{2,18},{3,19},{4,20},{5,21},{6,22},{7,23},{8,24},{9,... | collective-permute-start | bytes 589832 | tf_op jit(solution)/shard_map/ppermute | solution.py:33
  263.6 22.7 %collective-permute-start.61 = (bf16[768,128]{1,0:T(8,128)(2,1)}, bf16[768,128]{1,0:T(8,128)(2,1)S(1)}, u32[]{:S(2)}, u32[]{:S(2)}) collective-permute-start(bf16[768,128]{1,0:T(8,128)(2,1)} %get-tuple-element.270), channel_id=1, source_target_pairs={{0,24},{1,25},{2,26},{3,27},{4,28},{5,29},{6,30},{7,31},{8,16},{9,... | collective-permute-start | bytes 589832 | tf_op jit(solution)/shard_map/ppermute | solution.py:33
  265.0 21.2 %collective-permute-start.58 = (bf16[4,32,1024]{2,1,0:T(8,128)(2,1)S(1)}, bf16[4,32,1024]{2,1,0:T(8,128)(2,1)}, u32[]{:S(2)}, u32[]{:S(2)}) collective-permute-start(bf16[4,32,1024]{2,1,0:T(8,128)(2,1)S(1)} %get-tuple-element.232), channel_id=1, source_target_pairs={{0,4},{1,5},{2,6},{3,7},{4,0},{5,1},{6,2},{7,3},{8,12},{9,13},{10,... | collective-permute-start | bytes 786440 | tf_op jit(solution)/shard_map/ppermute | solution.py:33
  266.6 16.8 %collective-permute-start.63 = (bf16[2,128,1024]{2,1,0:T(8,128)(2,1)}, bf16[2,128,1024]{2,1,0:T(8,128)(2,1)}, u32[]{:S(2)}, u32[]{:S(2)}) collective-permute-start(bf16[2,128,1024]{2,1,0:T(8,128)(2,1)} %fusion.21), channel_id=1, source_target_pairs={{0,2},{2,0},{1,3},{3,1},{4,6},{6,4},{5,7},{7,5},{8,10},{10,8},{9,1... | collective-permute-start | bytes 1572872 | tf_op jit(solution)/shard_map/ppermute | solution.py:56
  (68 other events, 333.3 us)
